TPU v7x, 32 devices: a whole 2x2x4 slice. The times are simulated.
32 devices in a mesh: tm: 8 (over z, core), space: 4 (over y, x).
Axes of the slice: x: 2, y: 2, z: 4, core: 2. Of those that a mesh axis runs over, the one named last changes fastest.
Arguments:
- snapshots: bfloat16 [4096, 1024], P('space', 'tm'), may hold values from -23 to 23
- energy: bfloat16 [32, 7, 128, 128], P('space'), may hold values from -0.375 to 0.375
- neighbours: int32 [32, 7], P('space'), may hold values from 0 to 31, as said below
- sketch: float32 [3, 256, 128], replicated, may hold values from -0.375 to 0.375
Outputs:
- modes: bfloat16 [4, 8, 4096, 128], P(None, 'tm', 'space')
Inputs may be any that keep to these rules, and one draw needn't show every extreme that they name: `neighbours`: entry [b, k] lies within 2 blocks of b.
All inputs are finite; a program needn't handle non-finite values.
Results may differ from a plain program's by a relative error of at most 0.017.
Values may be sent and summed in bfloat16 or wider, within the bound.
No kernel may reach another device: no remote copies, remote signals or barrier semaphores. Data moves between devices by JAX's collectives and lax.ppermute only.
A program may use at most 64 MiB of HBM per device.

v0:
```python
import jax
import jax.numpy as jnp
from jax import lax
from jax.sharding import PartitionSpec as P

HB = 2


def padded_2(cells, sides, width):
    for axis, dim in sides:
        count = lax.axis_size(axis)
        ends = count - 1
        head = lax.slice_in_dim(cells, 0, width, axis=dim)
        tail = lax.slice_in_dim(cells, cells.shape[dim] - width, cells.shape[dim], axis=dim)
        cells = jnp.concatenate(
            [
                lax.ppermute(tail, axis, [(i, (i + 1) % count) for i in range(ends)]),
                cells,
                lax.ppermute(head, axis, [((i + 1) % count, i) for i in range(ends)]),
            ],
            axis=dim,
        )
    return cells


def from_partner(value, axis, bit):
    mask = 2**bit
    pairs = [(source, source ^ mask) for source in range(lax.axis_size(axis))]
    return lax.ppermute(value, axis, pairs)


def blocked(matrix_rows, block_rows):
    return matrix_rows.reshape(matrix_rows.shape[0] // block_rows, block_rows, matrix_rows.shape[1])


def image_of(padded, source, energy, local_index):
    block_rows = energy.shape[2]
    running = 3.0 * blocked(source, block_rows).astype(jnp.float32)
    for slot_index in range(energy.shape[1]):
        gathered = jnp.take(padded, local_index[:, slot_index], axis=0)
        running = running + jnp.einsum(
            "nij,njw->niw", energy[:, slot_index], gathered, preferred_element_type=jnp.float32
        )
    return running.astype(jnp.bfloat16).reshape(source.shape[0], source.shape[1])


def gram_of(energy_image):
    return jnp.einsum("rc,rd->cd", energy_image, energy_image, preferred_element_type=jnp.float32)


def side_by_side(upper_half, first, second, axis_number):
    return jnp.where(
        upper_half,
        jnp.concatenate([second, first], axis_number),
        jnp.concatenate([first, second], axis_number),
    )


def on_device(snapshots, energy, neighbours, sketch):
    block_rows = energy.shape[2]
    block_count = energy.shape[0]
    rows_dev = snapshots.shape[0]
    total_rows = rows_dev * lax.axis_size("space")
    first_block = lax.axis_index("space") * block_count - HB
    local_index = neighbours - first_block
    window_index = lax.axis_index("tm")
    highest = lax.Precision.HIGHEST
    padded = padded_2(blocked(snapshots, block_rows), (("space", 0),), HB)
    energy_image = image_of(padded, snapshots, energy, local_index)
    gram_matrix = lax.psum(gram_of(energy_image), "space") / total_rows
    lower_factor = jnp.linalg.cholesky(gram_matrix)
    identity = jnp.eye(snapshots.shape[1], dtype=jnp.float32)
    coefficients = jax.scipy.linalg.solve_triangular(lower_factor, identity, lower=True).T.astype(
        jnp.bfloat16
    )
    current = jnp.dot(snapshots, coefficients, preferred_element_type=jnp.float32).astype(
        jnp.bfloat16
    )
    images = jnp.dot(energy_image, coefficients, preferred_element_type=jnp.float32).astype(
        jnp.bfloat16
    )
    levels_kept = [current]
    for tree_level in range(sketch.shape[0]):
        upper_half = window_index // 2**tree_level % 2 == 1
        partner, partner_image = from_partner((current, images), "tm", tree_level)
        joined = side_by_side(upper_half, current, partner, 1)
        joined_image = side_by_side(upper_half, images, partner_image, 1)
        sketch_level = sketch[tree_level]
        gram_matrix = lax.psum(gram_of(joined_image), "space") / total_rows
        columns = jnp.dot(gram_matrix, sketch_level, precision=highest)
        inner_gram = jnp.dot(
            columns.T, jnp.dot(gram_matrix, columns, precision=highest), precision=highest
        )
        lower_factor = jnp.linalg.cholesky(inner_gram)
        coefficients = jax.scipy.linalg.solve_triangular(
            lower_factor, columns.T, lower=True
        ).T.astype(jnp.bfloat16)
        new_modes = jnp.dot(joined, coefficients, preferred_element_type=jnp.float32).astype(
            jnp.bfloat16
        )
        new_image = jnp.dot(joined_image, coefficients, preferred_element_type=jnp.float32).astype(
            jnp.bfloat16
        )
        current = new_modes
        images = new_image
        levels_kept.append(current)
    return jnp.stack(levels_kept)[:, None]


def solution(mesh):
    placed = (P("space", "tm"), P("space", None, None, None), P("space", None), P())
    return jax.shard_map(
        on_device,
        mesh=mesh,
        in_specs=placed,
        out_specs=P(None, "tm", "space", None),
        check_vma=False,
    )
```

profile of v0, /device:TPU:0, one launch (start us, length us, event | category | flops | bytes accessed | tf_op | source)
XLA Modules:
  0.0 343.3 jit_solution(3305505052904443484)
XLA Ops:
  7.4 1.3 collective-permute-start.1
  8.7 5.5 %collective-permute-start = (bf16[2,128,128]{2,1,0:T(8,128)(2,1)S(1)}, bf16[2,128,128]{2,1,0:T(8,128)(2,1)S(1)}, u32[]{:S(2)}, u32[]{:S(2)}) collective-permute-start(bf16[2,128,128]{2,1,0:T(8,128)(2,1)S(1)} %bitcast.162), channel_id=1, source_target_pairs={{0,1},{1,2},{2,3},{4,5},{5,6},{6,7},{8,9},{9,10},{10,11},{12,13},{... | collective-permute-start | bytes 196616 | tf_op jit(solution)/shard_map/ppermute | solution.py:17
  19.9 1.3 gather_fusion.3
  21.8 1.3 gather_fusion.1
  23.7 1.3 convolution_bitcast_fusion.5
  29.1 44.5 %all-reduce.5.cloned.1.call-done = f32[128,128]{0,1:T(8,128)} async-done(((f32[128,128]{0,1:T(8,128)}), f32[128,128]{0,1:T(8,128)}) %all-reduce.5.cloned.1.call-update) | async-done | bytes 65552 | tf_op jit(solution)/shard_map/psum | solution.py:70
  75.4 11.7 %cholesky.74 = f32[128,128]{1,0:T(8,128)S(1)} custom-call(f32[128,128]{1,0:T(8,128)S(1)} %fusion.109), custom_call_target="Cholesky" | custom-call | tf_op jit(solution)/shard_map/jit(cholesky)/cholesky | solution.py:71
  88.4 9.8 %custom-call.9 = f32[1,128,128]{1,2,0:T(8,128)S(1)} custom-call(f32[1,128,128]{2,1,0:T(8,128)S(1)} %fusion.98), custom_call_target="InvertDiagBlocksLowerTriangular" | custom-call | tf_op jit(solution)/shard_map/jit(_solve_triangular)/triangular_solve | solution.py:73
  98.9 1.5 collective-permute-done.3
  100.4 1.1 fusion.97
  101.8 43.0 %all-reduce.7.cloned.1.call-done = f32[256,256]{1,0:T(8,128)} async-done(((f32[256,256]{1,0:T(8,128)}), f32[256,256]{1,0:T(8,128)}) %all-reduce.7.cloned.1.call-update) | async-done | bytes 262160 | tf_op jit(solution)/shard_map/psum | solution.py:89
  144.7 1.3 fusion.72
  146.1 1.3 fusion.70
  147.9 11.7 %cholesky.85 = f32[128,128]{1,0:T(8,128)S(1)} custom-call(f32[128,128]{1,0:T(8,128)S(1)} %fusion.107), custom_call_target="Cholesky" | custom-call | tf_op jit(solution)/shard_map/jit(cholesky)/cholesky | solution.py:94
  161.0 9.8 %custom-call.12 = f32[1,128,128]{1,2,0:T(8,128)S(1)} custom-call(f32[1,128,128]{2,1,0:T(8,128)S(1)} %fusion.99), custom_call_target="InvertDiagBlocksLowerTriangular" | custom-call | tf_op jit(solution)/shard_map/jit(_solve_triangular)/triangular_solve | solution.py:95
  171.4 1.6 collective-permute-start.5
  172.9 6.1 %collective-permute-done.5 = bf16[1024,128]{0,1:T(8,128)(2,1)S(1)} collective-permute-done((bf16[1024,128]{0,1:T(8,128)(2,1)S(1)}, bf16[1024,128]{0,1:T(8,128)(2,1)S(1)}, u32[]{:S(2)}, u32[]{:S(2)}) %collective-permute-start.5) | collective-permute-done | bytes 262176 | tf_op jit(solution)/shard_map/ppermute | solution.py:29
  180.8 42.6 %all-reduce.9.cloned.1.call-done = f32[256,256]{1,0:T(8,128)} async-done(((f32[256,256]{1,0:T(8,128)}), f32[256,256]{1,0:T(8,128)}) %all-reduce.9.cloned.1.call-update) | async-done | bytes 262160 | tf_op jit(solution)/shard_map/psum | solution.py:89
  223.3 1.3 fusion.68
  224.7 1.3 fusion.66
  226.5 11.7 %cholesky.96 = f32[128,128]{1,0:T(8,128)S(1)} custom-call(f32[128,128]{1,0:T(8,128)S(1)} %fusion.105), custom_call_target="Cholesky" | custom-call | tf_op jit(solution)/shard_map/jit(cholesky)/cholesky | solution.py:94
  239.6 9.8 %custom-call.13 = f32[1,128,128]{1,2,0:T(8,128)S(1)} custom-call(f32[1,128,128]{2,1,0:T(8,128)S(1)} %fusion.100), custom_call_target="InvertDiagBlocksLowerTriangular" | custom-call | tf_op jit(solution)/shard_map/jit(_solve_triangular)/triangular_solve | solution.py:95
  250.0 2.5 collective-permute-start.7
  252.8 1.6 collective-permute-start.4
  254.3 9.9 %collective-permute-done.7 = bf16[1024,128]{0,1:T(8,128)(2,1)S(1)} collective-permute-done((bf16[1024,128]{0,1:T(8,128)(2,1)S(1)}, bf16[1024,128]{0,1:T(8,128)(2,1)S(1)}, u32[]{:S(2)}, u32[]{:S(2)}) %collective-permute-start.7) | collective-permute-done | bytes 262176 | tf_op jit(solution)/shard_map/ppermute | solution.py:29
  264.2 1.1 fusion.19
  266.0 42.4 %all-reduce.11.cloned.1.call-done = f32[256,256]{1,0:T(8,128)} async-done(((f32[256,256]{1,0:T(8,128)}), f32[256,256]{1,0:T(8,128)}) %all-reduce.11.cloned.1.call-update) | async-done | bytes 262160 | tf_op jit(solution)/shard_map/psum | solution.py:89
  308.4 1.3 fusion.64
  309.8 1.3 fusion.62
  311.6 12.0 %cholesky.107 = f32[128,128]{1,0:T(8,128)S(1)} custom-call(f32[128,128]{1,0:T(8,128)S(1)} %fusion.103), custom_call_target="Cholesky" | custom-call | tf_op jit(solution)/shard_map/jit(cholesky)/cholesky | solution.py:94
  324.9 9.8 %custom-call.14 = f32[1,128,128]{1,2,0:T(8,128)S(1)} custom-call(f32[1,128,128]{2,1,0:T(8,128)S(1)} %fusion.101), custom_call_target="InvertDiagBlocksLowerTriangular" | custom-call | tf_op jit(solution)/shard_map/jit(_solve_triangular)/triangular_solve | solution.py:95
  335.5 1.3 copy.19
  (94 shorter events, 25.7 us)
Async XLA Ops:
  6.5 67.0 %all-reduce.5.cloned.1.call-start = ((), (), s32[]{:S(2)}) async-start(), calls=%async_computation | async-start | bytes 131072 | tf_op jit(solution)/shard_map/psum | solution.py:70
  7.4 9.6 %collective-permute-start.1 = (bf16[2,128,128]{2,1,0:T(8,128)(2,1)S(1)}, bf16[2,128,128]{2,1,0:T(8,128)(2,1)S(1)}, u32[]{:S(2)}, u32[]{:S(2)}) collective-permute-start(bf16[2,128,128]{2,1,0:T(8,128)(2,1)S(1)} %bitcast.163), channel_id=1, source_target_pairs={{1,0},{2,1},{3,2},{5,4},{6,5},{7,6},{9,8},{10,9},{11,10},{13,12},{... | collective-permute-start | bytes 196616 | tf_op jit(solution)/shard_map/ppermute | solution.py:19
  8.7 8.3 %collective-permute-start = (bf16[2,128,128]{2,1,0:T(8,128)(2,1)S(1)}, bf16[2,128,128]{2,1,0:T(8,128)(2,1)S(1)}, u32[]{:S(2)}, u32[]{:S(2)}) collective-permute-start(bf16[2,128,128]{2,1,0:T(8,128)(2,1)S(1)} %bitcast.162), channel_id=1, source_target_pairs={{0,1},{1,2},{2,3},{4,5},{5,6},{6,7},{8,9},{9,10},{10,11},{12,13},{... | collective-permute-start | bytes 196616 | tf_op jit(solution)/shard_map/ppermute | solution.py:17
  18.1 5.6 %copy-start.1 = (bf16[8,7,128,128]{3,2,1,0:T(8,128)(2,1)S(1)}, bf16[8,7,128,128]{3,2,1,0:T(8,128)(2,1)}, u32[]{:S(2)}) copy-start(bf16[8,7,128,128]{3,2,1,0:T(8,128)(2,1)} %param.10) | copy-start | bytes 5505028
  23.7 2.2 copy-start.2
  26.8 1.0 copy-start
  26.8 0.9 copy-start.4
  29.0 115.7 %all-reduce.7.cloned.1.call-start = ((), (), s32[]{:S(2)}) async-start(), calls=%async_computation.1 | async-start | bytes 524288 | tf_op jit(solution)/shard_map/psum | solution.py:89
  87.1 57.6 %copy-start.3 = (f32[3,256,128]{2,1,0:T(8,128)S(1)}, f32[3,256,128]{2,1,0:T(8,128)}, u32[]{:S(2)}) copy-start(f32[3,256,128]{2,1,0:T(8,128)} %param.12) | copy-start | bytes 1179652
  98.8 1.6 collective-permute-start.3
  101.5 121.8 %all-reduce.9.cloned.1.call-start = ((), (), s32[]{:S(2)}) async-start(), calls=%async_computation.2 | async-start | bytes 524288 | tf_op jit(solution)/shard_map/psum | solution.py:89
  171.4 7.6 %collective-permute-start.5 = (bf16[1024,128]{0,1:T(8,128)(2,1)S(1)}, bf16[1024,128]{0,1:T(8,128)(2,1)S(1)}, u32[]{:S(2)}, u32[]{:S(2)}) collective-permute-start(bf16[1024,128]{0,1:T(8,128)(2,1)S(1)} %convolution_convert_fusion.3), channel_id=1, source_target_pairs={{0,8},{4,12},{8,0},{12,4},{16,24},{20,28},{24,16},{28,20},{1,9},{5... | collective-permute-start | bytes 786440 | tf_op jit(solution)/shard_map/ppermute | solution.py:29
  180.2 128.3 %all-reduce.11.cloned.1.call-start = ((), (), s32[]{:S(2)}) async-start(), calls=%async_computation.3 | async-start | bytes 524288 | tf_op jit(solution)/shard_map/psum | solution.py:89
  180.7 71.8 %collective-permute-start.2 = (bf16[1024,128]{0,1:T(8,128)(2,1)S(1)}, bf16[1024,128]{0,1:T(8,128)(2,1)S(1)}, u32[]{:S(2)}, u32[]{:S(2)}) collective-permute-start(bf16[1024,128]{0,1:T(8,128)(2,1)S(1)} %bitcast.157), channel_id=1, source_target_pairs={{0,4},{4,0},{8,12},{12,8},{16,20},{20,16},{24,28},{28,24},{1,5},{5... | collective-permute-start | bytes 786440 | tf_op jit(solution)/shard_map/ppermute | solution.py:29
  250.0 14.3 %collective-permute-start.7 = (bf16[1024,128]{0,1:T(8,128)(2,1)S(1)}, bf16[1024,128]{0,1:T(8,128)(2,1)S(1)}, u32[]{:S(2)}, u32[]{:S(2)}) collective-permute-start(bf16[1024,128]{0,1:T(8,128)(2,1)S(1)} %convolution_convert_fusion.1), channel_id=1, source_target_pairs={{0,16},{4,20},{8,24},{12,28},{16,0},{20,4},{24,8},{28,12},{1,17},{... | collective-permute-start | bytes 786440 | tf_op jit(solution)/shard_map/ppermute | solution.py:29
  252.8 12.6 %collective-permute-start.4 = (bf16[1024,128]{0,1:T(8,128)(2,1)S(1)}, bf16[1024,128]{0,1:T(8,128)(2,1)S(1)}, u32[]{:S(2)}, u32[]{:S(2)}) collective-permute-start(bf16[1024,128]{0,1:T(8,128)(2,1)S(1)} %convolution_convert_fusion.4), channel_id=1, source_target_pairs={{0,8},{4,12},{8,0},{12,4},{16,24},{20,28},{24,16},{28,20},{1,9},{5... | collective-permute-start | bytes 786440 | tf_op jit(solution)/shard_map/ppermute | solution.py:29
  265.7 69.4 %collective-permute-start.6 = (bf16[1024,128]{0,1:T(8,128)(2,1)S(1)}, bf16[1024,128]{0,1:T(8,128)(2,1)S(1)}, u32[]{:S(2)}, u32[]{:S(2)}) collective-permute-start(bf16[1024,128]{0,1:T(8,128)(2,1)S(1)} %convolution_convert_fusion.2), channel_id=1, source_target_pairs={{0,16},{4,20},{8,24},{12,28},{16,0},{20,4},{24,8},{28,12},{1,17},{... | collective-permute-start | bytes 786440 | tf_op jit(solution)/shard_map/ppermute | solution.py:29
Sparse Core Ops, SparseCore 0:
  29.2 44.3 all-reduce.4
  101.7 43.0 all-reduce.6
  180.3 43.0 all-reduce.8
  265.5 42.9 all-reduce.10
where the time goes:
time: 344 us; the launch traced here: 343 us
  waiting for transfers between devices  190 us (55%)
  other arithmetic  97 us (28%)
  matrix products  20.8 us (6%)
  between operations  13.7 us (4%)
  starting transfers between devices  13.4 us (4%)
  local copies, waits for them, and re-layouts  8.4 us (2%)
    psum x3, waiting for transfers between devices, on_device(): gram_matrix = lax.psum(gram_of(joined_image), 'space') / total_rows  128 us
    psum x1, waiting for transfers between devices, on_device(): gram_matrix = lax.psum(gram_of(energy_image), 'space') / total_rows  44.5 us
    another operation x9, other arithmetic, on_device(): lower_factor = jnp.linalg.cholesky(inner_gram)  37.4 us
    another operation x6, other arithmetic, on_device(): jax.scipy.linalg.solve_triangular(lower_factor, columns.T, lower=True)  31.4 us
    ppermute x6, waiting for transfers between devices, from_partner(): return lax.ppermute(value, axis, pairs)  17.5 us
    another operation x3, other arithmetic, on_device(): lower_factor = jnp.linalg.cholesky(gram_matrix)  12.4 us
    another operation x2, other arithmetic, on_device(): jax.scipy.linalg.solve_triangular(lower_factor, identity, lower=True)  10.5 us
  transfers between devices with their start and end apart: 12, of which 7 were waited for; matrix products, arithmetic and copies ran while one was open for 17% of the time, Pallas kernels for 0%

commit v1 on v0

--- a/solution.py
+++ b/solution.py
@@ -27,6 +27,23 @@
     mask = 2**bit
     pairs = [(source, source ^ mask) for source in range(lax.axis_size(axis))]
     return lax.ppermute(value, axis, pairs)
+
+
+def sum_over(value, axis):
+    count = lax.axis_size(axis)
+    done = 1
+    while done < count:
+        radix = 4 if count // done % 4 == 0 else 2
+        parts = [value]
+        for step in range(1, radix):
+            mask = step * done
+            pairs = [(source, source ^ mask) for source in range(count)]
+            parts.append(lax.ppermute(value, axis, pairs))
+        value = parts[0] + parts[1]
+        if radix == 4:
+            value = value + (parts[2] + parts[3])
+        done *= radix
+    return value
 
 
 def blocked(matrix_rows, block_rows):
@@ -67,7 +84,7 @@
     highest = lax.Precision.HIGHEST
     padded = padded_2(blocked(snapshots, block_rows), (("space", 0),), HB)
     energy_image = image_of(padded, snapshots, energy, local_index)
-    gram_matrix = lax.psum(gram_of(energy_image), "space") / total_rows
+    gram_matrix = sum_over(gram_of(energy_image), "space") / total_rows
     lower_factor = jnp.linalg.cholesky(gram_matrix)
     identity = jnp.eye(snapshots.shape[1], dtype=jnp.float32)
     coefficients = jax.scipy.linalg.solve_triangular(lower_factor, identity, lower=True).T.astype(
@@ -86,7 +103,7 @@
         joined = side_by_side(upper_half, current, partner, 1)
         joined_image = side_by_side(upper_half, images, partner_image, 1)
         sketch_level = sketch[tree_level]
-        gram_matrix = lax.psum(gram_of(joined_image), "space") / total_rows
+        gram_matrix = sum_over(gram_of(joined_image), "space") / total_rows
         columns = jnp.dot(gram_matrix, sketch_level, precision=highest)
         inner_gram = jnp.dot(
             columns.T, jnp.dot(gram_matrix, columns, precision=highest), precision=highest

time: 344 us -> 199 us (0.58)
  waiting for transfers between devices: 190 us -> 53 us
  starting transfers between devices: 13.4 us -> 29 us
  between operations: 13.7 us -> 0.6 us
  matrix products: 20.8 us -> 12.4 us
    psum x4 -> x0, waiting for transfers between devices: 172 us -> none  [the longest x3 128 us: on_device(): gram_matrix = lax.psum(gram_of(joined_image), 'space') / total_rows]
    ppermute x0 -> x12, waiting for transfers between devices: none -> 34.7 us  [sum_over(): parts.append(lax.ppermute(value, axis, pairs))]
    ppermute x0 -> x12, starting transfers between devices: none -> 16 us  [sum_over(): parts.append(lax.ppermute(value, axis, pairs))]
  transfers between devices with their start and end apart: 12 -> 20, of which waited for: 7 -> 12; matrix products, arithmetic and copies ran while one was open for 17% -> 27% of each run, Pallas kernels for 0% -> 0%
where the time goes in v1:
time: 199 us
  other arithmetic  95.7 us (48%)
  waiting for transfers between devices  53 us (27%)
  starting transfers between devices  29 us (15%)
  matrix products  12.4 us (6%)
  local copies, waits for them, and re-layouts  8.4 us (4%)
    another operation x9, other arithmetic, on_device(): lower_factor = jnp.linalg.cholesky(inner_gram)  37.3 us
    ppermute x12, waiting for transfers between devices, sum_over(): parts.append(lax.ppermute(value, axis, pairs))  34.7 us
    another operation x6, other arithmetic, on_device(): jax.scipy.linalg.solve_triangular(lower_factor, columns.T, lower=True)  31.6 us
    ppermute x6, waiting for transfers between devices, from_partner(): return lax.ppermute(value, axis, pairs)  18.3 us
    ppermute x12, starting transfers between devices, sum_over(): parts.append(lax.ppermute(value, axis, pairs))  16 us
    another operation x3, other arithmetic, on_device(): lower_factor = jnp.linalg.cholesky(gram_matrix)  12.4 us
    another operation x2, other arithmetic, on_device(): jax.scipy.linalg.solve_triangular(lower_factor, identity, lower=True)  10.5 us
    ppermute x6, starting transfers between devices, from_partner(): return lax.ppermute(value, axis, pairs)  6.14 us
  transfers between devices with their start and end apart: 20, of which 12 were waited for; matrix products, arithmetic and copies ran while one was open for 27% of the time, Pallas kernels for 0%

profile of v1, /device:TPU:0, one launch (start us, length us, event | category | flops | bytes accessed | tf_op | source)
XLA Modules:
  0.0 199.0 jit_solution(15304711543044463387)
XLA Ops:
  0.9 1.3 collective-permute-start.1
  2.2 5.5 %collective-permute-start = (bf16[2,128,128]{2,1,0:T(8,128)(2,1)S(1)}, bf16[2,128,128]{2,1,0:T(8,128)(2,1)S(1)}, u32[]{:S(2)}, u32[]{:S(2)}) collective-permute-start(bf16[2,128,128]{2,1,0:T(8,128)(2,1)S(1)} %bitcast.172), channel_id=1, source_target_pairs={{0,1},{1,2},{2,3},{4,5},{5,6},{6,7},{8,9},{9,10},{10,11},{12,13},{... | collective-permute-start | bytes 196616 | tf_op jit(solution)/shard_map/ppermute | solution.py:17
  17.1 1.3 convolution_bitcast_fusion.5
  21.8 3.8 %collective-permute-start.3 = (f32[128,128]{0,1:T(8,128)S(1)}, f32[128,128]{0,1:T(8,128)S(1)}, u32[]{:S(2)}, u32[]{:S(2)}) collective-permute-start(f32[128,128]{0,1:T(8,128)S(1)} %convolution_bitcast_fusion.7), channel_id=1, source_target_pairs={{0,2},{1,3},{2,0},{3,1},{4,6},{5,7},{6,4},{7,5},{8,10},{9,11},{10,... | collective-permute-start | bytes 196616 | tf_op jit(solution)/shard_map/ppermute | solution.py:41
  25.7 1.5 collective-permute-start.4
  27.2 1.4 collective-permute-done.3
  28.6 1.3 collective-permute-done.2
  31.0 11.7 %cholesky.74 = f32[128,128]{1,0:T(8,128)S(1)} custom-call(f32[128,128]{1,0:T(8,128)S(1)} %fusion.94), custom_call_target="Cholesky" | custom-call | tf_op jit(solution)/shard_map/jit(cholesky)/cholesky | solution.py:88
  44.0 9.8 %custom-call.9 = f32[1,128,128]{1,2,0:T(8,128)S(1)} custom-call(f32[1,128,128]{2,1,0:T(8,128)S(1)} %fusion.83), custom_call_target="InvertDiagBlocksLowerTriangular" | custom-call | tf_op jit(solution)/shard_map/jit(_solve_triangular)/triangular_solve | solution.py:90
  54.5 1.5 collective-permute-done.6
  56.4 1.6 collective-permute-start.9
  58.0 1.9 collective-permute-start.8
  60.0 6.6 %collective-permute-done.9 = f32[256,256]{1,0:T(8,128)S(1)} collective-permute-done((f32[256,256]{1,0:T(8,128)S(1)}, f32[256,256]{1,0:T(8,128)S(1)}, u32[]{:S(2)}, u32[]{:S(2)}) %collective-permute-start.9) | collective-permute-done | bytes 262176 | tf_op jit(solution)/shard_map/ppermute | solution.py:41
  66.6 4.7 %collective-permute-done.8 = f32[256,256]{1,0:T(8,128)S(1)} collective-permute-done((f32[256,256]{1,0:T(8,128)S(1)}, f32[256,256]{1,0:T(8,128)S(1)}, u32[]{:S(2)}, u32[]{:S(2)}) %collective-permute-start.8) | collective-permute-done | bytes 262176 | tf_op jit(solution)/shard_map/ppermute | solution.py:41
  72.7 11.9 %cholesky.85 = f32[128,128]{1,0:T(8,128)S(1)} custom-call(f32[128,128]{1,0:T(8,128)S(1)} %fusion.92), custom_call_target="Cholesky" | custom-call | tf_op jit(solution)/shard_map/jit(cholesky)/cholesky | solution.py:111
  85.9 9.8 %custom-call.12 = f32[1,128,128]{1,2,0:T(8,128)S(1)} custom-call(f32[1,128,128]{2,1,0:T(8,128)S(1)} %fusion.84), custom_call_target="InvertDiagBlocksLowerTriangular" | custom-call | tf_op jit(solution)/shard_map/jit(_solve_triangular)/triangular_solve | solution.py:112
  96.3 1.6 collective-permute-start.11
  98.0 6.7 %collective-permute-done.11 = bf16[1024,128]{0,1:T(8,128)(2,1)S(1)} collective-permute-done((bf16[1024,128]{0,1:T(8,128)(2,1)S(1)}, bf16[1024,128]{0,1:T(8,128)(2,1)S(1)}, u32[]{:S(2)}, u32[]{:S(2)}) %collective-permute-start.11) | collective-permute-done | bytes 262176 | tf_op jit(solution)/shard_map/ppermute | solution.py:29
  105.1 1.6 collective-permute-start.14
  108.9 6.3 %collective-permute-done.14 = f32[256,256]{1,0:T(8,128)S(1)} collective-permute-done((f32[256,256]{1,0:T(8,128)S(1)}, f32[256,256]{1,0:T(8,128)S(1)}, u32[]{:S(2)}, u32[]{:S(2)}) %collective-permute-start.14) | collective-permute-done | bytes 262176 | tf_op jit(solution)/shard_map/ppermute | solution.py:41
  115.2 3.6 %collective-permute-done.13 = f32[256,256]{1,0:T(8,128)S(1)} collective-permute-done((f32[256,256]{1,0:T(8,128)S(1)}, f32[256,256]{1,0:T(8,128)S(1)}, u32[]{:S(2)}, u32[]{:S(2)}) %collective-permute-start.13) | collective-permute-done | bytes 262176 | tf_op jit(solution)/shard_map/ppermute | solution.py:41
  120.2 11.7 %cholesky.96 = f32[128,128]{1,0:T(8,128)S(1)} custom-call(f32[128,128]{1,0:T(8,128)S(1)} %fusion.90), custom_call_target="Cholesky" | custom-call | tf_op jit(solution)/shard_map/jit(cholesky)/cholesky | solution.py:111
  133.3 10.0 %custom-call.13 = f32[1,128,128]{1,2,0:T(8,128)S(1)} custom-call(f32[1,128,128]{2,1,0:T(8,128)S(1)} %fusion.85), custom_call_target="InvertDiagBlocksLowerTriangular" | custom-call | tf_op jit(solution)/shard_map/jit(_solve_triangular)/triangular_solve | solution.py:112
  143.9 2.7 %collective-permute-start.16 = (bf16[1024,128]{0,1:T(8,128)(2,1)S(1)}, bf16[1024,128]{0,1:T(8,128)(2,1)S(1)}, u32[]{:S(2)}, u32[]{:S(2)}) collective-permute-start(bf16[1024,128]{0,1:T(8,128)(2,1)S(1)} %convolution_convert_fusion.1), channel_id=1, source_target_pairs={{0,16},{4,20},{8,24},{12,28},{16,0},{20,4},{24,8},{28,12},{1,17},{... | collective-permute-start | bytes 786440 | tf_op jit(solution)/shard_map/ppermute | solution.py:29
  146.8 1.6 collective-permute-start.10
  148.4 10.1 %collective-permute-done.16 = bf16[1024,128]{0,1:T(8,128)(2,1)S(1)} collective-permute-done((bf16[1024,128]{0,1:T(8,128)(2,1)S(1)}, bf16[1024,128]{0,1:T(8,128)(2,1)S(1)}, u32[]{:S(2)}, u32[]{:S(2)}) %collective-permute-start.16) | collective-permute-done | bytes 262176 | tf_op jit(solution)/shard_map/ppermute | solution.py:29
  159.0 1.4 collective-permute-start.19
  162.9 6.2 %collective-permute-done.19 = f32[256,256]{1,0:T(8,128)S(1)} collective-permute-done((f32[256,256]{1,0:T(8,128)S(1)}, f32[256,256]{1,0:T(8,128)S(1)}, u32[]{:S(2)}, u32[]{:S(2)}) %collective-permute-start.19) | collective-permute-done | bytes 262176 | tf_op jit(solution)/shard_map/ppermute | solution.py:41
  169.1 3.6 %collective-permute-done.18 = f32[256,256]{1,0:T(8,128)S(1)} collective-permute-done((f32[256,256]{1,0:T(8,128)S(1)}, f32[256,256]{1,0:T(8,128)S(1)}, u32[]{:S(2)}, u32[]{:S(2)}) %collective-permute-start.18) | collective-permute-done | bytes 262176 | tf_op jit(solution)/shard_map/ppermute | solution.py:41
  174.1 11.7 %cholesky.107 = f32[128,128]{1,0:T(8,128)S(1)} custom-call(f32[128,128]{1,0:T(8,128)S(1)} %fusion.88), custom_call_target="Cholesky" | custom-call | tf_op jit(solution)/shard_map/jit(cholesky)/cholesky | solution.py:111
  187.1 9.8 %custom-call.14 = f32[1,128,128]{1,2,0:T(8,128)S(1)} custom-call(f32[1,128,128]{2,1,0:T(8,128)S(1)} %fusion.86), custom_call_target="InvertDiagBlocksLowerTriangular" | custom-call | tf_op jit(solution)/shard_map/jit(_solve_triangular)/triangular_solve | solution.py:112
  197.7 1.3 copy.22
  (109 shorter events, 32.7 us)
Async XLA Ops:
  0.9 9.6 %collective-permute-start.1 = (bf16[2,128,128]{2,1,0:T(8,128)(2,1)S(1)}, bf16[2,128,128]{2,1,0:T(8,128)(2,1)S(1)}, u32[]{:S(2)}, u32[]{:S(2)}) collective-permute-start(bf16[2,128,128]{2,1,0:T(8,128)(2,1)S(1)} %bitcast.173), channel_id=1, source_target_pairs={{1,0},{2,1},{3,2},{5,4},{6,5},{7,6},{9,8},{10,9},{11,10},{13,12},{... | collective-permute-start | bytes 196616 | tf_op jit(solution)/shard_map/ppermute | solution.py:19
  2.2 8.3 %collective-permute-start = (bf16[2,128,128]{2,1,0:T(8,128)(2,1)S(1)}, bf16[2,128,128]{2,1,0:T(8,128)(2,1)S(1)}, u32[]{:S(2)}, u32[]{:S(2)}) collective-permute-start(bf16[2,128,128]{2,1,0:T(8,128)(2,1)S(1)} %bitcast.172), channel_id=1, source_target_pairs={{0,1},{1,2},{2,3},{4,5},{5,6},{6,7},{8,9},{9,10},{10,11},{12,13},{... | collective-permute-start | bytes 196616 | tf_op jit(solution)/shard_map/ppermute | solution.py:17
  11.5 5.6 %copy-start.1 = (bf16[8,7,128,128]{3,2,1,0:T(8,128)(2,1)S(1)}, bf16[8,7,128,128]{3,2,1,0:T(8,128)(2,1)}, u32[]{:S(2)}) copy-start(bf16[8,7,128,128]{3,2,1,0:T(8,128)(2,1)} %param.10) | copy-start | bytes 5505028
  17.1 2.2 %copy-start.2 = (bf16[8,128,128]{2,1,0:T(8,128)(2,1)S(1)}, bf16[8,128,128]{2,1,0:T(8,128)(2,1)}, u32[]{:S(2)}) copy-start(bf16[8,128,128]{2,1,0:T(8,128)(2,1)} %gather_fusion.3) | copy-start | bytes 786436
  20.2 1.0 copy-start
  20.2 0.9 copy-start.4
  21.8 6.8 %collective-permute-start.3 = (f32[128,128]{0,1:T(8,128)S(1)}, f32[128,128]{0,1:T(8,128)S(1)}, u32[]{:S(2)}, u32[]{:S(2)}) collective-permute-start(f32[128,128]{0,1:T(8,128)S(1)} %convolution_bitcast_fusion.7), channel_id=1, source_target_pairs={{0,2},{1,3},{2,0},{3,1},{4,6},{5,7},{6,4},{7,5},{8,10},{9,11},{10,... | collective-permute-start | bytes 196616 | tf_op jit(solution)/shard_map/ppermute | solution.py:41
  25.7 4.3 %collective-permute-start.2 = (f32[128,128]{0,1:T(8,128)S(1)}, f32[128,128]{0,1:T(8,128)S(1)}, u32[]{:S(2)}, u32[]{:S(2)}) collective-permute-start(f32[128,128]{0,1:T(8,128)S(1)} %convolution_bitcast_fusion.7), channel_id=1, source_target_pairs={{0,1},{1,0},{2,3},{3,2},{4,5},{5,4},{6,7},{7,6},{8,9},{9,8},{10,11... | collective-permute-start | bytes 196616 | tf_op jit(solution)/shard_map/ppermute | solution.py:41
  25.7 5.2 %collective-permute-start.4 = (f32[128,128]{0,1:T(8,128)S(1)}, f32[128,128]{0,1:T(8,128)S(1)}, u32[]{:S(2)}, u32[]{:S(2)}) collective-permute-start(f32[128,128]{0,1:T(8,128)S(1)} %convolution_bitcast_fusion.7), channel_id=1, source_target_pairs={{0,3},{1,2},{2,1},{3,0},{4,7},{5,6},{6,5},{7,4},{8,11},{9,10},{10,... | collective-permute-start | bytes 196616 | tf_op jit(solution)/shard_map/ppermute | solution.py:41
  54.4 1.6 collective-permute-start.6
  54.5 16.9 %copy-start.3 = (f32[3,256,128]{2,1,0:T(8,128)S(1)}, f32[3,256,128]{2,1,0:T(8,128)}, u32[]{:S(2)}) copy-start(f32[3,256,128]{2,1,0:T(8,128)} %param.12) | copy-start | bytes 1179652
  56.4 10.2 %collective-permute-start.9 = (f32[256,256]{1,0:T(8,128)S(1)}, f32[256,256]{1,0:T(8,128)S(1)}, u32[]{:S(2)}, u32[]{:S(2)}) collective-permute-start(f32[256,256]{1,0:T(8,128)S(1)} %fusion.82), channel_id=1, source_target_pairs={{0,3},{1,2},{2,1},{3,0},{4,7},{5,6},{6,5},{7,4},{8,11},{9,10},{10,... | collective-permute-start | bytes 786440 | tf_op jit(solution)/shard_map/ppermute | solution.py:41
  58.0 13.3 %collective-permute-start.8 = (f32[256,256]{1,0:T(8,128)S(1)}, f32[256,256]{1,0:T(8,128)S(1)}, u32[]{:S(2)}, u32[]{:S(2)}) collective-permute-start(f32[256,256]{1,0:T(8,128)S(1)} %fusion.82), channel_id=1, source_target_pairs={{0,2},{1,3},{2,0},{3,1},{4,6},{5,7},{6,4},{7,5},{8,10},{9,11},{10,... | collective-permute-start | bytes 786440 | tf_op jit(solution)/shard_map/ppermute | solution.py:41
  59.9 11.4 %collective-permute-start.7 = (f32[256,256]{1,0:T(8,128)S(1)}, f32[256,256]{1,0:T(8,128)S(1)}, u32[]{:S(2)}, u32[]{:S(2)}) collective-permute-start(f32[256,256]{1,0:T(8,128)S(1)} %fusion.82), channel_id=1, source_target_pairs={{0,1},{1,0},{2,3},{3,2},{4,5},{5,4},{6,7},{7,6},{8,9},{9,8},{10,11... | collective-permute-start | bytes 786440 | tf_op jit(solution)/shard_map/ppermute | solution.py:41
  96.3 8.3 %collective-permute-start.11 = (bf16[1024,128]{0,1:T(8,128)(2,1)S(1)}, bf16[1024,128]{0,1:T(8,128)(2,1)S(1)}, u32[]{:S(2)}, u32[]{:S(2)}) collective-permute-start(bf16[1024,128]{0,1:T(8,128)(2,1)S(1)} %convolution_convert_fusion.3), channel_id=1, source_target_pairs={{0,8},{4,12},{8,0},{12,4},{16,24},{20,28},{24,16},{28,20},{1,9},{5... | collective-permute-start | bytes 786440 | tf_op jit(solution)/shard_map/ppermute | solution.py:29
  105.1 10.1 %collective-permute-start.14 = (f32[256,256]{1,0:T(8,128)S(1)}, f32[256,256]{1,0:T(8,128)S(1)}, u32[]{:S(2)}, u32[]{:S(2)}) collective-permute-start(f32[256,256]{1,0:T(8,128)S(1)} %fusion.81), channel_id=1, source_target_pairs={{0,3},{1,2},{2,1},{3,0},{4,7},{5,6},{6,5},{7,4},{8,11},{9,10},{10,... | collective-permute-start | bytes 786440 | tf_op jit(solution)/shard_map/ppermute | solution.py:41
  106.7 12.2 %collective-permute-start.13 = (f32[256,256]{1,0:T(8,128)S(1)}, f32[256,256]{1,0:T(8,128)S(1)}, u32[]{:S(2)}, u32[]{:S(2)}) collective-permute-start(f32[256,256]{1,0:T(8,128)S(1)} %fusion.81), channel_id=1, source_target_pairs={{0,2},{1,3},{2,0},{3,1},{4,6},{5,7},{6,4},{7,5},{8,10},{9,11},{10,... | collective-permute-start | bytes 786440 | tf_op jit(solution)/shard_map/ppermute | solution.py:41
  107.6 11.2 %collective-permute-start.12 = (f32[256,256]{1,0:T(8,128)S(1)}, f32[256,256]{1,0:T(8,128)S(1)}, u32[]{:S(2)}, u32[]{:S(2)}) collective-permute-start(f32[256,256]{1,0:T(8,128)S(1)} %fusion.81), channel_id=1, source_target_pairs={{0,1},{1,0},{2,3},{3,2},{4,5},{5,4},{6,7},{7,6},{8,9},{9,8},{10,11... | collective-permute-start | bytes 786440 | tf_op jit(solution)/shard_map/ppermute | solution.py:41
  108.9 37.7 %collective-permute-start.5 = (bf16[1024,128]{0,1:T(8,128)(2,1)S(1)}, bf16[1024,128]{0,1:T(8,128)(2,1)S(1)}, u32[]{:S(2)}, u32[]{:S(2)}) collective-permute-start(bf16[1024,128]{0,1:T(8,128)(2,1)S(1)} %bitcast.167), channel_id=1, source_target_pairs={{0,4},{4,0},{8,12},{12,8},{16,20},{20,16},{24,28},{28,24},{1,5},{5... | collective-permute-start | bytes 786440 | tf_op jit(solution)/shard_map/ppermute | solution.py:29
  143.9 14.7 %collective-permute-start.16 = (bf16[1024,128]{0,1:T(8,128)(2,1)S(1)}, bf16[1024,128]{0,1:T(8,128)(2,1)S(1)}, u32[]{:S(2)}, u32[]{:S(2)}) collective-permute-start(bf16[1024,128]{0,1:T(8,128)(2,1)S(1)} %convolution_convert_fusion.1), channel_id=1, source_target_pairs={{0,16},{4,20},{8,24},{12,28},{16,0},{20,4},{24,8},{28,12},{1,17},{... | collective-permute-start | bytes 786440 | tf_op jit(solution)/shard_map/ppermute | solution.py:29
  146.8 15.7 %collective-permute-start.10 = (bf16[1024,128]{0,1:T(8,128)(2,1)S(1)}, bf16[1024,128]{0,1:T(8,128)(2,1)S(1)}, u32[]{:S(2)}, u32[]{:S(2)}) collective-permute-start(bf16[1024,128]{0,1:T(8,128)(2,1)S(1)} %convolution_convert_fusion.4), channel_id=1, source_target_pairs={{0,8},{4,12},{8,0},{12,4},{16,24},{20,28},{24,16},{28,20},{1,9},{5... | collective-permute-start | bytes 786440 | tf_op jit(solution)/shard_map/ppermute | solution.py:29
  159.0 10.2 %collective-permute-start.19 = (f32[256,256]{1,0:T(8,128)S(1)}, f32[256,256]{1,0:T(8,128)S(1)}, u32[]{:S(2)}, u32[]{:S(2)}) collective-permute-start(f32[256,256]{1,0:T(8,128)S(1)} %fusion.19), channel_id=1, source_target_pairs={{0,3},{1,2},{2,1},{3,0},{4,7},{5,6},{6,5},{7,4},{8,11},{9,10},{10,... | collective-permute-start | bytes 786440 | tf_op jit(solution)/shard_map/ppermute | solution.py:41
  160.4 12.3 %collective-permute-start.18 = (f32[256,256]{1,0:T(8,128)S(1)}, f32[256,256]{1,0:T(8,128)S(1)}, u32[]{:S(2)}, u32[]{:S(2)}) collective-permute-start(f32[256,256]{1,0:T(8,128)S(1)} %fusion.19), channel_id=1, source_target_pairs={{0,2},{1,3},{2,0},{3,1},{4,6},{5,7},{6,4},{7,5},{8,10},{9,11},{10,... | collective-permute-start | bytes 786440 | tf_op jit(solution)/shard_map/ppermute | solution.py:41
  161.4 11.3 %collective-permute-start.17 = (f32[256,256]{1,0:T(8,128)S(1)}, f32[256,256]{1,0:T(8,128)S(1)}, u32[]{:S(2)}, u32[]{:S(2)}) collective-permute-start(f32[256,256]{1,0:T(8,128)S(1)} %fusion.19), channel_id=1, source_target_pairs={{0,1},{1,0},{2,3},{3,2},{4,5},{5,4},{6,7},{7,6},{8,9},{9,8},{10,11... | collective-permute-start | bytes 786440 | tf_op jit(solution)/shard_map/ppermute | solution.py:41
  162.8 34.4 %collective-permute-start.15 = (bf16[1024,128]{0,1:T(8,128)(2,1)S(1)}, bf16[1024,128]{0,1:T(8,128)(2,1)S(1)}, u32[]{:S(2)}, u32[]{:S(2)}) collective-permute-start(bf16[1024,128]{0,1:T(8,128)(2,1)S(1)} %convolution_convert_fusion.2), channel_id=1, source_target_pairs={{0,16},{4,20},{8,24},{12,28},{16,0},{20,4},{24,8},{28,12},{1,17},{... | collective-permute-start | bytes 786440 | tf_op jit(solution)/shard_map/ppermute | solution.py:29

commit v2 on v0

v2 whole, which is shorter than its diff:
```python
import functools

import jax
import jax.numpy as jnp
from jax import lax
from jax.experimental import pallas as pl
from jax.experimental.pallas import tpu as pltpu
from jax.sharding import PartitionSpec as P

HB = 2
PANEL = 8
F32 = jnp.float32
BF16 = jnp.bfloat16


def swap(value, axis, mask):
    pairs = [(source, source ^ mask) for source in range(lax.axis_size(axis))]
    return lax.ppermute(value, axis, pairs)


def summands(value, axis):
    count = lax.axis_size(axis)
    done = 1
    parts = [value]
    while done < count:
        value = total_of(parts)
        radix = 4 if count // done % 4 == 0 else 2
        parts = [value] + [swap(value, axis, step * done) for step in range(1, radix)]
        done *= radix
    return parts


def total_of(parts):
    values = [part[...] for part in parts]
    while len(values) > 1:
        values = [a + b for a, b in zip(values[::2], values[1::2])]
    return values[0]


def dot_nn(a, b):
    return lax.dot_general(a, b, (((1,), (0,)), ((), ())), preferred_element_type=F32)


def dot_nt(a, b):
    return lax.dot_general(a, b, (((1,), (1,)), ((), ())), preferred_element_type=F32)


def dot_tn(a, b):
    return lax.dot_general(a, b, (((0,), (0,)), ((), ())), preferred_element_type=F32)


def halves_of(value):
    high = value.astype(BF16)
    return high, (value - high.astype(F32)).astype(BF16)


def full(dot, a, b):
    a_high, a_low = halves_of(a)
    b_high, b_low = halves_of(b)
    return dot(a_high, b_high) + (dot(a_high, b_low) + dot(a_low, b_high))


nn_full = functools.partial(full, dot_nn)
nt_full = functools.partial(full, dot_nt)


def inverse_factor(matrix):
    size = matrix.shape[0]
    panels = size // PANEL
    shape = (PANEL, size)
    lane = lax.broadcasted_iota(jnp.int32, shape, 1)
    sub = lax.broadcasted_iota(jnp.int32, shape, 0)

    def column(rows, index):
        return jnp.broadcast_to(rows[:, index : index + 1], shape)

    def row(rows, index):
        return jnp.broadcast_to(rows[index : index + 1, :], shape)

    rows_of = [matrix[PANEL * i : PANEL * (i + 1), :] for i in range(panels)]
    out = []
    block = [column(rows_of[0], j) for j in range(PANEL)]
    for k in range(panels):
        base = PANEL * k
        active = rows_of[k]
        ahead = (
            [column(active, base + PANEL + j) for j in range(PANEL)] if k + 1 < panels else []
        )
        here = (lane >= base) & (lane < base + PANEL)
        active = jnp.where(here, jnp.where(lane == sub + base, 1.0, 0.0), active)
        kept = active
        pivots = block[0]
        for j in range(PANEL):
            pivot = row(block[j], j)
            factor = jnp.where(sub == j, 0.0, block[j]) * (1.0 / pivot)
            kept = jnp.where(sub == j, active, kept)
            pivots = jnp.where(sub == j, pivot, pivots)
            active = active - factor * row(active, j)
            for q in range(j + 1, PANEL):
                block[q] = block[q] - factor * row(block[q], j)
            ahead = [item - factor * row(item, j) for item in ahead]
        out.append(jnp.where(lane < base + PANEL, kept * lax.rsqrt(pivots), 0.0))
        if k + 1 == panels:
            break
        scale = 1.0 / pivots
        solved = active * scale
        solved_rows = [row(solved, j) for j in range(PANEL)]
        block = []
        for i in range(k + 1, panels):
            old = rows_of[i]
            columns = [column(old, base + j) for j in range(PANEL)]
            if i == k + 1:
                for q in range(PANEL):
                    item = column(old, base + PANEL + q)
                    scaled = ahead[q] * scale
                    for j in range(PANEL):
                        item = item - columns[j] * row(scaled, j)
                    block.append(item)
            new = jnp.where(here, 0.0, old)
            for j in range(PANEL):
                new = new - columns[j] * solved_rows[j]
            rows_of[i] = new
    return jnp.concatenate(out, axis=0)


def run_kernel(body, outs, *operands):
    return pl.pallas_call(
        body,
        out_shape=outs,
        cost_estimate=pl.CostEstimate(flops=2_000_000_000, bytes_accessed=1_000_000, transcendentals=0),
    )(*operands)


def image_kernel(index_ref, energy_ref, padded_ref, image_ref, gram_ref):
    b = pl.program_id(0)
    own = padded_ref[b + HB]
    total = 3.0 * own.astype(F32)
    for slot in range(energy_ref.shape[1]):
        total = total + dot_nn(energy_ref[0, slot], padded_ref[index_ref[b, slot]])
    image = total.astype(BF16)
    image_ref[0] = image

    @pl.when(b == 0)
    def _():
        gram_ref[...] = jnp.zeros_like(gram_ref)

    gram_ref[...] += dot_tn(image, image)


def image_and_gram(local_index, energy, padded):
    blocks, slots, rows, _ = energy.shape
    width = padded.shape[2]
    grid_spec = pltpu.PrefetchScalarGridSpec(
        num_scalar_prefetch=1,
        grid=(blocks,),
        in_specs=[
            pl.BlockSpec((1, slots, rows, rows), lambda b, index: (b, 0, 0, 0)),
            pl.BlockSpec(padded.shape, lambda b, index: (0, 0, 0)),
        ],
        out_specs=[
            pl.BlockSpec((1, rows, width), lambda b, index: (b, 0, 0)),
            pl.BlockSpec((width, width), lambda b, index: (0, 0)),
        ],
    )
    image, gram = pl.pallas_call(
        image_kernel,
        out_shape=[
            jax.ShapeDtypeStruct((blocks, rows, width), BF16),
            jax.ShapeDtypeStruct((width, width), F32),
        ],
        grid_spec=grid_spec,
    )(local_index, energy, padded)
    return image.reshape(blocks * rows, width), gram


def leaf_kernel(total_rows, count, *refs):
    parts, (inverse_ref,) = refs[:count], refs[count:]
    inverse_ref[...] = inverse_factor(total_of(parts) / total_rows)


def merge(cross, sketch_own, sketch_other):
    columns_own = sketch_own + nt_full(sketch_other, cross)
    columns_other = nn_full(sketch_own, cross) + sketch_other
    image_own = columns_own + nt_full(columns_other, cross)
    image_other = nn_full(columns_own, cross) + columns_other
    inner = nt_full(columns_own, image_own) + nt_full(columns_other, image_other)
    inverse = inverse_factor(inner)
    return nn_full(inverse, columns_own), nn_full(inverse, columns_other)


def first_merge_kernel(total_rows, count, last, *refs):
    parts, refs = refs[:count], refs[count:]
    own_ref, other_ref, sketch_own, sketch_other, refs = *refs[:4], refs[4:]
    cross = nt_full(nn_full(own_ref[...], total_of(parts) / total_rows), other_ref[...])
    half_own, half_other = merge(cross, sketch_own[...], sketch_other[...])
    if not last:
        image_own, image_other, far_image, refs = *refs[:3], refs[3:]
        mine = nn_full(half_own, own_ref[...])
        theirs = nn_full(half_other, other_ref[...])
        image_t = dot_nt(mine.astype(BF16), image_own[...]) + dot_nt(
            theirs.astype(BF16), image_other[...]
        )
        image_t = image_t.astype(BF16)
        refs[2][...] = mine
        refs[3][...] = image_t
        refs[4][...] = dot_nn(image_t, far_image[...])
    refs[0][...] = half_own.astype(BF16)
    refs[1][...] = half_other.astype(BF16)


def later_merge_kernel(count, last, *refs):
    parts, refs = refs[:count], refs[count:]
    sketch_own, sketch_other, refs = *refs[:2], refs[2:]
    half_own, half_other = merge(total_of(parts), sketch_own[...], sketch_other[...])
    if not last:
        mine_ref, image_own, image_other, far_image, refs = *refs[:4], refs[4:]
        image_t = dot_nn(half_own.astype(BF16), image_own[...]) + dot_nn(
            half_other.astype(BF16), image_other[...]
        )
        image_t = image_t.astype(BF16)
        refs[2][...] = nn_full(half_own, mine_ref[...])
        refs[3][...] = image_t
        refs[4][...] = dot_nn(image_t, far_image[...])
    refs[0][...] = half_own.astype(BF16)
    refs[1][...] = half_other.astype(BF16)


def cross_kernel(total_rows, count, *refs):
    parts, (far_ref, out_ref) = refs[:count], refs[count:]
    out_ref[...] = nt_full(total_of(parts) / total_rows, far_ref[...])


def on_device(snapshots, energy, neighbours, sketch):
    block_count, _, block_rows, _ = energy.shape
    rows_dev, width = snapshots.shape
    space = lax.axis_size("space")
    total_rows = rows_dev * space
    levels = sketch.shape[0]
    window = lax.axis_index("tm")
    blocks = snapshots.reshape(block_count, block_rows, width)
    ends = space - 1
    before = lax.ppermute(blocks[-HB:], "space", [(i, i + 1) for i in range(ends)])
    after = lax.ppermute(blocks[:HB], "space", [(i + 1, i) for i in range(ends)])
    padded = jnp.concatenate([before, blocks, after], axis=0)
    local_index = neighbours - (lax.axis_index("space") * block_count - HB)
    sketch_t = jnp.swapaxes(sketch, 1, 2)

    def sketch_halves(level):
        lower, upper = sketch_t[level, :, :width], sketch_t[level, :, width:]
        is_upper = window // 2**level % 2 == 1
        return jnp.where(is_upper, upper, lower), jnp.where(is_upper, lower, upper)

    square = jax.ShapeDtypeStruct((width, width), F32)
    half = jax.ShapeDtypeStruct((width, width), BF16)
    long = jax.ShapeDtypeStruct((width, rows_dev), BF16)

    image, gram = image_and_gram(local_index, energy, padded)
    parts = summands(gram, "space")
    far_images = [swap(image, "tm", 2**level) for level in range(levels)]
    cross_parts = summands(dot_tn(image, far_images[0]), "space")
    inverse = run_kernel(
        functools.partial(leaf_kernel, total_rows, len(parts)), square, *parts
    )
    current = dot_nt(snapshots, inverse.astype(BF16)).astype(BF16)
    kept = [current]
    other_inverse = swap(inverse, "tm", 1)
    mine = image_t = None
    for level in range(levels):
        last = level + 1 == levels
        outs = [half, half] if last else [half, half, square, long, square]
        partner = swap(current, "tm", 2**level)
        halves = sketch_halves(level)
        if level == 0:
            operands = [*cross_parts, inverse, other_inverse, *halves]
            if not last:
                operands += [image, far_images[0], far_images[1]]
            body = functools.partial(first_merge_kernel, total_rows, len(cross_parts), last)
        else:
            far_mine = swap(mine, "tm", 2**level)
            if not last:
                far_image_t = swap(image_t, "tm", 2**level)
            parts = summands(probe, "space")
            cross = run_kernel(
                functools.partial(cross_kernel, total_rows, len(parts)), square, *parts, far_mine
            )
            for bit in range(level - 1):
                cross = cross + swap(cross, "tm", 2**bit)
            parts = [cross, swap(cross, "tm", 2 ** (level - 1))]
            operands = [*parts, *halves]
            if not last:
                operands += [mine, image_t, far_image_t, far_images[level + 1]]
            body = functools.partial(later_merge_kernel, len(parts), last)
        results = run_kernel(body, outs, *operands)
        half_own, half_other = results[:2]
        if not last:
            mine, image_t, probe = results[2:]
        current = (dot_nt(current, half_own) + dot_nt(partner, half_other)).astype(BF16)
        kept.append(current)
    return jnp.stack(kept)[:, None]


def solution(mesh):
    placed = (P("space", "tm"), P("space", None, None, None), P("space", None), P())
    return jax.shard_map(
        on_device,
        mesh=mesh,
        in_specs=placed,
        out_specs=P(None, "tm", "space", None),
        check_vma=False,
    )
```

time: 344 us -> 106 us (0.31)
  waiting for transfers between devices: 190 us -> 15.1 us
  other arithmetic: 97 us -> 4.78 us
  Pallas kernels: 0 us -> 34.8 us
  starting transfers between devices: 13.4 us -> 37.1 us
  matrix products: 20.8 us -> 6.4 us
  between operations: 13.7 us -> 0.36 us
    psum x4 -> x0, waiting for transfers between devices: 172 us -> none  [the longest x3 128 us: on_device(): gram_matrix = lax.psum(gram_of(joined_image), 'space') / total_rows]
    another operation x20 -> x0, other arithmetic: 91.7 us -> none  [the longest x9 37.4 us: on_device(): lower_factor = jnp.linalg.cholesky(inner_gram)]
    pallas_call x0 -> x7, Pallas kernels: none -> 34.8 us  [the longest x6 27.3 us: run_kernel(): pl.pallas_call(body, out_shape=outs, cost_estimate=pl.CostEstimate(flops=...]
    ppermute x8 -> x27, starting transfers between devices: 12.8 us -> 37.1 us  [the longest x25 30.3 us: swap(): return lax.ppermute(value, axis, pairs)]
    dot_general x27 -> x8, matrix products: 19.6 us -> 6.4 us  [the longest x7 6.13 us: dot_nt(): lax.dot_general(a, b, (((1,), (1,)), ((), ())), preferred_element_type=F32)]
    gather x7 -> x0, local copies, waits for them, and re-layouts: 5.54 us -> none  [image_of(): gathered = jnp.take(padded, local_index[:, slot_index], axis=0)]
    unnamed x10 -> x55, local copies, waits for them, and re-layouts: 0.07 us -> 4.6 us
    ppermute x8 -> x27, waiting for transfers between devices: 17.5 us -> 15.1 us  [the longest x25 14.6 us: swap(): return lax.ppermute(value, axis, pairs)]
  transfers between devices with their start and end apart: 12 -> 27, of which waited for: 7 -> 8; matrix products, arithmetic and copies ran while one was open for 17% -> 7% of each run, Pallas kernels for 0% -> 24%
where the time goes in v2:
time: 106 us; the launch traced here: 105 us
  starting transfers between devices  37.1 us (35%)
  Pallas kernels  34.8 us (33%)
  waiting for transfers between devices  15.1 us (14%)
  local copies, waits for them, and re-layouts  6.84 us (6%)
  matrix products  6.4 us (6%)
  other arithmetic  4.78 us (5%)
    ppermute x25, starting transfers between devices, swap(): return lax.ppermute(value, axis, pairs)  30.3 us
    pallas_call x6, Pallas kernels, run_kernel(): pl.pallas_call(body, out_shape=outs, cost_estimate=pl.CostEstimate(flops=...  27.3 us
    ppermute x25, waiting for transfers between devices, swap(): return lax.ppermute(value, axis, pairs)  14.6 us
    pallas_call x1, Pallas kernels, image_and_gram(): pl.pallas_call(image_kernel, out_shape=[jax.ShapeDtypeStruct((blocks, row...  7.49 us
    dot_general x7, matrix products, dot_nt(): lax.dot_general(a, b, (((1,), (1,)), ((), ())), preferred_element_type=F32)  6.13 us
    ppermute x1, starting transfers between devices, on_device(): lax.ppermute(blocks[-HB:], 'space', [(i, i + 1) for i in range(ends)])  5.5 us
    unnamed x55, local copies, waits for them, and re-layouts  4.6 us
  transfers between devices with their start and end apart: 27, of which 8 were waited for; matrix products, arithmetic and copies ran while one was open for 7% of the time, Pallas kernels for 24%

profile of v2, /device:TPU:0, one launch (start us, length us, event | category | flops | bytes accessed | tf_op | source)
XLA Modules:
  0.0 105.4 jit_solution(7919204029308258387)
XLA Ops:
  0.9 1.3 %collective-permute-start.1 = (bf16[2,128,128]{2,1,0:T(8,128)(2,1)S(1)}, bf16[2,128,128]{2,1,0:T(8,128)(2,1)S(1)}, u32[]{:S(2)}, u32[]{:S(2)}) collective-permute-start(bf16[2,128,128]{2,1,0:T(8,128)(2,1)S(1)} %bitcast.53), channel_id=1, source_target_pairs={{1,0},{2,1},{3,2},{5,4},{6,5},{7,6},{9,8},{10,9},{11,10},{13,12},{... | collective-permute-start | bytes 196616 | tf_op jit(solution)/shard_map/ppermute | solution.py:243
  2.2 5.5 %collective-permute-start = (bf16[2,128,128]{2,1,0:T(8,128)(2,1)S(1)}, bf16[2,128,128]{2,1,0:T(8,128)(2,1)S(1)}, u32[]{:S(2)}, u32[]{:S(2)}) collective-permute-start(bf16[2,128,128]{2,1,0:T(8,128)(2,1)S(1)} %bitcast.52), channel_id=1, source_target_pairs={{0,1},{1,2},{2,3},{4,5},{5,6},{6,7},{8,9},{9,10},{10,11},{12,13},{... | collective-permute-start | bytes 196616 | tf_op jit(solution)/shard_map/ppermute | solution.py:242
  7.8 1.3 %broadcast_subtract_fusion.index_ref = s32[8,7]{1,0:T(8,128)} fusion(s32[8,7]{1,0:T(8,128)} %param.6, s32[]{:T(128)S(6)} %sub.17), kind=kLoop, calls=%fused_computation.17 | loop fusion | flops 56 | bytes 452 | tf_op jit(solution)/shard_map/sub | solution.py:245
  9.6 1.7 %pad_maximum_fusion.padded_ref = bf16[12,128,128]{2,1,0:T(8,128)(2,1)} fusion(bf16[2,128,128]{2,1,0:T(8,128)(2,1)S(1)} %collective-permute-done.1, bf16[8,128,128]{2,1,0:T(8,128)(2,1)} %bitcast.45, bf16[2,128,128]{2,1,0:T(8,128)(2,1)S(1)} %collective-permute-done), kind=kLoop, calls=%fused_computation.9 | loop fusion | flops 393216 | bytes 786432 | tf_op jit(solution)/shard_map/concatenate | solution.py:244
  11.4 7.5 %shard_map.46 = (bf16[8,128,128]{2,1,0:T(8,128)(2,1)}, f32[128,128]{1,0:T(8,128)}) custom-call(s32[8,7]{1,0:T(8,128)} %broadcast_subtract_fusion.index_ref, bf16[8,7,128,128]{3,2,1,0:T(8,128)(2,1)} %energy_ref.1, bf16[12,128,128]{2,1,0:T(8,128)(2,1)} %pad_maximum_fusion.padded_ref), custom_call_target="tpu_custom_call" | custom-call | tf_op jit(solution)/shard_map/pallas_call | solution.py:165
  18.9 2.9 %collective-permute-start.2 = (f32[128,128]{1,0:T(8,128)}, f32[128,128]{1,0:T(8,128)S(1)}, u32[]{:S(2)}, u32[]{:S(2)}) collective-permute-start(f32[128,128]{1,0:T(8,128)} %get-tuple-element.18.refs_0_), channel_id=1, source_target_pairs={{0,1},{1,0},{2,3},{3,2},{4,5},{5,4},{6,7},{7,6},{8,9},{9,8},{10,11... | collective-permute-start | bytes 196616 | tf_op jit(solution)/shard_map/ppermute | solution.py:18
  21.8 1.9 %collective-permute-start.3 = (f32[128,128]{1,0:T(8,128)}, f32[128,128]{1,0:T(8,128)S(1)}, u32[]{:S(2)}, u32[]{:S(2)}) collective-permute-start(f32[128,128]{1,0:T(8,128)} %get-tuple-element.18.refs_0_), channel_id=1, source_target_pairs={{0,2},{1,3},{2,0},{3,1},{4,6},{5,7},{6,4},{7,5},{8,10},{9,11},{10,... | collective-permute-start | bytes 196616 | tf_op jit(solution)/shard_map/ppermute | solution.py:18
  23.6 1.4 %collective-permute-start.4 = (f32[128,128]{1,0:T(8,128)}, f32[128,128]{1,0:T(8,128)S(1)}, u32[]{:S(2)}, u32[]{:S(2)}) collective-permute-start(f32[128,128]{1,0:T(8,128)} %get-tuple-element.18.refs_0_), channel_id=1, source_target_pairs={{0,3},{1,2},{2,1},{3,0},{4,7},{5,6},{6,5},{7,4},{8,11},{9,10},{10,... | collective-permute-start | bytes 196616 | tf_op jit(solution)/shard_map/ppermute | solution.py:18
  25.3 1.6 %collective-permute-start.10 = (bf16[1024,128]{1,0:T(8,128)(2,1)}, bf16[1024,128]{1,0:T(8,128)(2,1)S(1)}, u32[]{:S(2)}, u32[]{:S(2)}) collective-permute-start(bf16[1024,128]{1,0:T(8,128)(2,1)} %bitcast.48), channel_id=1, source_target_pairs={{0,8},{4,12},{8,0},{12,4},{16,24},{20,28},{24,16},{28,20},{1,9},{5... | collective-permute-start | bytes 786440 | tf_op jit(solution)/shard_map/ppermute | solution.py:18
  27.0 2.0 %collective-permute-done.4.refs_3_ = f32[128,128]{1,0:T(8,128)S(1)} collective-permute-done((f32[128,128]{1,0:T(8,128)}, f32[128,128]{1,0:T(8,128)S(1)}, u32[]{:S(2)}, u32[]{:S(2)}) %collective-permute-start.4) | collective-permute-done | bytes 65568 | tf_op jit(solution)/shard_map/ppermute | solution.py:18
  29.6 4.7 %shard_map.47.refs_4_ = f32[128,128]{1,0:T(8,128)} custom-call(f32[128,128]{1,0:T(8,128)} %get-tuple-element.18.refs_0_, f32[128,128]{1,0:T(8,128)} %copy-done.10, f32[128,128]{1,0:T(8,128)} %copy-done.11, f32[128,128]{1,0:T(8,128)} %copy-done.12), custom_call_target="tpu_custom_call" | custom-call | flops 2000000000 | bytes 1000000 | tf_op jit(solution)/shard_map/pallas_call | solution.py:127
  36.3 2.0 %collective-permute-start.6 = (f32[128,128]{1,0:T(8,128)S(1)}, f32[128,128]{1,0:T(8,128)S(1)}, u32[]{:S(2)}, u32[]{:S(2)}) collective-permute-start(f32[128,128]{1,0:T(8,128)S(1)} %fusion.6.refs_0_), channel_id=1, source_target_pairs={{0,1},{1,0},{2,3},{3,2},{4,5},{5,4},{6,7},{7,6},{8,9},{9,8},{10,11... | collective-permute-start | bytes 196616 | tf_op jit(solution)/shard_map/ppermute | solution.py:18
  38.3 1.5 %collective-permute-start.8 = (f32[128,128]{1,0:T(8,128)S(1)}, f32[128,128]{1,0:T(8,128)S(1)}, u32[]{:S(2)}, u32[]{:S(2)}) collective-permute-start(f32[128,128]{1,0:T(8,128)S(1)} %fusion.6.refs_0_), channel_id=1, source_target_pairs={{0,3},{1,2},{2,1},{3,0},{4,7},{5,6},{6,5},{7,4},{8,11},{9,10},{10,... | collective-permute-start | bytes 196616 | tf_op jit(solution)/shard_map/ppermute | solution.py:18
  40.6 2.6 %collective-permute-start.18 = (bf16[1024,128]{1,0:T(8,128)(2,1)S(1)}, bf16[1024,128]{1,0:T(8,128)(2,1)S(1)}, u32[]{:S(2)}, u32[]{:S(2)}) collective-permute-start(bf16[1024,128]{1,0:T(8,128)(2,1)S(1)} %bitcast.51), channel_id=1, source_target_pairs={{0,16},{4,20},{8,24},{12,28},{16,0},{20,4},{24,8},{28,12},{1,17},{... | collective-permute-start | bytes 786440 | tf_op jit(solution)/shard_map/ppermute | solution.py:18
  44.4 6.9 %shard_map.48 = (bf16[128,128]{1,0:T(8,128)(2,1)}, bf16[128,128]{1,0:T(8,128)(2,1)}, f32[128,128]{1,0:T(8,128)}, bf16[128,1024]{1,0:T(8,128)(2,1)}, f32[128,128]{1,0:T(8,128)}) custom-call(f32[128,128]{1,0:T(8,128)} %copy-done.4, f32[128,128]{1,0:T(8,128)} %copy-done.14, f32[128,128]{1,0:T(8,128)} %copy-done.15, f32[128,128]{1,0:T(8,128)} %copy-done.18, ...), custom_call_target="tpu_custom_call" | custom-call | flops 2000000000 | bytes 1000000 | tf_op jit(solution)/shard_map/pallas_call | solution.py:127
  51.3 1.5 %collective-permute-start.12 = (f32[128,128]{1,0:T(8,128)}, f32[128,128]{1,0:T(8,128)S(1)}, u32[]{:S(2)}, u32[]{:S(2)}) collective-permute-start(f32[128,128]{1,0:T(8,128)} %get-tuple-element.22.refs_0_), channel_id=1, source_target_pairs={{0,1},{1,0},{2,3},{3,2},{4,5},{5,4},{6,7},{7,6},{8,9},{9,8},{10,11... | collective-permute-start | bytes 196616 | tf_op jit(solution)/shard_map/ppermute | solution.py:18
  53.1 1.7 %collective-permute-start.14 = (f32[128,128]{1,0:T(8,128)}, f32[128,128]{1,0:T(8,128)S(1)}, u32[]{:S(2)}, u32[]{:S(2)}) collective-permute-start(f32[128,128]{1,0:T(8,128)} %get-tuple-element.22.refs_0_), channel_id=1, source_target_pairs={{0,3},{1,2},{2,1},{3,0},{4,7},{5,6},{6,5},{7,4},{8,11},{9,10},{10,... | collective-permute-start | bytes 196616 | tf_op jit(solution)/shard_map/ppermute | solution.py:18
  54.8 1.6 %collective-permute-start.15 = (f32[128,128]{1,0:T(8,128)}, f32[128,128]{1,0:T(8,128)S(1)}, u32[]{:S(2)}, u32[]{:S(2)}) collective-permute-start(f32[128,128]{1,0:T(8,128)} %get-tuple-element.23.refs_4_), channel_id=1, source_target_pairs={{0,8},{4,12},{8,0},{12,4},{16,24},{20,28},{24,16},{28,20},{1,9},{5... | collective-permute-start | bytes 196616 | tf_op jit(solution)/shard_map/ppermute | solution.py:18
  58.9 1.6 %collective-permute-start.19 = (bf16[1024,128]{0,1:T(8,128)(2,1)S(1)}, bf16[1024,128]{0,1:T(8,128)(2,1)S(1)}, u32[]{:S(2)}, u32[]{:S(2)}) collective-permute-start(bf16[1024,128]{0,1:T(8,128)(2,1)S(1)} %fusion), channel_id=1, source_target_pairs={{0,8},{4,12},{8,0},{12,4},{16,24},{20,28},{24,16},{28,20},{1,9},{5... | collective-permute-start | bytes 786440 | tf_op jit(solution)/shard_map/ppermute | solution.py:18
  61.7 1.8 %shard_map.49.refs_0_ = f32[128,128]{1,0:T(8,128)} custom-call(f32[128,128]{1,0:T(8,128)} %get-tuple-element.22.refs_0_, f32[128,128]{1,0:T(8,128)} %copy-done.16, f32[128,128]{1,0:T(8,128)} %copy-done.17, f32[128,128]{1,0:T(8,128)} %copy-done.19, f32[128,128]{1,0:T(8,128)} %copy-done.21), custom_call_target="tpu_custom_call" | custom-call | flops 2000000000 | bytes 1000000 | tf_op jit(solution)/shard_map/pallas_call | solution.py:127
  63.5 1.5 %collective-permute-done.16.refs_1_ = f32[128,128]{1,0:T(8,128)S(1)} collective-permute-done((f32[128,128]{1,0:T(8,128)}, f32[128,128]{1,0:T(8,128)S(1)}, u32[]{:S(2)}, u32[]{:S(2)}) %collective-permute-start.16) | collective-permute-done | bytes 65568 | tf_op jit(solution)/shard_map/ppermute | solution.py:18
  65.0 1.8 %collective-permute-done.17.refs_6_ = bf16[128,1024]{1,0:T(8,128)(2,1)S(1)} collective-permute-done((bf16[128,1024]{1,0:T(8,128)(2,1)}, bf16[128,1024]{1,0:T(8,128)(2,1)S(1)}, u32[]{:S(2)}, u32[]{:S(2)}) %collective-permute-start.17) | collective-permute-done | bytes 262176 | tf_op jit(solution)/shard_map/ppermute | solution.py:18
  67.5 6.5 %shard_map.50 = (bf16[128,128]{1,0:T(8,128)(2,1)}, bf16[128,128]{1,0:T(8,128)(2,1)}, f32[128,128]{1,0:T(8,128)}, bf16[128,1024]{1,0:T(8,128)(2,1)}, f32[128,128]{1,0:T(8,128)}) custom-call(f32[128,128]{1,0:T(8,128)} %shard_map.49.refs_0_, f32[128,128]{1,0:T(8,128)} %copy-done.25, f32[128,128]{1,0:T(8,128)} %get-tuple-element.33.refs_2_, ...), custom_call_target="tpu_custom_call" | custom-call | flops 2000000000 | bytes 1000000 | tf_op jit(solution)/shard_map/pallas_call | solution.py:127
  74.0 1.5 %collective-permute-start.20 = (f32[128,128]{1,0:T(8,128)}, f32[128,128]{1,0:T(8,128)S(1)}, u32[]{:S(2)}, u32[]{:S(2)}) collective-permute-start(f32[128,128]{1,0:T(8,128)} %get-tuple-element.27.refs_0_), channel_id=1, source_target_pairs={{0,1},{1,0},{2,3},{3,2},{4,5},{5,4},{6,7},{7,6},{8,9},{9,8},{10,11... | collective-permute-start | bytes 196616 | tf_op jit(solution)/shard_map/ppermute | solution.py:18
  75.8 1.7 %collective-permute-start.22 = (f32[128,128]{1,0:T(8,128)}, f32[128,128]{1,0:T(8,128)S(1)}, u32[]{:S(2)}, u32[]{:S(2)}) collective-permute-start(f32[128,128]{1,0:T(8,128)} %get-tuple-element.27.refs_0_), channel_id=1, source_target_pairs={{0,3},{1,2},{2,1},{3,0},{4,7},{5,6},{6,5},{7,4},{8,11},{9,10},{10,... | collective-permute-start | bytes 196616 | tf_op jit(solution)/shard_map/ppermute | solution.py:18
  77.5 2.4 %collective-permute-start.23 = (f32[128,128]{1,0:T(8,128)}, f32[128,128]{1,0:T(8,128)S(1)}, u32[]{:S(2)}, u32[]{:S(2)}) collective-permute-start(f32[128,128]{1,0:T(8,128)} %get-tuple-element.28), channel_id=1, source_target_pairs={{0,16},{4,20},{8,24},{12,28},{16,0},{20,4},{24,8},{28,12},{1,17},{... | collective-permute-start | bytes 196616 | tf_op jit(solution)/shard_map/ppermute | solution.py:18
  81.2 2.3 %collective-permute-done.23.refs_4_ = f32[128,128]{1,0:T(8,128)S(1)} collective-permute-done((f32[128,128]{1,0:T(8,128)}, f32[128,128]{1,0:T(8,128)S(1)}, u32[]{:S(2)}, u32[]{:S(2)}) %collective-permute-start.23) | collective-permute-done | bytes 65568 | tf_op jit(solution)/shard_map/ppermute | solution.py:18
  84.0 1.8 %shard_map.51 = f32[128,128]{1,0:T(8,128)} custom-call(f32[128,128]{1,0:T(8,128)} %get-tuple-element.27.refs_0_, f32[128,128]{1,0:T(8,128)} %copy-done.20, f32[128,128]{1,0:T(8,128)} %copy-done.22, f32[128,128]{1,0:T(8,128)} %copy-done.23, f32[128,128]{1,0:T(8,128)} %copy-done.24), custom_call_target="tpu_custom_call" | custom-call | flops 2000000000 | bytes 1000000 | tf_op jit(solution)/shard_map/pallas_call | solution.py:127
  86.1 1.9 %collective-permute-start.26 = (bf16[1024,128]{0,1:T(8,128)(2,1)S(1)}, bf16[1024,128]{0,1:T(8,128)(2,1)S(1)}, u32[]{:S(2)}, u32[]{:S(2)}) collective-permute-start(bf16[1024,128]{0,1:T(8,128)(2,1)S(1)} %fusion.1), channel_id=1, source_target_pairs={{0,16},{4,20},{8,24},{12,28},{16,0},{20,4},{24,8},{28,12},{1,17},{... | collective-permute-start | bytes 786440 | tf_op jit(solution)/shard_map/ppermute | solution.py:18
  89.4 6.3 %collective-permute-done.25.refs_1_ = f32[128,128]{1,0:T(8,128)S(1)} collective-permute-done((f32[128,128]{1,0:T(8,128)S(1)}, f32[128,128]{1,0:T(8,128)S(1)}, u32[]{:S(2)}, u32[]{:S(2)}) %collective-permute-start.25) | collective-permute-done | bytes 65568 | tf_op jit(solution)/shard_map/ppermute | solution.py:18
  96.3 5.7 %shard_map.52 = (bf16[128,128]{1,0:T(8,128)(2,1)}, bf16[128,128]{1,0:T(8,128)(2,1)}) custom-call(f32[128,128]{1,0:T(8,128)} %copy-done.5, f32[128,128]{1,0:T(8,128)} %copy-done.26, f32[128,128]{1,0:T(8,128)} %get-tuple-element.32.refs_2_, f32[128,128]{1,0:T(8,128)} %get-tuple-element.31.refs_3_), custom_call_target="tpu_custom_call" | custom-call | flops 2000000000 | bytes 1000000 | tf_op jit(solution)/shard_map/pallas_call | solution.py:127
  104.1 1.3 %copy.12 = bf16[4,1,1024,128]{3,2,1,0:T(8,128)(2,1)} copy(bf16[4,1,1024,128]{2,3,0,1:T(8,128)(2,1)S(1)} %maximum_bitcast_fusion) | data formatting | bytes 2097152 | tf_op jit(solution)/shard_map/broadcast_in_dim | solution.py:299
  (99 shorter events, 17.3 us)
Async XLA Ops:
  0.0 25.0 %copy-start.1 = (f32[3,256,128]{2,1,0:T(8,128)S(1)}, f32[3,256,128]{2,1,0:T(8,128)}, u32[]{:S(2)}) copy-start(f32[3,256,128]{2,1,0:T(8,128)} %param.7) | copy-start | bytes 1179652
  0.9 8.1 %collective-permute-start.1 = (bf16[2,128,128]{2,1,0:T(8,128)(2,1)S(1)}, bf16[2,128,128]{2,1,0:T(8,128)(2,1)S(1)}, u32[]{:S(2)}, u32[]{:S(2)}) collective-permute-start(bf16[2,128,128]{2,1,0:T(8,128)(2,1)S(1)} %bitcast.53), channel_id=1, source_target_pairs={{1,0},{2,1},{3,2},{5,4},{6,5},{7,6},{9,8},{10,9},{11,10},{13,12},{... | collective-permute-start | bytes 196616 | tf_op jit(solution)/shard_map/ppermute | solution.py:243
  2.2 7.4 %collective-permute-start = (bf16[2,128,128]{2,1,0:T(8,128)(2,1)S(1)}, bf16[2,128,128]{2,1,0:T(8,128)(2,1)S(1)}, u32[]{:S(2)}, u32[]{:S(2)}) collective-permute-start(bf16[2,128,128]{2,1,0:T(8,128)(2,1)S(1)} %bitcast.52), channel_id=1, source_target_pairs={{0,1},{1,2},{2,3},{4,5},{5,6},{6,7},{8,9},{9,10},{10,11},{12,13},{... | collective-permute-start | bytes 196616 | tf_op jit(solution)/shard_map/ppermute | solution.py:242
  18.9 8.1 %collective-permute-start.2 = (f32[128,128]{1,0:T(8,128)}, f32[128,128]{1,0:T(8,128)S(1)}, u32[]{:S(2)}, u32[]{:S(2)}) collective-permute-start(f32[128,128]{1,0:T(8,128)} %get-tuple-element.18.refs_0_), channel_id=1, source_target_pairs={{0,1},{1,0},{2,3},{3,2},{4,5},{5,4},{6,7},{7,6},{8,9},{9,8},{10,11... | collective-permute-start | bytes 196616 | tf_op jit(solution)/shard_map/ppermute | solution.py:18
  21.8 5.2 %collective-permute-start.3 = (f32[128,128]{1,0:T(8,128)}, f32[128,128]{1,0:T(8,128)S(1)}, u32[]{:S(2)}, u32[]{:S(2)}) collective-permute-start(f32[128,128]{1,0:T(8,128)} %get-tuple-element.18.refs_0_), channel_id=1, source_target_pairs={{0,2},{1,3},{2,0},{3,1},{4,6},{5,7},{6,4},{7,5},{8,10},{9,11},{10,... | collective-permute-start | bytes 196616 | tf_op jit(solution)/shard_map/ppermute | solution.py:18
  23.6 5.4 %collective-permute-start.4 = (f32[128,128]{1,0:T(8,128)}, f32[128,128]{1,0:T(8,128)S(1)}, u32[]{:S(2)}, u32[]{:S(2)}) collective-permute-start(f32[128,128]{1,0:T(8,128)} %get-tuple-element.18.refs_0_), channel_id=1, source_target_pairs={{0,3},{1,2},{2,1},{3,0},{4,7},{5,6},{6,5},{7,4},{8,11},{9,10},{10,... | collective-permute-start | bytes 196616 | tf_op jit(solution)/shard_map/ppermute | solution.py:18
  25.2 9.1 %copy-start = (bf16[1024,128]{1,0:T(8,128)(2,1)S(1)}, bf16[1024,128]{1,0:T(8,128)(2,1)}, u32[]{:S(2)}) copy-start(bf16[1024,128]{1,0:T(8,128)(2,1)} %param.4) | copy-start | bytes 786436
  25.3 10.7 %copy-start.2 = (bf16[8,128,128]{2,1,0:T(8,128)(2,1)S(1)}, bf16[8,128,128]{2,1,0:T(8,128)(2,1)}, u32[]{:S(2)}) copy-start(bf16[8,128,128]{2,1,0:T(8,128)(2,1)} %get-tuple-element.19) | copy-start | bytes 786436
  25.3 10.7 %collective-permute-start.5 = (bf16[1024,128]{1,0:T(8,128)(2,1)}, bf16[1024,128]{1,0:T(8,128)(2,1)S(1)}, u32[]{:S(2)}, u32[]{:S(2)}) collective-permute-start(bf16[1024,128]{1,0:T(8,128)(2,1)} %bitcast.47), channel_id=1, source_target_pairs={{0,4},{4,0},{8,12},{12,8},{16,20},{20,16},{24,28},{28,24},{1,5},{5... | collective-permute-start | bytes 786440 | tf_op jit(solution)/shard_map/ppermute | solution.py:18
  25.3 15.3 %collective-permute-start.10 = (bf16[1024,128]{1,0:T(8,128)(2,1)}, bf16[1024,128]{1,0:T(8,128)(2,1)S(1)}, u32[]{:S(2)}, u32[]{:S(2)}) collective-permute-start(bf16[1024,128]{1,0:T(8,128)(2,1)} %bitcast.48), channel_id=1, source_target_pairs={{0,8},{4,12},{8,0},{12,4},{16,24},{20,28},{24,16},{28,20},{1,9},{5... | collective-permute-start | bytes 786440 | tf_op jit(solution)/shard_map/ppermute | solution.py:18
  34.3 4.0 %collective-permute-start.9 = (f32[128,128]{1,0:T(8,128)}, f32[128,128]{1,0:T(8,128)S(1)}, u32[]{:S(2)}, u32[]{:S(2)}) collective-permute-start(f32[128,128]{1,0:T(8,128)} %shard_map.47.refs_4_), channel_id=1, source_target_pairs={{0,4},{4,0},{8,12},{12,8},{16,20},{20,16},{24,28},{28,24},{1,5},{5... | collective-permute-start | bytes 196616 | tf_op jit(solution)/shard_map/ppermute | solution.py:18
  35.4 19.4 %collective-permute-start.11 = (bf16[1024,128]{0,1:T(8,128)(2,1)S(1)}, bf16[1024,128]{0,1:T(8,128)(2,1)S(1)}, u32[]{:S(2)}, u32[]{:S(2)}) collective-permute-start(bf16[1024,128]{0,1:T(8,128)(2,1)S(1)} %bitcast.41), channel_id=1, source_target_pairs={{0,4},{4,0},{8,12},{12,8},{16,20},{20,16},{24,28},{28,24},{1,5},{5... | collective-permute-start | bytes 786440 | tf_op jit(solution)/shard_map/ppermute | solution.py:18
  36.0 7.8 %copy-start.3 = (bf16[1024,128]{1,0:T(8,128)(2,1)}, bf16[1024,128]{1,0:T(8,128)(2,1)S(1)}, u32[]{:S(2)}) copy-start(bf16[1024,128]{1,0:T(8,128)(2,1)S(1)} %collective-permute-done.5.refs_9_) | copy-start | bytes 786436
  36.2 7.5 %copy-start.4 = (f32[128,128]{1,0:T(8,128)}, f32[128,128]{1,0:T(8,128)S(1)}, u32[]{:S(2)}) copy-start(f32[128,128]{1,0:T(8,128)S(1)} %fusion.6.refs_0_) | copy-start | bytes 196612
  36.3 7.0 %collective-permute-start.6 = (f32[128,128]{1,0:T(8,128)S(1)}, f32[128,128]{1,0:T(8,128)S(1)}, u32[]{:S(2)}, u32[]{:S(2)}) collective-permute-start(f32[128,128]{1,0:T(8,128)S(1)} %fusion.6.refs_0_), channel_id=1, source_target_pairs={{0,1},{1,0},{2,3},{3,2},{4,5},{5,4},{6,7},{7,6},{8,9},{9,8},{10,11... | collective-permute-start | bytes 196616 | tf_op jit(solution)/shard_map/ppermute | solution.py:18
  38.3 5.4 %collective-permute-start.7 = (f32[128,128]{1,0:T(8,128)S(1)}, f32[128,128]{1,0:T(8,128)S(1)}, u32[]{:S(2)}, u32[]{:S(2)}) collective-permute-start(f32[128,128]{1,0:T(8,128)S(1)} %fusion.6.refs_0_), channel_id=1, source_target_pairs={{0,2},{1,3},{2,0},{3,1},{4,6},{5,7},{6,4},{7,5},{8,10},{9,11},{10,... | collective-permute-start | bytes 196616 | tf_op jit(solution)/shard_map/ppermute | solution.py:18
  38.3 5.4 %collective-permute-start.8 = (f32[128,128]{1,0:T(8,128)S(1)}, f32[128,128]{1,0:T(8,128)S(1)}, u32[]{:S(2)}, u32[]{:S(2)}) collective-permute-start(f32[128,128]{1,0:T(8,128)S(1)} %fusion.6.refs_0_), channel_id=1, source_target_pairs={{0,3},{1,2},{2,1},{3,0},{4,7},{5,6},{6,5},{7,4},{8,11},{9,10},{10,... | collective-permute-start | bytes 196616 | tf_op jit(solution)/shard_map/ppermute | solution.py:18
  40.6 22.9 %collective-permute-start.18 = (bf16[1024,128]{1,0:T(8,128)(2,1)S(1)}, bf16[1024,128]{1,0:T(8,128)(2,1)S(1)}, u32[]{:S(2)}, u32[]{:S(2)}) collective-permute-start(bf16[1024,128]{1,0:T(8,128)(2,1)S(1)} %bitcast.51), channel_id=1, source_target_pairs={{0,16},{4,20},{8,24},{12,28},{16,0},{20,4},{24,8},{28,12},{1,17},{... | collective-permute-start | bytes 786440 | tf_op jit(solution)/shard_map/ppermute | solution.py:18
  51.3 6.0 %collective-permute-start.12 = (f32[128,128]{1,0:T(8,128)}, f32[128,128]{1,0:T(8,128)S(1)}, u32[]{:S(2)}, u32[]{:S(2)}) collective-permute-start(f32[128,128]{1,0:T(8,128)} %get-tuple-element.22.refs_0_), channel_id=1, source_target_pairs={{0,1},{1,0},{2,3},{3,2},{4,5},{5,4},{6,7},{7,6},{8,9},{9,8},{10,11... | collective-permute-start | bytes 196616 | tf_op jit(solution)/shard_map/ppermute | solution.py:18
  52.8 6.0 %collective-permute-start.13 = (f32[128,128]{1,0:T(8,128)}, f32[128,128]{1,0:T(8,128)S(1)}, u32[]{:S(2)}, u32[]{:S(2)}) collective-permute-start(f32[128,128]{1,0:T(8,128)} %get-tuple-element.22.refs_0_), channel_id=1, source_target_pairs={{0,2},{1,3},{2,0},{3,1},{4,6},{5,7},{6,4},{7,5},{8,10},{9,11},{10,... | collective-permute-start | bytes 196616 | tf_op jit(solution)/shard_map/ppermute | solution.py:18
  53.1 7.4 %collective-permute-start.14 = (f32[128,128]{1,0:T(8,128)}, f32[128,128]{1,0:T(8,128)S(1)}, u32[]{:S(2)}, u32[]{:S(2)}) collective-permute-start(f32[128,128]{1,0:T(8,128)} %get-tuple-element.22.refs_0_), channel_id=1, source_target_pairs={{0,3},{1,2},{2,1},{3,0},{4,7},{5,6},{6,5},{7,4},{8,11},{9,10},{10,... | collective-permute-start | bytes 196616 | tf_op jit(solution)/shard_map/ppermute | solution.py:18
  54.8 5.7 %collective-permute-start.15 = (f32[128,128]{1,0:T(8,128)}, f32[128,128]{1,0:T(8,128)S(1)}, u32[]{:S(2)}, u32[]{:S(2)}) collective-permute-start(f32[128,128]{1,0:T(8,128)} %get-tuple-element.23.refs_4_), channel_id=1, source_target_pairs={{0,8},{4,12},{8,0},{12,4},{16,24},{20,28},{24,16},{28,20},{1,9},{5... | collective-permute-start | bytes 196616 | tf_op jit(solution)/shard_map/ppermute | solution.py:18
  57.4 9.5 %collective-permute-start.17 = (bf16[128,1024]{1,0:T(8,128)(2,1)}, bf16[128,1024]{1,0:T(8,128)(2,1)S(1)}, u32[]{:S(2)}, u32[]{:S(2)}) collective-permute-start(bf16[128,1024]{1,0:T(8,128)(2,1)} %get-tuple-element.24.refs_5_), channel_id=1, source_target_pairs={{0,8},{4,12},{8,0},{12,4},{16,24},{20,28},{24,16},{28,20},{1,9},{5... | collective-permute-start | bytes 786440 | tf_op jit(solution)/shard_map/ppermute | solution.py:18
  58.9 21.0 %collective-permute-start.19 = (bf16[1024,128]{0,1:T(8,128)(2,1)S(1)}, bf16[1024,128]{0,1:T(8,128)(2,1)S(1)}, u32[]{:S(2)}, u32[]{:S(2)}) collective-permute-start(bf16[1024,128]{0,1:T(8,128)(2,1)S(1)} %fusion), channel_id=1, source_target_pairs={{0,8},{4,12},{8,0},{12,4},{16,24},{20,28},{24,16},{28,20},{1,9},{5... | collective-permute-start | bytes 786440 | tf_op jit(solution)/shard_map/ppermute | solution.py:18
  63.5 1.5 %collective-permute-start.16 = (f32[128,128]{1,0:T(8,128)}, f32[128,128]{1,0:T(8,128)S(1)}, u32[]{:S(2)}, u32[]{:S(2)}) collective-permute-start(f32[128,128]{1,0:T(8,128)} %shard_map.49.refs_0_), channel_id=1, source_target_pairs={{0,4},{4,0},{8,12},{12,8},{16,20},{20,16},{24,28},{28,24},{1,5},{5... | collective-permute-start | bytes 196616 | tf_op jit(solution)/shard_map/ppermute | solution.py:18
  74.0 6.9 %collective-permute-start.20 = (f32[128,128]{1,0:T(8,128)}, f32[128,128]{1,0:T(8,128)S(1)}, u32[]{:S(2)}, u32[]{:S(2)}) collective-permute-start(f32[128,128]{1,0:T(8,128)} %get-tuple-element.27.refs_0_), channel_id=1, source_target_pairs={{0,1},{1,0},{2,3},{3,2},{4,5},{5,4},{6,7},{7,6},{8,9},{9,8},{10,11... | collective-permute-start | bytes 196616 | tf_op jit(solution)/shard_map/ppermute | solution.py:18
  75.5 5.4 %collective-permute-start.21 = (f32[128,128]{1,0:T(8,128)}, f32[128,128]{1,0:T(8,128)S(1)}, u32[]{:S(2)}, u32[]{:S(2)}) collective-permute-start(f32[128,128]{1,0:T(8,128)} %get-tuple-element.27.refs_0_), channel_id=1, source_target_pairs={{0,2},{1,3},{2,0},{3,1},{4,6},{5,7},{6,4},{7,5},{8,10},{9,11},{10,... | collective-permute-start | bytes 196616 | tf_op jit(solution)/shard_map/ppermute | solution.py:18
  75.8 5.4 %collective-permute-start.22 = (f32[128,128]{1,0:T(8,128)}, f32[128,128]{1,0:T(8,128)S(1)}, u32[]{:S(2)}, u32[]{:S(2)}) collective-permute-start(f32[128,128]{1,0:T(8,128)} %get-tuple-element.27.refs_0_), channel_id=1, source_target_pairs={{0,3},{1,2},{2,1},{3,0},{4,7},{5,6},{6,5},{7,4},{8,11},{9,10},{10,... | collective-permute-start | bytes 196616 | tf_op jit(solution)/shard_map/ppermute | solution.py:18
  77.5 6.0 %collective-permute-start.23 = (f32[128,128]{1,0:T(8,128)}, f32[128,128]{1,0:T(8,128)S(1)}, u32[]{:S(2)}, u32[]{:S(2)}) collective-permute-start(f32[128,128]{1,0:T(8,128)} %get-tuple-element.28), channel_id=1, source_target_pairs={{0,16},{4,20},{8,24},{12,28},{16,0},{20,4},{24,8},{28,12},{1,17},{... | collective-permute-start | bytes 196616 | tf_op jit(solution)/shard_map/ppermute | solution.py:18
  85.8 2.2 %collective-permute-start.24 = (f32[128,128]{1,0:T(8,128)}, f32[128,128]{1,0:T(8,128)S(1)}, u32[]{:S(2)}, u32[]{:S(2)}) collective-permute-start(f32[128,128]{1,0:T(8,128)} %shard_map.51), channel_id=1, source_target_pairs={{0,4},{4,0},{8,12},{12,8},{16,20},{20,16},{24,28},{28,24},{1,5},{5... | collective-permute-start | bytes 196616 | tf_op jit(solution)/shard_map/ppermute | solution.py:18
  86.1 15.9 %collective-permute-start.26 = (bf16[1024,128]{0,1:T(8,128)(2,1)S(1)}, bf16[1024,128]{0,1:T(8,128)(2,1)S(1)}, u32[]{:S(2)}, u32[]{:S(2)}) collective-permute-start(bf16[1024,128]{0,1:T(8,128)(2,1)S(1)} %fusion.1), channel_id=1, source_target_pairs={{0,16},{4,20},{8,24},{12,28},{16,0},{20,4},{24,8},{28,12},{1,17},{... | collective-permute-start | bytes 786440 | tf_op jit(solution)/shard_map/ppermute | solution.py:18
  88.9 6.8 %collective-permute-start.25 = (f32[128,128]{1,0:T(8,128)S(1)}, f32[128,128]{1,0:T(8,128)S(1)}, u32[]{:S(2)}, u32[]{:S(2)}) collective-permute-start(f32[128,128]{1,0:T(8,128)S(1)} %add.30.refs_0_), channel_id=1, source_target_pairs={{0,8},{4,12},{8,0},{12,4},{16,24},{20,28},{24,16},{28,20},{1,9},{5... | collective-permute-start | bytes 196616 | tf_op jit(solution)/shard_map/ppermute | solution.py:18
  (22 other events, 47.3 us)

commit v3 on v2

v3 whole, which is shorter than its diff:
```python
import functools

import jax
import jax.numpy as jnp
from jax import lax
from jax.experimental import pallas as pl
from jax.experimental.pallas import tpu as pltpu
from jax.sharding import PartitionSpec as P

HB = 2
PANEL = 8
F32 = jnp.float32
BF16 = jnp.bfloat16
PARAMS = pltpu.CompilerParams(vmem_limit_bytes=16 * 1024 * 1024)


def swap(value, axis, mask):
    pairs = [(source, source ^ mask) for source in range(lax.axis_size(axis))]
    return lax.ppermute(value, axis, pairs)


def summands(value, axis, count):
    done = 1
    parts = [value]
    while done < count:
        value = total_of(parts)
        radix = 4 if count // done % 4 == 0 else 2
        parts = [value] + [swap(value, axis, step * done) for step in range(1, radix)]
        done *= radix
    return parts


def total_of(parts):
    values = [part[...] for part in parts]
    while len(values) > 1:
        values = [a + b for a, b in zip(values[::2], values[1::2])]
    return values[0]


def dot_nn(a, b):
    return lax.dot_general(a, b, (((1,), (0,)), ((), ())), preferred_element_type=F32)


def dot_nt(a, b):
    return lax.dot_general(a, b, (((1,), (1,)), ((), ())), preferred_element_type=F32)


def split(value):
    high = value.astype(BF16)
    return high, (value - high.astype(F32)).astype(BF16)


def full(dot, axis, a, b):
    a_high, a_low = split(a)
    b_high, b_low = split(b)
    left = jnp.concatenate([a_high, a_high, a_low], axis=1)
    return dot(left, jnp.concatenate([b_high, b_low, b_high], axis=axis))


nn_full = functools.partial(full, dot_nn, 0)
nt_full = functools.partial(full, dot_nt, 1)


def inverse_factor(matrix):
    size = matrix.shape[0]
    panels = size // PANEL
    shape = (PANEL, size)
    lane = lax.broadcasted_iota(jnp.int32, shape, 1)
    sub = lax.broadcasted_iota(jnp.int32, shape, 0)

    def column(rows, index):
        return jnp.broadcast_to(rows[:, index : index + 1], shape)

    def row(rows, index):
        return jnp.broadcast_to(rows[index : index + 1, :], shape)

    rows_of = [matrix[PANEL * i : PANEL * (i + 1), :] for i in range(panels)]
    out = []
    block = [column(rows_of[0], j) for j in range(PANEL)]
    for k in range(panels):
        base = PANEL * k
        active = rows_of[k]
        ahead = (
            [column(active, base + PANEL + j) for j in range(PANEL)] if k + 1 < panels else []
        )
        here = (lane >= base) & (lane < base + PANEL)
        active = jnp.where(here, jnp.where(lane == sub + base, 1.0, 0.0), active)
        kept = active
        pivots = block[0]
        for j in range(PANEL):
            pivot = row(block[j], j)
            factor = jnp.where(sub == j, 0.0, block[j]) * (1.0 / pivot)
            kept = jnp.where(sub == j, active, kept)
            pivots = jnp.where(sub == j, pivot, pivots)
            active = active - factor * row(active, j)
            for q in range(j + 1, PANEL):
                block[q] = block[q] - factor * row(block[q], j)
            ahead = [item - factor * row(item, j) for item in ahead]
        out.append(jnp.where(lane < base + PANEL, kept * lax.rsqrt(pivots), 0.0))
        if k + 1 == panels:
            break
        scale = 1.0 / pivots
        solved = active * scale
        solved_rows = [row(solved, j) for j in range(PANEL)]
        block = []
        for i in range(k + 1, panels):
            old = rows_of[i]
            columns = [column(old, base + j) for j in range(PANEL)]
            if i == k + 1:
                for q in range(PANEL):
                    item = column(old, base + PANEL + q)
                    scaled = ahead[q] * scale
                    for j in range(PANEL):
                        item = item - columns[j] * row(scaled, j)
                    block.append(item)
            new = jnp.where(here, 0.0, old)
            for j in range(PANEL):
                new = new - columns[j] * solved_rows[j]
            rows_of[i] = new
    return jnp.concatenate(out, axis=0)


def run_kernel(body, outs, *operands):
    cost = pl.CostEstimate(flops=2_000_000_000, bytes_accessed=1_000_000, transcendentals=0)
    return pl.pallas_call(
        body, out_shape=outs, cost_estimate=cost, compiler_params=PARAMS
    )(*operands)


def coupled(energy_ref, place, slots, lookup):
    left = jnp.concatenate([energy_ref[place, slot] for slot in range(slots)], axis=1)
    right = jnp.concatenate([lookup(slot) for slot in range(slots)], axis=0)
    return dot_nn(left, right)


def interior_kernel(index_ref, energy_ref, blocks_ref, sketch_ref, image_ref, sketch_out):
    count, slots = energy_ref.shape[:2]
    first = lax.axis_index("space") * blocks_ref.shape[0]
    width = sketch_out.shape[2]
    window = lax.axis_index("tm")
    step = pl.program_id(0)
    for place in range(count):
        b = (step + 1) * count + place
        value = 3.0 * blocks_ref[b].astype(F32) + coupled(
            energy_ref, place, slots, lambda slot: blocks_ref[index_ref[b, slot] - first]
        )
        image_ref[place] = value.astype(BF16)

    @pl.when(step == 0)
    def _():
        for level in range(sketch_ref.shape[0]):
            upper = window // 2**level % 2
            for half in range(2):
                start = pl.multiple_of((upper ^ half) * width, width)
                sketch_out[level, half] = sketch_ref[level, pl.ds(start, width), :].T


def edge_kernel(
    index_ref, energy_ref, before_ref, blocks_ref, after_ref, inner_ref,
    image_ref, image_t_ref, gram_ref, padded_ref,
):
    count, slots = energy_ref.shape[:2]
    blocks = blocks_ref.shape[0]
    step = pl.program_id(0)
    first = lax.axis_index("space") * blocks - HB + step * (blocks - HB)

    @pl.when(step == 0)
    def _():
        padded_ref[:HB] = before_ref[...]
        padded_ref[HB:] = blocks_ref[: 2 * HB]
        image_ref[HB : blocks - HB] = inner_ref[...]

    @pl.when(step == 1)
    def _():
        padded_ref[: 2 * HB] = blocks_ref[blocks - 2 * HB :]
        padded_ref[2 * HB :] = after_ref[...]

    for place in range(count):
        b = step * (blocks - HB) + place
        value = 3.0 * blocks_ref[b].astype(F32) + coupled(
            energy_ref, place, slots, lambda slot: padded_ref[index_ref[b, slot] - first]
        )
        image_ref[b] = value.astype(BF16)

    @pl.when(step == 1)
    def _():
        image = image_ref[...].reshape(image_t_ref.shape[1], image_t_ref.shape[0])
        image_t = image.T
        image_t_ref[...] = image_t
        gram_ref[...] = dot_nn(image_t, image)


def images_of(neighbours, energy, before, blocks, after, sketch):
    count, slots, rows, _ = energy.shape
    width = blocks.shape[2]
    levels = sketch.shape[0]

    def whole(array):
        return pl.BlockSpec(array.shape, lambda i, index: (0,) * array.ndim)

    inner_shape = jax.ShapeDtypeStruct((count - 2 * HB, rows, width), BF16)
    sketch_shape = jax.ShapeDtypeStruct((levels, 2, width, width), F32)
    energy_block = (HB, slots, rows, rows)
    steps = count // HB
    inner, sketch_t = pl.pallas_call(
        interior_kernel,
        out_shape=[inner_shape, sketch_shape],
        grid_spec=pltpu.PrefetchScalarGridSpec(
            num_scalar_prefetch=1,
            grid=(steps - 2,),
            in_specs=[
                pl.BlockSpec(energy_block, lambda i, index: (i + 1, 0, 0, 0)),
                whole(blocks),
                whole(sketch),
            ],
            out_specs=[
                pl.BlockSpec((HB, rows, width), lambda i, index: (i, 0, 0)),
                whole(sketch_shape),
            ],
        ),
        compiler_params=PARAMS,
    )(neighbours, energy, blocks, sketch)
    outs = [
        jax.ShapeDtypeStruct((count, rows, width), BF16),
        jax.ShapeDtypeStruct((width, count * rows), BF16),
        jax.ShapeDtypeStruct((width, width), F32),
    ]
    image, image_t, gram = pl.pallas_call(
        edge_kernel,
        out_shape=outs,
        grid_spec=pltpu.PrefetchScalarGridSpec(
            num_scalar_prefetch=1,
            grid=(2,),
            in_specs=[
                pl.BlockSpec(energy_block, lambda i, index: (i * (steps - 1), 0, 0, 0)),
                whole(before),
                whole(blocks),
                whole(after),
                whole(inner),
            ],
            out_specs=[whole(item) for item in outs],
            scratch_shapes=[pltpu.VMEM((3 * HB, rows, width), BF16)],
        ),
        compiler_params=PARAMS,
    )(neighbours, energy, before, blocks, after, inner)
    return image.reshape(count * rows, width), image_t, gram, sketch_t


def pair_kernel(gram_ref, image_t_ref, other_ref, out_ref):
    width = gram_ref.shape[0]
    out_ref[:width] = gram_ref[...]
    out_ref[width:] = dot_nn(image_t_ref[...], other_ref[...])


def leaf_kernel(total_rows, count, *refs):
    parts, refs = refs[:count], refs[count:]
    snapshots_ref, inverse_ref, cross_ref, modes_ref = refs
    width = inverse_ref.shape[0]
    grams = total_of(parts) / total_rows
    cross_ref[...] = grams[width:]
    inverse = inverse_factor(grams[:width])
    inverse_ref[...] = inverse
    modes_ref[...] = dot_nt(snapshots_ref[...], inverse.astype(BF16)).astype(BF16)


def merge(cross_t, sketch_ref):
    sketch_own, sketch_other = sketch_ref[0], sketch_ref[1]
    columns_own = sketch_own + nn_full(sketch_other, cross_t)
    columns_other = nt_full(sketch_own, cross_t) + sketch_other
    image_own = columns_own + nn_full(columns_other, cross_t)
    image_other = nt_full(columns_own, cross_t) + columns_other
    inner = nt_full(
        jnp.concatenate([columns_own, columns_other], axis=1),
        jnp.concatenate([image_own, image_other], axis=1),
    )
    inverse = inverse_factor(inner)
    return nn_full(inverse, columns_own), nn_full(inverse, columns_other)


def combined(own, other, half_own, half_other):
    joined = jnp.concatenate([own, other], axis=1)
    halves = jnp.concatenate([half_own.astype(BF16), half_other.astype(BF16)], axis=1)
    return dot_nt(joined, halves).astype(BF16)


def first_merge_kernel(
    cross_ref, own_ref, other_ref, sketch_ref, modes_own, modes_other,
    image_own, image_other, far_image_t, mine_ref, probe_ref, bulk_ref,
):
    rows = modes_own.shape[0]
    cross_t = nt_full(other_ref[...], nn_full(own_ref[...], cross_ref[...]))
    half_own, half_other = merge(cross_t, sketch_ref)
    mine = nn_full(half_own, own_ref[...])
    theirs = nn_full(half_other, other_ref[...])
    mine_ref[...] = mine
    image = combined(image_own[...], image_other[...], mine, theirs)
    probe_ref[...] = dot_nn(far_image_t[...], image)
    bulk_ref[:rows] = combined(modes_own[...], modes_other[...], half_own, half_other)
    bulk_ref[rows:] = image


def later_merge_kernel(
    count, *refs,
):
    parts, refs = refs[:count], refs[count:]
    sketch_ref, old_ref, bulk_own, bulk_other, far_image_t, mine_ref, probe_ref, bulk_ref = refs
    rows = far_image_t.shape[1]
    half_own, half_other = merge(total_of(parts), sketch_ref)
    mine_ref[...] = nn_full(half_own, old_ref[...])
    image = combined(bulk_own[rows:], bulk_other[rows:], half_own, half_other)
    probe_ref[...] = dot_nn(far_image_t[...], image)
    bulk_ref[:rows] = combined(bulk_own[:rows], bulk_other[:rows], half_own, half_other)
    if bulk_ref.shape[0] > rows:
        bulk_ref[rows:] = image


def last_merge_kernel(count, *refs):
    parts, refs = refs[:count], refs[count:]
    sketch_ref, own_ref, other_ref, refs = *refs[:3], refs[3:]
    *earlier, out_ref = refs
    half_own, half_other = merge(total_of(parts), sketch_ref)
    rows = out_ref.shape[1]
    for level, modes_ref in enumerate(earlier):
        out_ref[level] = modes_ref[:rows]
    out_ref[len(earlier)] = own_ref[:rows]
    out_ref[len(earlier) + 1] = combined(
        own_ref[:rows], other_ref[:rows], half_own, half_other
    )


def cross_kernel(total_rows, count, *refs):
    parts, (far_ref, out_ref) = refs[:count], refs[count:]
    out_ref[...] = nn_full(far_ref[...], total_of(parts) / total_rows)


def on_device(snapshots, energy, neighbours, sketch):
    block_count, _, block_rows, _ = energy.shape
    rows_dev, width = snapshots.shape
    space = lax.axis_size("space")
    total_rows = rows_dev * space
    levels = sketch.shape[0]
    blocks = snapshots.reshape(block_count, block_rows, width)
    ends = space - 1
    before = lax.ppermute(blocks[-HB:], "space", [(i, i + 1) for i in range(ends)])
    after = lax.ppermute(blocks[:HB], "space", [(i + 1, i) for i in range(ends)])
    square = jax.ShapeDtypeStruct((width, width), F32)

    image, image_t, gram, sketch_t = images_of(
        neighbours, energy, before, blocks, after, sketch
    )
    other_image = swap(image, "tm", 1)
    pair = run_kernel(
        pair_kernel,
        jax.ShapeDtypeStruct((2 * width, width), F32),
        gram, image_t, other_image,
    )
    parts = summands(pair, "space", space)
    far_images = [swap(image_t, "tm", 2**level) for level in range(1, levels)]
    modes_shape = jax.ShapeDtypeStruct((rows_dev, width), BF16)
    inverse, cross, current = run_kernel(
        functools.partial(leaf_kernel, total_rows, len(parts)),
        [square, square, modes_shape],
        *parts, snapshots,
    )
    other_inverse = swap(inverse, "tm", 1)
    other = swap(current, "tm", 1)
    kept = [current]
    for level in range(levels):
        bulk_shape = jax.ShapeDtypeStruct(
            (rows_dev * (2 if level + 2 < levels else 1), width), BF16
        )
        outs = [square, square, bulk_shape]
        if level == 0:
            mine, probe, current = run_kernel(
                first_merge_kernel, outs,
                cross, inverse, other_inverse, sketch_t[level],
                current, other, image, other_image, far_images[level],
            )
        else:
            far_mine = swap(mine, "tm", 2**level)
            parts = summands(probe, "space", space)
            other = swap(current, "tm", 2**level)
            cross = run_kernel(
                functools.partial(cross_kernel, total_rows, len(parts)), square, *parts, far_mine
            )
            parts = summands(cross, "tm", 2**level)
            if level + 1 < levels:
                mine, probe, current = run_kernel(
                    functools.partial(later_merge_kernel, len(parts)), outs,
                    *parts, sketch_t[level], mine, current, other, far_images[level],
                )
            else:
                out = run_kernel(
                    functools.partial(last_merge_kernel, len(parts)),
                    jax.ShapeDtypeStruct((levels + 1, rows_dev, width), BF16),
                    *parts, sketch_t[level], current, other, *kept[:-1],
                )
        kept.append(current)
    return out[:, None]


def solution(mesh):
    placed = (P("space", "tm"), P("space", None, None, None), P("space", None), P())
    return jax.shard_map(
        on_device,
        mesh=mesh,
        in_specs=placed,
        out_specs=P(None, "tm", "space", None),
        check_vma=False,
    )
```

time: 106 us -> 94.9 us (0.90)
  waiting for transfers between devices: 15.1 us -> 35.8 us
  Pallas kernels: 34.8 us -> 21.9 us
  matrix products: 6.4 us -> 0 us
  starting transfers between devices: 37.1 us -> 31.7 us
  other arithmetic: 4.78 us -> 0 us
  local copies, waits for them, and re-layouts: 6.84 us -> 5.03 us
    ppermute x25 -> x22, waiting for transfers between devices: 14.6 us -> 35.8 us  [swap(): return lax.ppermute(value, axis, pairs)]
    pallas_call x7 -> x9, Pallas kernels: 34.8 us -> 21.9 us  [the longest x7 19 us: run_kernel(): pl.pallas_call(body, out_shape=outs, cost_estimate=cost, compiler_params=...]
    dot_general x8 -> x0, matrix products: 6.4 us -> none  [the longest x7 6.13 us: dot_nt(): lax.dot_general(a, b, (((1,), (1,)), ((), ())), preferred_element_type=F32)]
    ppermute x25 -> x22, starting transfers between devices: 30.3 us -> 25.5 us  [swap(): return lax.ppermute(value, axis, pairs)]
    concatenate x1 -> x0, other arithmetic: 1.74 us -> none  [on_device(): padded = jnp.concatenate([before, blocks, after], axis=0)]
    broadcast_in_dim x1 -> x0, local copies, waits for them, and re-layouts: 1.31 us -> none  [on_device(): return jnp.stack(kept)[:, None]]
    sub x1 -> x0, other arithmetic: 1.28 us -> none  [on_device(): local_index = neighbours - (lax.axis_index('space') * block_count - HB)]
    unnamed x55 -> x8, local copies, waits for them, and re-layouts: 4.6 us -> 4.13 us
  transfers between devices with their start and end apart: 27 -> 24, of which waited for: 8 -> 11; matrix products, arithmetic and copies ran while one was open for 7% -> 0% of each run, Pallas kernels for 24% -> 6%
where the time goes in v3:
time: 94.9 us; the launch traced here: 94.6 us
  waiting for transfers between devices  35.8 us (38%)
  starting transfers between devices  31.7 us (33%)
  Pallas kernels  21.9 us (23%)
  local copies, waits for them, and re-layouts  5.03 us (5%)
    ppermute x22, waiting for transfers between devices, swap(): return lax.ppermute(value, axis, pairs)  35.8 us
    ppermute x22, starting transfers between devices, swap(): return lax.ppermute(value, axis, pairs)  25.5 us
    pallas_call x7, Pallas kernels, run_kernel(): pl.pallas_call(body, out_shape=outs, cost_estimate=cost, compiler_params=...  19 us
    ppermute x1, starting transfers between devices, on_device(): lax.ppermute(blocks[-HB:], 'space', [(i, i + 1) for i in range(ends)])  4.87 us
    unnamed x8, local copies, waits for them, and re-layouts  4.13 us
  transfers between devices with their start and end apart: 24, of which 11 were waited for; matrix products, arithmetic and copies ran while one was open for 0% of the time, Pallas kernels for 6%

profile of v3, /device:TPU:0, one launch (start us, length us, event | category | flops | bytes accessed | tf_op | source)
XLA Modules:
  0.0 94.6 jit_solution(12051883842062677089)
XLA Ops:
  0.9 4.9 %collective-permute-start = (bf16[2,128,128]{2,1,0:T(8,128)(2,1)S(1)}, bf16[2,128,128]{2,1,0:T(8,128)(2,1)S(1)}, u32[]{:S(2)}, u32[]{:S(2)}) collective-permute-start(bf16[2,128,128]{2,1,0:T(8,128)(2,1)S(1)} %bitcast.18), channel_id=1, source_target_pairs={{0,1},{1,2},{2,3},{4,5},{5,6},{6,7},{8,9},{9,10},{10,11},{12,13},{... | collective-permute-start | bytes 196616 | tf_op jit(solution)/shard_map/ppermute | solution.py:344
  5.8 1.3 %collective-permute-start.1 = (bf16[2,128,128]{2,1,0:T(8,128)(2,1)S(1)}, bf16[2,128,128]{2,1,0:T(8,128)(2,1)S(1)}, u32[]{:S(2)}, u32[]{:S(2)}) collective-permute-start(bf16[2,128,128]{2,1,0:T(8,128)(2,1)S(1)} %bitcast.17), channel_id=1, source_target_pairs={{1,0},{2,1},{3,2},{5,4},{6,5},{7,6},{9,8},{10,9},{11,10},{13,12},{... | collective-permute-start | bytes 196616 | tf_op jit(solution)/shard_map/ppermute | solution.py:345
  7.1 1.5 %copy-done = bf16[8,7,128,128]{3,2,1,0:T(8,128)(2,1)S(1)} copy-done((bf16[8,7,128,128]{3,2,1,0:T(8,128)(2,1)S(1)}, bf16[8,7,128,128]{3,2,1,0:T(8,128)(2,1)}, u32[]{:S(2)}) %copy-start) | copy-done | bytes 1835032
  8.6 0.9 %copy-done.1 = bf16[1024,128]{1,0:T(8,128)(2,1)S(1)} copy-done((bf16[1024,128]{1,0:T(8,128)(2,1)S(1)}, bf16[1024,128]{1,0:T(8,128)(2,1)}, u32[]{:S(2)}) %copy-start.1) | copy-done | bytes 262168
  9.5 1.0 %copy-done.2 = f32[3,256,128]{2,1,0:T(8,128)S(1)} copy-done((f32[3,256,128]{2,1,0:T(8,128)S(1)}, f32[3,256,128]{2,1,0:T(8,128)}, u32[]{:S(2)}) %copy-start.2) | copy-done | bytes 393240
  11.2 1.4 %shard_map.46 = (bf16[4,128,128]{2,1,0:T(8,128)(2,1)S(1)}, f32[3,2,128,128]{3,2,1,0:T(8,128)S(1)}) custom-call(s32[8,7]{1,0:T(8,128)S(1)} %copy-done.3, bf16[8,7,128,128]{3,2,1,0:T(8,128)(2,1)S(1)} %copy-done, bf16[8,128,128]{2,1,0:T(8,128)(2,1)S(1)} %bitcast.13, f32[3,256,128]{2,1,0:T(8,128)S(1)} %copy-done.2), custom_call_target="tpu_custom_call" | custom-call | tf_op jit(solution)/shard_map/pallas_call | solution.py:205
  12.6 1.5 %shard_map.47 = (bf16[8,128,128]{2,1,0:T(8,128)(2,1)S(1)}, bf16[128,1024]{1,0:T(8,128)(2,1)S(1)}, f32[128,128]{1,0:T(8,128)S(1)}) custom-call(s32[8,7]{1,0:T(8,128)S(1)} %copy-done.3, bf16[8,7,128,128]{3,2,1,0:T(8,128)(2,1)S(1)} %copy-done, bf16[2,128,128]{2,1,0:T(8,128)(2,1)S(1)} %collective-permute-done.before_ref, bf16[8,128,128]{2,1,0:T(8,128)(2,1)S(1)} %bitcast.14, ...), custom_call_target="tpu_custom_call" | custom-call | tf_op jit(solution)/shard_map/pallas_call | solution.py:228
  14.2 1.5 %collective-permute-done.2.other_ref.image_other = bf16[1024,128]{1,0:T(8,128)(2,1)S(1)} collective-permute-done((bf16[1024,128]{1,0:T(8,128)(2,1)S(1)}, bf16[1024,128]{1,0:T(8,128)(2,1)S(1)}, u32[]{:S(2)}, u32[]{:S(2)}) %collective-permute-start.2) | collective-permute-done | bytes 262176 | tf_op jit(solution)/shard_map/ppermute | solution.py:19
  16.0 3.7 %collective-permute-start.5 = (f32[256,128]{1,0:T(8,128)S(1)}, f32[256,128]{1,0:T(8,128)S(1)}, u32[]{:S(2)}, u32[]{:S(2)}) collective-permute-start(f32[256,128]{1,0:T(8,128)S(1)} %shard_map.48.refs_0_), channel_id=1, source_target_pairs={{0,3},{1,2},{2,1},{3,0},{4,7},{5,6},{6,5},{7,4},{8,11},{9,10},{10,... | collective-permute-start | bytes 393224 | tf_op jit(solution)/shard_map/ppermute | solution.py:19
  20.1 0.9 collective-permute-start.3
  21.1 1.6 %collective-permute-start.8 = (bf16[128,1024]{1,0:T(8,128)(2,1)S(1)}, bf16[128,1024]{1,0:T(8,128)(2,1)S(1)}, u32[]{:S(2)}, u32[]{:S(2)}) collective-permute-start(bf16[128,1024]{1,0:T(8,128)(2,1)S(1)} %get-tuple-element.21.image_t_ref), channel_id=1, source_target_pairs={{0,8},{4,12},{8,0},{12,4},{16,24},{20,28},{24,16},{28,20},{1,9},{5... | collective-permute-start | bytes 786440 | tf_op jit(solution)/shard_map/ppermute | solution.py:19
  22.6 0.9 %collective-permute-done.5.refs_3_ = f32[256,128]{1,0:T(8,128)S(1)} collective-permute-done((f32[256,128]{1,0:T(8,128)S(1)}, f32[256,128]{1,0:T(8,128)S(1)}, u32[]{:S(2)}, u32[]{:S(2)}) %collective-permute-start.5) | collective-permute-done | bytes 131104 | tf_op jit(solution)/shard_map/ppermute | solution.py:19
  23.6 2.6 %collective-permute-done.4.refs_2_ = f32[256,128]{1,0:T(8,128)S(1)} collective-permute-done((f32[256,128]{1,0:T(8,128)S(1)}, f32[256,128]{1,0:T(8,128)S(1)}, u32[]{:S(2)}, u32[]{:S(2)}) %collective-permute-start.4) | collective-permute-done | bytes 131104 | tf_op jit(solution)/shard_map/ppermute | solution.py:19
  26.2 1.2 %collective-permute-done.3.refs_1_ = f32[256,128]{1,0:T(8,128)S(1)} collective-permute-done((f32[256,128]{1,0:T(8,128)S(1)}, f32[256,128]{1,0:T(8,128)S(1)}, u32[]{:S(2)}, u32[]{:S(2)}) %collective-permute-start.3) | collective-permute-done | bytes 131104 | tf_op jit(solution)/shard_map/ppermute | solution.py:19
  27.4 3.5 %shard_map.49 = (f32[128,128]{1,0:T(8,128)S(1)}, f32[128,128]{1,0:T(8,128)S(1)}, bf16[1024,128]{1,0:T(8,128)(2,1)S(1)}) custom-call(f32[256,128]{1,0:T(8,128)S(1)} %shard_map.48.refs_0_, f32[256,128]{1,0:T(8,128)S(1)} %collective-permute-done.3.refs_1_, f32[256,128]{1,0:T(8,128)S(1)} %collective-permute-done.4.refs_2_, ...), custom_call_target="tpu_custom_call" | custom-call | flops 2000000000 | bytes 1000000 | tf_op jit(solution)/shard_map/pallas_call | solution.py:125
  31.5 1.1 %collective-permute-done.6.other_ref = f32[128,128]{1,0:T(8,128)S(1)} collective-permute-done((f32[128,128]{1,0:T(8,128)S(1)}, f32[128,128]{1,0:T(8,128)S(1)}, u32[]{:S(2)}, u32[]{:S(2)}) %collective-permute-start.6) | collective-permute-done | bytes 65568 | tf_op jit(solution)/shard_map/ppermute | solution.py:19
  32.6 5.1 %shard_map.50 = (f32[128,128]{1,0:T(8,128)S(1)}, f32[128,128]{1,0:T(8,128)S(1)}, bf16[2048,128]{1,0:T(8,128)(2,1)S(1)}) custom-call(f32[128,128]{1,0:T(8,128)S(1)} %get-tuple-element.23.cross_ref, f32[128,128]{1,0:T(8,128)S(1)} %get-tuple-element.24.own_ref, f32[128,128]{1,0:T(8,128)S(1)} %collective-permute-done.6.other_ref, ...), custom_call_target="tpu_custom_call" | custom-call | flops 2000000000 | bytes 1000000 | tf_op jit(solution)/shard_map/pallas_call | solution.py:125
  37.6 1.6 %collective-permute-start.14 = (bf16[2048,128]{1,0:T(8,128)(2,1)S(1)}, bf16[2048,128]{1,0:T(8,128)(2,1)S(1)}, u32[]{:S(2)}, u32[]{:S(2)}) collective-permute-start(bf16[2048,128]{1,0:T(8,128)(2,1)S(1)} %get-tuple-element.29.refs_4_.refs_8_), channel_id=1, source_target_pairs={{0,8},{4,12},{8,0},{12,4},{16,24},{20,28},{24,16},{28,20},{1,9},{5... | collective-permute-start | bytes 1572872 | tf_op jit(solution)/shard_map/ppermute | solution.py:19
  39.7 1.4 %collective-permute-start.11 = (f32[128,128]{1,0:T(8,128)S(1)}, f32[128,128]{1,0:T(8,128)S(1)}, u32[]{:S(2)}, u32[]{:S(2)}) collective-permute-start(f32[128,128]{1,0:T(8,128)S(1)} %get-tuple-element.27.refs_0_), channel_id=1, source_target_pairs={{0,3},{1,2},{2,1},{3,0},{4,7},{5,6},{6,5},{7,4},{8,11},{9,10},{10,... | collective-permute-start | bytes 196616 | tf_op jit(solution)/shard_map/ppermute | solution.py:19
  41.8 1.4 %collective-permute-start.9 = (f32[128,128]{1,0:T(8,128)S(1)}, f32[128,128]{1,0:T(8,128)S(1)}, u32[]{:S(2)}, u32[]{:S(2)}) collective-permute-start(f32[128,128]{1,0:T(8,128)S(1)} %get-tuple-element.27.refs_0_), channel_id=1, source_target_pairs={{0,1},{1,0},{2,3},{3,2},{4,5},{5,4},{6,7},{7,6},{8,9},{9,8},{10,11... | collective-permute-start | bytes 196616 | tf_op jit(solution)/shard_map/ppermute | solution.py:19
  43.2 9.8 %collective-permute-done.12.refs_4_ = f32[128,128]{1,0:T(8,128)S(1)} collective-permute-done((f32[128,128]{1,0:T(8,128)S(1)}, f32[128,128]{1,0:T(8,128)S(1)}, u32[]{:S(2)}, u32[]{:S(2)}) %collective-permute-start.12) | collective-permute-done | bytes 65568 | tf_op jit(solution)/shard_map/ppermute | solution.py:19
  53.1 2.6 %collective-permute-start.15 = (bf16[128,1024]{1,0:T(8,128)(2,1)S(1)}, bf16[128,1024]{1,0:T(8,128)(2,1)S(1)}, u32[]{:S(2)}, u32[]{:S(2)}) collective-permute-start(bf16[128,1024]{1,0:T(8,128)(2,1)S(1)} %get-tuple-element.21.image_t_ref), channel_id=1, source_target_pairs={{0,16},{4,20},{8,24},{12,28},{16,0},{20,4},{24,8},{28,12},{1,17},{... | collective-permute-start | bytes 786440 | tf_op jit(solution)/shard_map/ppermute | solution.py:19
  55.9 11.1 %collective-permute-done.15.refs_6_ = bf16[128,1024]{1,0:T(8,128)(2,1)S(1)} collective-permute-done((bf16[128,1024]{1,0:T(8,128)(2,1)S(1)}, bf16[128,1024]{1,0:T(8,128)(2,1)S(1)}, u32[]{:S(2)}, u32[]{:S(2)}) %collective-permute-start.15) | collective-permute-done | bytes 262176 | tf_op jit(solution)/shard_map/ppermute | solution.py:19
  67.1 4.6 %shard_map.52 = (f32[128,128]{1,0:T(8,128)S(1)}, f32[128,128]{1,0:T(8,128)S(1)}, bf16[1024,128]{1,0:T(8,128)(2,1)S(1)}) custom-call(f32[128,128]{1,0:T(8,128)S(1)} %shard_map.51.refs_0_, f32[128,128]{1,0:T(8,128)S(1)} %collective-permute-done.13.refs_1_, f32[2,128,128]{2,1,0:T(8,128)S(1)} %get-tuple-element.34.refs_2_, ...), custom_call_target="tpu_custom_call" | custom-call | flops 2000000000 | bytes 1000000 | tf_op jit(solution)/shard_map/pallas_call | solution.py:125
  71.8 1.5 %collective-permute-start.18 = (f32[128,128]{1,0:T(8,128)S(1)}, f32[128,128]{1,0:T(8,128)S(1)}, u32[]{:S(2)}, u32[]{:S(2)}) collective-permute-start(f32[128,128]{1,0:T(8,128)S(1)} %get-tuple-element.30.refs_0_), channel_id=1, source_target_pairs={{0,3},{1,2},{2,1},{3,0},{4,7},{5,6},{6,5},{7,4},{8,11},{9,10},{10,... | collective-permute-start | bytes 196616 | tf_op jit(solution)/shard_map/ppermute | solution.py:19
  73.9 1.4 %collective-permute-start.16 = (f32[128,128]{1,0:T(8,128)S(1)}, f32[128,128]{1,0:T(8,128)S(1)}, u32[]{:S(2)}, u32[]{:S(2)}) collective-permute-start(f32[128,128]{1,0:T(8,128)S(1)} %get-tuple-element.30.refs_0_), channel_id=1, source_target_pairs={{0,1},{1,0},{2,3},{3,2},{4,5},{5,4},{6,7},{7,6},{8,9},{9,8},{10,11... | collective-permute-start | bytes 196616 | tf_op jit(solution)/shard_map/ppermute | solution.py:19
  75.3 2.8 %collective-permute-start.23 = (bf16[1024,128]{1,0:T(8,128)(2,1)S(1)}, bf16[1024,128]{1,0:T(8,128)(2,1)S(1)}, u32[]{:S(2)}, u32[]{:S(2)}) collective-permute-start(bf16[1024,128]{1,0:T(8,128)(2,1)S(1)} %get-tuple-element.32.refs_5_), channel_id=1, source_target_pairs={{0,16},{4,20},{8,24},{12,28},{16,0},{20,4},{24,8},{28,12},{1,17},{... | collective-permute-start | bytes 786440 | tf_op jit(solution)/shard_map/ppermute | solution.py:19
  79.2 1.9 %collective-permute-start.22 = (f32[128,128]{1,0:T(8,128)S(1)}, f32[128,128]{1,0:T(8,128)S(1)}, u32[]{:S(2)}, u32[]{:S(2)}) collective-permute-start(f32[128,128]{1,0:T(8,128)S(1)} %shard_map.53.refs_0_), channel_id=1, source_target_pairs={{0,12},{4,8},{8,4},{12,0},{16,28},{20,24},{24,20},{28,16},{1,13},{... | collective-permute-start | bytes 196616 | tf_op jit(solution)/shard_map/ppermute | solution.py:19
  81.1 1.5 %collective-permute-start.21 = (f32[128,128]{1,0:T(8,128)S(1)}, f32[128,128]{1,0:T(8,128)S(1)}, u32[]{:S(2)}, u32[]{:S(2)}) collective-permute-start(f32[128,128]{1,0:T(8,128)S(1)} %shard_map.53.refs_0_), channel_id=1, source_target_pairs={{0,8},{4,12},{8,0},{12,4},{16,24},{20,28},{24,16},{28,20},{1,9},{5... | collective-permute-start | bytes 196616 | tf_op jit(solution)/shard_map/ppermute | solution.py:19
  83.1 4.0 %collective-permute-done.21.refs_2_ = f32[128,128]{1,0:T(8,128)S(1)} collective-permute-done((f32[128,128]{1,0:T(8,128)S(1)}, f32[128,128]{1,0:T(8,128)S(1)}, u32[]{:S(2)}, u32[]{:S(2)}) %collective-permute-start.21) | collective-permute-done | bytes 65568 | tf_op jit(solution)/shard_map/ppermute | solution.py:19
  87.1 2.4 %collective-permute-done.23.refs_6_ = bf16[1024,128]{1,0:T(8,128)(2,1)S(1)} collective-permute-done((bf16[1024,128]{1,0:T(8,128)(2,1)S(1)}, bf16[1024,128]{1,0:T(8,128)(2,1)S(1)}, u32[]{:S(2)}, u32[]{:S(2)}) %collective-permute-start.23) | collective-permute-done | bytes 262176 | tf_op jit(solution)/shard_map/ppermute | solution.py:19
  89.5 5.1 %shard_map.54 = bf16[4,1024,128]{2,1,0:T(8,128)(2,1)} custom-call(f32[128,128]{1,0:T(8,128)S(1)} %shard_map.53.refs_0_, f32[128,128]{1,0:T(8,128)S(1)} %collective-permute-done.20.refs_1_, f32[128,128]{1,0:T(8,128)S(1)} %collective-permute-done.21.refs_2_, f32[128,128]{1,0:T(8,128)S(1)} %collective-permute-done.22.refs_3_, ...), custom_call_target="tpu_custom_call" | custom-call | flops 2000000000 | bytes 1000000 | tf_op jit(solution)/shard_map/pallas_call | solution.py:125
  (35 shorter events, 6.4 us)
Async XLA Ops:
  0.9 11.7 %collective-permute-start = (bf16[2,128,128]{2,1,0:T(8,128)(2,1)S(1)}, bf16[2,128,128]{2,1,0:T(8,128)(2,1)S(1)}, u32[]{:S(2)}, u32[]{:S(2)}) collective-permute-start(bf16[2,128,128]{2,1,0:T(8,128)(2,1)S(1)} %bitcast.18), channel_id=1, source_target_pairs={{0,1},{1,2},{2,3},{4,5},{5,6},{6,7},{8,9},{9,10},{10,11},{12,13},{... | collective-permute-start | bytes 196616 | tf_op jit(solution)/shard_map/ppermute | solution.py:344
  5.8 6.8 %collective-permute-start.1 = (bf16[2,128,128]{2,1,0:T(8,128)(2,1)S(1)}, bf16[2,128,128]{2,1,0:T(8,128)(2,1)S(1)}, u32[]{:S(2)}, u32[]{:S(2)}) collective-permute-start(bf16[2,128,128]{2,1,0:T(8,128)(2,1)S(1)} %bitcast.17), channel_id=1, source_target_pairs={{1,0},{2,1},{3,2},{5,4},{6,5},{7,6},{9,8},{10,9},{11,10},{13,12},{... | collective-permute-start | bytes 196616 | tf_op jit(solution)/shard_map/ppermute | solution.py:345
  7.1 1.5 %copy-start = (bf16[8,7,128,128]{3,2,1,0:T(8,128)(2,1)S(1)}, bf16[8,7,128,128]{3,2,1,0:T(8,128)(2,1)}, u32[]{:S(2)}) copy-start(bf16[8,7,128,128]{3,2,1,0:T(8,128)(2,1)} %energy_ref.3) | copy-start | bytes 5505028
  8.6 0.9 %copy-start.1 = (bf16[1024,128]{1,0:T(8,128)(2,1)S(1)}, bf16[1024,128]{1,0:T(8,128)(2,1)}, u32[]{:S(2)}) copy-start(bf16[1024,128]{1,0:T(8,128)(2,1)} %refs_4_.1) | copy-start | bytes 786436
  9.5 1.0 %copy-start.2 = (f32[3,256,128]{2,1,0:T(8,128)S(1)}, f32[3,256,128]{2,1,0:T(8,128)}, u32[]{:S(2)}) copy-start(f32[3,256,128]{2,1,0:T(8,128)} %sketch_ref.1) | copy-start | bytes 1179652
  10.5 0.7 copy-start.3
  14.1 1.6 %collective-permute-start.2 = (bf16[1024,128]{1,0:T(8,128)(2,1)S(1)}, bf16[1024,128]{1,0:T(8,128)(2,1)S(1)}, u32[]{:S(2)}, u32[]{:S(2)}) collective-permute-start(bf16[1024,128]{1,0:T(8,128)(2,1)S(1)} %bitcast.15), channel_id=1, source_target_pairs={{0,4},{4,0},{8,12},{12,8},{16,20},{20,16},{24,28},{28,24},{1,5},{5... | collective-permute-start | bytes 786440 | tf_op jit(solution)/shard_map/ppermute | solution.py:19
  16.0 7.6 %collective-permute-start.5 = (f32[256,128]{1,0:T(8,128)S(1)}, f32[256,128]{1,0:T(8,128)S(1)}, u32[]{:S(2)}, u32[]{:S(2)}) collective-permute-start(f32[256,128]{1,0:T(8,128)S(1)} %shard_map.48.refs_0_), channel_id=1, source_target_pairs={{0,3},{1,2},{2,1},{3,0},{4,7},{5,6},{6,5},{7,4},{8,11},{9,10},{10,... | collective-permute-start | bytes 393224 | tf_op jit(solution)/shard_map/ppermute | solution.py:19
  19.6 6.6 %collective-permute-start.4 = (f32[256,128]{1,0:T(8,128)S(1)}, f32[256,128]{1,0:T(8,128)S(1)}, u32[]{:S(2)}, u32[]{:S(2)}) collective-permute-start(f32[256,128]{1,0:T(8,128)S(1)} %shard_map.48.refs_0_), channel_id=1, source_target_pairs={{0,2},{1,3},{2,0},{3,1},{4,6},{5,7},{6,4},{7,5},{8,10},{9,11},{10,... | collective-permute-start | bytes 393224 | tf_op jit(solution)/shard_map/ppermute | solution.py:19
  20.1 7.3 %collective-permute-start.3 = (f32[256,128]{1,0:T(8,128)S(1)}, f32[256,128]{1,0:T(8,128)S(1)}, u32[]{:S(2)}, u32[]{:S(2)}) collective-permute-start(f32[256,128]{1,0:T(8,128)S(1)} %shard_map.48.refs_0_), channel_id=1, source_target_pairs={{0,1},{1,0},{2,3},{3,2},{4,5},{5,4},{6,7},{7,6},{8,9},{9,8},{10,11... | collective-permute-start | bytes 393224 | tf_op jit(solution)/shard_map/ppermute | solution.py:19
  21.1 10.4 %collective-permute-start.8 = (bf16[128,1024]{1,0:T(8,128)(2,1)S(1)}, bf16[128,1024]{1,0:T(8,128)(2,1)S(1)}, u32[]{:S(2)}, u32[]{:S(2)}) collective-permute-start(bf16[128,1024]{1,0:T(8,128)(2,1)S(1)} %get-tuple-element.21.image_t_ref), channel_id=1, source_target_pairs={{0,8},{4,12},{8,0},{12,4},{16,24},{20,28},{24,16},{28,20},{1,9},{5... | collective-permute-start | bytes 786440 | tf_op jit(solution)/shard_map/ppermute | solution.py:19
  30.9 1.7 %collective-permute-start.7 = (bf16[1024,128]{1,0:T(8,128)(2,1)S(1)}, bf16[1024,128]{1,0:T(8,128)(2,1)S(1)}, u32[]{:S(2)}, u32[]{:S(2)}) collective-permute-start(bf16[1024,128]{1,0:T(8,128)(2,1)S(1)} %get-tuple-element.26.modes_own.refs_7_), channel_id=1, source_target_pairs={{0,4},{4,0},{8,12},{12,8},{16,20},{20,16},{24,28},{28,24},{1,5},{5... | collective-permute-start | bytes 786440 | tf_op jit(solution)/shard_map/ppermute | solution.py:19
  31.0 1.6 %collective-permute-start.6 = (f32[128,128]{1,0:T(8,128)S(1)}, f32[128,128]{1,0:T(8,128)S(1)}, u32[]{:S(2)}, u32[]{:S(2)}) collective-permute-start(f32[128,128]{1,0:T(8,128)S(1)} %get-tuple-element.24.own_ref), channel_id=1, source_target_pairs={{0,4},{4,0},{8,12},{12,8},{16,20},{20,16},{24,28},{28,24},{1,5},{5... | collective-permute-start | bytes 196616 | tf_op jit(solution)/shard_map/ppermute | solution.py:19
  37.6 29.4 %collective-permute-start.14 = (bf16[2048,128]{1,0:T(8,128)(2,1)S(1)}, bf16[2048,128]{1,0:T(8,128)(2,1)S(1)}, u32[]{:S(2)}, u32[]{:S(2)}) collective-permute-start(bf16[2048,128]{1,0:T(8,128)(2,1)S(1)} %get-tuple-element.29.refs_4_.refs_8_), channel_id=1, source_target_pairs={{0,8},{4,12},{8,0},{12,4},{16,24},{20,28},{24,16},{28,20},{1,9},{5... | collective-permute-start | bytes 1572872 | tf_op jit(solution)/shard_map/ppermute | solution.py:19
  39.3 13.8 %collective-permute-start.12 = (f32[128,128]{1,0:T(8,128)S(1)}, f32[128,128]{1,0:T(8,128)S(1)}, u32[]{:S(2)}, u32[]{:S(2)}) collective-permute-start(f32[128,128]{1,0:T(8,128)S(1)} %get-tuple-element.28.refs_3_), channel_id=1, source_target_pairs={{0,8},{4,12},{8,0},{12,4},{16,24},{20,28},{24,16},{28,20},{1,9},{5... | collective-permute-start | bytes 196616 | tf_op jit(solution)/shard_map/ppermute | solution.py:19
  39.7 15.9 %collective-permute-start.11 = (f32[128,128]{1,0:T(8,128)S(1)}, f32[128,128]{1,0:T(8,128)S(1)}, u32[]{:S(2)}, u32[]{:S(2)}) collective-permute-start(f32[128,128]{1,0:T(8,128)S(1)} %get-tuple-element.27.refs_0_), channel_id=1, source_target_pairs={{0,3},{1,2},{2,1},{3,0},{4,7},{5,6},{6,5},{7,4},{8,11},{9,10},{10,... | collective-permute-start | bytes 196616 | tf_op jit(solution)/shard_map/ppermute | solution.py:19
  41.2 14.5 %collective-permute-start.10 = (f32[128,128]{1,0:T(8,128)S(1)}, f32[128,128]{1,0:T(8,128)S(1)}, u32[]{:S(2)}, u32[]{:S(2)}) collective-permute-start(f32[128,128]{1,0:T(8,128)S(1)} %get-tuple-element.27.refs_0_), channel_id=1, source_target_pairs={{0,2},{1,3},{2,0},{3,1},{4,6},{5,7},{6,4},{7,5},{8,10},{9,11},{10,... | collective-permute-start | bytes 196616 | tf_op jit(solution)/shard_map/ppermute | solution.py:19
  41.8 13.9 %collective-permute-start.9 = (f32[128,128]{1,0:T(8,128)S(1)}, f32[128,128]{1,0:T(8,128)S(1)}, u32[]{:S(2)}, u32[]{:S(2)}) collective-permute-start(f32[128,128]{1,0:T(8,128)S(1)} %get-tuple-element.27.refs_0_), channel_id=1, source_target_pairs={{0,1},{1,0},{2,3},{3,2},{4,5},{5,4},{6,7},{7,6},{8,9},{9,8},{10,11... | collective-permute-start | bytes 196616 | tf_op jit(solution)/shard_map/ppermute | solution.py:19
  53.1 14.0 %collective-permute-start.15 = (bf16[128,1024]{1,0:T(8,128)(2,1)S(1)}, bf16[128,1024]{1,0:T(8,128)(2,1)S(1)}, u32[]{:S(2)}, u32[]{:S(2)}) collective-permute-start(bf16[128,1024]{1,0:T(8,128)(2,1)S(1)} %get-tuple-element.21.image_t_ref), channel_id=1, source_target_pairs={{0,16},{4,20},{8,24},{12,28},{16,0},{20,4},{24,8},{28,12},{1,17},{... | collective-permute-start | bytes 786440 | tf_op jit(solution)/shard_map/ppermute | solution.py:19
  55.9 11.2 %collective-permute-start.13 = (f32[128,128]{1,0:T(8,128)S(1)}, f32[128,128]{1,0:T(8,128)S(1)}, u32[]{:S(2)}, u32[]{:S(2)}) collective-permute-start(f32[128,128]{1,0:T(8,128)S(1)} %shard_map.51.refs_0_), channel_id=1, source_target_pairs={{0,4},{4,0},{8,12},{12,8},{16,20},{20,16},{24,28},{28,24},{1,5},{5... | collective-permute-start | bytes 196616 | tf_op jit(solution)/shard_map/ppermute | solution.py:19
  71.7 7.2 %collective-permute-start.19 = (f32[128,128]{1,0:T(8,128)S(1)}, f32[128,128]{1,0:T(8,128)S(1)}, u32[]{:S(2)}, u32[]{:S(2)}) collective-permute-start(f32[128,128]{1,0:T(8,128)S(1)} %get-tuple-element.31), channel_id=1, source_target_pairs={{0,16},{4,20},{8,24},{12,28},{16,0},{20,4},{24,8},{28,12},{1,17},{... | collective-permute-start | bytes 196616 | tf_op jit(solution)/shard_map/ppermute | solution.py:19
  71.8 7.1 %collective-permute-start.18 = (f32[128,128]{1,0:T(8,128)S(1)}, f32[128,128]{1,0:T(8,128)S(1)}, u32[]{:S(2)}, u32[]{:S(2)}) collective-permute-start(f32[128,128]{1,0:T(8,128)S(1)} %get-tuple-element.30.refs_0_), channel_id=1, source_target_pairs={{0,3},{1,2},{2,1},{3,0},{4,7},{5,6},{6,5},{7,4},{8,11},{9,10},{10,... | collective-permute-start | bytes 196616 | tf_op jit(solution)/shard_map/ppermute | solution.py:19
  73.3 5.6 %collective-permute-start.17 = (f32[128,128]{1,0:T(8,128)S(1)}, f32[128,128]{1,0:T(8,128)S(1)}, u32[]{:S(2)}, u32[]{:S(2)}) collective-permute-start(f32[128,128]{1,0:T(8,128)S(1)} %get-tuple-element.30.refs_0_), channel_id=1, source_target_pairs={{0,2},{1,3},{2,0},{3,1},{4,6},{5,7},{6,4},{7,5},{8,10},{9,11},{10,... | collective-permute-start | bytes 196616 | tf_op jit(solution)/shard_map/ppermute | solution.py:19
  73.9 5.0 %collective-permute-start.16 = (f32[128,128]{1,0:T(8,128)S(1)}, f32[128,128]{1,0:T(8,128)S(1)}, u32[]{:S(2)}, u32[]{:S(2)}) collective-permute-start(f32[128,128]{1,0:T(8,128)S(1)} %get-tuple-element.30.refs_0_), channel_id=1, source_target_pairs={{0,1},{1,0},{2,3},{3,2},{4,5},{5,4},{6,7},{7,6},{8,9},{9,8},{10,11... | collective-permute-start | bytes 196616 | tf_op jit(solution)/shard_map/ppermute | solution.py:19
  75.3 14.1 %collective-permute-start.23 = (bf16[1024,128]{1,0:T(8,128)(2,1)S(1)}, bf16[1024,128]{1,0:T(8,128)(2,1)S(1)}, u32[]{:S(2)}, u32[]{:S(2)}) collective-permute-start(bf16[1024,128]{1,0:T(8,128)(2,1)S(1)} %get-tuple-element.32.refs_5_), channel_id=1, source_target_pairs={{0,16},{4,20},{8,24},{12,28},{16,0},{20,4},{24,8},{28,12},{1,17},{... | collective-permute-start | bytes 786440 | tf_op jit(solution)/shard_map/ppermute | solution.py:19
  79.2 3.9 %collective-permute-start.22 = (f32[128,128]{1,0:T(8,128)S(1)}, f32[128,128]{1,0:T(8,128)S(1)}, u32[]{:S(2)}, u32[]{:S(2)}) collective-permute-start(f32[128,128]{1,0:T(8,128)S(1)} %shard_map.53.refs_0_), channel_id=1, source_target_pairs={{0,12},{4,8},{8,4},{12,0},{16,28},{20,24},{24,20},{28,16},{1,13},{... | collective-permute-start | bytes 196616 | tf_op jit(solution)/shard_map/ppermute | solution.py:19
  81.1 5.9 %collective-permute-start.21 = (f32[128,128]{1,0:T(8,128)S(1)}, f32[128,128]{1,0:T(8,128)S(1)}, u32[]{:S(2)}, u32[]{:S(2)}) collective-permute-start(f32[128,128]{1,0:T(8,128)S(1)} %shard_map.53.refs_0_), channel_id=1, source_target_pairs={{0,8},{4,12},{8,0},{12,4},{16,24},{20,28},{24,16},{28,20},{1,9},{5... | collective-permute-start | bytes 196616 | tf_op jit(solution)/shard_map/ppermute | solution.py:19
  82.7 4.4 %collective-permute-start.20 = (f32[128,128]{1,0:T(8,128)S(1)}, f32[128,128]{1,0:T(8,128)S(1)}, u32[]{:S(2)}, u32[]{:S(2)}) collective-permute-start(f32[128,128]{1,0:T(8,128)S(1)} %shard_map.53.refs_0_), channel_id=1, source_target_pairs={{0,4},{4,0},{8,12},{12,8},{16,20},{20,16},{24,28},{28,24},{1,5},{5... | collective-permute-start | bytes 196616 | tf_op jit(solution)/shard_map/ppermute | solution.py:19

commit v4 on v3

v4 whole, which is shorter than its diff:
```python
import functools

import jax
import jax.numpy as jnp
from jax import lax
from jax.experimental import pallas as pl
from jax.experimental.pallas import tpu as pltpu
from jax.sharding import PartitionSpec as P


HB = 2
PANEL = 8
F32 = jnp.float32
BF16 = jnp.bfloat16
PARAMS = pltpu.CompilerParams(vmem_limit_bytes=16 * 1024 * 1024)
WIDE = pltpu.CompilerParams(vmem_limit_bytes=62_000_000)


def swap(value, axis, mask):
    pairs = [(source, source ^ mask) for source in range(lax.axis_size(axis))]
    return lax.ppermute(value, axis, pairs)


def summands(value, axis, count, widest):
    done = 1
    parts = [value]
    while done < count:
        if len(parts) > 1:
            value = run_kernel(add_kernel, jax.ShapeDtypeStruct(value.shape, F32), *parts)
        radix = 4 if widest == 4 and count // done % 4 == 0 else 2
        parts = [value]
        for step in range(1, radix):
            parts.append(swap(value, axis, step * done))
        done *= radix
    return parts


def add_kernel(*refs):
    refs[-1][...] = total_of(refs[:-1])


def total_of(parts):
    values = [part[...] for part in parts]
    while len(values) > 1:
        values = [a + b for a, b in zip(values[::2], values[1::2])]
    return values[0]


def dot_nn(a, b):
    return lax.dot_general(a, b, (((1,), (0,)), ((), ())), preferred_element_type=F32)


def dot_nt(a, b):
    return lax.dot_general(a, b, (((1,), (1,)), ((), ())), preferred_element_type=F32)


def split(value):
    high = value.astype(BF16)
    return high, (value - high.astype(F32)).astype(BF16)


def full(dot, axis, a, b):
    a_high, a_low = split(a)
    b_high, b_low = split(b)
    left = jnp.concatenate([a_high, a_high, a_low], axis=1)
    return dot(left, jnp.concatenate([b_high, b_low, b_high], axis=axis))


nn_full = functools.partial(full, dot_nn, 0)
nt_full = functools.partial(full, dot_nt, 1)


def inverse_factor(matrix):
    size = matrix.shape[0]
    panels = size // PANEL
    shape = (PANEL, size)
    lane = lax.broadcasted_iota(jnp.int32, shape, 1)
    sub = lax.broadcasted_iota(jnp.int32, shape, 0)

    def column(rows, index):
        return jnp.broadcast_to(rows[:, index : index + 1], shape)

    def row(rows, index):
        return jnp.broadcast_to(rows[index : index + 1, :], shape)

    rows_of = [matrix[PANEL * i : PANEL * (i + 1), :] for i in range(panels)]
    out = []
    block = [column(rows_of[0], j) for j in range(PANEL)]
    for k in range(panels):
        base = PANEL * k
        active = rows_of[k]
        ahead = (
            [column(active, base + PANEL + j) for j in range(PANEL)] if k + 1 < panels else []
        )
        here = (lane >= base) & (lane < base + PANEL)
        active = jnp.where(here, jnp.where(lane == sub + base, 1.0, 0.0), active)
        kept = active
        pivots = block[0]
        for j in range(PANEL):
            pivot = row(block[j], j)
            factor = jnp.where(sub == j, 0.0, block[j]) * (1.0 / pivot)
            kept = jnp.where(sub == j, active, kept)
            pivots = jnp.where(sub == j, pivot, pivots)
            active = active - factor * row(active, j)
            for q in range(j + 1, PANEL):
                block[q] = block[q] - factor * row(block[q], j)
            ahead = [item - factor * row(item, j) for item in ahead]
        out.append(jnp.where(lane < base + PANEL, kept * lax.rsqrt(pivots), 0.0))
        if k + 1 == panels:
            break
        scale = 1.0 / pivots
        solved = active * scale
        solved_rows = [row(solved, j) for j in range(PANEL)]
        block = []
        for i in range(k + 1, panels):
            old = rows_of[i]
            columns = [column(old, base + j) for j in range(PANEL)]
            if i == k + 1:
                for q in range(PANEL):
                    item = column(old, base + PANEL + q)
                    scaled = ahead[q] * scale
                    for j in range(PANEL):
                        item = item - columns[j] * row(scaled, j)
                    block.append(item)
            new = jnp.where(here, 0.0, old)
            for j in range(PANEL):
                new = new - columns[j] * solved_rows[j]
            rows_of[i] = new
    return jnp.concatenate(out, axis=0)


def run_kernel(body, outs, *operands):
    cost = pl.CostEstimate(flops=2_000_000_000, bytes_accessed=1_000_000, transcendentals=0)
    return pl.pallas_call(
        body, out_shape=outs, cost_estimate=cost, compiler_params=PARAMS
    )(*operands)


def coupled(energy_ref, place, slots, lookup):
    left = jnp.concatenate([energy_ref[place, slot] for slot in range(slots)], axis=1)
    right = jnp.concatenate([lookup(slot) for slot in range(slots)], axis=0)
    return dot_nn(left, right)


def interior_kernel(
    index_hbm, energy_hbm, blocks_hbm, sketch_hbm,
    image_ref, sketch_out, edges_ref, blocks_ref, index_ref, energy_ref, sketch_ref, sems,
):
    count = blocks_ref.shape[0]
    inner, slots = energy_ref.shape[:2]
    width = sketch_out.shape[2]
    copies = [
        pltpu.make_async_copy(source, target, sems.at[place])
        for place, (source, target) in enumerate(
            [
                (index_hbm, index_ref),
                (blocks_hbm, blocks_ref),
                (energy_hbm.at[pl.ds(HB, inner)], energy_ref),
                (sketch_hbm, sketch_ref),
                (energy_hbm.at[pl.ds(0, HB)], edges_ref.at[0]),
                (energy_hbm.at[pl.ds(count - HB, HB)], edges_ref.at[1]),
            ]
        )
    ]
    for copy in copies:
        copy.start()
    first = lax.axis_index("space") * count
    window = lax.axis_index("tm")
    for copy in copies[:3]:
        copy.wait()
    for place in range(inner):
        b = HB + place
        value = 3.0 * blocks_ref[b].astype(F32) + coupled(
            energy_ref, place, slots, lambda slot: blocks_ref[index_ref[b, slot] - first]
        )
        image_ref[place] = value.astype(BF16)
    copies[3].wait()
    for level in range(sketch_ref.shape[0]):
        upper = window // 2**level % 2
        for half in range(2):
            start = pl.multiple_of((upper ^ half) * width, width)
            sketch_out[level, half] = sketch_ref[level, pl.ds(start, width), :].T
    for copy in copies[4:]:
        copy.wait()


def edge_kernel(
    index_ref, edges_ref, before_ref, blocks_ref, after_ref, inner_ref,
    image_ref, image_t_ref, gram_ref, padded_ref,
):
    slots = edges_ref.shape[2]
    blocks = blocks_ref.shape[0]
    padded_ref[0, :HB] = before_ref[...]
    padded_ref[0, HB:] = blocks_ref[: 2 * HB]
    padded_ref[1, : 2 * HB] = blocks_ref[blocks - 2 * HB :]
    padded_ref[1, 2 * HB :] = after_ref[...]
    image_ref[HB : blocks - HB] = inner_ref[...]
    for side in range(2):
        first = lax.axis_index("space") * blocks - HB + side * (blocks - HB)
        for place in range(HB):
            b = side * (blocks - HB) + place
            value = 3.0 * blocks_ref[b].astype(F32) + coupled(
                edges_ref.at[side], place, slots,
                lambda slot: padded_ref[side, index_ref[b, slot] - first],
            )
            image_ref[b] = value.astype(BF16)
    image = image_ref[...].reshape(image_t_ref.shape[1], image_t_ref.shape[0])
    image_t = image.T
    image_t_ref[...] = image_t
    gram_ref[...] = dot_nn(image_t, image)


def interior_of(neighbours, energy, blocks, sketch):
    count, slots, rows, _ = energy.shape
    width = blocks.shape[2]
    levels = sketch.shape[0]
    inner = count - 2 * HB
    return pl.pallas_call(
        interior_kernel,
        out_shape=[
            jax.ShapeDtypeStruct((inner, rows, width), BF16),
            jax.ShapeDtypeStruct((levels, 2, width, width), F32),
            jax.ShapeDtypeStruct((2, HB, slots, rows, rows), BF16),
            jax.ShapeDtypeStruct(blocks.shape, BF16),
        ],
        in_specs=[pl.BlockSpec(memory_space=pltpu.HBM)] * 4,
        scratch_shapes=[
            pltpu.SMEM(neighbours.shape, jnp.int32),
            pltpu.VMEM((inner, slots, rows, rows), BF16),
            pltpu.VMEM(sketch.shape, F32),
            pltpu.SemaphoreType.DMA((6,)),
        ],
        compiler_params=WIDE,
    )(neighbours, energy, blocks, sketch)


def edge_of(neighbours, edges, before, blocks, after, inner):
    count, rows, width = blocks.shape
    image, image_t, gram = pl.pallas_call(
        edge_kernel,
        out_shape=[
            jax.ShapeDtypeStruct((count, rows, width), BF16),
            jax.ShapeDtypeStruct((width, count * rows), BF16),
            jax.ShapeDtypeStruct((width, width), F32),
        ],
        in_specs=[pl.BlockSpec(memory_space=pltpu.SMEM)]
        + [pl.BlockSpec(memory_space=pltpu.VMEM)] * 5,
        scratch_shapes=[pltpu.VMEM((2, 3 * HB, rows, width), BF16)],
        compiler_params=PARAMS,
    )(neighbours, edges, before, blocks, after, inner)
    return image.reshape(count * rows, width), image_t, gram


def pair_kernel(gram_ref, image_t_ref, other_ref, out_ref):
    width = gram_ref.shape[0]
    out_ref[:width] = gram_ref[...]
    out_ref[width:] = dot_nn(image_t_ref[...], other_ref[...])


def leaf_kernel(total_rows, count, *refs):
    parts, refs = refs[:count], refs[count:]
    snapshots_ref, inverse_ref, cross_ref, modes_ref = refs
    width = inverse_ref.shape[0]
    grams = total_of(parts) / total_rows
    cross_ref[...] = grams[width:]
    inverse = inverse_factor(grams[:width])
    inverse_ref[...] = inverse
    modes_ref[...] = dot_nt(snapshots_ref[...], inverse.astype(BF16)).astype(BF16)


def merge(cross_t, sketch_ref):
    sketch_own, sketch_other = sketch_ref[0], sketch_ref[1]
    columns_own = sketch_own + nn_full(sketch_other, cross_t)
    columns_other = nt_full(sketch_own, cross_t) + sketch_other
    image_own = columns_own + nn_full(columns_other, cross_t)
    image_other = nt_full(columns_own, cross_t) + columns_other
    inner = nt_full(
        jnp.concatenate([columns_own, columns_other], axis=1),
        jnp.concatenate([image_own, image_other], axis=1),
    )
    inverse = inverse_factor(inner)
    return nn_full(inverse, columns_own), nn_full(inverse, columns_other)


def combined(own, other, half_own, half_other):
    joined = jnp.concatenate([own, other], axis=1)
    halves = jnp.concatenate([half_own.astype(BF16), half_other.astype(BF16)], axis=1)
    return dot_nt(joined, halves).astype(BF16)


def choose(first, second):
    odd = lax.axis_index("tm") % 2 == 1
    return jnp.where(odd, second, first), jnp.where(odd, first, second)


def write_bulk(refs, modes, image):
    modes_ref, *image_ref, outgoing_ref = refs
    modes_ref[...] = modes
    if image_ref:
        image_ref[0][...] = image
        outgoing_ref[...] = choose(modes, image)[0]
    else:
        part = outgoing_ref.shape[0]
        outgoing_ref[...] = choose(modes[:part], modes[part:])[0]


def read_modes(came_ref, shared_ref, rows):
    first, second = choose(came_ref[...], shared_ref[...])
    if first.shape[0] == rows:
        return first
    return jnp.concatenate([first, second], axis=0)


def first_merge_kernel(
    cross_ref, own_ref, other_ref, sketch_ref, modes_own, modes_other,
    image_own, image_other, far_image_t, mine_ref, probe_ref, *bulk_refs,
):
    cross_t = nt_full(other_ref[...], nn_full(own_ref[...], cross_ref[...]))
    half_own, half_other = merge(cross_t, sketch_ref)
    mine = nn_full(half_own, own_ref[...])
    theirs = nn_full(half_other, other_ref[...])
    mine_ref[...] = mine
    image = combined(image_own[...], image_other[...], mine, theirs)
    probe_ref[...] = dot_nn(far_image_t[...], image)
    modes = combined(modes_own[...], modes_other[...], half_own, half_other)
    write_bulk(bulk_refs, modes, image)


def merge_kernel(count, *refs):
    parts, (sketch_ref, old_ref, halves_ref, mine_ref) = refs[:count], refs[count:]
    half_own, half_other = merge(total_of(parts), sketch_ref)
    halves_ref[0] = half_own.astype(BF16)
    halves_ref[1] = half_other.astype(BF16)
    mine_ref[...] = nn_full(half_own, old_ref[...])


def apply_kernel(
    halves_ref, modes_own, image_own, came_ref, shared_ref, far_image_t, probe_ref, *bulk_refs
):
    modes_other, image_other = choose(came_ref[...], shared_ref[...])
    image = combined(image_own[...], image_other, halves_ref[0], halves_ref[1])
    probe_ref[...] = dot_nn(far_image_t[...], image)
    modes = combined(modes_own[...], modes_other, halves_ref[0], halves_ref[1])
    write_bulk(bulk_refs, modes, image)


def output_kernel(halves_ref, came_ref, shared_ref, *refs):
    *earlier, out_ref = refs
    for level, modes_ref in enumerate(earlier):
        out_ref[level] = modes_ref[...]
    modes_other = read_modes(came_ref, shared_ref, out_ref.shape[1])
    out_ref[len(earlier)] = combined(
        earlier[-1][...], modes_other, halves_ref[0], halves_ref[1]
    )


def cross_kernel(total_rows, count, *refs):
    parts, (far_ref, out_ref) = refs[:count], refs[count:]
    out_ref[...] = nn_full(far_ref[...], total_of(parts) / total_rows)


def modes_of(snapshots, energy, neighbours, sketch):
    block_count, _, block_rows, _ = energy.shape
    rows_dev, width = snapshots.shape
    space = lax.axis_size("space")
    total_rows = rows_dev * space
    levels = sketch.shape[0]
    blocks = snapshots.reshape(block_count, block_rows, width)
    ends = space - 1
    before = lax.ppermute(blocks[-HB:], "space", [(i, i + 1) for i in range(ends)])
    after = lax.ppermute(blocks[:HB], "space", [(i + 1, i) for i in range(ends)])
    square = jax.ShapeDtypeStruct((width, width), F32)
    modes_shape = jax.ShapeDtypeStruct((rows_dev, width), BF16)
    half_shape = jax.ShapeDtypeStruct((rows_dev // 2, width), BF16)
    halves_shape = jax.ShapeDtypeStruct((2, width, width), BF16)

    inner, sketch_t, edges, blocks = interior_of(neighbours, energy, blocks, sketch)
    image, image_t, gram = edge_of(neighbours, edges, before, blocks, after, inner)
    other_image = swap(image, "tm", 1)
    pair = run_kernel(
        pair_kernel,
        jax.ShapeDtypeStruct((2 * width, width), F32),
        gram, image_t, other_image,
    )
    parts = summands(pair, "space", space, 4)
    far_images = [swap(image_t, "tm", 2**level) for level in range(1, levels)]
    inverse, cross, modes = run_kernel(
        functools.partial(leaf_kernel, total_rows, len(parts)),
        [square, square, modes_shape],
        *parts, blocks.reshape(rows_dev, width),
    )
    other_inverse = swap(inverse, "tm", 1)
    other = swap(modes, "tm", 1)
    kept = [modes]
    for level in range(levels):
        deep = level + 2 < levels
        outs = [square, square, modes_shape] + ([modes_shape] * 2 if deep else [half_shape])
        if level == 0:
            mine, probe, *bulk = run_kernel(
                first_merge_kernel, outs,
                cross, inverse, other_inverse, sketch_t[level],
                modes, other, image, other_image, far_images[level],
            )
        else:
            far_mine = swap(mine, "tm", 2**level)
            parts = summands(probe, "space", space, 4)
            came = swap(bulk[-1], "tm", 2**level)
            shared = swap(came, "tm", 1)
            cross = run_kernel(
                functools.partial(cross_kernel, total_rows, len(parts)),
                square, *parts, far_mine,
            )
            parts = summands(cross, "tm", 2**level, 2)
            halves, mine = run_kernel(
                functools.partial(merge_kernel, len(parts)), [halves_shape, square],
                *parts, sketch_t[level], mine,
            )
            if level + 1 < levels:
                probe, *bulk = run_kernel(
                    apply_kernel, outs[1:],
                    halves, *bulk[:2], came, shared, far_images[level],
                )
            else:
                out = run_kernel(
                    output_kernel,
                    jax.ShapeDtypeStruct((levels + 1, rows_dev, width), BF16),
                    halves, came, shared, *kept,
                )
        kept.append(bulk[0])
    return out[:, None]


def solution(mesh):
    placed = (P("space", "tm"), P("space", None, None, None), P("space", None), P())
    return jax.shard_map(
        modes_of,
        mesh=mesh,
        in_specs=placed,
        out_specs=P(None, "tm", "space", None),
        check_vma=False,
    )
```

time: 94.9 us -> 88.3 us (0.930)
  starting transfers between devices: 31.7 us -> 27.5 us
  waiting for transfers between devices: 35.8 us -> 32.2 us
  Pallas kernels: 21.9 us -> 24.1 us
  local copies, waits for them, and re-layouts: 5.03 us -> 3.96 us
    ppermute x22 -> x23, waiting for transfers between devices: 35.8 us -> 30.4 us  [swap(): return lax.ppermute(value, axis, pairs)]
    ppermute x22 -> x23, starting transfers between devices: 25.5 us -> 21.3 us  [swap(): return lax.ppermute(value, axis, pairs)]
    ppermute x2, waiting for transfers between devices: 0.01 us -> 1.75 us  [the longest x1 1.75 us: modes_of(): lax.ppermute(blocks[:HB], 'space', [(i + 1, i) for i in range(ends)])]
    pallas_call x2, Pallas kernels: 2.9 us -> 4.34 us  [the longest x1 3.09 us: interior_of(): pl.pallas_call(interior_kernel, out_shape=[jax.ShapeDtypeStruct((inner, r...]
    unnamed x8 -> x12, local copies, waits for them, and re-layouts: 4.13 us -> 3.04 us
    pallas_call x7 -> x10, Pallas kernels: 19 us -> 19.8 us  [run_kernel(): pl.pallas_call(body, out_shape=outs, cost_estimate=cost, compiler_params=...]
  transfers between devices with their start and end apart: 24 -> 25, of which waited for: 11 -> 14; matrix products, arithmetic and copies ran while one was open for 0% -> 0% of each run, Pallas kernels for 6% -> 18%
where the time goes in v4:
time: 88.3 us; the launch traced here: 87.9 us
  waiting for transfers between devices  32.2 us (36%)
  starting transfers between devices  27.5 us (31%)
  Pallas kernels  24.1 us (27%)
  local copies, waits for them, and re-layouts  3.96 us (4%)
    ppermute x23, waiting for transfers between devices, swap(): return lax.ppermute(value, axis, pairs)  30.4 us
    ppermute x23, starting transfers between devices, swap(): return lax.ppermute(value, axis, pairs)  21.3 us
    pallas_call x10, Pallas kernels, run_kernel(): pl.pallas_call(body, out_shape=outs, cost_estimate=cost, compiler_params=...  19.8 us
    ppermute x1, starting transfers between devices, modes_of(): lax.ppermute(blocks[-HB:], 'space', [(i, i + 1) for i in range(ends)])  4.87 us
    pallas_call x1, Pallas kernels, interior_of(): pl.pallas_call(interior_kernel, out_shape=[jax.ShapeDtypeStruct((inner, r...  3.09 us
    unnamed x12, local copies, waits for them, and re-layouts  3.04 us
  transfers between devices with their start and end apart: 25, of which 14 were waited for; matrix products, arithmetic and copies ran while one was open for 0% of the time, Pallas kernels for 18%

profile of v4, /device:TPU:0, one launch (start us, length us, event | category | flops | bytes accessed | tf_op | source)
XLA Modules:
  0.0 87.9 jit_solution(9151102783801179468)
XLA Ops:
  0.9 4.9 %collective-permute-start = (bf16[2,128,128]{2,1,0:T(8,128)(2,1)S(1)}, bf16[2,128,128]{2,1,0:T(8,128)(2,1)S(1)}, u32[]{:S(2)}, u32[]{:S(2)}) collective-permute-start(bf16[2,128,128]{2,1,0:T(8,128)(2,1)S(1)} %bitcast.19), channel_id=1, source_target_pairs={{0,1},{1,2},{2,3},{4,5},{5,6},{6,7},{8,9},{9,10},{10,11},{12,13},{... | collective-permute-start | bytes 196616 | tf_op jit(solution)/shard_map/ppermute | solution.py:370
  5.8 1.3 %collective-permute-start.1 = (bf16[2,128,128]{2,1,0:T(8,128)(2,1)S(1)}, bf16[2,128,128]{2,1,0:T(8,128)(2,1)S(1)}, u32[]{:S(2)}, u32[]{:S(2)}) collective-permute-start(bf16[2,128,128]{2,1,0:T(8,128)(2,1)S(1)} %bitcast.18), channel_id=1, source_target_pairs={{1,0},{2,1},{3,2},{5,4},{6,5},{7,6},{9,8},{10,9},{11,10},{13,12},{... | collective-permute-start | bytes 196616 | tf_op jit(solution)/shard_map/ppermute | solution.py:371
  7.1 3.1 %shard_map.46 = (bf16[4,128,128]{2,1,0:T(8,128)(2,1)}, f32[3,2,128,128]{3,2,1,0:T(8,128)}, bf16[2,2,7,128,128]{4,3,2,1,0:T(8,128)(2,1)}, bf16[8,128,128]{2,1,0:T(8,128)(2,1)}) custom-call(s32[8,7]{1,0:T(8,128)} %index_ref.1, bf16[8,7,128,128]{3,2,1,0:T(8,128)(2,1)} %energy_hbm.1, bf16[8,128,128]{2,1,0:T(8,128)(2,1)} %bitcast.17, f32[3,256,128]{2,1,0:T(8,128)} %sketch_hbm.1), custom_call_target="tpu_custom_call" | custom-call | tf_op jit(solution)/shard_map/pallas_call | solution.py:218
  10.2 1.8 %collective-permute-done.1.after_ref = bf16[2,128,128]{2,1,0:T(8,128)(2,1)S(1)} collective-permute-done((bf16[2,128,128]{2,1,0:T(8,128)(2,1)S(1)}, bf16[2,128,128]{2,1,0:T(8,128)(2,1)S(1)}, u32[]{:S(2)}, u32[]{:S(2)}) %collective-permute-start.1) | collective-permute-done | bytes 65568 | tf_op jit(solution)/shard_map/ppermute | solution.py:371
  11.9 1.2 %copy-done = bf16[2,2,7,128,128]{4,3,2,1,0:T(8,128)(2,1)S(1)} copy-done((bf16[2,2,7,128,128]{4,3,2,1,0:T(8,128)(2,1)S(1)}, bf16[2,2,7,128,128]{4,3,2,1,0:T(8,128)(2,1)}, u32[]{:S(2)}) %copy-start) | copy-done | bytes 917528
  15.0 1.3 %shard_map.47 = (bf16[8,128,128]{2,1,0:T(8,128)(2,1)S(1)}, bf16[128,1024]{1,0:T(8,128)(2,1)S(1)}, f32[128,128]{1,0:T(8,128)S(1)}) custom-call(s32[8,7]{1,0:T(8,128)S(1)} %copy-done.4, bf16[2,2,7,128,128]{4,3,2,1,0:T(8,128)(2,1)S(1)} %copy-done, bf16[2,128,128]{2,1,0:T(8,128)(2,1)S(1)} %collective-permute-done.before_ref, bf16[8,128,128]{2,1,0:T(8,128)(2,1)S(1)} %copy-done.1, ...), custom_call_target="tpu_custom_call" | custom-call | tf_op jit(solution)/shard_map/pallas_call | solution.py:239
  16.3 1.5 %collective-permute-done.2.other_ref.image_other = bf16[1024,128]{1,0:T(8,128)(2,1)S(1)} collective-permute-done((bf16[1024,128]{1,0:T(8,128)(2,1)S(1)}, bf16[1024,128]{1,0:T(8,128)(2,1)S(1)}, u32[]{:S(2)}, u32[]{:S(2)}) %collective-permute-start.2) | collective-permute-done | bytes 262176 | tf_op jit(solution)/shard_map/ppermute | solution.py:21
  18.1 1.9 %collective-permute-start.5 = (f32[256,128]{1,0:T(8,128)S(1)}, f32[256,128]{1,0:T(8,128)S(1)}, u32[]{:S(2)}, u32[]{:S(2)}) collective-permute-start(f32[256,128]{1,0:T(8,128)S(1)} %shard_map.48.refs_0_), channel_id=1, source_target_pairs={{0,3},{1,2},{2,1},{3,0},{4,7},{5,6},{6,5},{7,4},{8,11},{9,10},{10,... | collective-permute-start | bytes 393224 | tf_op jit(solution)/shard_map/ppermute | solution.py:21
  20.0 2.0 %collective-permute-start.4 = (f32[256,128]{1,0:T(8,128)S(1)}, f32[256,128]{1,0:T(8,128)S(1)}, u32[]{:S(2)}, u32[]{:S(2)}) collective-permute-start(f32[256,128]{1,0:T(8,128)S(1)} %shard_map.48.refs_0_), channel_id=1, source_target_pairs={{0,2},{1,3},{2,0},{3,1},{4,6},{5,7},{6,4},{7,5},{8,10},{9,11},{10,... | collective-permute-start | bytes 393224 | tf_op jit(solution)/shard_map/ppermute | solution.py:21
  22.0 1.6 %collective-permute-start.8 = (bf16[128,1024]{1,0:T(8,128)(2,1)S(1)}, bf16[128,1024]{1,0:T(8,128)(2,1)S(1)}, u32[]{:S(2)}, u32[]{:S(2)}) collective-permute-start(bf16[128,1024]{1,0:T(8,128)(2,1)S(1)} %get-tuple-element.30.image_t_ref), channel_id=1, source_target_pairs={{0,8},{4,12},{8,0},{12,4},{16,24},{20,28},{24,16},{28,20},{1,9},{5... | collective-permute-start | bytes 786440 | tf_op jit(solution)/shard_map/ppermute | solution.py:21
  23.6 1.7 %collective-permute-done.5.refs_3_ = f32[256,128]{1,0:T(8,128)S(1)} collective-permute-done((f32[256,128]{1,0:T(8,128)S(1)}, f32[256,128]{1,0:T(8,128)S(1)}, u32[]{:S(2)}, u32[]{:S(2)}) %collective-permute-start.5) | collective-permute-done | bytes 131104 | tf_op jit(solution)/shard_map/ppermute | solution.py:21
  25.3 2.1 %collective-permute-done.4.refs_2_ = f32[256,128]{1,0:T(8,128)S(1)} collective-permute-done((f32[256,128]{1,0:T(8,128)S(1)}, f32[256,128]{1,0:T(8,128)S(1)}, u32[]{:S(2)}, u32[]{:S(2)}) %collective-permute-start.4) | collective-permute-done | bytes 131104 | tf_op jit(solution)/shard_map/ppermute | solution.py:21
  27.8 3.4 %shard_map.49 = (f32[128,128]{1,0:T(8,128)S(1)}, f32[128,128]{1,0:T(8,128)S(1)}, bf16[1024,128]{1,0:T(8,128)(2,1)S(1)}) custom-call(f32[256,128]{1,0:T(8,128)S(1)} %shard_map.48.refs_0_, f32[256,128]{1,0:T(8,128)S(1)} %collective-permute-done.3.refs_1_, f32[256,128]{1,0:T(8,128)S(1)} %collective-permute-done.4.refs_2_, ...), custom_call_target="tpu_custom_call" | custom-call | flops 2000000000 | bytes 1000000 | tf_op jit(solution)/shard_map/pallas_call | solution.py:134
  31.8 1.1 %collective-permute-done.6.other_ref = f32[128,128]{1,0:T(8,128)S(1)} collective-permute-done((f32[128,128]{1,0:T(8,128)S(1)}, f32[128,128]{1,0:T(8,128)S(1)}, u32[]{:S(2)}, u32[]{:S(2)}) %collective-permute-start.6) | collective-permute-done | bytes 65568 | tf_op jit(solution)/shard_map/ppermute | solution.py:21
  32.9 5.0 %shard_map.50 = (f32[128,128]{1,0:T(8,128)S(1)}, f32[128,128]{1,0:T(8,128)S(1)}, bf16[1024,128]{1,0:T(8,128)(2,1)S(1)}, bf16[1024,128]{1,0:T(8,128)(2,1)S(1)}, bf16[1024,128]{1,0:T(8,128)(2,1)S(1)}) custom-call(f32[128,128]{1,0:T(8,128)S(1)} %get-tuple-element.32.cross_ref, f32[128,128]{1,0:T(8,128)S(1)} %get-tuple-element.33.own_ref, ...), custom_call_target="tpu_custom_call" | custom-call | flops 2000000000 | bytes 1000000 | tf_op jit(solution)/shard_map/pallas_call | solution.py:134
  37.9 1.6 %collective-permute-start.14 = (bf16[1024,128]{1,0:T(8,128)(2,1)S(1)}, bf16[1024,128]{1,0:T(8,128)(2,1)S(1)}, u32[]{:S(2)}, u32[]{:S(2)}) collective-permute-start(bf16[1024,128]{1,0:T(8,128)(2,1)S(1)} %get-tuple-element.41), channel_id=1, source_target_pairs={{0,8},{4,12},{8,0},{12,4},{16,24},{20,28},{24,16},{28,20},{1,9},{5... | collective-permute-start | bytes 786440 | tf_op jit(solution)/shard_map/ppermute | solution.py:21
  40.0 2.1 %collective-permute-start.11 = (f32[128,128]{1,0:T(8,128)S(1)}, f32[128,128]{1,0:T(8,128)S(1)}, u32[]{:S(2)}, u32[]{:S(2)}) collective-permute-start(f32[128,128]{1,0:T(8,128)S(1)} %get-tuple-element.36.refs_0_), channel_id=1, source_target_pairs={{0,3},{1,2},{2,1},{3,0},{4,7},{5,6},{6,5},{7,4},{8,11},{9,10},{10,... | collective-permute-start | bytes 196616 | tf_op jit(solution)/shard_map/ppermute | solution.py:21
  42.1 1.2 %collective-permute-start.10 = (f32[128,128]{1,0:T(8,128)S(1)}, f32[128,128]{1,0:T(8,128)S(1)}, u32[]{:S(2)}, u32[]{:S(2)}) collective-permute-start(f32[128,128]{1,0:T(8,128)S(1)} %get-tuple-element.36.refs_0_), channel_id=1, source_target_pairs={{0,2},{1,3},{2,0},{3,1},{4,6},{5,7},{6,4},{7,5},{8,10},{9,11},{10,... | collective-permute-start | bytes 196616 | tf_op jit(solution)/shard_map/ppermute | solution.py:21
  43.5 4.2 %collective-permute-done.12.refs_4_ = f32[128,128]{1,0:T(8,128)S(1)} collective-permute-done((f32[128,128]{1,0:T(8,128)S(1)}, f32[128,128]{1,0:T(8,128)S(1)}, u32[]{:S(2)}, u32[]{:S(2)}) %collective-permute-start.12) | collective-permute-done | bytes 65568 | tf_op jit(solution)/shard_map/ppermute | solution.py:21
  47.8 2.6 %collective-permute-start.16 = (bf16[128,1024]{1,0:T(8,128)(2,1)S(1)}, bf16[128,1024]{1,0:T(8,128)(2,1)S(1)}, u32[]{:S(2)}, u32[]{:S(2)}) collective-permute-start(bf16[128,1024]{1,0:T(8,128)(2,1)S(1)} %get-tuple-element.30.image_t_ref), channel_id=1, source_target_pairs={{0,16},{4,20},{8,24},{12,28},{16,0},{20,4},{24,8},{28,12},{1,17},{... | collective-permute-start | bytes 786440 | tf_op jit(solution)/shard_map/ppermute | solution.py:21
  52.0 4.1 %shard_map.52 = (bf16[2,128,128]{2,1,0:T(8,128)(2,1)S(1)}, f32[128,128]{1,0:T(8,128)S(1)}) custom-call(f32[128,128]{1,0:T(8,128)S(1)} %shard_map.51.refs_0_, f32[128,128]{1,0:T(8,128)S(1)} %collective-permute-done.13.refs_1_, f32[2,128,128]{2,1,0:T(8,128)S(1)} %get-tuple-element.48.refs_2_, f32[128,128]{1,0:T(8,128)S(1)} %get-tuple-element.37.refs_3_), custom_call_target="tpu_custom_call" | custom-call | flops 2000000000 | bytes 1000000 | tf_op jit(solution)/shard_map/pallas_call | solution.py:134
  56.5 7.3 %collective-permute-done.16.far_image_t = bf16[128,1024]{1,0:T(8,128)(2,1)S(1)} collective-permute-done((bf16[128,1024]{1,0:T(8,128)(2,1)S(1)}, bf16[128,1024]{1,0:T(8,128)(2,1)S(1)}, u32[]{:S(2)}, u32[]{:S(2)}) %collective-permute-start.16) | collective-permute-done | bytes 262176 | tf_op jit(solution)/shard_map/ppermute | solution.py:21
  64.7 2.2 %collective-permute-start.19 = (f32[128,128]{1,0:T(8,128)S(1)}, f32[128,128]{1,0:T(8,128)S(1)}, u32[]{:S(2)}, u32[]{:S(2)}) collective-permute-start(f32[128,128]{1,0:T(8,128)S(1)} %get-tuple-element.42.refs_0_), channel_id=1, source_target_pairs={{0,3},{1,2},{2,1},{3,0},{4,7},{5,6},{6,5},{7,4},{8,11},{9,10},{10,... | collective-permute-start | bytes 196616 | tf_op jit(solution)/shard_map/ppermute | solution.py:21
  66.8 1.1 %collective-permute-start.18 = (f32[128,128]{1,0:T(8,128)S(1)}, f32[128,128]{1,0:T(8,128)S(1)}, u32[]{:S(2)}, u32[]{:S(2)}) collective-permute-start(f32[128,128]{1,0:T(8,128)S(1)} %get-tuple-element.42.refs_0_), channel_id=1, source_target_pairs={{0,2},{1,3},{2,0},{3,1},{4,6},{5,7},{6,4},{7,5},{8,10},{9,11},{10,... | collective-permute-start | bytes 196616 | tf_op jit(solution)/shard_map/ppermute | solution.py:21
  68.2 1.7 %collective-permute-done.19.refs_3_ = f32[128,128]{1,0:T(8,128)S(1)} collective-permute-done((f32[128,128]{1,0:T(8,128)S(1)}, f32[128,128]{1,0:T(8,128)S(1)}, u32[]{:S(2)}, u32[]{:S(2)}) %collective-permute-start.19) | collective-permute-done | bytes 65568 | tf_op jit(solution)/shard_map/ppermute | solution.py:21
  69.9 1.2 %collective-permute-done.18.refs_2_ = f32[128,128]{1,0:T(8,128)S(1)} collective-permute-done((f32[128,128]{1,0:T(8,128)S(1)}, f32[128,128]{1,0:T(8,128)S(1)}, u32[]{:S(2)}, u32[]{:S(2)}) %collective-permute-start.18) | collective-permute-done | bytes 65568 | tf_op jit(solution)/shard_map/ppermute | solution.py:21
  71.1 1.1 %collective-permute-done.17.refs_1_ = f32[128,128]{1,0:T(8,128)S(1)} collective-permute-done((f32[128,128]{1,0:T(8,128)S(1)}, f32[128,128]{1,0:T(8,128)S(1)}, u32[]{:S(2)}, u32[]{:S(2)}) %collective-permute-start.17) | collective-permute-done | bytes 65568 | tf_op jit(solution)/shard_map/ppermute | solution.py:21
  72.6 1.2 %collective-permute-done.21.refs_1_ = f32[128,128]{1,0:T(8,128)S(1)} collective-permute-done((f32[128,128]{1,0:T(8,128)S(1)}, f32[128,128]{1,0:T(8,128)S(1)}, u32[]{:S(2)}, u32[]{:S(2)}) %collective-permute-start.21) | collective-permute-done | bytes 65568 | tf_op jit(solution)/shard_map/ppermute | solution.py:21
  73.7 2.3 %collective-permute-start.22 = (f32[128,128]{1,0:T(8,128)S(1)}, f32[128,128]{1,0:T(8,128)S(1)}, u32[]{:S(2)}, u32[]{:S(2)}) collective-permute-start(f32[128,128]{1,0:T(8,128)S(1)} %shard_map.55.refs_0_), channel_id=1, source_target_pairs={{0,8},{4,12},{8,0},{12,4},{16,24},{20,28},{24,16},{28,20},{1,9},{5... | collective-permute-start | bytes 196616 | tf_op jit(solution)/shard_map/ppermute | solution.py:21
  76.1 6.0 %collective-permute-done.23.came_ref = bf16[512,128]{1,0:T(8,128)(2,1)S(1)} collective-permute-done((bf16[512,128]{1,0:T(8,128)(2,1)S(1)}, bf16[512,128]{1,0:T(8,128)(2,1)S(1)}, u32[]{:S(2)}, u32[]{:S(2)}) %collective-permute-start.23) | collective-permute-done | bytes 131104 | tf_op jit(solution)/shard_map/ppermute | solution.py:21
  82.1 4.6 %shard_map.56 = (bf16[2,128,128]{2,1,0:T(8,128)(2,1)S(1)}, f32[128,128]{1,0:T(8,128)}) custom-call(f32[128,128]{1,0:T(8,128)S(1)} %shard_map.55.refs_0_, f32[128,128]{1,0:T(8,128)S(1)} %collective-permute-done.22.refs_1_, f32[2,128,128]{2,1,0:T(8,128)S(1)} %get-tuple-element.47.refs_2_, f32[128,128]{1,0:T(8,128)S(1)} %get-tuple-element.43.refs_3_), custom_call_target="tpu_custom_call" | custom-call | flops 2000000000 | bytes 1000000 | tf_op jit(solution)/shard_map/pallas_call | solution.py:134
  86.7 1.3 %shard_map.57 = bf16[4,1024,128]{2,1,0:T(8,128)(2,1)} custom-call(bf16[2,128,128]{2,1,0:T(8,128)(2,1)S(1)} %get-tuple-element.44.halves_ref, bf16[512,128]{1,0:T(8,128)(2,1)S(1)} %collective-permute-done.23.came_ref, bf16[512,128]{1,0:T(8,128)(2,1)S(1)} %collective-permute-done.24.shared_ref, bf16[1024,128]{1,0:T(8,128)(2,1)S(1)} %get-tuple-element.35.modes_own.refs_0_, ...), custom_call_target="tpu_custom_call" | custom-call | flops 2000000000 | bytes 1000000 | tf_op jit(solution)/shard_map/pallas_call | solution.py:134
  (44 shorter events, 8.2 us)
Async XLA Ops:
  0.0 11.9 %copy-start.4 = (s32[8,7]{1,0:T(8,128)S(1)}, s32[8,7]{1,0:T(8,128)}, u32[]{:S(2)}) copy-start(s32[8,7]{1,0:T(8,128)} %index_ref.1) | copy-start | bytes 676
  0.9 9.3 %collective-permute-start = (bf16[2,128,128]{2,1,0:T(8,128)(2,1)S(1)}, bf16[2,128,128]{2,1,0:T(8,128)(2,1)S(1)}, u32[]{:S(2)}, u32[]{:S(2)}) collective-permute-start(bf16[2,128,128]{2,1,0:T(8,128)(2,1)S(1)} %bitcast.19), channel_id=1, source_target_pairs={{0,1},{1,2},{2,3},{4,5},{5,6},{6,7},{8,9},{9,10},{10,11},{12,13},{... | collective-permute-start | bytes 196616 | tf_op jit(solution)/shard_map/ppermute | solution.py:370
  5.8 6.2 %collective-permute-start.1 = (bf16[2,128,128]{2,1,0:T(8,128)(2,1)S(1)}, bf16[2,128,128]{2,1,0:T(8,128)(2,1)S(1)}, u32[]{:S(2)}, u32[]{:S(2)}) collective-permute-start(bf16[2,128,128]{2,1,0:T(8,128)(2,1)S(1)} %bitcast.18), channel_id=1, source_target_pairs={{1,0},{2,1},{3,2},{5,4},{6,5},{7,6},{9,8},{10,9},{11,10},{13,12},{... | collective-permute-start | bytes 196616 | tf_op jit(solution)/shard_map/ppermute | solution.py:371
  11.9 1.2 %copy-start = (bf16[2,2,7,128,128]{4,3,2,1,0:T(8,128)(2,1)S(1)}, bf16[2,2,7,128,128]{4,3,2,1,0:T(8,128)(2,1)}, u32[]{:S(2)}) copy-start(bf16[2,2,7,128,128]{4,3,2,1,0:T(8,128)(2,1)} %get-tuple-element.26.edges_ref) | copy-start | bytes 2752516
  13.1 0.9 %copy-start.1 = (bf16[8,128,128]{2,1,0:T(8,128)(2,1)S(1)}, bf16[8,128,128]{2,1,0:T(8,128)(2,1)}, u32[]{:S(2)}) copy-start(bf16[8,128,128]{2,1,0:T(8,128)(2,1)} %get-tuple-element.27.blocks_ref) | copy-start | bytes 786436
  14.1 0.9 %copy-start.3 = (bf16[4,128,128]{2,1,0:T(8,128)(2,1)S(1)}, bf16[4,128,128]{2,1,0:T(8,128)(2,1)}, u32[]{:S(2)}) copy-start(bf16[4,128,128]{2,1,0:T(8,128)(2,1)} %get-tuple-element.28.inner_ref) | copy-start | bytes 393220
  16.2 1.6 %collective-permute-start.2 = (bf16[1024,128]{1,0:T(8,128)(2,1)S(1)}, bf16[1024,128]{1,0:T(8,128)(2,1)S(1)}, u32[]{:S(2)}, u32[]{:S(2)}) collective-permute-start(bf16[1024,128]{1,0:T(8,128)(2,1)S(1)} %bitcast.15), channel_id=1, source_target_pairs={{0,4},{4,0},{8,12},{12,8},{16,20},{20,16},{24,28},{28,24},{1,5},{5... | collective-permute-start | bytes 786440 | tf_op jit(solution)/shard_map/ppermute | solution.py:21
  17.8 9.9 %copy-start.2 = (bf16[8,128,128]{2,1,0:T(8,128)(2,1)S(1)}, bf16[8,128,128]{2,1,0:T(8,128)(2,1)}, u32[]{:S(2)}) copy-start(bf16[8,128,128]{2,1,0:T(8,128)(2,1)} %get-tuple-element.27.blocks_ref) | copy-start | bytes 786436
  18.1 7.2 %collective-permute-start.5 = (f32[256,128]{1,0:T(8,128)S(1)}, f32[256,128]{1,0:T(8,128)S(1)}, u32[]{:S(2)}, u32[]{:S(2)}) collective-permute-start(f32[256,128]{1,0:T(8,128)S(1)} %shard_map.48.refs_0_), channel_id=1, source_target_pairs={{0,3},{1,2},{2,1},{3,0},{4,7},{5,6},{6,5},{7,4},{8,11},{9,10},{10,... | collective-permute-start | bytes 393224 | tf_op jit(solution)/shard_map/ppermute | solution.py:21
  20.0 7.4 %collective-permute-start.4 = (f32[256,128]{1,0:T(8,128)S(1)}, f32[256,128]{1,0:T(8,128)S(1)}, u32[]{:S(2)}, u32[]{:S(2)}) collective-permute-start(f32[256,128]{1,0:T(8,128)S(1)} %shard_map.48.refs_0_), channel_id=1, source_target_pairs={{0,2},{1,3},{2,0},{3,1},{4,6},{5,7},{6,4},{7,5},{8,10},{9,11},{10,... | collective-permute-start | bytes 393224 | tf_op jit(solution)/shard_map/ppermute | solution.py:21
  22.0 5.8 %collective-permute-start.3 = (f32[256,128]{1,0:T(8,128)S(1)}, f32[256,128]{1,0:T(8,128)S(1)}, u32[]{:S(2)}, u32[]{:S(2)}) collective-permute-start(f32[256,128]{1,0:T(8,128)S(1)} %shard_map.48.refs_0_), channel_id=1, source_target_pairs={{0,1},{1,0},{2,3},{3,2},{4,5},{5,4},{6,7},{7,6},{8,9},{9,8},{10,11... | collective-permute-start | bytes 393224 | tf_op jit(solution)/shard_map/ppermute | solution.py:21
  22.0 9.8 %collective-permute-start.8 = (bf16[128,1024]{1,0:T(8,128)(2,1)S(1)}, bf16[128,1024]{1,0:T(8,128)(2,1)S(1)}, u32[]{:S(2)}, u32[]{:S(2)}) collective-permute-start(bf16[128,1024]{1,0:T(8,128)(2,1)S(1)} %get-tuple-element.30.image_t_ref), channel_id=1, source_target_pairs={{0,8},{4,12},{8,0},{12,4},{16,24},{20,28},{24,16},{28,20},{1,9},{5... | collective-permute-start | bytes 786440 | tf_op jit(solution)/shard_map/ppermute | solution.py:21
  27.8 4.0 %copy-start.5 = (f32[3,2,128,128]{3,2,1,0:T(8,128)S(1)}, f32[3,2,128,128]{3,2,1,0:T(8,128)}, u32[]{:S(2)}) copy-start(f32[3,2,128,128]{3,2,1,0:T(8,128)} %get-tuple-element.34) | copy-start | bytes 1179652
  31.2 1.7 %collective-permute-start.7 = (bf16[1024,128]{1,0:T(8,128)(2,1)S(1)}, bf16[1024,128]{1,0:T(8,128)(2,1)S(1)}, u32[]{:S(2)}, u32[]{:S(2)}) collective-permute-start(bf16[1024,128]{1,0:T(8,128)(2,1)S(1)} %get-tuple-element.35.modes_own.refs_0_), channel_id=1, source_target_pairs={{0,4},{4,0},{8,12},{12,8},{16,20},{20,16},{24,28},{28,24},{1,5},{5... | collective-permute-start | bytes 786440 | tf_op jit(solution)/shard_map/ppermute | solution.py:21
  31.3 1.6 %collective-permute-start.6 = (f32[128,128]{1,0:T(8,128)S(1)}, f32[128,128]{1,0:T(8,128)S(1)}, u32[]{:S(2)}, u32[]{:S(2)}) collective-permute-start(f32[128,128]{1,0:T(8,128)S(1)} %get-tuple-element.33.own_ref), channel_id=1, source_target_pairs={{0,4},{4,0},{8,12},{12,8},{16,20},{20,16},{24,28},{28,24},{1,5},{5... | collective-permute-start | bytes 196616 | tf_op jit(solution)/shard_map/ppermute | solution.py:21
  37.9 12.4 %collective-permute-start.14 = (bf16[1024,128]{1,0:T(8,128)(2,1)S(1)}, bf16[1024,128]{1,0:T(8,128)(2,1)S(1)}, u32[]{:S(2)}, u32[]{:S(2)}) collective-permute-start(bf16[1024,128]{1,0:T(8,128)(2,1)S(1)} %get-tuple-element.41), channel_id=1, source_target_pairs={{0,8},{4,12},{8,0},{12,4},{16,24},{20,28},{24,16},{28,20},{1,9},{5... | collective-permute-start | bytes 786440 | tf_op jit(solution)/shard_map/ppermute | solution.py:21
  39.6 8.2 %collective-permute-start.12 = (f32[128,128]{1,0:T(8,128)S(1)}, f32[128,128]{1,0:T(8,128)S(1)}, u32[]{:S(2)}, u32[]{:S(2)}) collective-permute-start(f32[128,128]{1,0:T(8,128)S(1)} %get-tuple-element.37.refs_3_), channel_id=1, source_target_pairs={{0,8},{4,12},{8,0},{12,4},{16,24},{20,28},{24,16},{28,20},{1,9},{5... | collective-permute-start | bytes 196616 | tf_op jit(solution)/shard_map/ppermute | solution.py:21
  40.0 10.3 %collective-permute-start.11 = (f32[128,128]{1,0:T(8,128)S(1)}, f32[128,128]{1,0:T(8,128)S(1)}, u32[]{:S(2)}, u32[]{:S(2)}) collective-permute-start(f32[128,128]{1,0:T(8,128)S(1)} %get-tuple-element.36.refs_0_), channel_id=1, source_target_pairs={{0,3},{1,2},{2,1},{3,0},{4,7},{5,6},{6,5},{7,4},{8,11},{9,10},{10,... | collective-permute-start | bytes 196616 | tf_op jit(solution)/shard_map/ppermute | solution.py:21
  42.1 8.3 %collective-permute-start.10 = (f32[128,128]{1,0:T(8,128)S(1)}, f32[128,128]{1,0:T(8,128)S(1)}, u32[]{:S(2)}, u32[]{:S(2)}) collective-permute-start(f32[128,128]{1,0:T(8,128)S(1)} %get-tuple-element.36.refs_0_), channel_id=1, source_target_pairs={{0,2},{1,3},{2,0},{3,1},{4,6},{5,7},{6,4},{7,5},{8,10},{9,11},{10,... | collective-permute-start | bytes 196616 | tf_op jit(solution)/shard_map/ppermute | solution.py:21
  43.3 7.1 %collective-permute-start.9 = (f32[128,128]{1,0:T(8,128)S(1)}, f32[128,128]{1,0:T(8,128)S(1)}, u32[]{:S(2)}, u32[]{:S(2)}) collective-permute-start(f32[128,128]{1,0:T(8,128)S(1)} %get-tuple-element.36.refs_0_), channel_id=1, source_target_pairs={{0,1},{1,0},{2,3},{3,2},{4,5},{5,4},{6,7},{7,6},{8,9},{9,8},{10,11... | collective-permute-start | bytes 196616 | tf_op jit(solution)/shard_map/ppermute | solution.py:21
  47.8 16.1 %collective-permute-start.16 = (bf16[128,1024]{1,0:T(8,128)(2,1)S(1)}, bf16[128,1024]{1,0:T(8,128)(2,1)S(1)}, u32[]{:S(2)}, u32[]{:S(2)}) collective-permute-start(bf16[128,1024]{1,0:T(8,128)(2,1)S(1)} %get-tuple-element.30.image_t_ref), channel_id=1, source_target_pairs={{0,16},{4,20},{8,24},{12,28},{16,0},{20,4},{24,8},{28,12},{1,17},{... | collective-permute-start | bytes 786440 | tf_op jit(solution)/shard_map/ppermute | solution.py:21
  50.4 13.5 %collective-permute-start.15 = (bf16[1024,128]{1,0:T(8,128)(2,1)S(1)}, bf16[1024,128]{1,0:T(8,128)(2,1)S(1)}, u32[]{:S(2)}, u32[]{:S(2)}) collective-permute-start(bf16[1024,128]{1,0:T(8,128)(2,1)S(1)} %collective-permute-done.14.came_ref), channel_id=1, source_target_pairs={{0,4},{4,0},{8,12},{12,8},{16,20},{20,16},{24,28},{28,24},{1,5},{5... | collective-permute-start | bytes 786440 | tf_op jit(solution)/shard_map/ppermute | solution.py:21
  50.6 1.5 %collective-permute-start.13 = (f32[128,128]{1,0:T(8,128)S(1)}, f32[128,128]{1,0:T(8,128)S(1)}, u32[]{:S(2)}, u32[]{:S(2)}) collective-permute-start(f32[128,128]{1,0:T(8,128)S(1)} %shard_map.51.refs_0_), channel_id=1, source_target_pairs={{0,4},{4,0},{8,12},{12,8},{16,20},{20,16},{24,28},{28,24},{1,5},{5... | collective-permute-start | bytes 196616 | tf_op jit(solution)/shard_map/ppermute | solution.py:21
  56.1 12.1 %collective-permute-start.20 = (f32[128,128]{1,0:T(8,128)S(1)}, f32[128,128]{1,0:T(8,128)S(1)}, u32[]{:S(2)}, u32[]{:S(2)}) collective-permute-start(f32[128,128]{1,0:T(8,128)S(1)} %get-tuple-element.43.refs_3_), channel_id=1, source_target_pairs={{0,16},{4,20},{8,24},{12,28},{16,0},{20,4},{24,8},{28,12},{1,17},{... | collective-permute-start | bytes 196616 | tf_op jit(solution)/shard_map/ppermute | solution.py:21
  64.7 5.2 %collective-permute-start.19 = (f32[128,128]{1,0:T(8,128)S(1)}, f32[128,128]{1,0:T(8,128)S(1)}, u32[]{:S(2)}, u32[]{:S(2)}) collective-permute-start(f32[128,128]{1,0:T(8,128)S(1)} %get-tuple-element.42.refs_0_), channel_id=1, source_target_pairs={{0,3},{1,2},{2,1},{3,0},{4,7},{5,6},{6,5},{7,4},{8,11},{9,10},{10,... | collective-permute-start | bytes 196616 | tf_op jit(solution)/shard_map/ppermute | solution.py:21
  66.8 4.3 %collective-permute-start.18 = (f32[128,128]{1,0:T(8,128)S(1)}, f32[128,128]{1,0:T(8,128)S(1)}, u32[]{:S(2)}, u32[]{:S(2)}) collective-permute-start(f32[128,128]{1,0:T(8,128)S(1)} %get-tuple-element.42.refs_0_), channel_id=1, source_target_pairs={{0,2},{1,3},{2,0},{3,1},{4,6},{5,7},{6,4},{7,5},{8,10},{9,11},{10,... | collective-permute-start | bytes 196616 | tf_op jit(solution)/shard_map/ppermute | solution.py:21
  68.0 4.3 %collective-permute-start.17 = (f32[128,128]{1,0:T(8,128)S(1)}, f32[128,128]{1,0:T(8,128)S(1)}, u32[]{:S(2)}, u32[]{:S(2)}) collective-permute-start(f32[128,128]{1,0:T(8,128)S(1)} %get-tuple-element.42.refs_0_), channel_id=1, source_target_pairs={{0,1},{1,0},{2,3},{3,2},{4,5},{5,4},{6,7},{7,6},{8,9},{9,8},{10,11... | collective-permute-start | bytes 196616 | tf_op jit(solution)/shard_map/ppermute | solution.py:21
  72.4 1.3 %collective-permute-start.21 = (f32[128,128]{1,0:T(8,128)S(1)}, f32[128,128]{1,0:T(8,128)S(1)}, u32[]{:S(2)}, u32[]{:S(2)}) collective-permute-start(f32[128,128]{1,0:T(8,128)S(1)} %shard_map.54.refs_0_), channel_id=1, source_target_pairs={{0,4},{4,0},{8,12},{12,8},{16,20},{20,16},{24,28},{28,24},{1,5},{5... | collective-permute-start | bytes 196616 | tf_op jit(solution)/shard_map/ppermute | solution.py:21
  72.5 9.6 %collective-permute-start.23 = (bf16[512,128]{1,0:T(8,128)(2,1)S(1)}, bf16[512,128]{1,0:T(8,128)(2,1)S(1)}, u32[]{:S(2)}, u32[]{:S(2)}) collective-permute-start(bf16[512,128]{1,0:T(8,128)(2,1)S(1)} %get-tuple-element.45), channel_id=1, source_target_pairs={{0,16},{4,20},{8,24},{12,28},{16,0},{20,4},{24,8},{28,12},{1,17},{... | collective-permute-start | bytes 393224 | tf_op jit(solution)/shard_map/ppermute | solution.py:21
  73.7 8.4 %collective-permute-start.22 = (f32[128,128]{1,0:T(8,128)S(1)}, f32[128,128]{1,0:T(8,128)S(1)}, u32[]{:S(2)}, u32[]{:S(2)}) collective-permute-start(f32[128,128]{1,0:T(8,128)S(1)} %shard_map.55.refs_0_), channel_id=1, source_target_pairs={{0,8},{4,12},{8,0},{12,4},{16,24},{20,28},{24,16},{28,20},{1,9},{5... | collective-permute-start | bytes 196616 | tf_op jit(solution)/shard_map/ppermute | solution.py:21
  82.1 4.6 %collective-permute-start.24 = (bf16[512,128]{1,0:T(8,128)(2,1)S(1)}, bf16[512,128]{1,0:T(8,128)(2,1)S(1)}, u32[]{:S(2)}, u32[]{:S(2)}) collective-permute-start(bf16[512,128]{1,0:T(8,128)(2,1)S(1)} %collective-permute-done.23.came_ref), channel_id=1, source_target_pairs={{0,4},{4,0},{8,12},{12,8},{16,20},{20,16},{24,28},{28,24},{1,5},{5... | collective-permute-start | bytes 393224 | tf_op jit(solution)/shard_map/ppermute | solution.py:21

commit v5 on v4

--- a/solution.py
+++ b/solution.py
@@ -13,7 +13,6 @@
 F32 = jnp.float32
 BF16 = jnp.bfloat16
 PARAMS = pltpu.CompilerParams(vmem_limit_bytes=16 * 1024 * 1024)
-WIDE = pltpu.CompilerParams(vmem_limit_bytes=62_000_000)
 
 
 def swap(value, axis, mask):
@@ -185,15 +184,16 @@
 
 
 def edge_kernel(
-    index_ref, edges_ref, before_ref, blocks_ref, after_ref, inner_ref,
+    index_ref, edges_ref, near_ref, blocks_ref, wide_ref, inner_ref,
     image_ref, image_t_ref, gram_ref, padded_ref,
 ):
     slots = edges_ref.shape[2]
     blocks = blocks_ref.shape[0]
-    padded_ref[0, :HB] = before_ref[...]
+    before, after = choose("space", wide_ref[...], near_ref[...])
+    padded_ref[0, :HB] = before
     padded_ref[0, HB:] = blocks_ref[: 2 * HB]
     padded_ref[1, : 2 * HB] = blocks_ref[blocks - 2 * HB :]
-    padded_ref[1, 2 * HB :] = after_ref[...]
+    padded_ref[1, 2 * HB :] = after
     image_ref[HB : blocks - HB] = inner_ref[...]
     for side in range(2):
         first = lax.axis_index("space") * blocks - HB + side * (blocks - HB)
@@ -230,11 +230,11 @@
             pltpu.VMEM(sketch.shape, F32),
             pltpu.SemaphoreType.DMA((6,)),
         ],
-        compiler_params=WIDE,
-    )(neighbours, energy, blocks, sketch)
-
-
-def edge_of(neighbours, edges, before, blocks, after, inner):
+        compiler_params=PARAMS,
+    )(*[pltpu.with_memory_space_constraint(item, pltpu.HBM) for item in (neighbours, energy, blocks, sketch)])
+
+
+def edge_of(neighbours, edges, came_near, blocks, came_wide, inner):
     count, rows, width = blocks.shape
     image, image_t, gram = pl.pallas_call(
         edge_kernel,
@@ -247,24 +247,25 @@
         + [pl.BlockSpec(memory_space=pltpu.VMEM)] * 5,
         scratch_shapes=[pltpu.VMEM((2, 3 * HB, rows, width), BF16)],
         compiler_params=PARAMS,
-    )(neighbours, edges, before, blocks, after, inner)
+    )(neighbours, edges, came_near, blocks, came_wide, inner)
     return image.reshape(count * rows, width), image_t, gram
 
 
 def pair_kernel(gram_ref, image_t_ref, other_ref, out_ref):
     width = gram_ref.shape[0]
     out_ref[:width] = gram_ref[...]
-    out_ref[width:] = dot_nn(image_t_ref[...], other_ref[...])
+    cross = dot_nn(image_t_ref[...], other_ref[...])
+    odd = lax.axis_index("tm") % 2 == 1
+    out_ref[width:] = jnp.where(odd, cross.T[width // 2 :], cross[: width // 2])
 
 
 def leaf_kernel(total_rows, count, *refs):
-    parts, refs = refs[:count], refs[count:]
-    snapshots_ref, inverse_ref, cross_ref, modes_ref = refs
-    width = inverse_ref.shape[0]
+    parts, (snapshots_ref, factor_ref, modes_ref) = refs[:count], refs[count:]
+    width = snapshots_ref.shape[1]
     grams = total_of(parts) / total_rows
-    cross_ref[...] = grams[width:]
+    factor_ref[width:] = grams[width:]
     inverse = inverse_factor(grams[:width])
-    inverse_ref[...] = inverse
+    factor_ref[:width] = inverse
     modes_ref[...] = dot_nt(snapshots_ref[...], inverse.astype(BF16)).astype(BF16)
 
 
@@ -288,8 +289,8 @@
     return dot_nt(joined, halves).astype(BF16)
 
 
-def choose(first, second):
-    odd = lax.axis_index("tm") % 2 == 1
+def choose(axis, first, second):
+    odd = (lax.axis_index(axis) & 1) == 1
     return jnp.where(odd, second, first), jnp.where(odd, first, second)
 
 
@@ -298,27 +299,32 @@
     modes_ref[...] = modes
     if image_ref:
         image_ref[0][...] = image
-        outgoing_ref[...] = choose(modes, image)[0]
+        outgoing_ref[...] = choose("tm", modes, image)[0]
     else:
         part = outgoing_ref.shape[0]
-        outgoing_ref[...] = choose(modes[:part], modes[part:])[0]
+        outgoing_ref[...] = choose("tm", modes[:part], modes[part:])[0]
 
 
 def read_modes(came_ref, shared_ref, rows):
-    first, second = choose(came_ref[...], shared_ref[...])
+    first, second = choose("tm", came_ref[...], shared_ref[...])
     if first.shape[0] == rows:
         return first
     return jnp.concatenate([first, second], axis=0)
 
 
 def first_merge_kernel(
-    cross_ref, own_ref, other_ref, sketch_ref, modes_own, modes_other,
+    own_ref, other_ref, sketch_ref, modes_own, modes_other,
     image_own, image_other, far_image_t, mine_ref, probe_ref, *bulk_refs,
 ):
-    cross_t = nt_full(other_ref[...], nn_full(own_ref[...], cross_ref[...]))
+    width = own_ref.shape[1]
+    own, other = own_ref[:width], other_ref[:width]
+    even, odd = choose("tm", own, other)
+    pair_gram = jnp.concatenate(choose("tm", own_ref[width:], other_ref[width:]), axis=0)
+    cross = nt_full(nn_full(even, pair_gram), odd)
+    cross_t = jnp.where(lax.axis_index("tm") % 2 == 1, cross, cross.T)
     half_own, half_other = merge(cross_t, sketch_ref)
-    mine = nn_full(half_own, own_ref[...])
-    theirs = nn_full(half_other, other_ref[...])
+    mine = nn_full(half_own, own)
+    theirs = nn_full(half_other, other)
     mine_ref[...] = mine
     image = combined(image_own[...], image_other[...], mine, theirs)
     probe_ref[...] = dot_nn(far_image_t[...], image)
@@ -337,7 +343,7 @@
 def apply_kernel(
     halves_ref, modes_own, image_own, came_ref, shared_ref, far_image_t, probe_ref, *bulk_refs
 ):
-    modes_other, image_other = choose(came_ref[...], shared_ref[...])
+    modes_other, image_other = choose("tm", came_ref[...], shared_ref[...])
     image = combined(image_own[...], image_other, halves_ref[0], halves_ref[1])
     probe_ref[...] = dot_nn(far_image_t[...], image)
     modes = combined(modes_own[...], modes_other, halves_ref[0], halves_ref[1])
@@ -366,30 +372,33 @@
     total_rows = rows_dev * space
     levels = sketch.shape[0]
     blocks = snapshots.reshape(block_count, block_rows, width)
-    ends = space - 1
-    before = lax.ppermute(blocks[-HB:], "space", [(i, i + 1) for i in range(ends)])
-    after = lax.ppermute(blocks[:HB], "space", [(i + 1, i) for i in range(ends)])
+    head, tail = blocks[:HB], blocks[block_count - HB :]
+    odd = (lax.axis_index("space") & 1) == 1
+    near = [(i, i ^ 1) for i in range(space)]
+    wide = [(i, (i + 2 * (i % 2) - 1) % space) for i in range(space)]
+    came_near = lax.ppermute(jnp.where(odd, head, tail), "space", near)
+    came_wide = lax.ppermute(jnp.where(odd, tail, head), "space", wide)
     square = jax.ShapeDtypeStruct((width, width), F32)
     modes_shape = jax.ShapeDtypeStruct((rows_dev, width), BF16)
     half_shape = jax.ShapeDtypeStruct((rows_dev // 2, width), BF16)
+    factor_shape = jax.ShapeDtypeStruct((width + width // 2, width), F32)
     halves_shape = jax.ShapeDtypeStruct((2, width, width), BF16)
 
     inner, sketch_t, edges, blocks = interior_of(neighbours, energy, blocks, sketch)
-    image, image_t, gram = edge_of(neighbours, edges, before, blocks, after, inner)
+    image, image_t, gram = edge_of(neighbours, edges, came_near, blocks, came_wide, inner)
     other_image = swap(image, "tm", 1)
     pair = run_kernel(
         pair_kernel,
-        jax.ShapeDtypeStruct((2 * width, width), F32),
-        gram, image_t, other_image,
+        factor_shape, gram, image_t, other_image,
     )
     parts = summands(pair, "space", space, 4)
     far_images = [swap(image_t, "tm", 2**level) for level in range(1, levels)]
-    inverse, cross, modes = run_kernel(
+    factor, modes = run_kernel(
         functools.partial(leaf_kernel, total_rows, len(parts)),
-        [square, square, modes_shape],
+        [factor_shape, modes_shape],
         *parts, blocks.reshape(rows_dev, width),
     )
-    other_inverse = swap(inverse, "tm", 1)
+    other_factor = swap(factor, "tm", 1)
     other = swap(modes, "tm", 1)
     kept = [modes]
     for level in range(levels):
@@ -398,7 +407,7 @@
         if level == 0:
             mine, probe, *bulk = run_kernel(
                 first_merge_kernel, outs,
-                cross, inverse, other_inverse, sketch_t[level],
+                factor, other_factor, sketch_t[level],
                 modes, other, image, other_image, far_images[level],
             )
         else:

time: 88.3 us -> 80 us (0.906)
  local copies, waits for them, and re-layouts: 3.96 us -> 0.03 us
  starting transfers between devices: 27.5 us -> 25.4 us
  waiting for transfers between devices: 32.2 us -> 30.1 us
  Pallas kernels: 24.1 us -> 23.1 us
  other arithmetic: 0 us -> 0.9 us
    unnamed x12 -> x2, local copies, waits for them, and re-layouts: 3.04 us -> 0.01 us
    ppermute x23, waiting for transfers between devices: 30.4 us -> 28.3 us  [swap(): return lax.ppermute(value, axis, pairs)]
    ppermute x2, starting transfers between devices: 6.17 us -> 4.52 us  [the longest x1 3.03 us: modes_of(): came_near = lax.ppermute(jnp.where(odd, head, tail), 'space', near)]
    pallas_call x1, Pallas kernels: 3.09 us -> 1.89 us  [interior_of(): pl.pallas_call(interior_kernel, out_shape=[jax.ShapeDtypeStruct((inner, r...]
    select_n x0 -> x1, other arithmetic: none -> 0.9 us  [modes_of(): came_wide = lax.ppermute(jnp.where(odd, tail, head), 'space', wide)]
    slice x1 -> x0, local copies, waits for them, and re-layouts: 0.89 us -> none  [modes_of(): blocks[:HB]]
  transfers between devices with their start and end apart: 25 -> 25, of which waited for: 14 -> 14; matrix products, arithmetic and copies ran while one was open for 0% -> 0% of each run, Pallas kernels for 18% -> 19%
where the time goes in v5:
time: 80 us; the launch traced here: 79.8 us
  waiting for transfers between devices  30.1 us (38%)
  starting transfers between devices  25.4 us (32%)
  Pallas kernels  23.1 us (29%)
  other arithmetic  0.9 us (1%)
    ppermute x23, waiting for transfers between devices, swap(): return lax.ppermute(value, axis, pairs)  28.3 us
    ppermute x23, starting transfers between devices, swap(): return lax.ppermute(value, axis, pairs)  20.9 us
    pallas_call x10, Pallas kernels, run_kernel(): pl.pallas_call(body, out_shape=outs, cost_estimate=cost, compiler_params=...  20 us
    ppermute x1, starting transfers between devices, modes_of(): came_near = lax.ppermute(jnp.where(odd, head, tail), 'space', near)  3.03 us
    pallas_call x1, Pallas kernels, interior_of(): pl.pallas_call(interior_kernel, out_shape=[jax.ShapeDtypeStruct((inner, r...  1.89 us
    ppermute x1, waiting for transfers between devices, modes_of(): came_wide = lax.ppermute(jnp.where(odd, tail, head), 'space', wide)  1.77 us
  transfers between devices with their start and end apart: 25, of which 14 were waited for; matrix products, arithmetic and copies ran while one was open for 0% of the time, Pallas kernels for 19%

profile of v5, /device:TPU:0, one launch (start us, length us, event | category | flops | bytes accessed | tf_op | source)
XLA Modules:
  0.0 79.8 jit_solution(13244733854955675268)
XLA Ops:
  0.9 3.0 %collective-permute-start = (bf16[2,128,128]{2,1,0:T(8,128)(2,1)S(1)}, bf16[2,128,128]{2,1,0:T(8,128)(2,1)S(1)}, u32[]{:S(2)}, u32[]{:S(2)}) collective-permute-start(bf16[2,128,128]{2,1,0:T(8,128)(2,1)S(1)} %bitcast.19), channel_id=1, source_target_pairs={{0,1},{1,0},{2,3},{3,2},{4,5},{5,4},{6,7},{7,6},{8,9},{9,8},{10,11... | collective-permute-start | bytes 196616 | tf_op jit(solution)/shard_map/ppermute | solution.py:379
  3.9 1.5 %collective-permute-start.1 = (bf16[2,128,128]{2,1,0:T(8,128)(2,1)S(1)}, bf16[2,128,128]{2,1,0:T(8,128)(2,1)S(1)}, u32[]{:S(2)}, u32[]{:S(2)}) collective-permute-start(bf16[2,128,128]{2,1,0:T(8,128)(2,1)S(1)} %bitcast.18), channel_id=1, source_target_pairs={{0,3},{1,2},{2,1},{3,0},{4,7},{5,6},{6,5},{7,4},{8,11},{9,10},{10,... | collective-permute-start | bytes 196616 | tf_op jit(solution)/shard_map/ppermute | solution.py:380
  5.4 1.9 %shard_map.46 = (bf16[4,128,128]{2,1,0:T(8,128)(2,1)S(1)}, f32[3,2,128,128]{3,2,1,0:T(8,128)S(1)}, bf16[2,2,7,128,128]{4,3,2,1,0:T(8,128)(2,1)S(1)}, bf16[8,128,128]{2,1,0:T(8,128)(2,1)S(1)}) custom-call(s32[8,7]{1,0:T(8,128)} %index_ref.1, bf16[8,7,128,128]{3,2,1,0:T(8,128)(2,1)} %energy_hbm.1, bf16[8,128,128]{2,1,0:T(8,128)(2,1)} %bitcast.17, ...), custom_call_target="tpu_custom_call" | custom-call | tf_op jit(solution)/shard_map/pallas_call | solution.py:218
  7.3 1.8 %collective-permute-done.1.wide_ref = bf16[2,128,128]{2,1,0:T(8,128)(2,1)S(1)} collective-permute-done((bf16[2,128,128]{2,1,0:T(8,128)(2,1)S(1)}, bf16[2,128,128]{2,1,0:T(8,128)(2,1)S(1)}, u32[]{:S(2)}, u32[]{:S(2)}) %collective-permute-start.1) | collective-permute-done | bytes 65568 | tf_op jit(solution)/shard_map/ppermute | solution.py:380
  9.1 1.3 %shard_map.47 = (bf16[8,128,128]{2,1,0:T(8,128)(2,1)S(1)}, bf16[128,1024]{1,0:T(8,128)(2,1)S(1)}, f32[128,128]{1,0:T(8,128)S(1)}) custom-call(s32[8,7]{1,0:T(8,128)S(1)} %copy-done, bf16[2,2,7,128,128]{4,3,2,1,0:T(8,128)(2,1)S(1)} %get-tuple-element.25.edges_ref, bf16[2,128,128]{2,1,0:T(8,128)(2,1)S(1)} %collective-permute-done.near_ref, ...), custom_call_target="tpu_custom_call" | custom-call | tf_op jit(solution)/shard_map/pallas_call | solution.py:239
  10.5 1.5 %collective-permute-done.2.other_ref.image_other = bf16[1024,128]{1,0:T(8,128)(2,1)S(1)} collective-permute-done((bf16[1024,128]{1,0:T(8,128)(2,1)S(1)}, bf16[1024,128]{1,0:T(8,128)(2,1)S(1)}, u32[]{:S(2)}, u32[]{:S(2)}) %collective-permute-start.2) | collective-permute-done | bytes 262176 | tf_op jit(solution)/shard_map/ppermute | solution.py:20
  12.3 1.6 %collective-permute-start.5 = (f32[192,128]{1,0:T(8,128)S(1)}, f32[192,128]{1,0:T(8,128)S(1)}, u32[]{:S(2)}, u32[]{:S(2)}) collective-permute-start(f32[192,128]{1,0:T(8,128)S(1)} %shard_map.48.refs_0_), channel_id=1, source_target_pairs={{0,3},{1,2},{2,1},{3,0},{4,7},{5,6},{6,5},{7,4},{8,11},{9,10},{10,... | collective-permute-start | bytes 294920 | tf_op jit(solution)/shard_map/ppermute | solution.py:20
  13.8 1.0 %collective-permute-start.4 = (f32[192,128]{1,0:T(8,128)S(1)}, f32[192,128]{1,0:T(8,128)S(1)}, u32[]{:S(2)}, u32[]{:S(2)}) collective-permute-start(f32[192,128]{1,0:T(8,128)S(1)} %shard_map.48.refs_0_), channel_id=1, source_target_pairs={{0,2},{1,3},{2,0},{3,1},{4,6},{5,7},{6,4},{7,5},{8,10},{9,11},{10,... | collective-permute-start | bytes 294920 | tf_op jit(solution)/shard_map/ppermute | solution.py:20
  14.8 1.0 %collective-permute-start.3 = (f32[192,128]{1,0:T(8,128)S(1)}, f32[192,128]{1,0:T(8,128)S(1)}, u32[]{:S(2)}, u32[]{:S(2)}) collective-permute-start(f32[192,128]{1,0:T(8,128)S(1)} %shard_map.48.refs_0_), channel_id=1, source_target_pairs={{0,1},{1,0},{2,3},{3,2},{4,5},{5,4},{6,7},{7,6},{8,9},{9,8},{10,11... | collective-permute-start | bytes 294920 | tf_op jit(solution)/shard_map/ppermute | solution.py:20
  15.8 1.6 %collective-permute-start.8 = (bf16[128,1024]{1,0:T(8,128)(2,1)S(1)}, bf16[128,1024]{1,0:T(8,128)(2,1)S(1)}, u32[]{:S(2)}, u32[]{:S(2)}) collective-permute-start(bf16[128,1024]{1,0:T(8,128)(2,1)S(1)} %get-tuple-element.29.image_t_ref), channel_id=1, source_target_pairs={{0,8},{4,12},{8,0},{12,4},{16,24},{20,28},{24,16},{28,20},{1,9},{5... | collective-permute-start | bytes 786440 | tf_op jit(solution)/shard_map/ppermute | solution.py:20
  17.4 1.3 %collective-permute-done.5.refs_3_ = f32[192,128]{1,0:T(8,128)S(1)} collective-permute-done((f32[192,128]{1,0:T(8,128)S(1)}, f32[192,128]{1,0:T(8,128)S(1)}, u32[]{:S(2)}, u32[]{:S(2)}) %collective-permute-start.5) | collective-permute-done | bytes 98336 | tf_op jit(solution)/shard_map/ppermute | solution.py:20
  18.7 1.5 %collective-permute-done.4.refs_2_ = f32[192,128]{1,0:T(8,128)S(1)} collective-permute-done((f32[192,128]{1,0:T(8,128)S(1)}, f32[192,128]{1,0:T(8,128)S(1)}, u32[]{:S(2)}, u32[]{:S(2)}) %collective-permute-start.4) | collective-permute-done | bytes 98336 | tf_op jit(solution)/shard_map/ppermute | solution.py:20
  20.3 3.4 %shard_map.49 = (f32[192,128]{1,0:T(8,128)S(1)}, bf16[1024,128]{1,0:T(8,128)(2,1)S(1)}) custom-call(f32[192,128]{1,0:T(8,128)S(1)} %shard_map.48.refs_0_, f32[192,128]{1,0:T(8,128)S(1)} %collective-permute-done.3.refs_1_, f32[192,128]{1,0:T(8,128)S(1)} %collective-permute-done.4.refs_2_, f32[192,128]{1,0:T(8,128)S(1)} %collective-permute-done.5.refs_3_, ...), custom_call_target="tpu_custom_call" | custom-call | flops 2000000000 | bytes 1000000 | tf_op jit(solution)/shard_map/pallas_call | solution.py:133
  24.4 1.1 %collective-permute-done.6.other_ref = f32[192,128]{1,0:T(8,128)S(1)} collective-permute-done((f32[192,128]{1,0:T(8,128)S(1)}, f32[192,128]{1,0:T(8,128)S(1)}, u32[]{:S(2)}, u32[]{:S(2)}) %collective-permute-start.6) | collective-permute-done | bytes 98336 | tf_op jit(solution)/shard_map/ppermute | solution.py:20
  25.5 5.1 %shard_map.50 = (f32[128,128]{1,0:T(8,128)S(1)}, f32[128,128]{1,0:T(8,128)S(1)}, bf16[1024,128]{1,0:T(8,128)(2,1)S(1)}, bf16[1024,128]{1,0:T(8,128)(2,1)S(1)}, bf16[1024,128]{1,0:T(8,128)(2,1)S(1)}) custom-call(f32[192,128]{1,0:T(8,128)S(1)} %get-tuple-element.31.own_ref, f32[192,128]{1,0:T(8,128)S(1)} %collective-permute-done.6.other_ref, ...), custom_call_target="tpu_custom_call" | custom-call | flops 2000000000 | bytes 1000000 | tf_op jit(solution)/shard_map/pallas_call | solution.py:133
  30.6 1.6 %collective-permute-start.14 = (bf16[1024,128]{1,0:T(8,128)(2,1)S(1)}, bf16[1024,128]{1,0:T(8,128)(2,1)S(1)}, u32[]{:S(2)}, u32[]{:S(2)}) collective-permute-start(bf16[1024,128]{1,0:T(8,128)(2,1)S(1)} %get-tuple-element.39), channel_id=1, source_target_pairs={{0,8},{4,12},{8,0},{12,4},{16,24},{20,28},{24,16},{28,20},{1,9},{5... | collective-permute-start | bytes 786440 | tf_op jit(solution)/shard_map/ppermute | solution.py:20
  32.7 1.4 %collective-permute-start.11 = (f32[128,128]{1,0:T(8,128)S(1)}, f32[128,128]{1,0:T(8,128)S(1)}, u32[]{:S(2)}, u32[]{:S(2)}) collective-permute-start(f32[128,128]{1,0:T(8,128)S(1)} %get-tuple-element.34.refs_0_), channel_id=1, source_target_pairs={{0,3},{1,2},{2,1},{3,0},{4,7},{5,6},{6,5},{7,4},{8,11},{9,10},{10,... | collective-permute-start | bytes 196616 | tf_op jit(solution)/shard_map/ppermute | solution.py:20
  34.1 1.0 %collective-permute-start.10 = (f32[128,128]{1,0:T(8,128)S(1)}, f32[128,128]{1,0:T(8,128)S(1)}, u32[]{:S(2)}, u32[]{:S(2)}) collective-permute-start(f32[128,128]{1,0:T(8,128)S(1)} %get-tuple-element.34.refs_0_), channel_id=1, source_target_pairs={{0,2},{1,3},{2,0},{3,1},{4,6},{5,7},{6,4},{7,5},{8,10},{9,11},{10,... | collective-permute-start | bytes 196616 | tf_op jit(solution)/shard_map/ppermute | solution.py:20
  35.1 1.1 %collective-permute-start.9 = (f32[128,128]{1,0:T(8,128)S(1)}, f32[128,128]{1,0:T(8,128)S(1)}, u32[]{:S(2)}, u32[]{:S(2)}) collective-permute-start(f32[128,128]{1,0:T(8,128)S(1)} %get-tuple-element.34.refs_0_), channel_id=1, source_target_pairs={{0,1},{1,0},{2,3},{3,2},{4,5},{5,4},{6,7},{7,6},{8,9},{9,8},{10,11... | collective-permute-start | bytes 196616 | tf_op jit(solution)/shard_map/ppermute | solution.py:20
  36.2 4.2 %collective-permute-done.12.refs_4_ = f32[128,128]{1,0:T(8,128)S(1)} collective-permute-done((f32[128,128]{1,0:T(8,128)S(1)}, f32[128,128]{1,0:T(8,128)S(1)}, u32[]{:S(2)}, u32[]{:S(2)}) %collective-permute-start.12) | collective-permute-done | bytes 65568 | tf_op jit(solution)/shard_map/ppermute | solution.py:20
  40.4 2.6 %collective-permute-start.16 = (bf16[128,1024]{1,0:T(8,128)(2,1)S(1)}, bf16[128,1024]{1,0:T(8,128)(2,1)S(1)}, u32[]{:S(2)}, u32[]{:S(2)}) collective-permute-start(bf16[128,1024]{1,0:T(8,128)(2,1)S(1)} %get-tuple-element.29.image_t_ref), channel_id=1, source_target_pairs={{0,16},{4,20},{8,24},{12,28},{16,0},{20,4},{24,8},{28,12},{1,17},{... | collective-permute-start | bytes 786440 | tf_op jit(solution)/shard_map/ppermute | solution.py:20
  44.7 4.1 %shard_map.52 = (bf16[2,128,128]{2,1,0:T(8,128)(2,1)S(1)}, f32[128,128]{1,0:T(8,128)S(1)}) custom-call(f32[128,128]{1,0:T(8,128)S(1)} %shard_map.51.refs_0_, f32[128,128]{1,0:T(8,128)S(1)} %collective-permute-done.13.refs_1_, f32[2,128,128]{2,1,0:T(8,128)S(1)} %get-tuple-element.46.refs_2_, f32[128,128]{1,0:T(8,128)S(1)} %get-tuple-element.35.refs_3_), custom_call_target="tpu_custom_call" | custom-call | flops 2000000000 | bytes 1000000 | tf_op jit(solution)/shard_map/pallas_call | solution.py:133
  49.2 7.3 %collective-permute-done.16.far_image_t = bf16[128,1024]{1,0:T(8,128)(2,1)S(1)} collective-permute-done((bf16[128,1024]{1,0:T(8,128)(2,1)S(1)}, bf16[128,1024]{1,0:T(8,128)(2,1)S(1)}, u32[]{:S(2)}, u32[]{:S(2)}) %collective-permute-start.16) | collective-permute-done | bytes 262176 | tf_op jit(solution)/shard_map/ppermute | solution.py:20
  57.3 1.5 %collective-permute-start.19 = (f32[128,128]{1,0:T(8,128)S(1)}, f32[128,128]{1,0:T(8,128)S(1)}, u32[]{:S(2)}, u32[]{:S(2)}) collective-permute-start(f32[128,128]{1,0:T(8,128)S(1)} %get-tuple-element.40.refs_0_), channel_id=1, source_target_pairs={{0,3},{1,2},{2,1},{3,0},{4,7},{5,6},{6,5},{7,4},{8,11},{9,10},{10,... | collective-permute-start | bytes 196616 | tf_op jit(solution)/shard_map/ppermute | solution.py:20
  58.8 1.0 %collective-permute-start.18 = (f32[128,128]{1,0:T(8,128)S(1)}, f32[128,128]{1,0:T(8,128)S(1)}, u32[]{:S(2)}, u32[]{:S(2)}) collective-permute-start(f32[128,128]{1,0:T(8,128)S(1)} %get-tuple-element.40.refs_0_), channel_id=1, source_target_pairs={{0,2},{1,3},{2,0},{3,1},{4,6},{5,7},{6,4},{7,5},{8,10},{9,11},{10,... | collective-permute-start | bytes 196616 | tf_op jit(solution)/shard_map/ppermute | solution.py:20
  59.8 1.1 %collective-permute-start.17 = (f32[128,128]{1,0:T(8,128)S(1)}, f32[128,128]{1,0:T(8,128)S(1)}, u32[]{:S(2)}, u32[]{:S(2)}) collective-permute-start(f32[128,128]{1,0:T(8,128)S(1)} %get-tuple-element.40.refs_0_), channel_id=1, source_target_pairs={{0,1},{1,0},{2,3},{3,2},{4,5},{5,4},{6,7},{7,6},{8,9},{9,8},{10,11... | collective-permute-start | bytes 196616 | tf_op jit(solution)/shard_map/ppermute | solution.py:20
  60.9 1.7 %collective-permute-done.19.refs_3_ = f32[128,128]{1,0:T(8,128)S(1)} collective-permute-done((f32[128,128]{1,0:T(8,128)S(1)}, f32[128,128]{1,0:T(8,128)S(1)}, u32[]{:S(2)}, u32[]{:S(2)}) %collective-permute-start.19) | collective-permute-done | bytes 65568 | tf_op jit(solution)/shard_map/ppermute | solution.py:20
  64.4 1.2 %collective-permute-done.21.refs_1_ = f32[128,128]{1,0:T(8,128)S(1)} collective-permute-done((f32[128,128]{1,0:T(8,128)S(1)}, f32[128,128]{1,0:T(8,128)S(1)}, u32[]{:S(2)}, u32[]{:S(2)}) %collective-permute-start.21) | collective-permute-done | bytes 65568 | tf_op jit(solution)/shard_map/ppermute | solution.py:20
  65.6 2.3 %collective-permute-start.22 = (f32[128,128]{1,0:T(8,128)S(1)}, f32[128,128]{1,0:T(8,128)S(1)}, u32[]{:S(2)}, u32[]{:S(2)}) collective-permute-start(f32[128,128]{1,0:T(8,128)S(1)} %shard_map.55.refs_0_), channel_id=1, source_target_pairs={{0,8},{4,12},{8,0},{12,4},{16,24},{20,28},{24,16},{28,20},{1,9},{5... | collective-permute-start | bytes 196616 | tf_op jit(solution)/shard_map/ppermute | solution.py:20
  67.9 6.0 %collective-permute-done.23.came_ref = bf16[512,128]{1,0:T(8,128)(2,1)S(1)} collective-permute-done((bf16[512,128]{1,0:T(8,128)(2,1)S(1)}, bf16[512,128]{1,0:T(8,128)(2,1)S(1)}, u32[]{:S(2)}, u32[]{:S(2)}) %collective-permute-start.23) | collective-permute-done | bytes 131104 | tf_op jit(solution)/shard_map/ppermute | solution.py:20
  73.9 4.6 %shard_map.56 = (bf16[2,128,128]{2,1,0:T(8,128)(2,1)S(1)}, f32[128,128]{1,0:T(8,128)}) custom-call(f32[128,128]{1,0:T(8,128)S(1)} %shard_map.55.refs_0_, f32[128,128]{1,0:T(8,128)S(1)} %collective-permute-done.22.refs_1_, f32[2,128,128]{2,1,0:T(8,128)S(1)} %get-tuple-element.45.refs_2_, f32[128,128]{1,0:T(8,128)S(1)} %get-tuple-element.41.refs_3_), custom_call_target="tpu_custom_call" | custom-call | flops 2000000000 | bytes 1000000 | tf_op jit(solution)/shard_map/pallas_call | solution.py:133
  78.5 1.3 %shard_map.57 = bf16[4,1024,128]{2,1,0:T(8,128)(2,1)} custom-call(bf16[2,128,128]{2,1,0:T(8,128)(2,1)S(1)} %get-tuple-element.42.halves_ref, bf16[512,128]{1,0:T(8,128)(2,1)S(1)} %collective-permute-done.23.came_ref, bf16[512,128]{1,0:T(8,128)(2,1)S(1)} %collective-permute-done.24.shared_ref, bf16[1024,128]{1,0:T(8,128)(2,1)S(1)} %get-tuple-element.33.modes_own.refs_0_, ...), custom_call_target="tpu_custom_call" | custom-call | flops 2000000000 | bytes 1000000 | tf_op jit(solution)/shard_map/pallas_call | solution.py:133
  (34 shorter events, 7.1 us)
Async XLA Ops:
  0.0 9.1 %copy-start = (s32[8,7]{1,0:T(8,128)S(1)}, s32[8,7]{1,0:T(8,128)}, u32[]{:S(2)}) copy-start(s32[8,7]{1,0:T(8,128)} %index_ref.1) | copy-start | bytes 676
  0.9 6.4 %collective-permute-start = (bf16[2,128,128]{2,1,0:T(8,128)(2,1)S(1)}, bf16[2,128,128]{2,1,0:T(8,128)(2,1)S(1)}, u32[]{:S(2)}, u32[]{:S(2)}) collective-permute-start(bf16[2,128,128]{2,1,0:T(8,128)(2,1)S(1)} %bitcast.19), channel_id=1, source_target_pairs={{0,1},{1,0},{2,3},{3,2},{4,5},{5,4},{6,7},{7,6},{8,9},{9,8},{10,11... | collective-permute-start | bytes 196616 | tf_op jit(solution)/shard_map/ppermute | solution.py:379
  3.9 5.2 %collective-permute-start.1 = (bf16[2,128,128]{2,1,0:T(8,128)(2,1)S(1)}, bf16[2,128,128]{2,1,0:T(8,128)(2,1)S(1)}, u32[]{:S(2)}, u32[]{:S(2)}) collective-permute-start(bf16[2,128,128]{2,1,0:T(8,128)(2,1)S(1)} %bitcast.18), channel_id=1, source_target_pairs={{0,3},{1,2},{2,1},{3,0},{4,7},{5,6},{6,5},{7,4},{8,11},{9,10},{10,... | collective-permute-start | bytes 196616 | tf_op jit(solution)/shard_map/ppermute | solution.py:380
  10.4 1.6 %collective-permute-start.2 = (bf16[1024,128]{1,0:T(8,128)(2,1)S(1)}, bf16[1024,128]{1,0:T(8,128)(2,1)S(1)}, u32[]{:S(2)}, u32[]{:S(2)}) collective-permute-start(bf16[1024,128]{1,0:T(8,128)(2,1)S(1)} %bitcast.15), channel_id=1, source_target_pairs={{0,4},{4,0},{8,12},{12,8},{16,20},{20,16},{24,28},{28,24},{1,5},{5... | collective-permute-start | bytes 786440 | tf_op jit(solution)/shard_map/ppermute | solution.py:20
  12.3 6.4 %collective-permute-start.5 = (f32[192,128]{1,0:T(8,128)S(1)}, f32[192,128]{1,0:T(8,128)S(1)}, u32[]{:S(2)}, u32[]{:S(2)}) collective-permute-start(f32[192,128]{1,0:T(8,128)S(1)} %shard_map.48.refs_0_), channel_id=1, source_target_pairs={{0,3},{1,2},{2,1},{3,0},{4,7},{5,6},{6,5},{7,4},{8,11},{9,10},{10,... | collective-permute-start | bytes 294920 | tf_op jit(solution)/shard_map/ppermute | solution.py:20
  13.8 6.4 %collective-permute-start.4 = (f32[192,128]{1,0:T(8,128)S(1)}, f32[192,128]{1,0:T(8,128)S(1)}, u32[]{:S(2)}, u32[]{:S(2)}) collective-permute-start(f32[192,128]{1,0:T(8,128)S(1)} %shard_map.48.refs_0_), channel_id=1, source_target_pairs={{0,2},{1,3},{2,0},{3,1},{4,6},{5,7},{6,4},{7,5},{8,10},{9,11},{10,... | collective-permute-start | bytes 294920 | tf_op jit(solution)/shard_map/ppermute | solution.py:20
  14.8 5.4 %collective-permute-start.3 = (f32[192,128]{1,0:T(8,128)S(1)}, f32[192,128]{1,0:T(8,128)S(1)}, u32[]{:S(2)}, u32[]{:S(2)}) collective-permute-start(f32[192,128]{1,0:T(8,128)S(1)} %shard_map.48.refs_0_), channel_id=1, source_target_pairs={{0,1},{1,0},{2,3},{3,2},{4,5},{5,4},{6,7},{7,6},{8,9},{9,8},{10,11... | collective-permute-start | bytes 294920 | tf_op jit(solution)/shard_map/ppermute | solution.py:20
  15.8 8.5 %collective-permute-start.8 = (bf16[128,1024]{1,0:T(8,128)(2,1)S(1)}, bf16[128,1024]{1,0:T(8,128)(2,1)S(1)}, u32[]{:S(2)}, u32[]{:S(2)}) collective-permute-start(bf16[128,1024]{1,0:T(8,128)(2,1)S(1)} %get-tuple-element.29.image_t_ref), channel_id=1, source_target_pairs={{0,8},{4,12},{8,0},{12,4},{16,24},{20,28},{24,16},{28,20},{1,9},{5... | collective-permute-start | bytes 786440 | tf_op jit(solution)/shard_map/ppermute | solution.py:20
  23.7 1.7 %collective-permute-start.7 = (bf16[1024,128]{1,0:T(8,128)(2,1)S(1)}, bf16[1024,128]{1,0:T(8,128)(2,1)S(1)}, u32[]{:S(2)}, u32[]{:S(2)}) collective-permute-start(bf16[1024,128]{1,0:T(8,128)(2,1)S(1)} %get-tuple-element.33.modes_own.refs_0_), channel_id=1, source_target_pairs={{0,4},{4,0},{8,12},{12,8},{16,20},{20,16},{24,28},{28,24},{1,5},{5... | collective-permute-start | bytes 786440 | tf_op jit(solution)/shard_map/ppermute | solution.py:20
  23.8 1.7 %collective-permute-start.6 = (f32[192,128]{1,0:T(8,128)S(1)}, f32[192,128]{1,0:T(8,128)S(1)}, u32[]{:S(2)}, u32[]{:S(2)}) collective-permute-start(f32[192,128]{1,0:T(8,128)S(1)} %get-tuple-element.31.own_ref), channel_id=1, source_target_pairs={{0,4},{4,0},{8,12},{12,8},{16,20},{20,16},{24,28},{28,24},{1,5},{5... | collective-permute-start | bytes 294920 | tf_op jit(solution)/shard_map/ppermute | solution.py:20
  30.6 12.4 %collective-permute-start.14 = (bf16[1024,128]{1,0:T(8,128)(2,1)S(1)}, bf16[1024,128]{1,0:T(8,128)(2,1)S(1)}, u32[]{:S(2)}, u32[]{:S(2)}) collective-permute-start(bf16[1024,128]{1,0:T(8,128)(2,1)S(1)} %get-tuple-element.39), channel_id=1, source_target_pairs={{0,8},{4,12},{8,0},{12,4},{16,24},{20,28},{24,16},{28,20},{1,9},{5... | collective-permute-start | bytes 786440 | tf_op jit(solution)/shard_map/ppermute | solution.py:20
  32.3 8.2 %collective-permute-start.12 = (f32[128,128]{1,0:T(8,128)S(1)}, f32[128,128]{1,0:T(8,128)S(1)}, u32[]{:S(2)}, u32[]{:S(2)}) collective-permute-start(f32[128,128]{1,0:T(8,128)S(1)} %get-tuple-element.35.refs_3_), channel_id=1, source_target_pairs={{0,8},{4,12},{8,0},{12,4},{16,24},{20,28},{24,16},{28,20},{1,9},{5... | collective-permute-start | bytes 196616 | tf_op jit(solution)/shard_map/ppermute | solution.py:20
  32.7 10.3 %collective-permute-start.11 = (f32[128,128]{1,0:T(8,128)S(1)}, f32[128,128]{1,0:T(8,128)S(1)}, u32[]{:S(2)}, u32[]{:S(2)}) collective-permute-start(f32[128,128]{1,0:T(8,128)S(1)} %get-tuple-element.34.refs_0_), channel_id=1, source_target_pairs={{0,3},{1,2},{2,1},{3,0},{4,7},{5,6},{6,5},{7,4},{8,11},{9,10},{10,... | collective-permute-start | bytes 196616 | tf_op jit(solution)/shard_map/ppermute | solution.py:20
  34.1 9.0 %collective-permute-start.10 = (f32[128,128]{1,0:T(8,128)S(1)}, f32[128,128]{1,0:T(8,128)S(1)}, u32[]{:S(2)}, u32[]{:S(2)}) collective-permute-start(f32[128,128]{1,0:T(8,128)S(1)} %get-tuple-element.34.refs_0_), channel_id=1, source_target_pairs={{0,2},{1,3},{2,0},{3,1},{4,6},{5,7},{6,4},{7,5},{8,10},{9,11},{10,... | collective-permute-start | bytes 196616 | tf_op jit(solution)/shard_map/ppermute | solution.py:20
  35.1 8.0 %collective-permute-start.9 = (f32[128,128]{1,0:T(8,128)S(1)}, f32[128,128]{1,0:T(8,128)S(1)}, u32[]{:S(2)}, u32[]{:S(2)}) collective-permute-start(f32[128,128]{1,0:T(8,128)S(1)} %get-tuple-element.34.refs_0_), channel_id=1, source_target_pairs={{0,1},{1,0},{2,3},{3,2},{4,5},{5,4},{6,7},{7,6},{8,9},{9,8},{10,11... | collective-permute-start | bytes 196616 | tf_op jit(solution)/shard_map/ppermute | solution.py:20
  40.4 16.1 %collective-permute-start.16 = (bf16[128,1024]{1,0:T(8,128)(2,1)S(1)}, bf16[128,1024]{1,0:T(8,128)(2,1)S(1)}, u32[]{:S(2)}, u32[]{:S(2)}) collective-permute-start(bf16[128,1024]{1,0:T(8,128)(2,1)S(1)} %get-tuple-element.29.image_t_ref), channel_id=1, source_target_pairs={{0,16},{4,20},{8,24},{12,28},{16,0},{20,4},{24,8},{28,12},{1,17},{... | collective-permute-start | bytes 786440 | tf_op jit(solution)/shard_map/ppermute | solution.py:20
  43.0 13.5 %collective-permute-start.15 = (bf16[1024,128]{1,0:T(8,128)(2,1)S(1)}, bf16[1024,128]{1,0:T(8,128)(2,1)S(1)}, u32[]{:S(2)}, u32[]{:S(2)}) collective-permute-start(bf16[1024,128]{1,0:T(8,128)(2,1)S(1)} %collective-permute-done.14.came_ref), channel_id=1, source_target_pairs={{0,4},{4,0},{8,12},{12,8},{16,20},{20,16},{24,28},{28,24},{1,5},{5... | collective-permute-start | bytes 786440 | tf_op jit(solution)/shard_map/ppermute | solution.py:20
  43.2 1.5 %collective-permute-start.13 = (f32[128,128]{1,0:T(8,128)S(1)}, f32[128,128]{1,0:T(8,128)S(1)}, u32[]{:S(2)}, u32[]{:S(2)}) collective-permute-start(f32[128,128]{1,0:T(8,128)S(1)} %shard_map.51.refs_0_), channel_id=1, source_target_pairs={{0,4},{4,0},{8,12},{12,8},{16,20},{20,16},{24,28},{28,24},{1,5},{5... | collective-permute-start | bytes 196616 | tf_op jit(solution)/shard_map/ppermute | solution.py:20
  48.8 12.1 %collective-permute-start.20 = (f32[128,128]{1,0:T(8,128)S(1)}, f32[128,128]{1,0:T(8,128)S(1)}, u32[]{:S(2)}, u32[]{:S(2)}) collective-permute-start(f32[128,128]{1,0:T(8,128)S(1)} %get-tuple-element.41.refs_3_), channel_id=1, source_target_pairs={{0,16},{4,20},{8,24},{12,28},{16,0},{20,4},{24,8},{28,12},{1,17},{... | collective-permute-start | bytes 196616 | tf_op jit(solution)/shard_map/ppermute | solution.py:20
  57.3 5.2 %collective-permute-start.19 = (f32[128,128]{1,0:T(8,128)S(1)}, f32[128,128]{1,0:T(8,128)S(1)}, u32[]{:S(2)}, u32[]{:S(2)}) collective-permute-start(f32[128,128]{1,0:T(8,128)S(1)} %get-tuple-element.40.refs_0_), channel_id=1, source_target_pairs={{0,3},{1,2},{2,1},{3,0},{4,7},{5,6},{6,5},{7,4},{8,11},{9,10},{10,... | collective-permute-start | bytes 196616 | tf_op jit(solution)/shard_map/ppermute | solution.py:20
  58.8 4.5 %collective-permute-start.18 = (f32[128,128]{1,0:T(8,128)S(1)}, f32[128,128]{1,0:T(8,128)S(1)}, u32[]{:S(2)}, u32[]{:S(2)}) collective-permute-start(f32[128,128]{1,0:T(8,128)S(1)} %get-tuple-element.40.refs_0_), channel_id=1, source_target_pairs={{0,2},{1,3},{2,0},{3,1},{4,6},{5,7},{6,4},{7,5},{8,10},{9,11},{10,... | collective-permute-start | bytes 196616 | tf_op jit(solution)/shard_map/ppermute | solution.py:20
  59.8 4.3 %collective-permute-start.17 = (f32[128,128]{1,0:T(8,128)S(1)}, f32[128,128]{1,0:T(8,128)S(1)}, u32[]{:S(2)}, u32[]{:S(2)}) collective-permute-start(f32[128,128]{1,0:T(8,128)S(1)} %get-tuple-element.40.refs_0_), channel_id=1, source_target_pairs={{0,1},{1,0},{2,3},{3,2},{4,5},{5,4},{6,7},{7,6},{8,9},{9,8},{10,11... | collective-permute-start | bytes 196616 | tf_op jit(solution)/shard_map/ppermute | solution.py:20
  64.3 1.3 %collective-permute-start.21 = (f32[128,128]{1,0:T(8,128)S(1)}, f32[128,128]{1,0:T(8,128)S(1)}, u32[]{:S(2)}, u32[]{:S(2)}) collective-permute-start(f32[128,128]{1,0:T(8,128)S(1)} %shard_map.54.refs_0_), channel_id=1, source_target_pairs={{0,4},{4,0},{8,12},{12,8},{16,20},{20,16},{24,28},{28,24},{1,5},{5... | collective-permute-start | bytes 196616 | tf_op jit(solution)/shard_map/ppermute | solution.py:20
  64.3 9.6 %collective-permute-start.23 = (bf16[512,128]{1,0:T(8,128)(2,1)S(1)}, bf16[512,128]{1,0:T(8,128)(2,1)S(1)}, u32[]{:S(2)}, u32[]{:S(2)}) collective-permute-start(bf16[512,128]{1,0:T(8,128)(2,1)S(1)} %get-tuple-element.43), channel_id=1, source_target_pairs={{0,16},{4,20},{8,24},{12,28},{16,0},{20,4},{24,8},{28,12},{1,17},{... | collective-permute-start | bytes 393224 | tf_op jit(solution)/shard_map/ppermute | solution.py:20
  65.6 8.4 %collective-permute-start.22 = (f32[128,128]{1,0:T(8,128)S(1)}, f32[128,128]{1,0:T(8,128)S(1)}, u32[]{:S(2)}, u32[]{:S(2)}) collective-permute-start(f32[128,128]{1,0:T(8,128)S(1)} %shard_map.55.refs_0_), channel_id=1, source_target_pairs={{0,8},{4,12},{8,0},{12,4},{16,24},{20,28},{24,16},{28,20},{1,9},{5... | collective-permute-start | bytes 196616 | tf_op jit(solution)/shard_map/ppermute | solution.py:20
  73.9 4.6 %collective-permute-start.24 = (bf16[512,128]{1,0:T(8,128)(2,1)S(1)}, bf16[512,128]{1,0:T(8,128)(2,1)S(1)}, u32[]{:S(2)}, u32[]{:S(2)}) collective-permute-start(bf16[512,128]{1,0:T(8,128)(2,1)S(1)} %collective-permute-done.23.came_ref), channel_id=1, source_target_pairs={{0,4},{4,0},{8,12},{12,8},{16,20},{20,16},{24,28},{28,24},{1,5},{5... | collective-permute-start | bytes 393224 | tf_op jit(solution)/shard_map/ppermute | solution.py:20

commit v6 on v5

--- a/solution.py
+++ b/solution.py
@@ -312,10 +312,7 @@
     return jnp.concatenate([first, second], axis=0)
 
 
-def first_merge_kernel(
-    own_ref, other_ref, sketch_ref, modes_own, modes_other,
-    image_own, image_other, far_image_t, mine_ref, probe_ref, *bulk_refs,
-):
+def first_merge_kernel(own_ref, other_ref, sketch_ref, halves_ref, mine_ref, slices_ref):
     width = own_ref.shape[1]
     own, other = own_ref[:width], other_ref[:width]
     even, odd = choose("tm", own, other)
@@ -323,12 +320,21 @@
     cross = nt_full(nn_full(even, pair_gram), odd)
     cross_t = jnp.where(lax.axis_index("tm") % 2 == 1, cross, cross.T)
     half_own, half_other = merge(cross_t, sketch_ref)
+    halves_ref[0] = half_own.astype(BF16)
+    halves_ref[1] = half_other.astype(BF16)
     mine = nn_full(half_own, own)
-    theirs = nn_full(half_other, other)
     mine_ref[...] = mine
-    image = combined(image_own[...], image_other[...], mine, theirs)
+    slices_ref[0] = mine.astype(BF16)
+    slices_ref[1] = nn_full(half_other, other).astype(BF16)
+
+
+def first_apply_kernel(
+    halves_ref, slices_ref, modes_own, modes_other, image_own, image_other, far_image_t,
+    probe_ref, *bulk_refs,
+):
+    image = combined(image_own[...], image_other[...], slices_ref[0], slices_ref[1])
     probe_ref[...] = dot_nn(far_image_t[...], image)
-    modes = combined(modes_own[...], modes_other[...], half_own, half_other)
+    modes = combined(modes_own[...], modes_other[...], halves_ref[0], halves_ref[1])
     write_bulk(bulk_refs, modes, image)
 
 
@@ -338,6 +344,21 @@
     halves_ref[0] = half_own.astype(BF16)
     halves_ref[1] = half_other.astype(BF16)
     mine_ref[...] = nn_full(half_own, old_ref[...])
+
+
+def last_merge_kernel(count, *refs):
+    parts, (sketch_ref, *kept, halves_ref, out_ref, sems) = refs[:count], refs[count:]
+    copies = [
+        pltpu.make_async_copy(modes_ref, out_ref.at[level], sems.at[level])
+        for level, modes_ref in enumerate(kept)
+    ]
+    for copy in copies:
+        copy.start()
+    half_own, half_other = merge(total_of(parts), sketch_ref)
+    halves_ref[0] = half_own.astype(BF16)
+    halves_ref[1] = half_other.astype(BF16)
+    for copy in copies:
+        copy.wait()
 
 
 def apply_kernel(
@@ -350,14 +371,55 @@
     write_bulk(bulk_refs, modes, image)
 
 
-def output_kernel(halves_ref, came_ref, shared_ref, *refs):
-    *earlier, out_ref = refs
-    for level, modes_ref in enumerate(earlier):
-        out_ref[level] = modes_ref[...]
-    modes_other = read_modes(came_ref, shared_ref, out_ref.shape[1])
-    out_ref[len(earlier)] = combined(
-        earlier[-1][...], modes_other, halves_ref[0], halves_ref[1]
-    )
+def output_kernel(halves_ref, modes_own, came_ref, shared_ref, _, out_ref, modes_ref, sems):
+    rows = modes_own.shape[0]
+    modes_other = read_modes(came_ref, shared_ref, rows)
+    part = rows // 2
+    copies = []
+    for half in range(2):
+        span = slice(half * part, (half + 1) * part)
+        modes_ref[span] = combined(
+            modes_own[span], modes_other[span], halves_ref[0], halves_ref[1]
+        )
+        copies.append(
+            pltpu.make_async_copy(
+                modes_ref.at[pl.ds(half * part, part)],
+                out_ref.at[out_ref.shape[0] - 1, pl.ds(half * part, part)],
+                sems.at[half],
+            )
+        )
+        copies[-1].start()
+    for copy in copies:
+        copy.wait()
+
+
+def last_level(parts, sketch_t, kept, halves_shape):
+    rows, width = kept[0].shape
+    levels = len(kept)
+    vmem = pl.BlockSpec(memory_space=pltpu.VMEM)
+    hbm = pl.BlockSpec(memory_space=pltpu.HBM)
+    return pl.pallas_call(
+        functools.partial(last_merge_kernel, len(parts)),
+        out_shape=[halves_shape, jax.ShapeDtypeStruct((levels + 1, rows, width), BF16)],
+        in_specs=[vmem] * (len(parts) + 1 + levels),
+        out_specs=[vmem, hbm],
+        scratch_shapes=[pltpu.SemaphoreType.DMA((levels,))],
+        compiler_params=PARAMS,
+    )(*parts, sketch_t, *kept)
+
+
+def last_modes(halves, modes, came, shared, out):
+    vmem = pl.BlockSpec(memory_space=pltpu.VMEM)
+    hbm = pl.BlockSpec(memory_space=pltpu.HBM)
+    return pl.pallas_call(
+        output_kernel,
+        out_shape=jax.ShapeDtypeStruct(out.shape, BF16),
+        in_specs=[vmem] * 4 + [hbm],
+        out_specs=hbm,
+        scratch_shapes=[pltpu.VMEM(modes.shape, BF16), pltpu.SemaphoreType.DMA((2,))],
+        input_output_aliases={4: 0},
+        compiler_params=PARAMS,
+    )(halves, modes, came, shared, out)
 
 
 def cross_kernel(total_rows, count, *refs):
@@ -405,10 +467,13 @@
         deep = level + 2 < levels
         outs = [square, square, modes_shape] + ([modes_shape] * 2 if deep else [half_shape])
         if level == 0:
-            mine, probe, *bulk = run_kernel(
-                first_merge_kernel, outs,
+            halves, mine, slices = run_kernel(
+                first_merge_kernel, [halves_shape, square, halves_shape],
                 factor, other_factor, sketch_t[level],
-                modes, other, image, other_image, far_images[level],
+            )
+            probe, *bulk = run_kernel(
+                first_apply_kernel, outs[1:],
+                halves, slices, modes, other, image, other_image, far_images[level],
             )
         else:
             far_mine = swap(mine, "tm", 2**level)
@@ -420,21 +485,18 @@
                 square, *parts, far_mine,
             )
             parts = summands(cross, "tm", 2**level, 2)
-            halves, mine = run_kernel(
-                functools.partial(merge_kernel, len(parts)), [halves_shape, square],
-                *parts, sketch_t[level], mine,
-            )
             if level + 1 < levels:
+                halves, mine = run_kernel(
+                    functools.partial(merge_kernel, len(parts)), [halves_shape, square],
+                    *parts, sketch_t[level], mine,
+                )
                 probe, *bulk = run_kernel(
                     apply_kernel, outs[1:],
                     halves, *bulk[:2], came, shared, far_images[level],
                 )
             else:
-                out = run_kernel(
-                    output_kernel,
-                    jax.ShapeDtypeStruct((levels + 1, rows_dev, width), BF16),
-                    halves, came, shared, *kept,
-                )
+                halves, out = last_level(parts, sketch_t[level], kept, halves_shape)
+                out = last_modes(halves, bulk[0], came, shared, out)
         kept.append(bulk[0])
     return out[:, None]
 

time: 80 us -> 78 us (0.975)
  starting transfers between devices: 25.4 us -> 23.1 us
    pallas_call x10 -> x9, Pallas kernels: 20 us -> 14.1 us  [run_kernel(): pl.pallas_call(body, out_shape=outs, cost_estimate=cost, compiler_params=...]
    pallas_call x0 -> x2, Pallas kernels: none -> 5.25 us  [the longest x1 4.23 us: last_level(): pl.pallas_call(functools.partial(last_merge_kernel, len(parts)), out_shap...]
    ppermute x23, starting transfers between devices: 20.9 us -> 18.6 us  [swap(): return lax.ppermute(value, axis, pairs)]
  transfers between devices with their start and end apart: 25 -> 25, of which waited for: 14 -> 14; matrix products, arithmetic and copies ran while one was open for 0% -> 0% of each run, Pallas kernels for 19% -> 25%
where the time goes in v6:
time: 78 us; the launch traced here: 77.8 us
  waiting for transfers between devices  30.9 us (40%)
  starting transfers between devices  23.1 us (30%)
  Pallas kernels  22.5 us (29%)
  other arithmetic  0.9 us (1%)
    ppermute x23, waiting for transfers between devices, swap(): return lax.ppermute(value, axis, pairs)  29.1 us
    ppermute x23, starting transfers between devices, swap(): return lax.ppermute(value, axis, pairs)  18.6 us
    pallas_call x9, Pallas kernels, run_kernel(): pl.pallas_call(body, out_shape=outs, cost_estimate=cost, compiler_params=...  14.1 us
    pallas_call x1, Pallas kernels, last_level(): pl.pallas_call(functools.partial(last_merge_kernel, len(parts)), out_shap...  4.23 us
    ppermute x1, starting transfers between devices, modes_of(): came_near = lax.ppermute(jnp.where(odd, head, tail), 'space', near)  3.03 us
    pallas_call x1, Pallas kernels, interior_of(): pl.pallas_call(interior_kernel, out_shape=[jax.ShapeDtypeStruct((inner, r...  1.89 us
    ppermute x1, waiting for transfers between devices, modes_of(): came_wide = lax.ppermute(jnp.where(odd, tail, head), 'space', wide)  1.77 us
  transfers between devices with their start and end apart: 25, of which 14 were waited for; matrix products, arithmetic and copies ran while one was open for 0% of the time, Pallas kernels for 25%

profile of v6, /device:TPU:0, one launch (start us, length us, event | category | flops | bytes accessed | tf_op | source)
XLA Modules:
  0.0 77.8 jit_solution(11205045053763150551)
XLA Ops:
  0.0 0.9 %broadcast_select_fusion = (bf16[256,128]{1,0:T(8,128)(2,1)S(1)}, bf16[256,128]{1,0:T(8,128)(2,1)S(1)}) fusion(pred[]{:T(512)S(6)} %eq.3, bf16[1024,128]{1,0:T(8,128)(2,1)} %param.4), kind=kLoop, calls=%fused_computation.3 | loop fusion | flops 65536 | bytes 262145 | tf_op jit(solution)/shard_map/jit(_where)/select_n | solution.py:442
  0.9 3.0 %collective-permute-start = (bf16[2,128,128]{2,1,0:T(8,128)(2,1)S(1)}, bf16[2,128,128]{2,1,0:T(8,128)(2,1)S(1)}, u32[]{:S(2)}, u32[]{:S(2)}) collective-permute-start(bf16[2,128,128]{2,1,0:T(8,128)(2,1)S(1)} %bitcast.19), channel_id=1, source_target_pairs={{0,1},{1,0},{2,3},{3,2},{4,5},{5,4},{6,7},{7,6},{8,9},{9,8},{10,11... | collective-permute-start | bytes 196616 | tf_op jit(solution)/shard_map/ppermute | solution.py:441
  3.9 1.5 %collective-permute-start.1 = (bf16[2,128,128]{2,1,0:T(8,128)(2,1)S(1)}, bf16[2,128,128]{2,1,0:T(8,128)(2,1)S(1)}, u32[]{:S(2)}, u32[]{:S(2)}) collective-permute-start(bf16[2,128,128]{2,1,0:T(8,128)(2,1)S(1)} %bitcast.18), channel_id=1, source_target_pairs={{0,3},{1,2},{2,1},{3,0},{4,7},{5,6},{6,5},{7,4},{8,11},{9,10},{10,... | collective-permute-start | bytes 196616 | tf_op jit(solution)/shard_map/ppermute | solution.py:442
  5.4 1.9 %shard_map.46 = (bf16[4,128,128]{2,1,0:T(8,128)(2,1)S(1)}, f32[3,2,128,128]{3,2,1,0:T(8,128)S(1)}, bf16[2,2,7,128,128]{4,3,2,1,0:T(8,128)(2,1)S(1)}, bf16[8,128,128]{2,1,0:T(8,128)(2,1)S(1)}) custom-call(s32[8,7]{1,0:T(8,128)} %index_ref.1, bf16[8,7,128,128]{3,2,1,0:T(8,128)(2,1)} %energy_hbm.1, bf16[8,128,128]{2,1,0:T(8,128)(2,1)} %bitcast.17, ...), custom_call_target="tpu_custom_call" | custom-call | tf_op jit(solution)/shard_map/pallas_call | solution.py:218
  7.3 1.8 %collective-permute-done.1.wide_ref = bf16[2,128,128]{2,1,0:T(8,128)(2,1)S(1)} collective-permute-done((bf16[2,128,128]{2,1,0:T(8,128)(2,1)S(1)}, bf16[2,128,128]{2,1,0:T(8,128)(2,1)S(1)}, u32[]{:S(2)}, u32[]{:S(2)}) %collective-permute-start.1) | collective-permute-done | bytes 65568 | tf_op jit(solution)/shard_map/ppermute | solution.py:442
  9.1 1.3 %shard_map.47 = (bf16[8,128,128]{2,1,0:T(8,128)(2,1)S(1)}, bf16[128,1024]{1,0:T(8,128)(2,1)S(1)}, f32[128,128]{1,0:T(8,128)S(1)}) custom-call(s32[8,7]{1,0:T(8,128)S(1)} %copy-done, bf16[2,2,7,128,128]{4,3,2,1,0:T(8,128)(2,1)S(1)} %get-tuple-element.28.edges_ref, bf16[2,128,128]{2,1,0:T(8,128)(2,1)S(1)} %collective-permute-done.near_ref, ...), custom_call_target="tpu_custom_call" | custom-call | tf_op jit(solution)/shard_map/pallas_call | solution.py:239
  10.5 1.5 %collective-permute-done.2.other_ref.image_other = bf16[1024,128]{1,0:T(8,128)(2,1)S(1)} collective-permute-done((bf16[1024,128]{1,0:T(8,128)(2,1)S(1)}, bf16[1024,128]{1,0:T(8,128)(2,1)S(1)}, u32[]{:S(2)}, u32[]{:S(2)}) %collective-permute-start.2) | collective-permute-done | bytes 262176 | tf_op jit(solution)/shard_map/ppermute | solution.py:20
  12.3 1.6 %collective-permute-start.5 = (f32[192,128]{1,0:T(8,128)S(1)}, f32[192,128]{1,0:T(8,128)S(1)}, u32[]{:S(2)}, u32[]{:S(2)}) collective-permute-start(f32[192,128]{1,0:T(8,128)S(1)} %shard_map.48.refs_0_), channel_id=1, source_target_pairs={{0,3},{1,2},{2,1},{3,0},{4,7},{5,6},{6,5},{7,4},{8,11},{9,10},{10,... | collective-permute-start | bytes 294920 | tf_op jit(solution)/shard_map/ppermute | solution.py:20
  13.8 1.0 %collective-permute-start.4 = (f32[192,128]{1,0:T(8,128)S(1)}, f32[192,128]{1,0:T(8,128)S(1)}, u32[]{:S(2)}, u32[]{:S(2)}) collective-permute-start(f32[192,128]{1,0:T(8,128)S(1)} %shard_map.48.refs_0_), channel_id=1, source_target_pairs={{0,2},{1,3},{2,0},{3,1},{4,6},{5,7},{6,4},{7,5},{8,10},{9,11},{10,... | collective-permute-start | bytes 294920 | tf_op jit(solution)/shard_map/ppermute | solution.py:20
  14.8 1.0 %collective-permute-start.3 = (f32[192,128]{1,0:T(8,128)S(1)}, f32[192,128]{1,0:T(8,128)S(1)}, u32[]{:S(2)}, u32[]{:S(2)}) collective-permute-start(f32[192,128]{1,0:T(8,128)S(1)} %shard_map.48.refs_0_), channel_id=1, source_target_pairs={{0,1},{1,0},{2,3},{3,2},{4,5},{5,4},{6,7},{7,6},{8,9},{9,8},{10,11... | collective-permute-start | bytes 294920 | tf_op jit(solution)/shard_map/ppermute | solution.py:20
  15.8 1.6 %collective-permute-start.8 = (bf16[128,1024]{1,0:T(8,128)(2,1)S(1)}, bf16[128,1024]{1,0:T(8,128)(2,1)S(1)}, u32[]{:S(2)}, u32[]{:S(2)}) collective-permute-start(bf16[128,1024]{1,0:T(8,128)(2,1)S(1)} %get-tuple-element.32.image_t_ref), channel_id=1, source_target_pairs={{0,8},{4,12},{8,0},{12,4},{16,24},{20,28},{24,16},{28,20},{1,9},{5... | collective-permute-start | bytes 786440 | tf_op jit(solution)/shard_map/ppermute | solution.py:20
  17.4 1.3 %collective-permute-done.5.refs_3_ = f32[192,128]{1,0:T(8,128)S(1)} collective-permute-done((f32[192,128]{1,0:T(8,128)S(1)}, f32[192,128]{1,0:T(8,128)S(1)}, u32[]{:S(2)}, u32[]{:S(2)}) %collective-permute-start.5) | collective-permute-done | bytes 98336 | tf_op jit(solution)/shard_map/ppermute | solution.py:20
  18.7 1.5 %collective-permute-done.4.refs_2_ = f32[192,128]{1,0:T(8,128)S(1)} collective-permute-done((f32[192,128]{1,0:T(8,128)S(1)}, f32[192,128]{1,0:T(8,128)S(1)}, u32[]{:S(2)}, u32[]{:S(2)}) %collective-permute-start.4) | collective-permute-done | bytes 98336 | tf_op jit(solution)/shard_map/ppermute | solution.py:20
  20.3 3.4 %shard_map.49 = (f32[192,128]{1,0:T(8,128)S(1)}, bf16[1024,128]{1,0:T(8,128)(2,1)S(1)}) custom-call(f32[192,128]{1,0:T(8,128)S(1)} %shard_map.48.refs_0_, f32[192,128]{1,0:T(8,128)S(1)} %collective-permute-done.3.refs_1_, f32[192,128]{1,0:T(8,128)S(1)} %collective-permute-done.4.refs_2_, f32[192,128]{1,0:T(8,128)S(1)} %collective-permute-done.5.refs_3_, ...), custom_call_target="tpu_custom_call" | custom-call | flops 2000000000 | bytes 1000000 | tf_op jit(solution)/shard_map/pallas_call | solution.py:133
  25.1 4.4 %shard_map.50 = (bf16[2,128,128]{2,1,0:T(8,128)(2,1)S(1)}, f32[128,128]{1,0:T(8,128)S(1)}, bf16[2,128,128]{2,1,0:T(8,128)(2,1)S(1)}) custom-call(f32[192,128]{1,0:T(8,128)S(1)} %get-tuple-element.34.own_ref, f32[192,128]{1,0:T(8,128)S(1)} %collective-permute-done.6.other_ref, f32[2,128,128]{2,1,0:T(8,128)S(1)} %get-tuple-element.53.sketch_ref), custom_call_target="tpu_custom_call" | custom-call | flops 2000000000 | bytes 1000000 | tf_op jit(solution)/shard_map/pallas_call | solution.py:133
  30.3 1.6 %collective-permute-start.14 = (bf16[1024,128]{1,0:T(8,128)(2,1)S(1)}, bf16[1024,128]{1,0:T(8,128)(2,1)S(1)}, u32[]{:S(2)}, u32[]{:S(2)}) collective-permute-start(bf16[1024,128]{1,0:T(8,128)(2,1)S(1)} %get-tuple-element.44), channel_id=1, source_target_pairs={{0,8},{4,12},{8,0},{12,4},{16,24},{20,28},{24,16},{28,20},{1,9},{5... | collective-permute-start | bytes 786440 | tf_op jit(solution)/shard_map/ppermute | solution.py:20
  32.4 1.4 %collective-permute-start.11 = (f32[128,128]{1,0:T(8,128)S(1)}, f32[128,128]{1,0:T(8,128)S(1)}, u32[]{:S(2)}, u32[]{:S(2)}) collective-permute-start(f32[128,128]{1,0:T(8,128)S(1)} %get-tuple-element.39.refs_0_), channel_id=1, source_target_pairs={{0,3},{1,2},{2,1},{3,0},{4,7},{5,6},{6,5},{7,4},{8,11},{9,10},{10,... | collective-permute-start | bytes 196616 | tf_op jit(solution)/shard_map/ppermute | solution.py:20
  33.8 1.0 %collective-permute-start.10 = (f32[128,128]{1,0:T(8,128)S(1)}, f32[128,128]{1,0:T(8,128)S(1)}, u32[]{:S(2)}, u32[]{:S(2)}) collective-permute-start(f32[128,128]{1,0:T(8,128)S(1)} %get-tuple-element.39.refs_0_), channel_id=1, source_target_pairs={{0,2},{1,3},{2,0},{3,1},{4,6},{5,7},{6,4},{7,5},{8,10},{9,11},{10,... | collective-permute-start | bytes 196616 | tf_op jit(solution)/shard_map/ppermute | solution.py:20
  34.8 1.1 %collective-permute-start.9 = (f32[128,128]{1,0:T(8,128)S(1)}, f32[128,128]{1,0:T(8,128)S(1)}, u32[]{:S(2)}, u32[]{:S(2)}) collective-permute-start(f32[128,128]{1,0:T(8,128)S(1)} %get-tuple-element.39.refs_0_), channel_id=1, source_target_pairs={{0,1},{1,0},{2,3},{3,2},{4,5},{5,4},{6,7},{7,6},{8,9},{9,8},{10,11... | collective-permute-start | bytes 196616 | tf_op jit(solution)/shard_map/ppermute | solution.py:20
  35.9 4.2 %collective-permute-done.12.refs_4_ = f32[128,128]{1,0:T(8,128)S(1)} collective-permute-done((f32[128,128]{1,0:T(8,128)S(1)}, f32[128,128]{1,0:T(8,128)S(1)}, u32[]{:S(2)}, u32[]{:S(2)}) %collective-permute-start.12) | collective-permute-done | bytes 65568 | tf_op jit(solution)/shard_map/ppermute | solution.py:20
  40.1 2.6 %collective-permute-start.16 = (bf16[128,1024]{1,0:T(8,128)(2,1)S(1)}, bf16[128,1024]{1,0:T(8,128)(2,1)S(1)}, u32[]{:S(2)}, u32[]{:S(2)}) collective-permute-start(bf16[128,1024]{1,0:T(8,128)(2,1)S(1)} %get-tuple-element.32.image_t_ref), channel_id=1, source_target_pairs={{0,16},{4,20},{8,24},{12,28},{16,0},{20,4},{24,8},{28,12},{1,17},{... | collective-permute-start | bytes 786440 | tf_op jit(solution)/shard_map/ppermute | solution.py:20
  43.5 0.9 %collective-permute-done.13.refs_1_ = f32[128,128]{1,0:T(8,128)S(1)} collective-permute-done((f32[128,128]{1,0:T(8,128)S(1)}, f32[128,128]{1,0:T(8,128)S(1)}, u32[]{:S(2)}, u32[]{:S(2)}) %collective-permute-start.13) | collective-permute-done | bytes 65568 | tf_op jit(solution)/shard_map/ppermute | solution.py:20
  44.4 4.1 %shard_map.53 = (bf16[2,128,128]{2,1,0:T(8,128)(2,1)S(1)}, f32[128,128]{1,0:T(8,128)S(1)}) custom-call(f32[128,128]{1,0:T(8,128)S(1)} %shard_map.52.refs_0_, f32[128,128]{1,0:T(8,128)S(1)} %collective-permute-done.13.refs_1_, f32[2,128,128]{2,1,0:T(8,128)S(1)} %get-tuple-element.52.refs_2_, f32[128,128]{1,0:T(8,128)S(1)} %get-tuple-element.40.refs_3_), custom_call_target="tpu_custom_call" | custom-call | flops 2000000000 | bytes 1000000 | tf_op jit(solution)/shard_map/pallas_call | solution.py:133
  48.9 7.3 %collective-permute-done.16.far_image_t = bf16[128,1024]{1,0:T(8,128)(2,1)S(1)} collective-permute-done((bf16[128,1024]{1,0:T(8,128)(2,1)S(1)}, bf16[128,1024]{1,0:T(8,128)(2,1)S(1)}, u32[]{:S(2)}, u32[]{:S(2)}) %collective-permute-start.16) | collective-permute-done | bytes 262176 | tf_op jit(solution)/shard_map/ppermute | solution.py:20
  57.0 1.5 %collective-permute-start.19 = (f32[128,128]{1,0:T(8,128)S(1)}, f32[128,128]{1,0:T(8,128)S(1)}, u32[]{:S(2)}, u32[]{:S(2)}) collective-permute-start(f32[128,128]{1,0:T(8,128)S(1)} %get-tuple-element.45.refs_0_), channel_id=1, source_target_pairs={{0,3},{1,2},{2,1},{3,0},{4,7},{5,6},{6,5},{7,4},{8,11},{9,10},{10,... | collective-permute-start | bytes 196616 | tf_op jit(solution)/shard_map/ppermute | solution.py:20
  58.5 1.0 %collective-permute-start.18 = (f32[128,128]{1,0:T(8,128)S(1)}, f32[128,128]{1,0:T(8,128)S(1)}, u32[]{:S(2)}, u32[]{:S(2)}) collective-permute-start(f32[128,128]{1,0:T(8,128)S(1)} %get-tuple-element.45.refs_0_), channel_id=1, source_target_pairs={{0,2},{1,3},{2,0},{3,1},{4,6},{5,7},{6,4},{7,5},{8,10},{9,11},{10,... | collective-permute-start | bytes 196616 | tf_op jit(solution)/shard_map/ppermute | solution.py:20
  59.5 1.1 %collective-permute-start.17 = (f32[128,128]{1,0:T(8,128)S(1)}, f32[128,128]{1,0:T(8,128)S(1)}, u32[]{:S(2)}, u32[]{:S(2)}) collective-permute-start(f32[128,128]{1,0:T(8,128)S(1)} %get-tuple-element.45.refs_0_), channel_id=1, source_target_pairs={{0,1},{1,0},{2,3},{3,2},{4,5},{5,4},{6,7},{7,6},{8,9},{9,8},{10,11... | collective-permute-start | bytes 196616 | tf_op jit(solution)/shard_map/ppermute | solution.py:20
  60.6 1.7 %collective-permute-done.19.refs_3_ = f32[128,128]{1,0:T(8,128)S(1)} collective-permute-done((f32[128,128]{1,0:T(8,128)S(1)}, f32[128,128]{1,0:T(8,128)S(1)}, u32[]{:S(2)}, u32[]{:S(2)}) %collective-permute-start.19) | collective-permute-done | bytes 65568 | tf_op jit(solution)/shard_map/ppermute | solution.py:20
  64.0 3.8 %collective-permute-done.23.came_ref = bf16[512,128]{1,0:T(8,128)(2,1)S(1)} collective-permute-done((bf16[512,128]{1,0:T(8,128)(2,1)S(1)}, bf16[512,128]{1,0:T(8,128)(2,1)S(1)}, u32[]{:S(2)}, u32[]{:S(2)}) %collective-permute-start.23) | collective-permute-done | bytes 131104 | tf_op jit(solution)/shard_map/ppermute | solution.py:20
  67.9 4.5 %collective-permute-done.22.refs_1_ = f32[128,128]{1,0:T(8,128)S(1)} collective-permute-done((f32[128,128]{1,0:T(8,128)S(1)}, f32[128,128]{1,0:T(8,128)S(1)}, u32[]{:S(2)}, u32[]{:S(2)}) %collective-permute-start.22) | collective-permute-done | bytes 65568 | tf_op jit(solution)/shard_map/ppermute | solution.py:20
  72.4 4.2 %shard_map.57 = (bf16[2,128,128]{2,1,0:T(8,128)(2,1)S(1)}, bf16[4,1024,128]{2,1,0:T(8,128)(2,1)}) custom-call(f32[128,128]{1,0:T(8,128)S(1)} %shard_map.56.refs_0_, f32[128,128]{1,0:T(8,128)S(1)} %collective-permute-done.22.refs_1_, f32[2,128,128]{2,1,0:T(8,128)S(1)} %get-tuple-element.51.refs_2_, bf16[1024,128]{1,0:T(8,128)(2,1)S(1)} %get-tuple-element.38.modes_own.refs_3_, ...), custom_call_target="tpu_custom_call" | custom-call | tf_op jit(solution)/shard_map/pallas_call | solution.py:401
  76.7 1.0 %shard_map.58 = bf16[4,1024,128]{2,1,0:T(8,128)(2,1)} custom-call(bf16[2,128,128]{2,1,0:T(8,128)(2,1)S(1)} %get-tuple-element.48.halves_ref, bf16[1024,128]{1,0:T(8,128)(2,1)S(1)} %get-tuple-element.47.refs_5_.modes_own, bf16[512,128]{1,0:T(8,128)(2,1)S(1)} %collective-permute-done.23.came_ref, ...), custom_call_target="tpu_custom_call", output_to_operand_aliasing={{}: (4, {})} | custom-call | tf_op jit(solution)/shard_map/pallas_call | solution.py:414
  (35 shorter events, 6.8 us)
Async XLA Ops:
  0.0 9.1 %copy-start = (s32[8,7]{1,0:T(8,128)S(1)}, s32[8,7]{1,0:T(8,128)}, u32[]{:S(2)}) copy-start(s32[8,7]{1,0:T(8,128)} %index_ref.1) | copy-start | bytes 676
  0.9 6.4 %collective-permute-start = (bf16[2,128,128]{2,1,0:T(8,128)(2,1)S(1)}, bf16[2,128,128]{2,1,0:T(8,128)(2,1)S(1)}, u32[]{:S(2)}, u32[]{:S(2)}) collective-permute-start(bf16[2,128,128]{2,1,0:T(8,128)(2,1)S(1)} %bitcast.19), channel_id=1, source_target_pairs={{0,1},{1,0},{2,3},{3,2},{4,5},{5,4},{6,7},{7,6},{8,9},{9,8},{10,11... | collective-permute-start | bytes 196616 | tf_op jit(solution)/shard_map/ppermute | solution.py:441
  3.9 5.2 %collective-permute-start.1 = (bf16[2,128,128]{2,1,0:T(8,128)(2,1)S(1)}, bf16[2,128,128]{2,1,0:T(8,128)(2,1)S(1)}, u32[]{:S(2)}, u32[]{:S(2)}) collective-permute-start(bf16[2,128,128]{2,1,0:T(8,128)(2,1)S(1)} %bitcast.18), channel_id=1, source_target_pairs={{0,3},{1,2},{2,1},{3,0},{4,7},{5,6},{6,5},{7,4},{8,11},{9,10},{10,... | collective-permute-start | bytes 196616 | tf_op jit(solution)/shard_map/ppermute | solution.py:442
  10.4 1.6 %collective-permute-start.2 = (bf16[1024,128]{1,0:T(8,128)(2,1)S(1)}, bf16[1024,128]{1,0:T(8,128)(2,1)S(1)}, u32[]{:S(2)}, u32[]{:S(2)}) collective-permute-start(bf16[1024,128]{1,0:T(8,128)(2,1)S(1)} %bitcast.15), channel_id=1, source_target_pairs={{0,4},{4,0},{8,12},{12,8},{16,20},{20,16},{24,28},{28,24},{1,5},{5... | collective-permute-start | bytes 786440 | tf_op jit(solution)/shard_map/ppermute | solution.py:20
  12.3 6.4 %collective-permute-start.5 = (f32[192,128]{1,0:T(8,128)S(1)}, f32[192,128]{1,0:T(8,128)S(1)}, u32[]{:S(2)}, u32[]{:S(2)}) collective-permute-start(f32[192,128]{1,0:T(8,128)S(1)} %shard_map.48.refs_0_), channel_id=1, source_target_pairs={{0,3},{1,2},{2,1},{3,0},{4,7},{5,6},{6,5},{7,4},{8,11},{9,10},{10,... | collective-permute-start | bytes 294920 | tf_op jit(solution)/shard_map/ppermute | solution.py:20
  13.8 6.4 %collective-permute-start.4 = (f32[192,128]{1,0:T(8,128)S(1)}, f32[192,128]{1,0:T(8,128)S(1)}, u32[]{:S(2)}, u32[]{:S(2)}) collective-permute-start(f32[192,128]{1,0:T(8,128)S(1)} %shard_map.48.refs_0_), channel_id=1, source_target_pairs={{0,2},{1,3},{2,0},{3,1},{4,6},{5,7},{6,4},{7,5},{8,10},{9,11},{10,... | collective-permute-start | bytes 294920 | tf_op jit(solution)/shard_map/ppermute | solution.py:20
  14.8 5.5 %collective-permute-start.3 = (f32[192,128]{1,0:T(8,128)S(1)}, f32[192,128]{1,0:T(8,128)S(1)}, u32[]{:S(2)}, u32[]{:S(2)}) collective-permute-start(f32[192,128]{1,0:T(8,128)S(1)} %shard_map.48.refs_0_), channel_id=1, source_target_pairs={{0,1},{1,0},{2,3},{3,2},{4,5},{5,4},{6,7},{7,6},{8,9},{9,8},{10,11... | collective-permute-start | bytes 294920 | tf_op jit(solution)/shard_map/ppermute | solution.py:20
  15.8 13.6 %collective-permute-start.8 = (bf16[128,1024]{1,0:T(8,128)(2,1)S(1)}, bf16[128,1024]{1,0:T(8,128)(2,1)S(1)}, u32[]{:S(2)}, u32[]{:S(2)}) collective-permute-start(bf16[128,1024]{1,0:T(8,128)(2,1)S(1)} %get-tuple-element.32.image_t_ref), channel_id=1, source_target_pairs={{0,8},{4,12},{8,0},{12,4},{16,24},{20,28},{24,16},{28,20},{1,9},{5... | collective-permute-start | bytes 786440 | tf_op jit(solution)/shard_map/ppermute | solution.py:20
  23.7 1.4 %collective-permute-start.6 = (f32[192,128]{1,0:T(8,128)S(1)}, f32[192,128]{1,0:T(8,128)S(1)}, u32[]{:S(2)}, u32[]{:S(2)}) collective-permute-start(f32[192,128]{1,0:T(8,128)S(1)} %get-tuple-element.34.own_ref), channel_id=1, source_target_pairs={{0,4},{4,0},{8,12},{12,8},{16,20},{20,16},{24,28},{28,24},{1,5},{5... | collective-permute-start | bytes 294920 | tf_op jit(solution)/shard_map/ppermute | solution.py:20
  23.8 5.7 %collective-permute-start.7 = (bf16[1024,128]{1,0:T(8,128)(2,1)S(1)}, bf16[1024,128]{1,0:T(8,128)(2,1)S(1)}, u32[]{:S(2)}, u32[]{:S(2)}) collective-permute-start(bf16[1024,128]{1,0:T(8,128)(2,1)S(1)} %get-tuple-element.38.modes_own.refs_3_), channel_id=1, source_target_pairs={{0,4},{4,0},{8,12},{12,8},{16,20},{20,16},{24,28},{28,24},{1,5},{5... | collective-permute-start | bytes 786440 | tf_op jit(solution)/shard_map/ppermute | solution.py:20
  30.3 12.4 %collective-permute-start.14 = (bf16[1024,128]{1,0:T(8,128)(2,1)S(1)}, bf16[1024,128]{1,0:T(8,128)(2,1)S(1)}, u32[]{:S(2)}, u32[]{:S(2)}) collective-permute-start(bf16[1024,128]{1,0:T(8,128)(2,1)S(1)} %get-tuple-element.44), channel_id=1, source_target_pairs={{0,8},{4,12},{8,0},{12,4},{16,24},{20,28},{24,16},{28,20},{1,9},{5... | collective-permute-start | bytes 786440 | tf_op jit(solution)/shard_map/ppermute | solution.py:20
  31.9 8.2 %collective-permute-start.12 = (f32[128,128]{1,0:T(8,128)S(1)}, f32[128,128]{1,0:T(8,128)S(1)}, u32[]{:S(2)}, u32[]{:S(2)}) collective-permute-start(f32[128,128]{1,0:T(8,128)S(1)} %get-tuple-element.40.refs_3_), channel_id=1, source_target_pairs={{0,8},{4,12},{8,0},{12,4},{16,24},{20,28},{24,16},{28,20},{1,9},{5... | collective-permute-start | bytes 196616 | tf_op jit(solution)/shard_map/ppermute | solution.py:20
  32.4 10.3 %collective-permute-start.11 = (f32[128,128]{1,0:T(8,128)S(1)}, f32[128,128]{1,0:T(8,128)S(1)}, u32[]{:S(2)}, u32[]{:S(2)}) collective-permute-start(f32[128,128]{1,0:T(8,128)S(1)} %get-tuple-element.39.refs_0_), channel_id=1, source_target_pairs={{0,3},{1,2},{2,1},{3,0},{4,7},{5,6},{6,5},{7,4},{8,11},{9,10},{10,... | collective-permute-start | bytes 196616 | tf_op jit(solution)/shard_map/ppermute | solution.py:20
  33.8 9.0 %collective-permute-start.10 = (f32[128,128]{1,0:T(8,128)S(1)}, f32[128,128]{1,0:T(8,128)S(1)}, u32[]{:S(2)}, u32[]{:S(2)}) collective-permute-start(f32[128,128]{1,0:T(8,128)S(1)} %get-tuple-element.39.refs_0_), channel_id=1, source_target_pairs={{0,2},{1,3},{2,0},{3,1},{4,6},{5,7},{6,4},{7,5},{8,10},{9,11},{10,... | collective-permute-start | bytes 196616 | tf_op jit(solution)/shard_map/ppermute | solution.py:20
  34.8 8.0 %collective-permute-start.9 = (f32[128,128]{1,0:T(8,128)S(1)}, f32[128,128]{1,0:T(8,128)S(1)}, u32[]{:S(2)}, u32[]{:S(2)}) collective-permute-start(f32[128,128]{1,0:T(8,128)S(1)} %get-tuple-element.39.refs_0_), channel_id=1, source_target_pairs={{0,1},{1,0},{2,3},{3,2},{4,5},{5,4},{6,7},{7,6},{8,9},{9,8},{10,11... | collective-permute-start | bytes 196616 | tf_op jit(solution)/shard_map/ppermute | solution.py:20
  40.1 16.1 %collective-permute-start.16 = (bf16[128,1024]{1,0:T(8,128)(2,1)S(1)}, bf16[128,1024]{1,0:T(8,128)(2,1)S(1)}, u32[]{:S(2)}, u32[]{:S(2)}) collective-permute-start(bf16[128,1024]{1,0:T(8,128)(2,1)S(1)} %get-tuple-element.32.image_t_ref), channel_id=1, source_target_pairs={{0,16},{4,20},{8,24},{12,28},{16,0},{20,4},{24,8},{28,12},{1,17},{... | collective-permute-start | bytes 786440 | tf_op jit(solution)/shard_map/ppermute | solution.py:20
  42.7 13.5 %collective-permute-start.15 = (bf16[1024,128]{1,0:T(8,128)(2,1)S(1)}, bf16[1024,128]{1,0:T(8,128)(2,1)S(1)}, u32[]{:S(2)}, u32[]{:S(2)}) collective-permute-start(bf16[1024,128]{1,0:T(8,128)(2,1)S(1)} %collective-permute-done.14.came_ref), channel_id=1, source_target_pairs={{0,4},{4,0},{8,12},{12,8},{16,20},{20,16},{24,28},{28,24},{1,5},{5... | collective-permute-start | bytes 786440 | tf_op jit(solution)/shard_map/ppermute | solution.py:20
  42.9 1.5 %collective-permute-start.13 = (f32[128,128]{1,0:T(8,128)S(1)}, f32[128,128]{1,0:T(8,128)S(1)}, u32[]{:S(2)}, u32[]{:S(2)}) collective-permute-start(f32[128,128]{1,0:T(8,128)S(1)} %shard_map.52.refs_0_), channel_id=1, source_target_pairs={{0,4},{4,0},{8,12},{12,8},{16,20},{20,16},{24,28},{28,24},{1,5},{5... | collective-permute-start | bytes 196616 | tf_op jit(solution)/shard_map/ppermute | solution.py:20
  48.5 12.1 %collective-permute-start.20 = (f32[128,128]{1,0:T(8,128)S(1)}, f32[128,128]{1,0:T(8,128)S(1)}, u32[]{:S(2)}, u32[]{:S(2)}) collective-permute-start(f32[128,128]{1,0:T(8,128)S(1)} %get-tuple-element.46), channel_id=1, source_target_pairs={{0,16},{4,20},{8,24},{12,28},{16,0},{20,4},{24,8},{28,12},{1,17},{... | collective-permute-start | bytes 196616 | tf_op jit(solution)/shard_map/ppermute | solution.py:20
  57.0 5.2 %collective-permute-start.19 = (f32[128,128]{1,0:T(8,128)S(1)}, f32[128,128]{1,0:T(8,128)S(1)}, u32[]{:S(2)}, u32[]{:S(2)}) collective-permute-start(f32[128,128]{1,0:T(8,128)S(1)} %get-tuple-element.45.refs_0_), channel_id=1, source_target_pairs={{0,3},{1,2},{2,1},{3,0},{4,7},{5,6},{6,5},{7,4},{8,11},{9,10},{10,... | collective-permute-start | bytes 196616 | tf_op jit(solution)/shard_map/ppermute | solution.py:20
  58.5 4.4 %collective-permute-start.18 = (f32[128,128]{1,0:T(8,128)S(1)}, f32[128,128]{1,0:T(8,128)S(1)}, u32[]{:S(2)}, u32[]{:S(2)}) collective-permute-start(f32[128,128]{1,0:T(8,128)S(1)} %get-tuple-element.45.refs_0_), channel_id=1, source_target_pairs={{0,2},{1,3},{2,0},{3,1},{4,6},{5,7},{6,4},{7,5},{8,10},{9,11},{10,... | collective-permute-start | bytes 196616 | tf_op jit(solution)/shard_map/ppermute | solution.py:20
  59.5 4.3 %collective-permute-start.17 = (f32[128,128]{1,0:T(8,128)S(1)}, f32[128,128]{1,0:T(8,128)S(1)}, u32[]{:S(2)}, u32[]{:S(2)}) collective-permute-start(f32[128,128]{1,0:T(8,128)S(1)} %get-tuple-element.45.refs_0_), channel_id=1, source_target_pairs={{0,1},{1,0},{2,3},{3,2},{4,5},{5,4},{6,7},{7,6},{8,9},{9,8},{10,11... | collective-permute-start | bytes 196616 | tf_op jit(solution)/shard_map/ppermute | solution.py:20
  60.6 7.2 %collective-permute-start.23 = (bf16[512,128]{1,0:T(8,128)(2,1)S(1)}, bf16[512,128]{1,0:T(8,128)(2,1)S(1)}, u32[]{:S(2)}, u32[]{:S(2)}) collective-permute-start(bf16[512,128]{1,0:T(8,128)(2,1)S(1)} %get-tuple-element.49), channel_id=1, source_target_pairs={{0,16},{4,20},{8,24},{12,28},{16,0},{20,4},{24,8},{28,12},{1,17},{... | collective-permute-start | bytes 393224 | tf_op jit(solution)/shard_map/ppermute | solution.py:20
  63.9 3.9 %collective-permute-start.21 = (f32[128,128]{1,0:T(8,128)S(1)}, f32[128,128]{1,0:T(8,128)S(1)}, u32[]{:S(2)}, u32[]{:S(2)}) collective-permute-start(f32[128,128]{1,0:T(8,128)S(1)} %shard_map.55.refs_0_), channel_id=1, source_target_pairs={{0,4},{4,0},{8,12},{12,8},{16,20},{20,16},{24,28},{28,24},{1,5},{5... | collective-permute-start | bytes 196616 | tf_op jit(solution)/shard_map/ppermute | solution.py:20
  67.8 8.8 %collective-permute-start.24 = (bf16[512,128]{1,0:T(8,128)(2,1)S(1)}, bf16[512,128]{1,0:T(8,128)(2,1)S(1)}, u32[]{:S(2)}, u32[]{:S(2)}) collective-permute-start(bf16[512,128]{1,0:T(8,128)(2,1)S(1)} %collective-permute-done.23.came_ref), channel_id=1, source_target_pairs={{0,4},{4,0},{8,12},{12,8},{16,20},{20,16},{24,28},{28,24},{1,5},{5... | collective-permute-start | bytes 393224 | tf_op jit(solution)/shard_map/ppermute | solution.py:20
  67.9 4.6 %collective-permute-start.22 = (f32[128,128]{1,0:T(8,128)S(1)}, f32[128,128]{1,0:T(8,128)S(1)}, u32[]{:S(2)}, u32[]{:S(2)}) collective-permute-start(f32[128,128]{1,0:T(8,128)S(1)} %shard_map.56.refs_0_), channel_id=1, source_target_pairs={{0,8},{4,12},{8,0},{12,4},{16,24},{20,28},{24,16},{28,20},{1,9},{5... | collective-permute-start | bytes 196616 | tf_op jit(solution)/shard_map/ppermute | solution.py:20

commit v7 on v6

--- a/solution.py
+++ b/solution.py
@@ -25,7 +25,7 @@
     parts = [value]
     while done < count:
         if len(parts) > 1:
-            value = run_kernel(add_kernel, jax.ShapeDtypeStruct(value.shape, F32), *parts)
+            value = run_kernel(add_kernel, jax.ShapeDtypeStruct(value.shape, value.dtype), *parts)
         radix = 4 if widest == 4 and count // done % 4 == 0 else 2
         parts = [value]
         for step in range(1, radix):
@@ -35,11 +35,11 @@
 
 
 def add_kernel(*refs):
-    refs[-1][...] = total_of(refs[:-1])
+    refs[-1][...] = total_of(refs[:-1]).astype(refs[-1].dtype)
 
 
 def total_of(parts):
-    values = [part[...] for part in parts]
+    values = [part[...].astype(F32) for part in parts]
     while len(values) > 1:
         values = [a + b for a, b in zip(values[::2], values[1::2])]
     return values[0]
@@ -260,12 +260,16 @@
 
 
 def leaf_kernel(total_rows, count, *refs):
-    parts, (snapshots_ref, factor_ref, modes_ref) = refs[:count], refs[count:]
-    width = snapshots_ref.shape[1]
+    parts, (factor_ref,) = refs[:count], refs[count:]
+    width = factor_ref.shape[1]
     grams = total_of(parts) / total_rows
     factor_ref[width:] = grams[width:]
     inverse = inverse_factor(grams[:width])
     factor_ref[:width] = inverse
+
+
+def leaf_modes_kernel(snapshots_ref, factor_ref, modes_ref):
+    inverse = factor_ref[: factor_ref.shape[1]]
     modes_ref[...] = dot_nt(snapshots_ref[...], inverse.astype(BF16)).astype(BF16)
 
 
@@ -294,12 +298,11 @@
     return jnp.where(odd, second, first), jnp.where(odd, first, second)
 
 
-def write_bulk(refs, modes, image):
-    modes_ref, *image_ref, outgoing_ref = refs
+def write_bulk(refs, modes, image_ref):
+    modes_ref, outgoing_ref = refs
     modes_ref[...] = modes
-    if image_ref:
-        image_ref[0][...] = image
-        outgoing_ref[...] = choose("tm", modes, image)[0]
+    if image_ref is not None:
+        outgoing_ref[...] = choose("tm", modes, image_ref[...])[0]
     else:
         part = outgoing_ref.shape[0]
         outgoing_ref[...] = choose("tm", modes[:part], modes[part:])[0]
@@ -328,14 +331,21 @@
     slices_ref[1] = nn_full(half_other, other).astype(BF16)
 
 
-def first_apply_kernel(
-    halves_ref, slices_ref, modes_own, modes_other, image_own, image_other, far_image_t,
-    probe_ref, *bulk_refs,
-):
+def write_probe(refs, far_image_t, image):
+    refs[0][...] = dot_nn(far_image_t[...], image).astype(BF16)
+    if len(refs) > 1:
+        refs[1][...] = image
+
+
+def first_apply_kernel(slices_ref, image_own, image_other, far_image_t, *refs):
     image = combined(image_own[...], image_other[...], slices_ref[0], slices_ref[1])
-    probe_ref[...] = dot_nn(far_image_t[...], image)
+    write_probe(refs, far_image_t, image)
+
+
+def first_modes_kernel(halves_ref, modes_own, modes_other, *refs):
+    *image_ref, modes_ref, outgoing_ref = refs
     modes = combined(modes_own[...], modes_other[...], halves_ref[0], halves_ref[1])
-    write_bulk(bulk_refs, modes, image)
+    write_bulk((modes_ref, outgoing_ref), modes, image_ref[0] if image_ref else None)
 
 
 def merge_kernel(count, *refs):
@@ -361,14 +371,17 @@
         copy.wait()
 
 
-def apply_kernel(
-    halves_ref, modes_own, image_own, came_ref, shared_ref, far_image_t, probe_ref, *bulk_refs
-):
-    modes_other, image_other = choose("tm", came_ref[...], shared_ref[...])
+def apply_kernel(halves_ref, image_own, came_ref, shared_ref, far_image_t, *refs):
+    image_other = choose("tm", came_ref[...], shared_ref[...])[1]
     image = combined(image_own[...], image_other, halves_ref[0], halves_ref[1])
-    probe_ref[...] = dot_nn(far_image_t[...], image)
+    write_probe(refs, far_image_t, image)
+
+
+def modes_kernel(halves_ref, modes_own, came_ref, shared_ref, *refs):
+    *image_ref, modes_ref, outgoing_ref = refs
+    modes_other = choose("tm", came_ref[...], shared_ref[...])[0]
     modes = combined(modes_own[...], modes_other, halves_ref[0], halves_ref[1])
-    write_bulk(bulk_refs, modes, image)
+    write_bulk((modes_ref, outgoing_ref), modes, image_ref[0] if image_ref else None)
 
 
 def output_kernel(halves_ref, modes_own, came_ref, shared_ref, _, out_ref, modes_ref, sems):
@@ -424,7 +437,7 @@
 
 def cross_kernel(total_rows, count, *refs):
     parts, (far_ref, out_ref) = refs[:count], refs[count:]
-    out_ref[...] = nn_full(far_ref[...], total_of(parts) / total_rows)
+    out_ref[...] = nn_full(far_ref[...], total_of(parts) / total_rows).astype(BF16)
 
 
 def modes_of(snapshots, energy, neighbours, sketch):
@@ -444,6 +457,7 @@
     modes_shape = jax.ShapeDtypeStruct((rows_dev, width), BF16)
     half_shape = jax.ShapeDtypeStruct((rows_dev // 2, width), BF16)
     factor_shape = jax.ShapeDtypeStruct((width + width // 2, width), F32)
+    half_square = jax.ShapeDtypeStruct((width, width), BF16)
     halves_shape = jax.ShapeDtypeStruct((2, width, width), BF16)
 
     inner, sketch_t, edges, blocks = interior_of(neighbours, energy, blocks, sketch)
@@ -455,49 +469,64 @@
     )
     parts = summands(pair, "space", space, 4)
     far_images = [swap(image_t, "tm", 2**level) for level in range(1, levels)]
-    factor, modes = run_kernel(
-        functools.partial(leaf_kernel, total_rows, len(parts)),
-        [factor_shape, modes_shape],
-        *parts, blocks.reshape(rows_dev, width),
+    factor = run_kernel(
+        functools.partial(leaf_kernel, total_rows, len(parts)), factor_shape, *parts
     )
     other_factor = swap(factor, "tm", 1)
+    modes = run_kernel(
+        leaf_modes_kernel, modes_shape, blocks.reshape(rows_dev, width), factor
+    )
     other = swap(modes, "tm", 1)
     kept = [modes]
     for level in range(levels):
+        last = level + 1 == levels
         deep = level + 2 < levels
-        outs = [square, square, modes_shape] + ([modes_shape] * 2 if deep else [half_shape])
+        probe_outs = [half_square] + ([modes_shape] if deep else [])
+        modes_outs = [modes_shape, modes_shape if deep else half_shape]
+        if level > 0:
+            far_mine = swap(mine, "tm", 2**level)
+            parts = summands(probe, "space", space, 4)
+            came = swap(outgoing, "tm", 2**level)
+            shared = swap(came, "tm", 1)
+            cross = run_kernel(
+                functools.partial(cross_kernel, total_rows, len(parts)),
+                half_square, *parts, far_mine,
+            )
+            parts = summands(cross, "tm", 2**level, 2)
         if level == 0:
             halves, mine, slices = run_kernel(
                 first_merge_kernel, [halves_shape, square, halves_shape],
                 factor, other_factor, sketch_t[level],
             )
-            probe, *bulk = run_kernel(
-                first_apply_kernel, outs[1:],
-                halves, slices, modes, other, image, other_image, far_images[level],
-            )
+        elif last:
+            halves, out = last_level(parts, sketch_t[level], kept, halves_shape)
         else:
-            far_mine = swap(mine, "tm", 2**level)
-            parts = summands(probe, "space", space, 4)
-            came = swap(bulk[-1], "tm", 2**level)
-            shared = swap(came, "tm", 1)
-            cross = run_kernel(
-                functools.partial(cross_kernel, total_rows, len(parts)),
-                square, *parts, far_mine,
-            )
-            parts = summands(cross, "tm", 2**level, 2)
-            if level + 1 < levels:
-                halves, mine = run_kernel(
-                    functools.partial(merge_kernel, len(parts)), [halves_shape, square],
-                    *parts, sketch_t[level], mine,
-                )
-                probe, *bulk = run_kernel(
-                    apply_kernel, outs[1:],
-                    halves, *bulk[:2], came, shared, far_images[level],
-                )
-            else:
-                halves, out = last_level(parts, sketch_t[level], kept, halves_shape)
-                out = last_modes(halves, bulk[0], came, shared, out)
-        kept.append(bulk[0])
+            halves, mine = run_kernel(
+                functools.partial(merge_kernel, len(parts)), [halves_shape, square],
+                *parts, sketch_t[level], mine,
+            )
+        if last:
+            out = last_modes(halves, modes, came, shared, out)
+            break
+        if level == 0:
+            probe, *image = run_kernel(
+                first_apply_kernel, probe_outs,
+                slices, image, other_image, far_images[level],
+            )
+        else:
+            probe, *image = run_kernel(
+                apply_kernel, probe_outs,
+                halves, image[0], came, shared, far_images[level],
+            )
+        if level == 0:
+            modes, outgoing = run_kernel(
+                first_modes_kernel, modes_outs, halves, modes, other, *image
+            )
+        else:
+            modes, outgoing = run_kernel(
+                modes_kernel, modes_outs, halves, modes, came, shared, *image
+            )
+        kept.append(modes)
     return out[:, None]
 
 

time: 78 us -> 70.9 us (0.909)
  waiting for transfers between devices: 30.9 us -> 20 us
  starting transfers between devices: 23.1 us -> 26.9 us
    ppermute x23, waiting for transfers between devices: 29.1 us -> 18.3 us  [swap(): return lax.ppermute(value, axis, pairs)]
    ppermute x23, starting transfers between devices: 18.6 us -> 22.4 us  [swap(): return lax.ppermute(value, axis, pairs)]
    pallas_call x9 -> x12, Pallas kernels: 14.1 us -> 14.1 us  [run_kernel(): pl.pallas_call(body, out_shape=outs, cost_estimate=cost, compiler_params=...]
  transfers between devices with their start and end apart: 25 -> 25, of which waited for: 14 -> 15; matrix products, arithmetic and copies ran while one was open for 0% -> 0% of each run, Pallas kernels for 25% -> 28%
where the time goes in v7:
time: 70.9 us; the launch traced here: 70.7 us
  starting transfers between devices  26.9 us (38%)
  Pallas kernels  22.6 us (32%)
  waiting for transfers between devices  20 us (28%)
  other arithmetic  0.9 us (1%)
    ppermute x23, starting transfers between devices, swap(): return lax.ppermute(value, axis, pairs)  22.4 us
    ppermute x23, waiting for transfers between devices, swap(): return lax.ppermute(value, axis, pairs)  18.3 us
    pallas_call x12, Pallas kernels, run_kernel(): pl.pallas_call(body, out_shape=outs, cost_estimate=cost, compiler_params=...  14.1 us
    pallas_call x1, Pallas kernels, last_level(): pl.pallas_call(functools.partial(last_merge_kernel, len(parts)), out_shap...  4.24 us
    ppermute x1, starting transfers between devices, modes_of(): came_near = lax.ppermute(jnp.where(odd, head, tail), 'space', near)  3.03 us
    pallas_call x1, Pallas kernels, interior_of(): pl.pallas_call(interior_kernel, out_shape=[jax.ShapeDtypeStruct((inner, r...  1.89 us
    ppermute x1, waiting for transfers between devices, modes_of(): came_wide = lax.ppermute(jnp.where(odd, tail, head), 'space', wide)  1.77 us
    ppermute x1, starting transfers between devices, modes_of(): came_wide = lax.ppermute(jnp.where(odd, tail, head), 'space', wide)  1.49 us
  transfers between devices with their start and end apart: 25, of which 15 were waited for; matrix products, arithmetic and copies ran while one was open for 0% of the time, Pallas kernels for 28%

profile of v7, /device:TPU:0, one launch (start us, length us, event | category | flops | bytes accessed | tf_op | source)
XLA Modules:
  0.0 70.7 jit_solution(2124000554939507824)
XLA Ops:
  0.9 3.0 %collective-permute-start = (bf16[2,128,128]{2,1,0:T(8,128)(2,1)S(1)}, bf16[2,128,128]{2,1,0:T(8,128)(2,1)S(1)}, u32[]{:S(2)}, u32[]{:S(2)}) collective-permute-start(bf16[2,128,128]{2,1,0:T(8,128)(2,1)S(1)} %bitcast.19), channel_id=1, source_target_pairs={{0,1},{1,0},{2,3},{3,2},{4,5},{5,4},{6,7},{7,6},{8,9},{9,8},{10,11... | collective-permute-start | bytes 196616 | tf_op jit(solution)/shard_map/ppermute | solution.py:454
  3.9 1.5 %collective-permute-start.1 = (bf16[2,128,128]{2,1,0:T(8,128)(2,1)S(1)}, bf16[2,128,128]{2,1,0:T(8,128)(2,1)S(1)}, u32[]{:S(2)}, u32[]{:S(2)}) collective-permute-start(bf16[2,128,128]{2,1,0:T(8,128)(2,1)S(1)} %bitcast.18), channel_id=1, source_target_pairs={{0,3},{1,2},{2,1},{3,0},{4,7},{5,6},{6,5},{7,4},{8,11},{9,10},{10,... | collective-permute-start | bytes 196616 | tf_op jit(solution)/shard_map/ppermute | solution.py:455
  5.4 1.9 %shard_map.46 = (bf16[4,128,128]{2,1,0:T(8,128)(2,1)S(1)}, f32[3,2,128,128]{3,2,1,0:T(8,128)S(1)}, bf16[2,2,7,128,128]{4,3,2,1,0:T(8,128)(2,1)S(1)}, bf16[8,128,128]{2,1,0:T(8,128)(2,1)S(1)}) custom-call(s32[8,7]{1,0:T(8,128)} %index_ref.1, bf16[8,7,128,128]{3,2,1,0:T(8,128)(2,1)} %energy_hbm.1, bf16[8,128,128]{2,1,0:T(8,128)(2,1)} %bitcast.17, ...), custom_call_target="tpu_custom_call" | custom-call | tf_op jit(solution)/shard_map/pallas_call | solution.py:218
  7.3 1.8 %collective-permute-done.1.wide_ref = bf16[2,128,128]{2,1,0:T(8,128)(2,1)S(1)} collective-permute-done((bf16[2,128,128]{2,1,0:T(8,128)(2,1)S(1)}, bf16[2,128,128]{2,1,0:T(8,128)(2,1)S(1)}, u32[]{:S(2)}, u32[]{:S(2)}) %collective-permute-start.1) | collective-permute-done | bytes 65568 | tf_op jit(solution)/shard_map/ppermute | solution.py:455
  9.1 1.3 %shard_map.47 = (bf16[8,128,128]{2,1,0:T(8,128)(2,1)S(1)}, bf16[128,1024]{1,0:T(8,128)(2,1)S(1)}, f32[128,128]{1,0:T(8,128)S(1)}) custom-call(s32[8,7]{1,0:T(8,128)S(1)} %copy-done, bf16[2,2,7,128,128]{4,3,2,1,0:T(8,128)(2,1)S(1)} %get-tuple-element.25.edges_ref, bf16[2,128,128]{2,1,0:T(8,128)(2,1)S(1)} %collective-permute-done.near_ref, ...), custom_call_target="tpu_custom_call" | custom-call | tf_op jit(solution)/shard_map/pallas_call | solution.py:239
  10.5 1.5 %collective-permute-done.2.other_ref.image_other = bf16[1024,128]{1,0:T(8,128)(2,1)S(1)} collective-permute-done((bf16[1024,128]{1,0:T(8,128)(2,1)S(1)}, bf16[1024,128]{1,0:T(8,128)(2,1)S(1)}, u32[]{:S(2)}, u32[]{:S(2)}) %collective-permute-start.2) | collective-permute-done | bytes 262176 | tf_op jit(solution)/shard_map/ppermute | solution.py:20
  12.3 1.6 %collective-permute-start.5 = (f32[192,128]{1,0:T(8,128)S(1)}, f32[192,128]{1,0:T(8,128)S(1)}, u32[]{:S(2)}, u32[]{:S(2)}) collective-permute-start(f32[192,128]{1,0:T(8,128)S(1)} %shard_map.48.refs_0_), channel_id=1, source_target_pairs={{0,3},{1,2},{2,1},{3,0},{4,7},{5,6},{6,5},{7,4},{8,11},{9,10},{10,... | collective-permute-start | bytes 294920 | tf_op jit(solution)/shard_map/ppermute | solution.py:20
  15.9 1.6 %collective-permute-start.7 = (bf16[128,1024]{1,0:T(8,128)(2,1)S(1)}, bf16[128,1024]{1,0:T(8,128)(2,1)S(1)}, u32[]{:S(2)}, u32[]{:S(2)}) collective-permute-start(bf16[128,1024]{1,0:T(8,128)(2,1)S(1)} %get-tuple-element.29.image_t_ref), channel_id=1, source_target_pairs={{0,8},{4,12},{8,0},{12,4},{16,24},{20,28},{24,16},{28,20},{1,9},{5... | collective-permute-start | bytes 786440 | tf_op jit(solution)/shard_map/ppermute | solution.py:20
  17.5 1.2 %collective-permute-done.5.refs_3_ = f32[192,128]{1,0:T(8,128)S(1)} collective-permute-done((f32[192,128]{1,0:T(8,128)S(1)}, f32[192,128]{1,0:T(8,128)S(1)}, u32[]{:S(2)}, u32[]{:S(2)}) %collective-permute-start.5) | collective-permute-done | bytes 98336 | tf_op jit(solution)/shard_map/ppermute | solution.py:20
  18.7 1.5 %collective-permute-done.4.refs_2_ = f32[192,128]{1,0:T(8,128)S(1)} collective-permute-done((f32[192,128]{1,0:T(8,128)S(1)}, f32[192,128]{1,0:T(8,128)S(1)}, u32[]{:S(2)}, u32[]{:S(2)}) %collective-permute-start.4) | collective-permute-done | bytes 98336 | tf_op jit(solution)/shard_map/ppermute | solution.py:20
  20.3 3.1 %shard_map.49.own_ref.factor_ref = f32[192,128]{1,0:T(8,128)S(1)} custom-call(f32[192,128]{1,0:T(8,128)S(1)} %shard_map.48.refs_0_, f32[192,128]{1,0:T(8,128)S(1)} %collective-permute-done.3.refs_1_, f32[192,128]{1,0:T(8,128)S(1)} %collective-permute-done.4.refs_2_, f32[192,128]{1,0:T(8,128)S(1)} %collective-permute-done.5.refs_3_), custom_call_target="tpu_custom_call" | custom-call | flops 2000000000 | bytes 1000000 | tf_op jit(solution)/shard_map/pallas_call | solution.py:133
  24.8 4.4 %shard_map.50 = (bf16[2,128,128]{2,1,0:T(8,128)(2,1)S(1)}, f32[128,128]{1,0:T(8,128)S(1)}, bf16[2,128,128]{2,1,0:T(8,128)(2,1)S(1)}) custom-call(f32[192,128]{1,0:T(8,128)S(1)} %shard_map.49.own_ref.factor_ref, f32[192,128]{1,0:T(8,128)S(1)} %collective-permute-done.6.other_ref, f32[2,128,128]{2,1,0:T(8,128)S(1)} %get-tuple-element.47.sketch_ref), custom_call_target="tpu_custom_call" | custom-call | flops 2000000000 | bytes 1000000 | tf_op jit(solution)/shard_map/pallas_call | solution.py:133
  30.0 1.6 %collective-permute-start.14 = (bf16[1024,128]{1,0:T(8,128)(2,1)S(1)}, bf16[1024,128]{1,0:T(8,128)(2,1)S(1)}, u32[]{:S(2)}, u32[]{:S(2)}) collective-permute-start(bf16[1024,128]{1,0:T(8,128)(2,1)S(1)} %get-tuple-element.38), channel_id=1, source_target_pairs={{0,8},{4,12},{8,0},{12,4},{16,24},{20,28},{24,16},{28,20},{1,9},{5... | collective-permute-start | bytes 786440 | tf_op jit(solution)/shard_map/ppermute | solution.py:20
  32.1 1.4 %collective-permute-start.10 = (bf16[128,128]{1,0:T(8,128)(2,1)S(1)}, bf16[128,128]{1,0:T(8,128)(2,1)S(1)}, u32[]{:S(2)}, u32[]{:S(2)}) collective-permute-start(bf16[128,128]{1,0:T(8,128)(2,1)S(1)} %get-tuple-element.33.refs_0_), channel_id=1, source_target_pairs={{0,3},{1,2},{2,1},{3,0},{4,7},{5,6},{6,5},{7,4},{8,11},{9,10},{10,... | collective-permute-start | bytes 98312 | tf_op jit(solution)/shard_map/ppermute | solution.py:20
  34.5 1.1 %collective-permute-start.8 = (bf16[128,128]{1,0:T(8,128)(2,1)S(1)}, bf16[128,128]{1,0:T(8,128)(2,1)S(1)}, u32[]{:S(2)}, u32[]{:S(2)}) collective-permute-start(bf16[128,128]{1,0:T(8,128)(2,1)S(1)} %get-tuple-element.33.refs_0_), channel_id=1, source_target_pairs={{0,1},{1,0},{2,3},{3,2},{4,5},{5,4},{6,7},{7,6},{8,9},{9,8},{10,11... | collective-permute-start | bytes 98312 | tf_op jit(solution)/shard_map/ppermute | solution.py:20
  35.6 1.7 %collective-permute-done.10.refs_3_ = bf16[128,128]{1,0:T(8,128)(2,1)S(1)} collective-permute-done((bf16[128,128]{1,0:T(8,128)(2,1)S(1)}, bf16[128,128]{1,0:T(8,128)(2,1)S(1)}, u32[]{:S(2)}, u32[]{:S(2)}) %collective-permute-start.10) | collective-permute-done | bytes 32800 | tf_op jit(solution)/shard_map/ppermute | solution.py:20
  37.2 2.6 %collective-permute-start.16 = (bf16[128,1024]{1,0:T(8,128)(2,1)S(1)}, bf16[128,1024]{1,0:T(8,128)(2,1)S(1)}, u32[]{:S(2)}, u32[]{:S(2)}) collective-permute-start(bf16[128,1024]{1,0:T(8,128)(2,1)S(1)} %get-tuple-element.29.image_t_ref), channel_id=1, source_target_pairs={{0,16},{4,20},{8,24},{12,28},{16,0},{20,4},{24,8},{28,12},{1,17},{... | collective-permute-start | bytes 786440 | tf_op jit(solution)/shard_map/ppermute | solution.py:20
  39.9 1.7 %collective-permute-done.14.came_ref = bf16[1024,128]{1,0:T(8,128)(2,1)S(1)} collective-permute-done((bf16[1024,128]{1,0:T(8,128)(2,1)S(1)}, bf16[1024,128]{1,0:T(8,128)(2,1)S(1)}, u32[]{:S(2)}, u32[]{:S(2)}) %collective-permute-start.14) | collective-permute-done | bytes 262176 | tf_op jit(solution)/shard_map/ppermute | solution.py:20
  41.5 1.4 %collective-permute-done.11.refs_4_ = f32[128,128]{1,0:T(8,128)S(1)} collective-permute-done((f32[128,128]{1,0:T(8,128)S(1)}, f32[128,128]{1,0:T(8,128)S(1)}, u32[]{:S(2)}, u32[]{:S(2)}) %collective-permute-start.11) | collective-permute-done | bytes 65568 | tf_op jit(solution)/shard_map/ppermute | solution.py:20
  43.2 1.2 %collective-permute-done.12.refs_1_ = bf16[128,128]{1,0:T(8,128)(2,1)S(1)} collective-permute-done((bf16[128,128]{1,0:T(8,128)(2,1)S(1)}, bf16[128,128]{1,0:T(8,128)(2,1)S(1)}, u32[]{:S(2)}, u32[]{:S(2)}) %collective-permute-start.12) | collective-permute-done | bytes 32800 | tf_op jit(solution)/shard_map/ppermute | solution.py:20
  44.4 4.1 %shard_map.53 = (bf16[2,128,128]{2,1,0:T(8,128)(2,1)S(1)}, f32[128,128]{1,0:T(8,128)S(1)}) custom-call(bf16[128,128]{1,0:T(8,128)(2,1)S(1)} %shard_map.52.refs_0_, bf16[128,128]{1,0:T(8,128)(2,1)S(1)} %collective-permute-done.12.refs_1_, f32[2,128,128]{2,1,0:T(8,128)S(1)} %get-tuple-element.46.refs_2_, f32[128,128]{1,0:T(8,128)S(1)} %get-tuple-element.34.refs_3_), custom_call_target="tpu_custom_call" | custom-call | flops 2000000000 | bytes 1000000 | tf_op jit(solution)/shard_map/pallas_call | solution.py:133
  48.9 1.2 %collective-permute-done.16.far_image_t = bf16[128,1024]{1,0:T(8,128)(2,1)S(1)} collective-permute-done((bf16[128,1024]{1,0:T(8,128)(2,1)S(1)}, bf16[128,1024]{1,0:T(8,128)(2,1)S(1)}, u32[]{:S(2)}, u32[]{:S(2)}) %collective-permute-start.16) | collective-permute-done | bytes 262176 | tf_op jit(solution)/shard_map/ppermute | solution.py:20
  50.7 1.4 %collective-permute-start.19 = (bf16[128,128]{1,0:T(8,128)(2,1)S(1)}, bf16[128,128]{1,0:T(8,128)(2,1)S(1)}, u32[]{:S(2)}, u32[]{:S(2)}) collective-permute-start(bf16[128,128]{1,0:T(8,128)(2,1)S(1)} %shard_map.56.refs_0_), channel_id=1, source_target_pairs={{0,3},{1,2},{2,1},{3,0},{4,7},{5,6},{6,5},{7,4},{8,11},{9,10},{10,... | collective-permute-start | bytes 98312 | tf_op jit(solution)/shard_map/ppermute | solution.py:20
  52.1 1.0 %collective-permute-start.18 = (bf16[128,128]{1,0:T(8,128)(2,1)S(1)}, bf16[128,128]{1,0:T(8,128)(2,1)S(1)}, u32[]{:S(2)}, u32[]{:S(2)}) collective-permute-start(bf16[128,128]{1,0:T(8,128)(2,1)S(1)} %shard_map.56.refs_0_), channel_id=1, source_target_pairs={{0,2},{1,3},{2,0},{3,1},{4,6},{5,7},{6,4},{7,5},{8,10},{9,11},{10,... | collective-permute-start | bytes 98312 | tf_op jit(solution)/shard_map/ppermute | solution.py:20
  53.1 1.1 %collective-permute-start.17 = (bf16[128,128]{1,0:T(8,128)(2,1)S(1)}, bf16[128,128]{1,0:T(8,128)(2,1)S(1)}, u32[]{:S(2)}, u32[]{:S(2)}) collective-permute-start(bf16[128,128]{1,0:T(8,128)(2,1)S(1)} %shard_map.56.refs_0_), channel_id=1, source_target_pairs={{0,1},{1,0},{2,3},{3,2},{4,5},{5,4},{6,7},{7,6},{8,9},{9,8},{10,11... | collective-permute-start | bytes 98312 | tf_op jit(solution)/shard_map/ppermute | solution.py:20
  54.6 1.4 %collective-permute-start.23 = (bf16[512,128]{1,0:T(8,128)(2,1)S(1)}, bf16[512,128]{1,0:T(8,128)(2,1)S(1)}, u32[]{:S(2)}, u32[]{:S(2)}) collective-permute-start(bf16[512,128]{1,0:T(8,128)(2,1)S(1)} %get-tuple-element.43), channel_id=1, source_target_pairs={{0,16},{4,20},{8,24},{12,28},{16,0},{20,4},{24,8},{28,12},{1,17},{... | collective-permute-start | bytes 393224 | tf_op jit(solution)/shard_map/ppermute | solution.py:20
  56.1 1.0 %collective-permute-done.17.refs_1_ = bf16[128,128]{1,0:T(8,128)(2,1)S(1)} collective-permute-done((bf16[128,128]{1,0:T(8,128)(2,1)S(1)}, bf16[128,128]{1,0:T(8,128)(2,1)S(1)}, u32[]{:S(2)}, u32[]{:S(2)}) %collective-permute-start.17) | collective-permute-done | bytes 32800 | tf_op jit(solution)/shard_map/ppermute | solution.py:20
  57.3 3.2 %collective-permute-done.23.came_ref = bf16[512,128]{1,0:T(8,128)(2,1)S(1)} collective-permute-done((bf16[512,128]{1,0:T(8,128)(2,1)S(1)}, bf16[512,128]{1,0:T(8,128)(2,1)S(1)}, u32[]{:S(2)}, u32[]{:S(2)}) %collective-permute-start.23) | collective-permute-done | bytes 131104 | tf_op jit(solution)/shard_map/ppermute | solution.py:20
  60.5 2.7 %collective-permute-start.22 = (bf16[128,128]{1,0:T(8,128)(2,1)S(1)}, bf16[128,128]{1,0:T(8,128)(2,1)S(1)}, u32[]{:S(2)}, u32[]{:S(2)}) collective-permute-start(bf16[128,128]{1,0:T(8,128)(2,1)S(1)} %shard_map.58.refs_0_), channel_id=1, source_target_pairs={{0,8},{4,12},{8,0},{12,4},{16,24},{20,28},{24,16},{28,20},{1,9},{5... | collective-permute-start | bytes 98312 | tf_op jit(solution)/shard_map/ppermute | solution.py:20
  63.3 2.1 %collective-permute-done.22.refs_1_ = bf16[128,128]{1,0:T(8,128)(2,1)S(1)} collective-permute-done((bf16[128,128]{1,0:T(8,128)(2,1)S(1)}, bf16[128,128]{1,0:T(8,128)(2,1)S(1)}, u32[]{:S(2)}, u32[]{:S(2)}) %collective-permute-start.22) | collective-permute-done | bytes 32800 | tf_op jit(solution)/shard_map/ppermute | solution.py:20
  65.3 4.2 %shard_map.60 = (bf16[2,128,128]{2,1,0:T(8,128)(2,1)S(1)}, bf16[4,1024,128]{2,1,0:T(8,128)(2,1)}) custom-call(bf16[128,128]{1,0:T(8,128)(2,1)S(1)} %shard_map.58.refs_0_, bf16[128,128]{1,0:T(8,128)(2,1)S(1)} %collective-permute-done.22.refs_1_, f32[2,128,128]{2,1,0:T(8,128)S(1)} %get-tuple-element.45.refs_2_, ...), custom_call_target="tpu_custom_call" | custom-call | tf_op jit(solution)/shard_map/pallas_call | solution.py:414
  69.6 1.0 %shard_map.61 = bf16[4,1024,128]{2,1,0:T(8,128)(2,1)} custom-call(bf16[2,128,128]{2,1,0:T(8,128)(2,1)S(1)} %get-tuple-element.42.halves_ref, bf16[1024,128]{1,0:T(8,128)(2,1)S(1)} %get-tuple-element.41.refs_5_.modes_own, bf16[512,128]{1,0:T(8,128)(2,1)S(1)} %collective-permute-done.23.came_ref, ...), custom_call_target="tpu_custom_call", output_to_operand_aliasing={{}: (4, {})} | custom-call | tf_op jit(solution)/shard_map/pallas_call | solution.py:427
  (38 shorter events, 8.9 us)
Async XLA Ops:
  0.0 9.1 %copy-start = (s32[8,7]{1,0:T(8,128)S(1)}, s32[8,7]{1,0:T(8,128)}, u32[]{:S(2)}) copy-start(s32[8,7]{1,0:T(8,128)} %index_ref.1) | copy-start | bytes 676
  0.9 6.4 %collective-permute-start = (bf16[2,128,128]{2,1,0:T(8,128)(2,1)S(1)}, bf16[2,128,128]{2,1,0:T(8,128)(2,1)S(1)}, u32[]{:S(2)}, u32[]{:S(2)}) collective-permute-start(bf16[2,128,128]{2,1,0:T(8,128)(2,1)S(1)} %bitcast.19), channel_id=1, source_target_pairs={{0,1},{1,0},{2,3},{3,2},{4,5},{5,4},{6,7},{7,6},{8,9},{9,8},{10,11... | collective-permute-start | bytes 196616 | tf_op jit(solution)/shard_map/ppermute | solution.py:454
  3.9 5.2 %collective-permute-start.1 = (bf16[2,128,128]{2,1,0:T(8,128)(2,1)S(1)}, bf16[2,128,128]{2,1,0:T(8,128)(2,1)S(1)}, u32[]{:S(2)}, u32[]{:S(2)}) collective-permute-start(bf16[2,128,128]{2,1,0:T(8,128)(2,1)S(1)} %bitcast.18), channel_id=1, source_target_pairs={{0,3},{1,2},{2,1},{3,0},{4,7},{5,6},{6,5},{7,4},{8,11},{9,10},{10,... | collective-permute-start | bytes 196616 | tf_op jit(solution)/shard_map/ppermute | solution.py:455
  10.4 1.6 %collective-permute-start.2 = (bf16[1024,128]{1,0:T(8,128)(2,1)S(1)}, bf16[1024,128]{1,0:T(8,128)(2,1)S(1)}, u32[]{:S(2)}, u32[]{:S(2)}) collective-permute-start(bf16[1024,128]{1,0:T(8,128)(2,1)S(1)} %bitcast.15), channel_id=1, source_target_pairs={{0,4},{4,0},{8,12},{12,8},{16,20},{20,16},{24,28},{28,24},{1,5},{5... | collective-permute-start | bytes 786440 | tf_op jit(solution)/shard_map/ppermute | solution.py:20
  12.3 6.4 %collective-permute-start.5 = (f32[192,128]{1,0:T(8,128)S(1)}, f32[192,128]{1,0:T(8,128)S(1)}, u32[]{:S(2)}, u32[]{:S(2)}) collective-permute-start(f32[192,128]{1,0:T(8,128)S(1)} %shard_map.48.refs_0_), channel_id=1, source_target_pairs={{0,3},{1,2},{2,1},{3,0},{4,7},{5,6},{6,5},{7,4},{8,11},{9,10},{10,... | collective-permute-start | bytes 294920 | tf_op jit(solution)/shard_map/ppermute | solution.py:20
  13.8 6.4 %collective-permute-start.4 = (f32[192,128]{1,0:T(8,128)S(1)}, f32[192,128]{1,0:T(8,128)S(1)}, u32[]{:S(2)}, u32[]{:S(2)}) collective-permute-start(f32[192,128]{1,0:T(8,128)S(1)} %shard_map.48.refs_0_), channel_id=1, source_target_pairs={{0,2},{1,3},{2,0},{3,1},{4,6},{5,7},{6,4},{7,5},{8,10},{9,11},{10,... | collective-permute-start | bytes 294920 | tf_op jit(solution)/shard_map/ppermute | solution.py:20
  14.8 5.5 %collective-permute-start.3 = (f32[192,128]{1,0:T(8,128)S(1)}, f32[192,128]{1,0:T(8,128)S(1)}, u32[]{:S(2)}, u32[]{:S(2)}) collective-permute-start(f32[192,128]{1,0:T(8,128)S(1)} %shard_map.48.refs_0_), channel_id=1, source_target_pairs={{0,1},{1,0},{2,3},{3,2},{4,5},{5,4},{6,7},{7,6},{8,9},{9,8},{10,11... | collective-permute-start | bytes 294920 | tf_op jit(solution)/shard_map/ppermute | solution.py:20
  15.9 13.3 %collective-permute-start.7 = (bf16[128,1024]{1,0:T(8,128)(2,1)S(1)}, bf16[128,1024]{1,0:T(8,128)(2,1)S(1)}, u32[]{:S(2)}, u32[]{:S(2)}) collective-permute-start(bf16[128,1024]{1,0:T(8,128)(2,1)S(1)} %get-tuple-element.29.image_t_ref), channel_id=1, source_target_pairs={{0,8},{4,12},{8,0},{12,4},{16,24},{20,28},{24,16},{28,20},{1,9},{5... | collective-permute-start | bytes 786440 | tf_op jit(solution)/shard_map/ppermute | solution.py:20
  23.4 1.4 %collective-permute-start.6 = (f32[192,128]{1,0:T(8,128)S(1)}, f32[192,128]{1,0:T(8,128)S(1)}, u32[]{:S(2)}, u32[]{:S(2)}) collective-permute-start(f32[192,128]{1,0:T(8,128)S(1)} %shard_map.49.own_ref.factor_ref), channel_id=1, source_target_pairs={{0,4},{4,0},{8,12},{12,8},{16,20},{20,16},{24,28},{28,24},{1,5},{5... | collective-permute-start | bytes 294920 | tf_op jit(solution)/shard_map/ppermute | solution.py:20
  23.7 6.0 %collective-permute-start.13 = (bf16[1024,128]{1,0:T(8,128)(2,1)S(1)}, bf16[1024,128]{1,0:T(8,128)(2,1)S(1)}, u32[]{:S(2)}, u32[]{:S(2)}) collective-permute-start(bf16[1024,128]{1,0:T(8,128)(2,1)S(1)} %shard_map.54.modes_own.refs_3_), channel_id=1, source_target_pairs={{0,4},{4,0},{8,12},{12,8},{16,20},{20,16},{24,28},{28,24},{1,5},{5... | collective-permute-start | bytes 786440 | tf_op jit(solution)/shard_map/ppermute | solution.py:20
  30.0 11.5 %collective-permute-start.14 = (bf16[1024,128]{1,0:T(8,128)(2,1)S(1)}, bf16[1024,128]{1,0:T(8,128)(2,1)S(1)}, u32[]{:S(2)}, u32[]{:S(2)}) collective-permute-start(bf16[1024,128]{1,0:T(8,128)(2,1)S(1)} %get-tuple-element.38), channel_id=1, source_target_pairs={{0,8},{4,12},{8,0},{12,4},{16,24},{20,28},{24,16},{28,20},{1,9},{5... | collective-permute-start | bytes 786440 | tf_op jit(solution)/shard_map/ppermute | solution.py:20
  31.7 11.3 %collective-permute-start.11 = (f32[128,128]{1,0:T(8,128)S(1)}, f32[128,128]{1,0:T(8,128)S(1)}, u32[]{:S(2)}, u32[]{:S(2)}) collective-permute-start(f32[128,128]{1,0:T(8,128)S(1)} %get-tuple-element.34.refs_3_), channel_id=1, source_target_pairs={{0,8},{4,12},{8,0},{12,4},{16,24},{20,28},{24,16},{28,20},{1,9},{5... | collective-permute-start | bytes 196616 | tf_op jit(solution)/shard_map/ppermute | solution.py:20
  32.1 5.1 %collective-permute-start.10 = (bf16[128,128]{1,0:T(8,128)(2,1)S(1)}, bf16[128,128]{1,0:T(8,128)(2,1)S(1)}, u32[]{:S(2)}, u32[]{:S(2)}) collective-permute-start(bf16[128,128]{1,0:T(8,128)(2,1)S(1)} %get-tuple-element.33.refs_0_), channel_id=1, source_target_pairs={{0,3},{1,2},{2,1},{3,0},{4,7},{5,6},{6,5},{7,4},{8,11},{9,10},{10,... | collective-permute-start | bytes 98312 | tf_op jit(solution)/shard_map/ppermute | solution.py:20
  33.5 8.0 %collective-permute-start.9 = (bf16[128,128]{1,0:T(8,128)(2,1)S(1)}, bf16[128,128]{1,0:T(8,128)(2,1)S(1)}, u32[]{:S(2)}, u32[]{:S(2)}) collective-permute-start(bf16[128,128]{1,0:T(8,128)(2,1)S(1)} %get-tuple-element.33.refs_0_), channel_id=1, source_target_pairs={{0,2},{1,3},{2,0},{3,1},{4,6},{5,7},{6,4},{7,5},{8,10},{9,11},{10,... | collective-permute-start | bytes 98312 | tf_op jit(solution)/shard_map/ppermute | solution.py:20
  34.5 7.0 %collective-permute-start.8 = (bf16[128,128]{1,0:T(8,128)(2,1)S(1)}, bf16[128,128]{1,0:T(8,128)(2,1)S(1)}, u32[]{:S(2)}, u32[]{:S(2)}) collective-permute-start(bf16[128,128]{1,0:T(8,128)(2,1)S(1)} %get-tuple-element.33.refs_0_), channel_id=1, source_target_pairs={{0,1},{1,0},{2,3},{3,2},{4,5},{5,4},{6,7},{7,6},{8,9},{9,8},{10,11... | collective-permute-start | bytes 98312 | tf_op jit(solution)/shard_map/ppermute | solution.py:20
  37.2 12.9 %collective-permute-start.16 = (bf16[128,1024]{1,0:T(8,128)(2,1)S(1)}, bf16[128,1024]{1,0:T(8,128)(2,1)S(1)}, u32[]{:S(2)}, u32[]{:S(2)}) collective-permute-start(bf16[128,1024]{1,0:T(8,128)(2,1)S(1)} %get-tuple-element.29.image_t_ref), channel_id=1, source_target_pairs={{0,16},{4,20},{8,24},{12,28},{16,0},{20,4},{24,8},{28,12},{1,17},{... | collective-permute-start | bytes 786440 | tf_op jit(solution)/shard_map/ppermute | solution.py:20
  41.5 8.6 %collective-permute-start.15 = (bf16[1024,128]{1,0:T(8,128)(2,1)S(1)}, bf16[1024,128]{1,0:T(8,128)(2,1)S(1)}, u32[]{:S(2)}, u32[]{:S(2)}) collective-permute-start(bf16[1024,128]{1,0:T(8,128)(2,1)S(1)} %collective-permute-done.14.came_ref), channel_id=1, source_target_pairs={{0,4},{4,0},{8,12},{12,8},{16,20},{20,16},{24,28},{28,24},{1,5},{5... | collective-permute-start | bytes 786440 | tf_op jit(solution)/shard_map/ppermute | solution.py:20
  43.1 1.3 %collective-permute-start.12 = (bf16[128,128]{1,0:T(8,128)(2,1)S(1)}, bf16[128,128]{1,0:T(8,128)(2,1)S(1)}, u32[]{:S(2)}, u32[]{:S(2)}) collective-permute-start(bf16[128,128]{1,0:T(8,128)(2,1)S(1)} %shard_map.52.refs_0_), channel_id=1, source_target_pairs={{0,4},{4,0},{8,12},{12,8},{16,20},{20,16},{24,28},{28,24},{1,5},{5... | collective-permute-start | bytes 98312 | tf_op jit(solution)/shard_map/ppermute | solution.py:20
  48.5 7.5 %collective-permute-start.20 = (f32[128,128]{1,0:T(8,128)S(1)}, f32[128,128]{1,0:T(8,128)S(1)}, u32[]{:S(2)}, u32[]{:S(2)}) collective-permute-start(f32[128,128]{1,0:T(8,128)S(1)} %get-tuple-element.39), channel_id=1, source_target_pairs={{0,16},{4,20},{8,24},{12,28},{16,0},{20,4},{24,8},{28,12},{1,17},{... | collective-permute-start | bytes 196616 | tf_op jit(solution)/shard_map/ppermute | solution.py:20
  50.7 5.3 %collective-permute-start.19 = (bf16[128,128]{1,0:T(8,128)(2,1)S(1)}, bf16[128,128]{1,0:T(8,128)(2,1)S(1)}, u32[]{:S(2)}, u32[]{:S(2)}) collective-permute-start(bf16[128,128]{1,0:T(8,128)(2,1)S(1)} %shard_map.56.refs_0_), channel_id=1, source_target_pairs={{0,3},{1,2},{2,1},{3,0},{4,7},{5,6},{6,5},{7,4},{8,11},{9,10},{10,... | collective-permute-start | bytes 98312 | tf_op jit(solution)/shard_map/ppermute | solution.py:20
  52.1 3.9 %collective-permute-start.18 = (bf16[128,128]{1,0:T(8,128)(2,1)S(1)}, bf16[128,128]{1,0:T(8,128)(2,1)S(1)}, u32[]{:S(2)}, u32[]{:S(2)}) collective-permute-start(bf16[128,128]{1,0:T(8,128)(2,1)S(1)} %shard_map.56.refs_0_), channel_id=1, source_target_pairs={{0,2},{1,3},{2,0},{3,1},{4,6},{5,7},{6,4},{7,5},{8,10},{9,11},{10,... | collective-permute-start | bytes 98312 | tf_op jit(solution)/shard_map/ppermute | solution.py:20
  53.1 3.9 %collective-permute-start.17 = (bf16[128,128]{1,0:T(8,128)(2,1)S(1)}, bf16[128,128]{1,0:T(8,128)(2,1)S(1)}, u32[]{:S(2)}, u32[]{:S(2)}) collective-permute-start(bf16[128,128]{1,0:T(8,128)(2,1)S(1)} %shard_map.56.refs_0_), channel_id=1, source_target_pairs={{0,1},{1,0},{2,3},{3,2},{4,5},{5,4},{6,7},{7,6},{8,9},{9,8},{10,11... | collective-permute-start | bytes 98312 | tf_op jit(solution)/shard_map/ppermute | solution.py:20
  54.6 5.9 %collective-permute-start.23 = (bf16[512,128]{1,0:T(8,128)(2,1)S(1)}, bf16[512,128]{1,0:T(8,128)(2,1)S(1)}, u32[]{:S(2)}, u32[]{:S(2)}) collective-permute-start(bf16[512,128]{1,0:T(8,128)(2,1)S(1)} %get-tuple-element.43), channel_id=1, source_target_pairs={{0,16},{4,20},{8,24},{12,28},{16,0},{20,4},{24,8},{28,12},{1,17},{... | collective-permute-start | bytes 393224 | tf_op jit(solution)/shard_map/ppermute | solution.py:20
  57.2 3.2 %collective-permute-start.21 = (bf16[128,128]{1,0:T(8,128)(2,1)S(1)}, bf16[128,128]{1,0:T(8,128)(2,1)S(1)}, u32[]{:S(2)}, u32[]{:S(2)}) collective-permute-start(bf16[128,128]{1,0:T(8,128)(2,1)S(1)} %shard_map.57.refs_0_), channel_id=1, source_target_pairs={{0,4},{4,0},{8,12},{12,8},{16,20},{20,16},{24,28},{28,24},{1,5},{5... | collective-permute-start | bytes 98312 | tf_op jit(solution)/shard_map/ppermute | solution.py:20
  60.5 9.1 %collective-permute-start.24 = (bf16[512,128]{1,0:T(8,128)(2,1)S(1)}, bf16[512,128]{1,0:T(8,128)(2,1)S(1)}, u32[]{:S(2)}, u32[]{:S(2)}) collective-permute-start(bf16[512,128]{1,0:T(8,128)(2,1)S(1)} %collective-permute-done.23.came_ref), channel_id=1, source_target_pairs={{0,4},{4,0},{8,12},{12,8},{16,20},{20,16},{24,28},{28,24},{1,5},{5... | collective-permute-start | bytes 393224 | tf_op jit(solution)/shard_map/ppermute | solution.py:20
  60.5 4.8 %collective-permute-start.22 = (bf16[128,128]{1,0:T(8,128)(2,1)S(1)}, bf16[128,128]{1,0:T(8,128)(2,1)S(1)}, u32[]{:S(2)}, u32[]{:S(2)}) collective-permute-start(bf16[128,128]{1,0:T(8,128)(2,1)S(1)} %shard_map.58.refs_0_), channel_id=1, source_target_pairs={{0,8},{4,12},{8,0},{12,4},{16,24},{20,28},{24,16},{28,20},{1,9},{5... | collective-permute-start | bytes 98312 | tf_op jit(solution)/shard_map/ppermute | solution.py:20

commit v8 on v7

--- a/solution.py
+++ b/solution.py
@@ -20,8 +20,18 @@
     return lax.ppermute(value, axis, pairs)
 
 
-def summands(value, axis, count, widest):
-    done = 1
+def mixed_swap(value, even, odd):
+    space = lax.axis_size("space")
+    pairs = []
+    for t in range(lax.axis_size("tm")):
+        masks = odd if t % 2 else even
+        for place in range(space):
+            target = (t ^ masks[0]) * space + (place ^ masks[1])
+            pairs.append((t * space + place, target))
+    return lax.ppermute(value, ("tm", "space"), pairs)
+
+
+def summands(value, axis, count, widest, done=1):
     parts = [value]
     while done < count:
         if len(parts) > 1:
@@ -315,7 +325,7 @@
     return jnp.concatenate([first, second], axis=0)
 
 
-def first_merge_kernel(own_ref, other_ref, sketch_ref, halves_ref, mine_ref, slices_ref):
+def first_merge_kernel(own_ref, other_ref, sketch_ref, halves_ref, slices_ref):
     width = own_ref.shape[1]
     own, other = own_ref[:width], other_ref[:width]
     even, odd = choose("tm", own, other)
@@ -325,21 +335,32 @@
     half_own, half_other = merge(cross_t, sketch_ref)
     halves_ref[0] = half_own.astype(BF16)
     halves_ref[1] = half_other.astype(BF16)
-    mine = nn_full(half_own, own)
-    mine_ref[...] = mine
-    slices_ref[0] = mine.astype(BF16)
-    slices_ref[1] = nn_full(half_other, other).astype(BF16)
-
-
-def write_probe(refs, far_image_t, image):
-    refs[0][...] = dot_nn(far_image_t[...], image).astype(BF16)
-    if len(refs) > 1:
-        refs[1][...] = image
-
-
-def first_apply_kernel(slices_ref, image_own, image_other, far_image_t, *refs):
-    image = combined(image_own[...], image_other[...], slices_ref[0], slices_ref[1])
-    write_probe(refs, far_image_t, image)
+    slices = choose("tm", nn_full(half_own, own), nn_full(half_other, other))
+    slices_ref[:width] = slices[0]
+    slices_ref[width:] = slices[1]
+
+
+def write_probes(refs, slices, far_t, shared_t, image):
+    probes_ref, second_ref, *image_ref = refs
+    probes = jnp.concatenate(
+        [dot_nn(far, image) for far in choose("tm", far_t[...], shared_t[...])], axis=0
+    ).astype(BF16)
+    probes_ref[...] = probes
+    second_ref[...] = choose("tm", probes, slices)[0]
+    if image_ref:
+        image_ref[0][...] = image
+
+
+def first_apply_kernel(slices_ref, image_own, image_other, far_t, shared_t, *refs):
+    slices = slices_ref[...].astype(BF16)
+    width = slices.shape[1]
+    own, other = choose("tm", slices[:width], slices[width:])
+    image = combined(image_own[...], image_other[...], own, other)
+    write_probes(refs, slices, far_t, shared_t, image)
+
+
+def pick_kernel(probes_ref, slices_ref, out_ref):
+    out_ref[...] = choose("tm", probes_ref[...], slices_ref[...].astype(BF16))[0]
 
 
 def first_modes_kernel(halves_ref, modes_own, modes_other, *refs):
@@ -348,12 +369,36 @@
     write_bulk((modes_ref, outgoing_ref), modes, image_ref[0] if image_ref else None)
 
 
-def merge_kernel(count, *refs):
-    parts, (sketch_ref, old_ref, halves_ref, mine_ref) = refs[:count], refs[count:]
-    half_own, half_other = merge(total_of(parts), sketch_ref)
+def cross_of(total_rows, own_ref, one_ref, two_ref, shared_one, shared_two):
+    first, second = choose("tm", one_ref[...], shared_one[...])
+    third, slices = choose("tm", two_ref[...], shared_two[...])
+    probes = (own_ref[...].astype(F32) + first.astype(F32)) + (
+        second.astype(F32) + third.astype(F32)
+    )
+    high, low = split(probes / total_rows)
+    width = slices.shape[1]
+    left = jnp.concatenate([slices[:width], slices[width:]] * 2, axis=1)
+    return dot_nn(left, jnp.concatenate([high, low], axis=0))
+
+
+def write_coefficients(halves_ref, slices_ref, old_ref, half_own, half_other):
     halves_ref[0] = half_own.astype(BF16)
     halves_ref[1] = half_other.astype(BF16)
-    mine_ref[...] = nn_full(half_own, old_ref[...])
+    width = old_ref.shape[1]
+    slices_ref[:width] = nn_full(half_own, old_ref[:width])
+    slices_ref[width:] = nn_full(half_own, old_ref[width:])
+
+
+def near_merge_kernel(total_rows, *refs):
+    *arrivals, sketch_ref, old_ref, halves_ref, slices_ref = refs
+    half_own, half_other = merge(cross_of(total_rows, *arrivals), sketch_ref)
+    write_coefficients(halves_ref, slices_ref, old_ref, half_own, half_other)
+
+
+def merge_kernel(count, *refs):
+    parts, (sketch_ref, old_ref, halves_ref, slices_ref) = refs[:count], refs[count:]
+    half_own, half_other = merge(total_of(parts), sketch_ref)
+    write_coefficients(halves_ref, slices_ref, old_ref, half_own, half_other)
 
 
 def last_merge_kernel(count, *refs):
@@ -371,10 +416,10 @@
         copy.wait()
 
 
-def apply_kernel(halves_ref, image_own, came_ref, shared_ref, far_image_t, *refs):
+def apply_kernel(halves_ref, slices_ref, image_own, came_ref, shared_ref, far_t, shared_t, *refs):
     image_other = choose("tm", came_ref[...], shared_ref[...])[1]
     image = combined(image_own[...], image_other, halves_ref[0], halves_ref[1])
-    write_probe(refs, far_image_t, image)
+    write_probes(refs, slices_ref[...].astype(BF16), far_t, shared_t, image)
 
 
 def modes_kernel(halves_ref, modes_own, came_ref, shared_ref, *refs):
@@ -435,9 +480,9 @@
     )(halves, modes, came, shared, out)
 
 
-def cross_kernel(total_rows, count, *refs):
-    parts, (far_ref, out_ref) = refs[:count], refs[count:]
-    out_ref[...] = nn_full(far_ref[...], total_of(parts) / total_rows).astype(BF16)
+def cross_kernel(total_rows, *refs):
+    *arrivals, out_ref = refs
+    out_ref[...] = cross_of(total_rows, *arrivals).astype(BF16)
 
 
 def modes_of(snapshots, energy, neighbours, sketch):
@@ -453,11 +498,12 @@
     wide = [(i, (i + 2 * (i % 2) - 1) % space) for i in range(space)]
     came_near = lax.ppermute(jnp.where(odd, head, tail), "space", near)
     came_wide = lax.ppermute(jnp.where(odd, tail, head), "space", wide)
-    square = jax.ShapeDtypeStruct((width, width), F32)
     modes_shape = jax.ShapeDtypeStruct((rows_dev, width), BF16)
     half_shape = jax.ShapeDtypeStruct((rows_dev // 2, width), BF16)
     factor_shape = jax.ShapeDtypeStruct((width + width // 2, width), F32)
     half_square = jax.ShapeDtypeStruct((width, width), BF16)
+    pair_square = jax.ShapeDtypeStruct((2 * width, width), BF16)
+    slices_shape = jax.ShapeDtypeStruct((2 * width, width), F32)
     halves_shape = jax.ShapeDtypeStruct((2, width, width), BF16)
 
     inner, sketch_t, edges, blocks = interior_of(neighbours, energy, blocks, sketch)
@@ -481,42 +527,58 @@
     for level in range(levels):
         last = level + 1 == levels
         deep = level + 2 < levels
-        probe_outs = [half_square] + ([modes_shape] if deep else [])
+        probe_outs = [pair_square] * 2 + ([modes_shape] if deep else [])
         modes_outs = [modes_shape, modes_shape if deep else half_shape]
         if level > 0:
-            far_mine = swap(mine, "tm", 2**level)
-            parts = summands(probe, "space", space, 4)
+            quarter = space // 4
+            if quarter > 1:
+                parts = summands(probes, "space", quarter, 4)
+                probes = run_kernel(add_kernel, pair_square, *parts)
+                second = run_kernel(pick_kernel, pair_square, probes, slices)
+            one = mixed_swap(probes, (0, quarter), (0, 2 * quarter))
+            two = mixed_swap(second, (0, 3 * quarter), (2**level, 0))
             came = swap(outgoing, "tm", 2**level)
             shared = swap(came, "tm", 1)
-            cross = run_kernel(
-                functools.partial(cross_kernel, total_rows, len(parts)),
-                half_square, *parts, far_mine,
-            )
-            parts = summands(cross, "tm", 2**level, 2)
+            arrivals = [
+                probes, one, two,
+                swap(one, "tm", 1), swap(two, "tm", 1),
+            ]
+            if level > 1:
+                cross = run_kernel(
+                    functools.partial(cross_kernel, total_rows), half_square, *arrivals
+                )
+                parts = summands(cross, "tm", 2**level, 2, done=2)
+        outs = [halves_shape, slices_shape]
         if level == 0:
-            halves, mine, slices = run_kernel(
-                first_merge_kernel, [halves_shape, square, halves_shape],
-                factor, other_factor, sketch_t[level],
+            halves, slices = run_kernel(
+                first_merge_kernel, outs, factor, other_factor, sketch_t[level]
             )
         elif last:
             halves, out = last_level(parts, sketch_t[level], kept, halves_shape)
+        elif level == 1:
+            halves, slices = run_kernel(
+                functools.partial(near_merge_kernel, total_rows), outs,
+                *arrivals, sketch_t[level], slices,
+            )
         else:
-            halves, mine = run_kernel(
-                functools.partial(merge_kernel, len(parts)), [halves_shape, square],
-                *parts, sketch_t[level], mine,
+            halves, slices = run_kernel(
+                functools.partial(merge_kernel, len(parts)), outs,
+                *parts, sketch_t[level], slices,
             )
         if last:
             out = last_modes(halves, modes, came, shared, out)
             break
+        far = far_images[level]
+        far_shared = swap(far, "tm", 1)
         if level == 0:
-            probe, *image = run_kernel(
+            probes, second, *image = run_kernel(
                 first_apply_kernel, probe_outs,
-                slices, image, other_image, far_images[level],
+                slices, image, other_image, far, far_shared,
             )
         else:
-            probe, *image = run_kernel(
+            probes, second, *image = run_kernel(
                 apply_kernel, probe_outs,
-                halves, image[0], came, shared, far_images[level],
+                halves, slices, image[0], came, shared, far, far_shared,
             )
         if level == 0:
             modes, outgoing = run_kernel(

time: 70.9 us -> 69.8 us (0.984)
  starting transfers between devices: 26.9 us -> 24.5 us
  waiting for transfers between devices: 20 us -> 20.8 us
    ppermute x23 -> x19, starting transfers between devices: 22.4 us -> 14.8 us  [swap(): return lax.ppermute(value, axis, pairs)]
    ppermute x0 -> x4, starting transfers between devices: none -> 5.16 us  [mixed_swap(): return lax.ppermute(value, ('tm', 'space'), pairs)]
    ppermute x0 -> x4, waiting for transfers between devices: none -> 3.73 us  [mixed_swap(): return lax.ppermute(value, ('tm', 'space'), pairs)]
    ppermute x23 -> x19, waiting for transfers between devices: 18.3 us -> 15.3 us  [swap(): return lax.ppermute(value, axis, pairs)]
    pallas_call x12 -> x10, Pallas kernels: 14.1 us -> 14.6 us  [run_kernel(): pl.pallas_call(body, out_shape=outs, cost_estimate=cost, compiler_params=...]
  transfers between devices with their start and end apart: 25 -> 25, of which waited for: 15 -> 9; matrix products, arithmetic and copies ran while one was open for 0% -> 0% of each run, Pallas kernels for 28% -> 29%
where the time goes in v8:
time: 69.8 us; the launch traced here: 69.6 us
  starting transfers between devices  24.5 us (35%)
  Pallas kernels  23.1 us (33%)
  waiting for transfers between devices  20.8 us (30%)
  other arithmetic  0.9 us (1%)
    ppermute x19, waiting for transfers between devices, swap(): return lax.ppermute(value, axis, pairs)  15.3 us
    ppermute x19, starting transfers between devices, swap(): return lax.ppermute(value, axis, pairs)  14.8 us
    pallas_call x10, Pallas kernels, run_kernel(): pl.pallas_call(body, out_shape=outs, cost_estimate=cost, compiler_params=...  14.6 us
    ppermute x4, starting transfers between devices, mixed_swap(): return lax.ppermute(value, ('tm', 'space'), pairs)  5.16 us
    pallas_call x1, Pallas kernels, last_level(): pl.pallas_call(functools.partial(last_merge_kernel, len(parts)), out_shap...  4.24 us
    ppermute x4, waiting for transfers between devices, mixed_swap(): return lax.ppermute(value, ('tm', 'space'), pairs)  3.73 us
    ppermute x1, starting transfers between devices, modes_of(): came_near = lax.ppermute(jnp.where(odd, head, tail), 'space', near)  3.03 us
    pallas_call x1, Pallas kernels, interior_of(): pl.pallas_call(interior_kernel, out_shape=[jax.ShapeDtypeStruct((inner, r...  1.89 us
  transfers between devices with their start and end apart: 25, of which 9 were waited for; matrix products, arithmetic and copies ran while one was open for 0% of the time, Pallas kernels for 29%

profile of v8, /device:TPU:0, one launch (start us, length us, event | category | flops | bytes accessed | tf_op | source)
XLA Modules:
  0.0 69.6 jit_solution(11975453324615696473)
XLA Ops:
  0.0 0.9 %broadcast_select_fusion = (bf16[256,128]{1,0:T(8,128)(2,1)S(1)}, bf16[256,128]{1,0:T(8,128)(2,1)S(1)}) fusion(pred[]{:T(512)S(6)} %eq.3, bf16[1024,128]{1,0:T(8,128)(2,1)} %param.4), kind=kLoop, calls=%fused_computation.3 | loop fusion | flops 65536 | bytes 262145 | tf_op jit(solution)/shard_map/jit(_where)/select_n | solution.py:500
  0.9 3.0 %collective-permute-start = (bf16[2,128,128]{2,1,0:T(8,128)(2,1)S(1)}, bf16[2,128,128]{2,1,0:T(8,128)(2,1)S(1)}, u32[]{:S(2)}, u32[]{:S(2)}) collective-permute-start(bf16[2,128,128]{2,1,0:T(8,128)(2,1)S(1)} %bitcast.19), channel_id=1, source_target_pairs={{0,1},{1,0},{2,3},{3,2},{4,5},{5,4},{6,7},{7,6},{8,9},{9,8},{10,11... | collective-permute-start | bytes 196616 | tf_op jit(solution)/shard_map/ppermute | solution.py:499
  3.9 1.5 %collective-permute-start.1 = (bf16[2,128,128]{2,1,0:T(8,128)(2,1)S(1)}, bf16[2,128,128]{2,1,0:T(8,128)(2,1)S(1)}, u32[]{:S(2)}, u32[]{:S(2)}) collective-permute-start(bf16[2,128,128]{2,1,0:T(8,128)(2,1)S(1)} %bitcast.18), channel_id=1, source_target_pairs={{0,3},{1,2},{2,1},{3,0},{4,7},{5,6},{6,5},{7,4},{8,11},{9,10},{10,... | collective-permute-start | bytes 196616 | tf_op jit(solution)/shard_map/ppermute | solution.py:500
  5.4 1.9 %shard_map.46 = (bf16[4,128,128]{2,1,0:T(8,128)(2,1)S(1)}, f32[3,2,128,128]{3,2,1,0:T(8,128)S(1)}, bf16[2,2,7,128,128]{4,3,2,1,0:T(8,128)(2,1)S(1)}, bf16[8,128,128]{2,1,0:T(8,128)(2,1)S(1)}) custom-call(s32[8,7]{1,0:T(8,128)} %index_ref.1, bf16[8,7,128,128]{3,2,1,0:T(8,128)(2,1)} %energy_hbm.1, bf16[8,128,128]{2,1,0:T(8,128)(2,1)} %bitcast.17, ...), custom_call_target="tpu_custom_call" | custom-call | tf_op jit(solution)/shard_map/pallas_call | solution.py:228
  7.3 1.8 %collective-permute-done.1.wide_ref = bf16[2,128,128]{2,1,0:T(8,128)(2,1)S(1)} collective-permute-done((bf16[2,128,128]{2,1,0:T(8,128)(2,1)S(1)}, bf16[2,128,128]{2,1,0:T(8,128)(2,1)S(1)}, u32[]{:S(2)}, u32[]{:S(2)}) %collective-permute-start.1) | collective-permute-done | bytes 65568 | tf_op jit(solution)/shard_map/ppermute | solution.py:500
  9.1 1.3 %shard_map.47 = (bf16[8,128,128]{2,1,0:T(8,128)(2,1)S(1)}, bf16[128,1024]{1,0:T(8,128)(2,1)S(1)}, f32[128,128]{1,0:T(8,128)S(1)}) custom-call(s32[8,7]{1,0:T(8,128)S(1)} %copy-done, bf16[2,2,7,128,128]{4,3,2,1,0:T(8,128)(2,1)S(1)} %get-tuple-element.27.edges_ref, bf16[2,128,128]{2,1,0:T(8,128)(2,1)S(1)} %collective-permute-done.near_ref, ...), custom_call_target="tpu_custom_call" | custom-call | tf_op jit(solution)/shard_map/pallas_call | solution.py:249
  10.5 1.6 %collective-permute-start.7 = (bf16[128,1024]{1,0:T(8,128)(2,1)S(1)}, bf16[128,1024]{1,0:T(8,128)(2,1)S(1)}, u32[]{:S(2)}, u32[]{:S(2)}) collective-permute-start(bf16[128,1024]{1,0:T(8,128)(2,1)S(1)} %get-tuple-element.31.image_t_ref), channel_id=1, source_target_pairs={{0,8},{4,12},{8,0},{12,4},{16,24},{20,28},{24,16},{28,20},{1,9},{5... | collective-permute-start | bytes 786440 | tf_op jit(solution)/shard_map/ppermute | solution.py:20
  12.4 1.1 %collective-permute-start.3 = (f32[192,128]{1,0:T(8,128)S(1)}, f32[192,128]{1,0:T(8,128)S(1)}, u32[]{:S(2)}, u32[]{:S(2)}) collective-permute-start(f32[192,128]{1,0:T(8,128)S(1)} %shard_map.48.refs_0_), channel_id=1, source_target_pairs={{0,1},{1,0},{2,3},{3,2},{4,5},{5,4},{6,7},{7,6},{8,9},{9,8},{10,11... | collective-permute-start | bytes 294920 | tf_op jit(solution)/shard_map/ppermute | solution.py:20
  13.5 1.0 %collective-permute-start.4 = (f32[192,128]{1,0:T(8,128)S(1)}, f32[192,128]{1,0:T(8,128)S(1)}, u32[]{:S(2)}, u32[]{:S(2)}) collective-permute-start(f32[192,128]{1,0:T(8,128)S(1)} %shard_map.48.refs_0_), channel_id=1, source_target_pairs={{0,2},{1,3},{2,0},{3,1},{4,6},{5,7},{6,4},{7,5},{8,10},{9,11},{10,... | collective-permute-start | bytes 294920 | tf_op jit(solution)/shard_map/ppermute | solution.py:20
  14.5 1.4 %collective-permute-start.5 = (f32[192,128]{1,0:T(8,128)S(1)}, f32[192,128]{1,0:T(8,128)S(1)}, u32[]{:S(2)}, u32[]{:S(2)}) collective-permute-start(f32[192,128]{1,0:T(8,128)S(1)} %shard_map.48.refs_0_), channel_id=1, source_target_pairs={{0,3},{1,2},{2,1},{3,0},{4,7},{5,6},{6,5},{7,4},{8,11},{9,10},{10,... | collective-permute-start | bytes 294920 | tf_op jit(solution)/shard_map/ppermute | solution.py:20
  16.0 2.7 %collective-permute-start.16 = (bf16[128,1024]{1,0:T(8,128)(2,1)S(1)}, bf16[128,1024]{1,0:T(8,128)(2,1)S(1)}, u32[]{:S(2)}, u32[]{:S(2)}) collective-permute-start(bf16[128,1024]{1,0:T(8,128)(2,1)S(1)} %get-tuple-element.31.image_t_ref), channel_id=1, source_target_pairs={{0,16},{4,20},{8,24},{12,28},{16,0},{20,4},{24,8},{28,12},{1,17},{... | collective-permute-start | bytes 786440 | tf_op jit(solution)/shard_map/ppermute | solution.py:20
  18.6 2.6 %collective-permute-done.7.far_t = bf16[128,1024]{1,0:T(8,128)(2,1)S(1)} collective-permute-done((bf16[128,1024]{1,0:T(8,128)(2,1)S(1)}, bf16[128,1024]{1,0:T(8,128)(2,1)S(1)}, u32[]{:S(2)}, u32[]{:S(2)}) %collective-permute-start.7) | collective-permute-done | bytes 262176 | tf_op jit(solution)/shard_map/ppermute | solution.py:20
  21.2 3.1 %shard_map.49.own_ref.factor_ref = f32[192,128]{1,0:T(8,128)S(1)} custom-call(f32[192,128]{1,0:T(8,128)S(1)} %shard_map.48.refs_0_, f32[192,128]{1,0:T(8,128)S(1)} %collective-permute-done.3.refs_1_, f32[192,128]{1,0:T(8,128)S(1)} %collective-permute-done.4.refs_2_, f32[192,128]{1,0:T(8,128)S(1)} %collective-permute-done.5.refs_3_), custom_call_target="tpu_custom_call" | custom-call | flops 2000000000 | bytes 1000000 | tf_op jit(solution)/shard_map/pallas_call | solution.py:143
  24.3 0.6 collective-permute-start.6
  25.2 0.6 collective-permute-done.6.other_ref
  25.8 4.4 %shard_map.50 = (bf16[2,128,128]{2,1,0:T(8,128)(2,1)S(1)}, f32[256,128]{1,0:T(8,128)S(1)}) custom-call(f32[192,128]{1,0:T(8,128)S(1)} %shard_map.49.own_ref.factor_ref, f32[192,128]{1,0:T(8,128)S(1)} %collective-permute-done.6.other_ref, f32[2,128,128]{2,1,0:T(8,128)S(1)} %get-tuple-element.51.sketch_ref), custom_call_target="tpu_custom_call" | custom-call | flops 2000000000 | bytes 1000000 | tf_op jit(solution)/shard_map/pallas_call | solution.py:143
  30.3 0.7 %shard_map.51 = (bf16[256,128]{1,0:T(8,128)(2,1)S(1)}, bf16[256,128]{1,0:T(8,128)(2,1)S(1)}, bf16[1024,128]{1,0:T(8,128)(2,1)S(1)}) custom-call(f32[256,128]{1,0:T(8,128)S(1)} %get-tuple-element.34.slices_ref.refs_6_, bf16[1024,128]{1,0:T(8,128)(2,1)S(1)} %bitcast.16, bf16[1024,128]{1,0:T(8,128)(2,1)S(1)} %collective-permute-done.2.other_ref.image_other, ...), custom_call_target="tpu_custom_call" | custom-call | flops 2000000000 | bytes 1000000 | tf_op jit(solution)/shard_map/pallas_call | solution.py:143
  31.9 1.2 %collective-permute-start.9 = (bf16[256,128]{1,0:T(8,128)(2,1)S(1)}, bf16[256,128]{1,0:T(8,128)(2,1)S(1)}, u32[]{:S(2)}, u32[]{:S(2)}) collective-permute-start(bf16[256,128]{1,0:T(8,128)(2,1)S(1)} %get-tuple-element.35.refs_0_), channel_id=1, source_target_pairs={{0,1},{1,0},{2,3},{3,2},{4,6},{5,7},{6,4},{7,5},{8,9},{9,8},{10,11... | collective-permute-start | bytes 196616 | tf_op jit(solution)/shard_map/ppermute | solution.py:31
  33.0 1.5 %collective-permute-start.10 = (bf16[256,128]{1,0:T(8,128)(2,1)S(1)}, bf16[256,128]{1,0:T(8,128)(2,1)S(1)}, u32[]{:S(2)}, u32[]{:S(2)}) collective-permute-start(bf16[256,128]{1,0:T(8,128)(2,1)S(1)} %get-tuple-element.36), channel_id=1, source_target_pairs={{0,3},{1,2},{2,1},{3,0},{4,12},{5,13},{6,14},{7,15},{8,11},{9,10},... | collective-permute-start | bytes 196616 | tf_op jit(solution)/shard_map/ppermute | solution.py:31
  34.5 6.1 %collective-permute-done.14.came_ref = bf16[1024,128]{1,0:T(8,128)(2,1)S(1)} collective-permute-done((bf16[1024,128]{1,0:T(8,128)(2,1)S(1)}, bf16[1024,128]{1,0:T(8,128)(2,1)S(1)}, u32[]{:S(2)}, u32[]{:S(2)}) %collective-permute-start.14) | collective-permute-done | bytes 262176 | tf_op jit(solution)/shard_map/ppermute | solution.py:20
  41.2 1.0 %collective-permute-done.11.refs_3_ = bf16[256,128]{1,0:T(8,128)(2,1)S(1)} collective-permute-done((bf16[256,128]{1,0:T(8,128)(2,1)S(1)}, bf16[256,128]{1,0:T(8,128)(2,1)S(1)}, u32[]{:S(2)}, u32[]{:S(2)}) %collective-permute-start.11) | collective-permute-done | bytes 65568 | tf_op jit(solution)/shard_map/ppermute | solution.py:20
  42.4 4.3 %shard_map.52 = (bf16[2,128,128]{2,1,0:T(8,128)(2,1)S(1)}, f32[256,128]{1,0:T(8,128)S(1)}) custom-call(bf16[256,128]{1,0:T(8,128)(2,1)S(1)} %get-tuple-element.35.refs_0_, bf16[256,128]{1,0:T(8,128)(2,1)S(1)} %collective-permute-done.9.refs_1_, bf16[256,128]{1,0:T(8,128)(2,1)S(1)} %collective-permute-done.10.refs_2_, ...), custom_call_target="tpu_custom_call" | custom-call | flops 2000000000 | bytes 1000000 | tf_op jit(solution)/shard_map/pallas_call | solution.py:143
  46.7 0.7 %shard_map.55 = (bf16[256,128]{1,0:T(8,128)(2,1)S(1)}, bf16[256,128]{1,0:T(8,128)(2,1)S(1)}) custom-call(bf16[2,128,128]{2,1,0:T(8,128)(2,1)S(1)} %get-tuple-element.37.halves_ref, f32[256,128]{1,0:T(8,128)S(1)} %get-tuple-element.38.slices_ref, bf16[1024,128]{1,0:T(8,128)(2,1)S(1)} %get-tuple-element.39.refs_0_.image_own, ...), custom_call_target="tpu_custom_call" | custom-call | flops 2000000000 | bytes 1000000 | tf_op jit(solution)/shard_map/pallas_call | solution.py:143
  47.4 1.1 %collective-permute-start.18 = (bf16[256,128]{1,0:T(8,128)(2,1)S(1)}, bf16[256,128]{1,0:T(8,128)(2,1)S(1)}, u32[]{:S(2)}, u32[]{:S(2)}) collective-permute-start(bf16[256,128]{1,0:T(8,128)(2,1)S(1)} %get-tuple-element.42.refs_0_), channel_id=1, source_target_pairs={{0,1},{1,0},{2,3},{3,2},{4,6},{5,7},{6,4},{7,5},{8,9},{9,8},{10,11... | collective-permute-start | bytes 196616 | tf_op jit(solution)/shard_map/ppermute | solution.py:31
  48.8 1.7 %collective-permute-start.23 = (bf16[512,128]{1,0:T(8,128)(2,1)S(1)}, bf16[512,128]{1,0:T(8,128)(2,1)S(1)}, u32[]{:S(2)}, u32[]{:S(2)}) collective-permute-start(bf16[512,128]{1,0:T(8,128)(2,1)S(1)} %get-tuple-element.47), channel_id=1, source_target_pairs={{0,16},{4,20},{8,24},{12,28},{16,0},{20,4},{24,8},{28,12},{1,17},{... | collective-permute-start | bytes 393224 | tf_op jit(solution)/shard_map/ppermute | solution.py:20
  50.5 1.4 %collective-permute-start.19 = (bf16[256,128]{1,0:T(8,128)(2,1)S(1)}, bf16[256,128]{1,0:T(8,128)(2,1)S(1)}, u32[]{:S(2)}, u32[]{:S(2)}) collective-permute-start(bf16[256,128]{1,0:T(8,128)(2,1)S(1)} %get-tuple-element.43), channel_id=1, source_target_pairs={{0,3},{1,2},{2,1},{3,0},{4,20},{5,21},{6,22},{7,23},{8,11},{9,10},... | collective-permute-start | bytes 196616 | tf_op jit(solution)/shard_map/ppermute | solution.py:31
  52.0 3.7 %collective-permute-done.19.refs_2_ = bf16[256,128]{1,0:T(8,128)(2,1)S(1)} collective-permute-done((bf16[256,128]{1,0:T(8,128)(2,1)S(1)}, bf16[256,128]{1,0:T(8,128)(2,1)S(1)}, u32[]{:S(2)}, u32[]{:S(2)}) %collective-permute-start.19) | collective-permute-done | bytes 65568 | tf_op jit(solution)/shard_map/ppermute | solution.py:31
  55.7 3.4 %collective-permute-start.21 = (bf16[256,128]{1,0:T(8,128)(2,1)S(1)}, bf16[256,128]{1,0:T(8,128)(2,1)S(1)}, u32[]{:S(2)}, u32[]{:S(2)}) collective-permute-start(bf16[256,128]{1,0:T(8,128)(2,1)S(1)} %collective-permute-done.19.refs_2_), channel_id=1, source_target_pairs={{0,4},{4,0},{8,12},{12,8},{16,20},{20,16},{24,28},{28,24},{1,5},{5... | collective-permute-start | bytes 196616 | tf_op jit(solution)/shard_map/ppermute | solution.py:20
  59.1 0.9 %collective-permute-done.21.refs_4_ = bf16[256,128]{1,0:T(8,128)(2,1)S(1)} collective-permute-done((bf16[256,128]{1,0:T(8,128)(2,1)S(1)}, bf16[256,128]{1,0:T(8,128)(2,1)S(1)}, u32[]{:S(2)}, u32[]{:S(2)}) %collective-permute-start.21) | collective-permute-done | bytes 65568 | tf_op jit(solution)/shard_map/ppermute | solution.py:20
  60.3 3.9 %collective-permute-done.22.refs_1_ = bf16[128,128]{1,0:T(8,128)(2,1)S(1)} collective-permute-done((bf16[128,128]{1,0:T(8,128)(2,1)S(1)}, bf16[128,128]{1,0:T(8,128)(2,1)S(1)}, u32[]{:S(2)}, u32[]{:S(2)}) %collective-permute-start.22) | collective-permute-done | bytes 32800 | tf_op jit(solution)/shard_map/ppermute | solution.py:20
  64.2 4.2 %shard_map.58 = (bf16[2,128,128]{2,1,0:T(8,128)(2,1)S(1)}, bf16[4,1024,128]{2,1,0:T(8,128)(2,1)}) custom-call(bf16[128,128]{1,0:T(8,128)(2,1)S(1)} %shard_map.56.refs_0_, bf16[128,128]{1,0:T(8,128)(2,1)S(1)} %collective-permute-done.22.refs_1_, f32[2,128,128]{2,1,0:T(8,128)S(1)} %get-tuple-element.49.refs_2_, ...), custom_call_target="tpu_custom_call" | custom-call | tf_op jit(solution)/shard_map/pallas_call | solution.py:459
  68.4 1.0 %shard_map.59 = bf16[4,1024,128]{2,1,0:T(8,128)(2,1)} custom-call(bf16[2,128,128]{2,1,0:T(8,128)(2,1)S(1)} %get-tuple-element.46.halves_ref, bf16[1024,128]{1,0:T(8,128)(2,1)S(1)} %get-tuple-element.45.refs_5_.modes_own, bf16[512,128]{1,0:T(8,128)(2,1)S(1)} %collective-permute-done.23.came_ref, ...), custom_call_target="tpu_custom_call", output_to_operand_aliasing={{}: (4, {})} | custom-call | tf_op jit(solution)/shard_map/pallas_call | solution.py:472
  (36 shorter events, 2.9 us)
Async XLA Ops:
  0.0 9.1 %copy-start = (s32[8,7]{1,0:T(8,128)S(1)}, s32[8,7]{1,0:T(8,128)}, u32[]{:S(2)}) copy-start(s32[8,7]{1,0:T(8,128)} %index_ref.1) | copy-start | bytes 676
  0.9 6.4 %collective-permute-start = (bf16[2,128,128]{2,1,0:T(8,128)(2,1)S(1)}, bf16[2,128,128]{2,1,0:T(8,128)(2,1)S(1)}, u32[]{:S(2)}, u32[]{:S(2)}) collective-permute-start(bf16[2,128,128]{2,1,0:T(8,128)(2,1)S(1)} %bitcast.19), channel_id=1, source_target_pairs={{0,1},{1,0},{2,3},{3,2},{4,5},{5,4},{6,7},{7,6},{8,9},{9,8},{10,11... | collective-permute-start | bytes 196616 | tf_op jit(solution)/shard_map/ppermute | solution.py:499
  3.9 5.2 %collective-permute-start.1 = (bf16[2,128,128]{2,1,0:T(8,128)(2,1)S(1)}, bf16[2,128,128]{2,1,0:T(8,128)(2,1)S(1)}, u32[]{:S(2)}, u32[]{:S(2)}) collective-permute-start(bf16[2,128,128]{2,1,0:T(8,128)(2,1)S(1)} %bitcast.18), channel_id=1, source_target_pairs={{0,3},{1,2},{2,1},{3,0},{4,7},{5,6},{6,5},{7,4},{8,11},{9,10},{10,... | collective-permute-start | bytes 196616 | tf_op jit(solution)/shard_map/ppermute | solution.py:500
  10.4 1.7 %collective-permute-start.2 = (bf16[1024,128]{1,0:T(8,128)(2,1)S(1)}, bf16[1024,128]{1,0:T(8,128)(2,1)S(1)}, u32[]{:S(2)}, u32[]{:S(2)}) collective-permute-start(bf16[1024,128]{1,0:T(8,128)(2,1)S(1)} %bitcast.15), channel_id=1, source_target_pairs={{0,4},{4,0},{8,12},{12,8},{16,20},{20,16},{24,28},{28,24},{1,5},{5... | collective-permute-start | bytes 786440 | tf_op jit(solution)/shard_map/ppermute | solution.py:20
  10.5 10.7 %collective-permute-start.7 = (bf16[128,1024]{1,0:T(8,128)(2,1)S(1)}, bf16[128,1024]{1,0:T(8,128)(2,1)S(1)}, u32[]{:S(2)}, u32[]{:S(2)}) collective-permute-start(bf16[128,1024]{1,0:T(8,128)(2,1)S(1)} %get-tuple-element.31.image_t_ref), channel_id=1, source_target_pairs={{0,8},{4,12},{8,0},{12,4},{16,24},{20,28},{24,16},{28,20},{1,9},{5... | collective-permute-start | bytes 786440 | tf_op jit(solution)/shard_map/ppermute | solution.py:20
  12.4 8.8 %collective-permute-start.3 = (f32[192,128]{1,0:T(8,128)S(1)}, f32[192,128]{1,0:T(8,128)S(1)}, u32[]{:S(2)}, u32[]{:S(2)}) collective-permute-start(f32[192,128]{1,0:T(8,128)S(1)} %shard_map.48.refs_0_), channel_id=1, source_target_pairs={{0,1},{1,0},{2,3},{3,2},{4,5},{5,4},{6,7},{7,6},{8,9},{9,8},{10,11... | collective-permute-start | bytes 294920 | tf_op jit(solution)/shard_map/ppermute | solution.py:20
  13.5 7.7 %collective-permute-start.4 = (f32[192,128]{1,0:T(8,128)S(1)}, f32[192,128]{1,0:T(8,128)S(1)}, u32[]{:S(2)}, u32[]{:S(2)}) collective-permute-start(f32[192,128]{1,0:T(8,128)S(1)} %shard_map.48.refs_0_), channel_id=1, source_target_pairs={{0,2},{1,3},{2,0},{3,1},{4,6},{5,7},{6,4},{7,5},{8,10},{9,11},{10,... | collective-permute-start | bytes 294920 | tf_op jit(solution)/shard_map/ppermute | solution.py:20
  14.5 6.7 %collective-permute-start.5 = (f32[192,128]{1,0:T(8,128)S(1)}, f32[192,128]{1,0:T(8,128)S(1)}, u32[]{:S(2)}, u32[]{:S(2)}) collective-permute-start(f32[192,128]{1,0:T(8,128)S(1)} %shard_map.48.refs_0_), channel_id=1, source_target_pairs={{0,3},{1,2},{2,1},{3,0},{4,7},{5,6},{6,5},{7,4},{8,11},{9,10},{10,... | collective-permute-start | bytes 294920 | tf_op jit(solution)/shard_map/ppermute | solution.py:20
  16.0 18.5 %collective-permute-start.16 = (bf16[128,1024]{1,0:T(8,128)(2,1)S(1)}, bf16[128,1024]{1,0:T(8,128)(2,1)S(1)}, u32[]{:S(2)}, u32[]{:S(2)}) collective-permute-start(bf16[128,1024]{1,0:T(8,128)(2,1)S(1)} %get-tuple-element.31.image_t_ref), channel_id=1, source_target_pairs={{0,16},{4,20},{8,24},{12,28},{16,0},{20,4},{24,8},{28,12},{1,17},{... | collective-permute-start | bytes 786440 | tf_op jit(solution)/shard_map/ppermute | solution.py:20
  21.2 9.1 %collective-permute-start.8 = (bf16[128,1024]{1,0:T(8,128)(2,1)S(1)}, bf16[128,1024]{1,0:T(8,128)(2,1)S(1)}, u32[]{:S(2)}, u32[]{:S(2)}) collective-permute-start(bf16[128,1024]{1,0:T(8,128)(2,1)S(1)} %collective-permute-done.7.far_t), channel_id=1, source_target_pairs={{0,4},{4,0},{8,12},{12,8},{16,20},{20,16},{24,28},{28,24},{1,5},{5... | collective-permute-start | bytes 786440 | tf_op jit(solution)/shard_map/ppermute | solution.py:20
  24.3 1.5 %collective-permute-start.6 = (f32[192,128]{1,0:T(8,128)S(1)}, f32[192,128]{1,0:T(8,128)S(1)}, u32[]{:S(2)}, u32[]{:S(2)}) collective-permute-start(f32[192,128]{1,0:T(8,128)S(1)} %shard_map.49.own_ref.factor_ref), channel_id=1, source_target_pairs={{0,4},{4,0},{8,12},{12,8},{16,20},{20,16},{24,28},{28,24},{1,5},{5... | collective-permute-start | bytes 294920 | tf_op jit(solution)/shard_map/ppermute | solution.py:20
  25.1 5.9 %collective-permute-start.13 = (bf16[1024,128]{1,0:T(8,128)(2,1)S(1)}, bf16[1024,128]{1,0:T(8,128)(2,1)S(1)}, u32[]{:S(2)}, u32[]{:S(2)}) collective-permute-start(bf16[1024,128]{1,0:T(8,128)(2,1)S(1)} %shard_map.53.modes_own.refs_3_), channel_id=1, source_target_pairs={{0,4},{4,0},{8,12},{12,8},{16,20},{20,16},{24,28},{28,24},{1,5},{5... | collective-permute-start | bytes 786440 | tf_op jit(solution)/shard_map/ppermute | solution.py:20
  31.4 9.2 %collective-permute-start.14 = (bf16[1024,128]{1,0:T(8,128)(2,1)S(1)}, bf16[1024,128]{1,0:T(8,128)(2,1)S(1)}, u32[]{:S(2)}, u32[]{:S(2)}) collective-permute-start(bf16[1024,128]{1,0:T(8,128)(2,1)S(1)} %get-tuple-element.41), channel_id=1, source_target_pairs={{0,8},{4,12},{8,0},{12,4},{16,24},{20,28},{24,16},{28,20},{1,9},{5... | collective-permute-start | bytes 786440 | tf_op jit(solution)/shard_map/ppermute | solution.py:20
  31.9 8.7 %collective-permute-start.9 = (bf16[256,128]{1,0:T(8,128)(2,1)S(1)}, bf16[256,128]{1,0:T(8,128)(2,1)S(1)}, u32[]{:S(2)}, u32[]{:S(2)}) collective-permute-start(bf16[256,128]{1,0:T(8,128)(2,1)S(1)} %get-tuple-element.35.refs_0_), channel_id=1, source_target_pairs={{0,1},{1,0},{2,3},{3,2},{4,6},{5,7},{6,4},{7,5},{8,9},{9,8},{10,11... | collective-permute-start | bytes 196616 | tf_op jit(solution)/shard_map/ppermute | solution.py:31
  33.0 8.1 %collective-permute-start.10 = (bf16[256,128]{1,0:T(8,128)(2,1)S(1)}, bf16[256,128]{1,0:T(8,128)(2,1)S(1)}, u32[]{:S(2)}, u32[]{:S(2)}) collective-permute-start(bf16[256,128]{1,0:T(8,128)(2,1)S(1)} %get-tuple-element.36), channel_id=1, source_target_pairs={{0,3},{1,2},{2,1},{3,0},{4,12},{5,13},{6,14},{7,15},{8,11},{9,10},... | collective-permute-start | bytes 196616 | tf_op jit(solution)/shard_map/ppermute | solution.py:31
  34.5 12.2 %collective-permute-start.17 = (bf16[128,1024]{1,0:T(8,128)(2,1)S(1)}, bf16[128,1024]{1,0:T(8,128)(2,1)S(1)}, u32[]{:S(2)}, u32[]{:S(2)}) collective-permute-start(bf16[128,1024]{1,0:T(8,128)(2,1)S(1)} %collective-permute-done.16.far_t), channel_id=1, source_target_pairs={{0,4},{4,0},{8,12},{12,8},{16,20},{20,16},{24,28},{28,24},{1,5},{5... | collective-permute-start | bytes 786440 | tf_op jit(solution)/shard_map/ppermute | solution.py:20
  40.6 6.1 %collective-permute-start.15 = (bf16[1024,128]{1,0:T(8,128)(2,1)S(1)}, bf16[1024,128]{1,0:T(8,128)(2,1)S(1)}, u32[]{:S(2)}, u32[]{:S(2)}) collective-permute-start(bf16[1024,128]{1,0:T(8,128)(2,1)S(1)} %collective-permute-done.14.came_ref), channel_id=1, source_target_pairs={{0,4},{4,0},{8,12},{12,8},{16,20},{20,16},{24,28},{28,24},{1,5},{5... | collective-permute-start | bytes 786440 | tf_op jit(solution)/shard_map/ppermute | solution.py:20
  40.6 1.6 %collective-permute-start.11 = (bf16[256,128]{1,0:T(8,128)(2,1)S(1)}, bf16[256,128]{1,0:T(8,128)(2,1)S(1)}, u32[]{:S(2)}, u32[]{:S(2)}) collective-permute-start(bf16[256,128]{1,0:T(8,128)(2,1)S(1)} %collective-permute-done.9.refs_1_), channel_id=1, source_target_pairs={{0,4},{4,0},{8,12},{12,8},{16,20},{20,16},{24,28},{28,24},{1,5},{5... | collective-permute-start | bytes 196616 | tf_op jit(solution)/shard_map/ppermute | solution.py:20
  41.1 1.3 %collective-permute-start.12 = (bf16[256,128]{1,0:T(8,128)(2,1)S(1)}, bf16[256,128]{1,0:T(8,128)(2,1)S(1)}, u32[]{:S(2)}, u32[]{:S(2)}) collective-permute-start(bf16[256,128]{1,0:T(8,128)(2,1)S(1)} %collective-permute-done.10.refs_2_), channel_id=1, source_target_pairs={{0,4},{4,0},{8,12},{12,8},{16,20},{20,16},{24,28},{28,24},{1,5},{5... | collective-permute-start | bytes 196616 | tf_op jit(solution)/shard_map/ppermute | solution.py:20
  47.4 4.5 %collective-permute-start.18 = (bf16[256,128]{1,0:T(8,128)(2,1)S(1)}, bf16[256,128]{1,0:T(8,128)(2,1)S(1)}, u32[]{:S(2)}, u32[]{:S(2)}) collective-permute-start(bf16[256,128]{1,0:T(8,128)(2,1)S(1)} %get-tuple-element.42.refs_0_), channel_id=1, source_target_pairs={{0,1},{1,0},{2,3},{3,2},{4,6},{5,7},{6,4},{7,5},{8,9},{9,8},{10,11... | collective-permute-start | bytes 196616 | tf_op jit(solution)/shard_map/ppermute | solution.py:31
  48.8 10.2 %collective-permute-start.23 = (bf16[512,128]{1,0:T(8,128)(2,1)S(1)}, bf16[512,128]{1,0:T(8,128)(2,1)S(1)}, u32[]{:S(2)}, u32[]{:S(2)}) collective-permute-start(bf16[512,128]{1,0:T(8,128)(2,1)S(1)} %get-tuple-element.47), channel_id=1, source_target_pairs={{0,16},{4,20},{8,24},{12,28},{16,0},{20,4},{24,8},{28,12},{1,17},{... | collective-permute-start | bytes 393224 | tf_op jit(solution)/shard_map/ppermute | solution.py:20
  50.5 5.2 %collective-permute-start.19 = (bf16[256,128]{1,0:T(8,128)(2,1)S(1)}, bf16[256,128]{1,0:T(8,128)(2,1)S(1)}, u32[]{:S(2)}, u32[]{:S(2)}) collective-permute-start(bf16[256,128]{1,0:T(8,128)(2,1)S(1)} %get-tuple-element.43), channel_id=1, source_target_pairs={{0,3},{1,2},{2,1},{3,0},{4,20},{5,21},{6,22},{7,23},{8,11},{9,10},... | collective-permute-start | bytes 196616 | tf_op jit(solution)/shard_map/ppermute | solution.py:31
  51.9 7.1 %collective-permute-start.20 = (bf16[256,128]{1,0:T(8,128)(2,1)S(1)}, bf16[256,128]{1,0:T(8,128)(2,1)S(1)}, u32[]{:S(2)}, u32[]{:S(2)}) collective-permute-start(bf16[256,128]{1,0:T(8,128)(2,1)S(1)} %collective-permute-done.18.refs_1_), channel_id=1, source_target_pairs={{0,4},{4,0},{8,12},{12,8},{16,20},{20,16},{24,28},{28,24},{1,5},{5... | collective-permute-start | bytes 196616 | tf_op jit(solution)/shard_map/ppermute | solution.py:20
  55.7 4.3 %collective-permute-start.21 = (bf16[256,128]{1,0:T(8,128)(2,1)S(1)}, bf16[256,128]{1,0:T(8,128)(2,1)S(1)}, u32[]{:S(2)}, u32[]{:S(2)}) collective-permute-start(bf16[256,128]{1,0:T(8,128)(2,1)S(1)} %collective-permute-done.19.refs_2_), channel_id=1, source_target_pairs={{0,4},{4,0},{8,12},{12,8},{16,20},{20,16},{24,28},{28,24},{1,5},{5... | collective-permute-start | bytes 196616 | tf_op jit(solution)/shard_map/ppermute | solution.py:20
  59.1 9.4 %collective-permute-start.24 = (bf16[512,128]{1,0:T(8,128)(2,1)S(1)}, bf16[512,128]{1,0:T(8,128)(2,1)S(1)}, u32[]{:S(2)}, u32[]{:S(2)}) collective-permute-start(bf16[512,128]{1,0:T(8,128)(2,1)S(1)} %collective-permute-done.23.came_ref), channel_id=1, source_target_pairs={{0,4},{4,0},{8,12},{12,8},{16,20},{20,16},{24,28},{28,24},{1,5},{5... | collective-permute-start | bytes 393224 | tf_op jit(solution)/shard_map/ppermute | solution.py:20
  60.2 4.0 %collective-permute-start.22 = (bf16[128,128]{1,0:T(8,128)(2,1)S(1)}, bf16[128,128]{1,0:T(8,128)(2,1)S(1)}, u32[]{:S(2)}, u32[]{:S(2)}) collective-permute-start(bf16[128,128]{1,0:T(8,128)(2,1)S(1)} %shard_map.56.refs_0_), channel_id=1, source_target_pairs={{0,8},{4,12},{8,0},{12,4},{16,24},{20,28},{24,16},{28,20},{1,9},{5... | collective-permute-start | bytes 98312 | tf_op jit(solution)/shard_map/ppermute | solution.py:20

commit v9 on v8

--- a/solution.py
+++ b/solution.py
@@ -79,7 +79,7 @@
 nt_full = functools.partial(full, dot_nt, 1)
 
 
-def inverse_factor(matrix):
+def inverse_factor(matrix, exact=False):
     size = matrix.shape[0]
     panels = size // PANEL
     shape = (PANEL, size)
@@ -93,48 +93,65 @@
         return jnp.broadcast_to(rows[index : index + 1, :], shape)
 
     rows_of = [matrix[PANEL * i : PANEL * (i + 1), :] for i in range(panels)]
+    zero = jnp.zeros(shape, F32)
     out = []
     block = [column(rows_of[0], j) for j in range(PANEL)]
     for k in range(panels):
         base = PANEL * k
+        final = k + 1 == panels
         active = rows_of[k]
-        ahead = (
-            [column(active, base + PANEL + j) for j in range(PANEL)] if k + 1 < panels else []
-        )
         here = (lane >= base) & (lane < base + PANEL)
+        if not final:
+            below = rows_of[k + 1]
+            under = [column(below, base + j) for j in range(PANEL)]
+            ahead = [column(active, base + PANEL + q) for q in range(PANEL)]
+            following = [column(below, base + PANEL + q) for q in range(PANEL)]
+            below = jnp.where(here, 0.0, below)
         active = jnp.where(here, jnp.where(lane == sub + base, 1.0, 0.0), active)
         kept = active
         pivots = block[0]
         for j in range(PANEL):
             pivot = row(block[j], j)
-            factor = jnp.where(sub == j, 0.0, block[j]) * (1.0 / pivot)
+            inverse = 1.0 / pivot
+            factor = jnp.where(sub == j, 0.0, block[j]) * inverse
+            leading = row(active, j)
             kept = jnp.where(sub == j, active, kept)
             pivots = jnp.where(sub == j, pivot, pivots)
-            active = active - factor * row(active, j)
+            active = active - factor * leading
+            if not final:
+                lower = under[j] * inverse
+                below = below - lower * leading
             for q in range(j + 1, PANEL):
-                block[q] = block[q] - factor * row(block[q], j)
-            ahead = [item - factor * row(item, j) for item in ahead]
+                item = row(block[q], j)
+                block[q] = block[q] - factor * item
+                if not final:
+                    under[q] = under[q] - lower * item
+            if not final:
+                for q in range(PANEL):
+                    item = row(ahead[q], j)
+                    ahead[q] = ahead[q] - factor * item
+                    following[q] = following[q] - lower * item
         out.append(jnp.where(lane < base + PANEL, kept * lax.rsqrt(pivots), 0.0))
-        if k + 1 == panels:
+        if final:
             break
-        scale = 1.0 / pivots
-        solved = active * scale
-        solved_rows = [row(solved, j) for j in range(PANEL)]
-        block = []
-        for i in range(k + 1, panels):
-            old = rows_of[i]
-            columns = [column(old, base + j) for j in range(PANEL)]
-            if i == k + 1:
-                for q in range(PANEL):
-                    item = column(old, base + PANEL + q)
-                    scaled = ahead[q] * scale
-                    for j in range(PANEL):
-                        item = item - columns[j] * row(scaled, j)
-                    block.append(item)
-            new = jnp.where(here, 0.0, old)
-            for j in range(PANEL):
-                new = new - columns[j] * solved_rows[j]
-            rows_of[i] = new
+        rows_of[k + 1] = below
+        block = following
+        if k + 2 < panels:
+            solved = active * (1.0 / pivots)
+            solved_rows = [row(solved, j) for j in range(PANEL)]
+            for i in range(k + 2, panels if exact else k + 3):
+                old = rows_of[i]
+                new = jnp.where(here, 0.0, old)
+                for j in range(PANEL):
+                    new = new - column(old, base + j) * solved_rows[j]
+                rows_of[i] = new
+        if k + 3 < panels and not exact:
+            rest = rows_of[k + 3 :]
+            spread = jnp.concatenate([zero] * k + [solved] + [zero] * (panels - k - 1), axis=0)
+            change = nn_full(jnp.concatenate(rest, axis=0), spread)
+            for i, old in enumerate(rest):
+                part = change[PANEL * i : PANEL * (i + 1)]
+                rows_of[k + 3 + i] = jnp.where(here, 0.0, old) - part
     return jnp.concatenate(out, axis=0)
 
 
@@ -274,7 +291,7 @@
     width = factor_ref.shape[1]
     grams = total_of(parts) / total_rows
     factor_ref[width:] = grams[width:]
-    inverse = inverse_factor(grams[:width])
+    inverse = inverse_factor(grams[:width], exact=True)
     factor_ref[:width] = inverse
 
 

time: 69.8 us -> 68.2 us (0.977)
  Pallas kernels: 23.1 us -> 21.5 us
    pallas_call x10, Pallas kernels: 14.6 us -> 13.4 us  [run_kernel(): pl.pallas_call(body, out_shape=outs, cost_estimate=cost, compiler_params=...]
  transfers between devices with their start and end apart: 25 -> 25, of which waited for: 9 -> 9; matrix products, arithmetic and copies ran while one was open for 0% -> 0% of each run, Pallas kernels for 29% -> 27%
where the time goes in v9:
time: 68.2 us; the launch traced here: 68 us
  starting transfers between devices  24.5 us (36%)
  Pallas kernels  21.5 us (32%)
  waiting for transfers between devices  20.8 us (30%)
  other arithmetic  0.9 us (1%)
    ppermute x19, waiting for transfers between devices, swap(): return lax.ppermute(value, axis, pairs)  15.3 us
    ppermute x19, starting transfers between devices, swap(): return lax.ppermute(value, axis, pairs)  14.8 us
    pallas_call x10, Pallas kernels, run_kernel(): pl.pallas_call(body, out_shape=outs, cost_estimate=cost, compiler_params=...  13.4 us
    ppermute x4, starting transfers between devices, mixed_swap(): return lax.ppermute(value, ('tm', 'space'), pairs)  5.17 us
    pallas_call x1, Pallas kernels, last_level(): pl.pallas_call(functools.partial(last_merge_kernel, len(parts)), out_shap...  3.82 us
    ppermute x4, waiting for transfers between devices, mixed_swap(): return lax.ppermute(value, ('tm', 'space'), pairs)  3.72 us
    ppermute x1, starting transfers between devices, modes_of(): came_near = lax.ppermute(jnp.where(odd, head, tail), 'space', near)  3.03 us
    pallas_call x1, Pallas kernels, interior_of(): pl.pallas_call(interior_kernel, out_shape=[jax.ShapeDtypeStruct((inner, r...  1.89 us
  transfers between devices with their start and end apart: 25, of which 9 were waited for; matrix products, arithmetic and copies ran while one was open for 0% of the time, Pallas kernels for 27%

profile of v9, /device:TPU:0, one launch (start us, length us, event | category | flops | bytes accessed | tf_op | source)
XLA Modules:
  0.0 68.0 jit_solution(11588481583944580526)
XLA Ops:
  0.0 0.9 %broadcast_select_fusion = (bf16[256,128]{1,0:T(8,128)(2,1)S(1)}, bf16[256,128]{1,0:T(8,128)(2,1)S(1)}) fusion(pred[]{:T(512)S(6)} %eq.3, bf16[1024,128]{1,0:T(8,128)(2,1)} %param.4), kind=kLoop, calls=%fused_computation.3 | loop fusion | flops 65536 | bytes 262145 | tf_op jit(solution)/shard_map/jit(_where)/select_n | solution.py:517
  0.9 3.0 %collective-permute-start = (bf16[2,128,128]{2,1,0:T(8,128)(2,1)S(1)}, bf16[2,128,128]{2,1,0:T(8,128)(2,1)S(1)}, u32[]{:S(2)}, u32[]{:S(2)}) collective-permute-start(bf16[2,128,128]{2,1,0:T(8,128)(2,1)S(1)} %bitcast.19), channel_id=1, source_target_pairs={{0,1},{1,0},{2,3},{3,2},{4,5},{5,4},{6,7},{7,6},{8,9},{9,8},{10,11... | collective-permute-start | bytes 196616 | tf_op jit(solution)/shard_map/ppermute | solution.py:516
  3.9 1.5 %collective-permute-start.1 = (bf16[2,128,128]{2,1,0:T(8,128)(2,1)S(1)}, bf16[2,128,128]{2,1,0:T(8,128)(2,1)S(1)}, u32[]{:S(2)}, u32[]{:S(2)}) collective-permute-start(bf16[2,128,128]{2,1,0:T(8,128)(2,1)S(1)} %bitcast.18), channel_id=1, source_target_pairs={{0,3},{1,2},{2,1},{3,0},{4,7},{5,6},{6,5},{7,4},{8,11},{9,10},{10,... | collective-permute-start | bytes 196616 | tf_op jit(solution)/shard_map/ppermute | solution.py:517
  5.4 1.9 %shard_map.46 = (bf16[4,128,128]{2,1,0:T(8,128)(2,1)S(1)}, f32[3,2,128,128]{3,2,1,0:T(8,128)S(1)}, bf16[2,2,7,128,128]{4,3,2,1,0:T(8,128)(2,1)S(1)}, bf16[8,128,128]{2,1,0:T(8,128)(2,1)S(1)}) custom-call(s32[8,7]{1,0:T(8,128)} %index_ref.1, bf16[8,7,128,128]{3,2,1,0:T(8,128)(2,1)} %energy_hbm.1, bf16[8,128,128]{2,1,0:T(8,128)(2,1)} %bitcast.17, ...), custom_call_target="tpu_custom_call" | custom-call | tf_op jit(solution)/shard_map/pallas_call | solution.py:245
  7.3 1.8 %collective-permute-done.1.wide_ref = bf16[2,128,128]{2,1,0:T(8,128)(2,1)S(1)} collective-permute-done((bf16[2,128,128]{2,1,0:T(8,128)(2,1)S(1)}, bf16[2,128,128]{2,1,0:T(8,128)(2,1)S(1)}, u32[]{:S(2)}, u32[]{:S(2)}) %collective-permute-start.1) | collective-permute-done | bytes 65568 | tf_op jit(solution)/shard_map/ppermute | solution.py:517
  9.1 1.3 %shard_map.47 = (bf16[8,128,128]{2,1,0:T(8,128)(2,1)S(1)}, bf16[128,1024]{1,0:T(8,128)(2,1)S(1)}, f32[128,128]{1,0:T(8,128)S(1)}) custom-call(s32[8,7]{1,0:T(8,128)S(1)} %copy-done, bf16[2,2,7,128,128]{4,3,2,1,0:T(8,128)(2,1)S(1)} %get-tuple-element.27.edges_ref, bf16[2,128,128]{2,1,0:T(8,128)(2,1)S(1)} %collective-permute-done.near_ref, ...), custom_call_target="tpu_custom_call" | custom-call | tf_op jit(solution)/shard_map/pallas_call | solution.py:266
  10.5 1.6 %collective-permute-start.7 = (bf16[128,1024]{1,0:T(8,128)(2,1)S(1)}, bf16[128,1024]{1,0:T(8,128)(2,1)S(1)}, u32[]{:S(2)}, u32[]{:S(2)}) collective-permute-start(bf16[128,1024]{1,0:T(8,128)(2,1)S(1)} %get-tuple-element.31.image_t_ref), channel_id=1, source_target_pairs={{0,8},{4,12},{8,0},{12,4},{16,24},{20,28},{24,16},{28,20},{1,9},{5... | collective-permute-start | bytes 786440 | tf_op jit(solution)/shard_map/ppermute | solution.py:20
  12.4 1.1 %collective-permute-start.3 = (f32[192,128]{1,0:T(8,128)S(1)}, f32[192,128]{1,0:T(8,128)S(1)}, u32[]{:S(2)}, u32[]{:S(2)}) collective-permute-start(f32[192,128]{1,0:T(8,128)S(1)} %shard_map.48.refs_0_), channel_id=1, source_target_pairs={{0,1},{1,0},{2,3},{3,2},{4,5},{5,4},{6,7},{7,6},{8,9},{9,8},{10,11... | collective-permute-start | bytes 294920 | tf_op jit(solution)/shard_map/ppermute | solution.py:20
  13.5 1.0 %collective-permute-start.4 = (f32[192,128]{1,0:T(8,128)S(1)}, f32[192,128]{1,0:T(8,128)S(1)}, u32[]{:S(2)}, u32[]{:S(2)}) collective-permute-start(f32[192,128]{1,0:T(8,128)S(1)} %shard_map.48.refs_0_), channel_id=1, source_target_pairs={{0,2},{1,3},{2,0},{3,1},{4,6},{5,7},{6,4},{7,5},{8,10},{9,11},{10,... | collective-permute-start | bytes 294920 | tf_op jit(solution)/shard_map/ppermute | solution.py:20
  14.5 1.4 %collective-permute-start.5 = (f32[192,128]{1,0:T(8,128)S(1)}, f32[192,128]{1,0:T(8,128)S(1)}, u32[]{:S(2)}, u32[]{:S(2)}) collective-permute-start(f32[192,128]{1,0:T(8,128)S(1)} %shard_map.48.refs_0_), channel_id=1, source_target_pairs={{0,3},{1,2},{2,1},{3,0},{4,7},{5,6},{6,5},{7,4},{8,11},{9,10},{10,... | collective-permute-start | bytes 294920 | tf_op jit(solution)/shard_map/ppermute | solution.py:20
  16.0 2.7 %collective-permute-start.16 = (bf16[128,1024]{1,0:T(8,128)(2,1)S(1)}, bf16[128,1024]{1,0:T(8,128)(2,1)S(1)}, u32[]{:S(2)}, u32[]{:S(2)}) collective-permute-start(bf16[128,1024]{1,0:T(8,128)(2,1)S(1)} %get-tuple-element.31.image_t_ref), channel_id=1, source_target_pairs={{0,16},{4,20},{8,24},{12,28},{16,0},{20,4},{24,8},{28,12},{1,17},{... | collective-permute-start | bytes 786440 | tf_op jit(solution)/shard_map/ppermute | solution.py:20
  18.6 2.6 %collective-permute-done.7.far_t = bf16[128,1024]{1,0:T(8,128)(2,1)S(1)} collective-permute-done((bf16[128,1024]{1,0:T(8,128)(2,1)S(1)}, bf16[128,1024]{1,0:T(8,128)(2,1)S(1)}, u32[]{:S(2)}, u32[]{:S(2)}) %collective-permute-start.7) | collective-permute-done | bytes 262176 | tf_op jit(solution)/shard_map/ppermute | solution.py:20
  21.2 3.0 %shard_map.49.own_ref.factor_ref = f32[192,128]{1,0:T(8,128)S(1)} custom-call(f32[192,128]{1,0:T(8,128)S(1)} %shard_map.48.refs_0_, f32[192,128]{1,0:T(8,128)S(1)} %collective-permute-done.3.refs_1_, f32[192,128]{1,0:T(8,128)S(1)} %collective-permute-done.4.refs_2_, f32[192,128]{1,0:T(8,128)S(1)} %collective-permute-done.5.refs_3_), custom_call_target="tpu_custom_call" | custom-call | flops 2000000000 | bytes 1000000 | tf_op jit(solution)/shard_map/pallas_call | solution.py:160
  24.2 0.6 collective-permute-start.6
  25.1 0.6 collective-permute-done.6.other_ref
  25.7 3.8 %shard_map.50 = (bf16[2,128,128]{2,1,0:T(8,128)(2,1)S(1)}, f32[256,128]{1,0:T(8,128)S(1)}) custom-call(f32[192,128]{1,0:T(8,128)S(1)} %shard_map.49.own_ref.factor_ref, f32[192,128]{1,0:T(8,128)S(1)} %collective-permute-done.6.other_ref, f32[2,128,128]{2,1,0:T(8,128)S(1)} %get-tuple-element.51.sketch_ref), custom_call_target="tpu_custom_call" | custom-call | flops 2000000000 | bytes 1000000 | tf_op jit(solution)/shard_map/pallas_call | solution.py:160
  29.6 0.7 %shard_map.51 = (bf16[256,128]{1,0:T(8,128)(2,1)S(1)}, bf16[256,128]{1,0:T(8,128)(2,1)S(1)}, bf16[1024,128]{1,0:T(8,128)(2,1)S(1)}) custom-call(f32[256,128]{1,0:T(8,128)S(1)} %get-tuple-element.34.slices_ref.refs_6_, bf16[1024,128]{1,0:T(8,128)(2,1)S(1)} %bitcast.16, bf16[1024,128]{1,0:T(8,128)(2,1)S(1)} %collective-permute-done.2.other_ref.image_other, ...), custom_call_target="tpu_custom_call" | custom-call | flops 2000000000 | bytes 1000000 | tf_op jit(solution)/shard_map/pallas_call | solution.py:160
  31.1 1.2 %collective-permute-start.9 = (bf16[256,128]{1,0:T(8,128)(2,1)S(1)}, bf16[256,128]{1,0:T(8,128)(2,1)S(1)}, u32[]{:S(2)}, u32[]{:S(2)}) collective-permute-start(bf16[256,128]{1,0:T(8,128)(2,1)S(1)} %get-tuple-element.35.refs_0_), channel_id=1, source_target_pairs={{0,1},{1,0},{2,3},{3,2},{4,6},{5,7},{6,4},{7,5},{8,9},{9,8},{10,11... | collective-permute-start | bytes 196616 | tf_op jit(solution)/shard_map/ppermute | solution.py:31
  32.3 1.5 %collective-permute-start.10 = (bf16[256,128]{1,0:T(8,128)(2,1)S(1)}, bf16[256,128]{1,0:T(8,128)(2,1)S(1)}, u32[]{:S(2)}, u32[]{:S(2)}) collective-permute-start(bf16[256,128]{1,0:T(8,128)(2,1)S(1)} %get-tuple-element.36), channel_id=1, source_target_pairs={{0,3},{1,2},{2,1},{3,0},{4,12},{5,13},{6,14},{7,15},{8,11},{9,10},... | collective-permute-start | bytes 196616 | tf_op jit(solution)/shard_map/ppermute | solution.py:31
  33.8 6.1 %collective-permute-done.14.came_ref = bf16[1024,128]{1,0:T(8,128)(2,1)S(1)} collective-permute-done((bf16[1024,128]{1,0:T(8,128)(2,1)S(1)}, bf16[1024,128]{1,0:T(8,128)(2,1)S(1)}, u32[]{:S(2)}, u32[]{:S(2)}) %collective-permute-start.14) | collective-permute-done | bytes 262176 | tf_op jit(solution)/shard_map/ppermute | solution.py:20
  40.5 1.0 %collective-permute-done.11.refs_3_ = bf16[256,128]{1,0:T(8,128)(2,1)S(1)} collective-permute-done((bf16[256,128]{1,0:T(8,128)(2,1)S(1)}, bf16[256,128]{1,0:T(8,128)(2,1)S(1)}, u32[]{:S(2)}, u32[]{:S(2)}) %collective-permute-start.11) | collective-permute-done | bytes 65568 | tf_op jit(solution)/shard_map/ppermute | solution.py:20
  41.6 3.7 %shard_map.52 = (bf16[2,128,128]{2,1,0:T(8,128)(2,1)S(1)}, f32[256,128]{1,0:T(8,128)S(1)}) custom-call(bf16[256,128]{1,0:T(8,128)(2,1)S(1)} %get-tuple-element.35.refs_0_, bf16[256,128]{1,0:T(8,128)(2,1)S(1)} %collective-permute-done.9.refs_1_, bf16[256,128]{1,0:T(8,128)(2,1)S(1)} %collective-permute-done.10.refs_2_, ...), custom_call_target="tpu_custom_call" | custom-call | flops 2000000000 | bytes 1000000 | tf_op jit(solution)/shard_map/pallas_call | solution.py:160
  45.3 0.9 %shard_map.55 = (bf16[256,128]{1,0:T(8,128)(2,1)S(1)}, bf16[256,128]{1,0:T(8,128)(2,1)S(1)}) custom-call(bf16[2,128,128]{2,1,0:T(8,128)(2,1)S(1)} %get-tuple-element.37.halves_ref, f32[256,128]{1,0:T(8,128)S(1)} %get-tuple-element.38.slices_ref, bf16[1024,128]{1,0:T(8,128)(2,1)S(1)} %get-tuple-element.39.refs_0_.image_own, ...), custom_call_target="tpu_custom_call" | custom-call | flops 2000000000 | bytes 1000000 | tf_op jit(solution)/shard_map/pallas_call | solution.py:160
  46.2 1.1 %collective-permute-start.18 = (bf16[256,128]{1,0:T(8,128)(2,1)S(1)}, bf16[256,128]{1,0:T(8,128)(2,1)S(1)}, u32[]{:S(2)}, u32[]{:S(2)}) collective-permute-start(bf16[256,128]{1,0:T(8,128)(2,1)S(1)} %get-tuple-element.42.refs_0_), channel_id=1, source_target_pairs={{0,1},{1,0},{2,3},{3,2},{4,6},{5,7},{6,4},{7,5},{8,9},{9,8},{10,11... | collective-permute-start | bytes 196616 | tf_op jit(solution)/shard_map/ppermute | solution.py:31
  47.7 1.7 %collective-permute-start.23 = (bf16[512,128]{1,0:T(8,128)(2,1)S(1)}, bf16[512,128]{1,0:T(8,128)(2,1)S(1)}, u32[]{:S(2)}, u32[]{:S(2)}) collective-permute-start(bf16[512,128]{1,0:T(8,128)(2,1)S(1)} %get-tuple-element.47), channel_id=1, source_target_pairs={{0,16},{4,20},{8,24},{12,28},{16,0},{20,4},{24,8},{28,12},{1,17},{... | collective-permute-start | bytes 393224 | tf_op jit(solution)/shard_map/ppermute | solution.py:20
  49.3 1.4 %collective-permute-start.19 = (bf16[256,128]{1,0:T(8,128)(2,1)S(1)}, bf16[256,128]{1,0:T(8,128)(2,1)S(1)}, u32[]{:S(2)}, u32[]{:S(2)}) collective-permute-start(bf16[256,128]{1,0:T(8,128)(2,1)S(1)} %get-tuple-element.43), channel_id=1, source_target_pairs={{0,3},{1,2},{2,1},{3,0},{4,20},{5,21},{6,22},{7,23},{8,11},{9,10},... | collective-permute-start | bytes 196616 | tf_op jit(solution)/shard_map/ppermute | solution.py:31
  50.8 3.7 %collective-permute-done.19.refs_2_ = bf16[256,128]{1,0:T(8,128)(2,1)S(1)} collective-permute-done((bf16[256,128]{1,0:T(8,128)(2,1)S(1)}, bf16[256,128]{1,0:T(8,128)(2,1)S(1)}, u32[]{:S(2)}, u32[]{:S(2)}) %collective-permute-start.19) | collective-permute-done | bytes 65568 | tf_op jit(solution)/shard_map/ppermute | solution.py:31
  54.5 3.4 %collective-permute-start.21 = (bf16[256,128]{1,0:T(8,128)(2,1)S(1)}, bf16[256,128]{1,0:T(8,128)(2,1)S(1)}, u32[]{:S(2)}, u32[]{:S(2)}) collective-permute-start(bf16[256,128]{1,0:T(8,128)(2,1)S(1)} %collective-permute-done.19.refs_2_), channel_id=1, source_target_pairs={{0,4},{4,0},{8,12},{12,8},{16,20},{20,16},{24,28},{28,24},{1,5},{5... | collective-permute-start | bytes 196616 | tf_op jit(solution)/shard_map/ppermute | solution.py:20
  57.9 0.9 %collective-permute-done.21.refs_4_ = bf16[256,128]{1,0:T(8,128)(2,1)S(1)} collective-permute-done((bf16[256,128]{1,0:T(8,128)(2,1)S(1)}, bf16[256,128]{1,0:T(8,128)(2,1)S(1)}, u32[]{:S(2)}, u32[]{:S(2)}) %collective-permute-start.21) | collective-permute-done | bytes 65568 | tf_op jit(solution)/shard_map/ppermute | solution.py:20
  59.1 3.9 %collective-permute-done.22.refs_1_ = bf16[128,128]{1,0:T(8,128)(2,1)S(1)} collective-permute-done((bf16[128,128]{1,0:T(8,128)(2,1)S(1)}, bf16[128,128]{1,0:T(8,128)(2,1)S(1)}, u32[]{:S(2)}, u32[]{:S(2)}) %collective-permute-start.22) | collective-permute-done | bytes 32800 | tf_op jit(solution)/shard_map/ppermute | solution.py:20
  63.0 3.8 %shard_map.58 = (bf16[2,128,128]{2,1,0:T(8,128)(2,1)S(1)}, bf16[4,1024,128]{2,1,0:T(8,128)(2,1)}) custom-call(bf16[128,128]{1,0:T(8,128)(2,1)S(1)} %shard_map.56.refs_0_, bf16[128,128]{1,0:T(8,128)(2,1)S(1)} %collective-permute-done.22.refs_1_, f32[2,128,128]{2,1,0:T(8,128)S(1)} %get-tuple-element.49.refs_2_, ...), custom_call_target="tpu_custom_call" | custom-call | tf_op jit(solution)/shard_map/pallas_call | solution.py:476
  66.8 1.0 %shard_map.59 = bf16[4,1024,128]{2,1,0:T(8,128)(2,1)} custom-call(bf16[2,128,128]{2,1,0:T(8,128)(2,1)S(1)} %get-tuple-element.46.halves_ref, bf16[1024,128]{1,0:T(8,128)(2,1)S(1)} %get-tuple-element.45.refs_5_.modes_own, bf16[512,128]{1,0:T(8,128)(2,1)S(1)} %collective-permute-done.23.came_ref, ...), custom_call_target="tpu_custom_call", output_to_operand_aliasing={{}: (4, {})} | custom-call | tf_op jit(solution)/shard_map/pallas_call | solution.py:489
  (36 shorter events, 2.9 us)
Async XLA Ops:
  0.0 9.1 %copy-start = (s32[8,7]{1,0:T(8,128)S(1)}, s32[8,7]{1,0:T(8,128)}, u32[]{:S(2)}) copy-start(s32[8,7]{1,0:T(8,128)} %index_ref.1) | copy-start | bytes 676
  0.9 6.4 %collective-permute-start = (bf16[2,128,128]{2,1,0:T(8,128)(2,1)S(1)}, bf16[2,128,128]{2,1,0:T(8,128)(2,1)S(1)}, u32[]{:S(2)}, u32[]{:S(2)}) collective-permute-start(bf16[2,128,128]{2,1,0:T(8,128)(2,1)S(1)} %bitcast.19), channel_id=1, source_target_pairs={{0,1},{1,0},{2,3},{3,2},{4,5},{5,4},{6,7},{7,6},{8,9},{9,8},{10,11... | collective-permute-start | bytes 196616 | tf_op jit(solution)/shard_map/ppermute | solution.py:516
  3.9 5.2 %collective-permute-start.1 = (bf16[2,128,128]{2,1,0:T(8,128)(2,1)S(1)}, bf16[2,128,128]{2,1,0:T(8,128)(2,1)S(1)}, u32[]{:S(2)}, u32[]{:S(2)}) collective-permute-start(bf16[2,128,128]{2,1,0:T(8,128)(2,1)S(1)} %bitcast.18), channel_id=1, source_target_pairs={{0,3},{1,2},{2,1},{3,0},{4,7},{5,6},{6,5},{7,4},{8,11},{9,10},{10,... | collective-permute-start | bytes 196616 | tf_op jit(solution)/shard_map/ppermute | solution.py:517
  10.4 1.7 %collective-permute-start.2 = (bf16[1024,128]{1,0:T(8,128)(2,1)S(1)}, bf16[1024,128]{1,0:T(8,128)(2,1)S(1)}, u32[]{:S(2)}, u32[]{:S(2)}) collective-permute-start(bf16[1024,128]{1,0:T(8,128)(2,1)S(1)} %bitcast.15), channel_id=1, source_target_pairs={{0,4},{4,0},{8,12},{12,8},{16,20},{20,16},{24,28},{28,24},{1,5},{5... | collective-permute-start | bytes 786440 | tf_op jit(solution)/shard_map/ppermute | solution.py:20
  10.5 10.7 %collective-permute-start.7 = (bf16[128,1024]{1,0:T(8,128)(2,1)S(1)}, bf16[128,1024]{1,0:T(8,128)(2,1)S(1)}, u32[]{:S(2)}, u32[]{:S(2)}) collective-permute-start(bf16[128,1024]{1,0:T(8,128)(2,1)S(1)} %get-tuple-element.31.image_t_ref), channel_id=1, source_target_pairs={{0,8},{4,12},{8,0},{12,4},{16,24},{20,28},{24,16},{28,20},{1,9},{5... | collective-permute-start | bytes 786440 | tf_op jit(solution)/shard_map/ppermute | solution.py:20
  12.4 8.8 %collective-permute-start.3 = (f32[192,128]{1,0:T(8,128)S(1)}, f32[192,128]{1,0:T(8,128)S(1)}, u32[]{:S(2)}, u32[]{:S(2)}) collective-permute-start(f32[192,128]{1,0:T(8,128)S(1)} %shard_map.48.refs_0_), channel_id=1, source_target_pairs={{0,1},{1,0},{2,3},{3,2},{4,5},{5,4},{6,7},{7,6},{8,9},{9,8},{10,11... | collective-permute-start | bytes 294920 | tf_op jit(solution)/shard_map/ppermute | solution.py:20
  13.5 7.7 %collective-permute-start.4 = (f32[192,128]{1,0:T(8,128)S(1)}, f32[192,128]{1,0:T(8,128)S(1)}, u32[]{:S(2)}, u32[]{:S(2)}) collective-permute-start(f32[192,128]{1,0:T(8,128)S(1)} %shard_map.48.refs_0_), channel_id=1, source_target_pairs={{0,2},{1,3},{2,0},{3,1},{4,6},{5,7},{6,4},{7,5},{8,10},{9,11},{10,... | collective-permute-start | bytes 294920 | tf_op jit(solution)/shard_map/ppermute | solution.py:20
  14.5 6.7 %collective-permute-start.5 = (f32[192,128]{1,0:T(8,128)S(1)}, f32[192,128]{1,0:T(8,128)S(1)}, u32[]{:S(2)}, u32[]{:S(2)}) collective-permute-start(f32[192,128]{1,0:T(8,128)S(1)} %shard_map.48.refs_0_), channel_id=1, source_target_pairs={{0,3},{1,2},{2,1},{3,0},{4,7},{5,6},{6,5},{7,4},{8,11},{9,10},{10,... | collective-permute-start | bytes 294920 | tf_op jit(solution)/shard_map/ppermute | solution.py:20
  16.0 17.8 %collective-permute-start.16 = (bf16[128,1024]{1,0:T(8,128)(2,1)S(1)}, bf16[128,1024]{1,0:T(8,128)(2,1)S(1)}, u32[]{:S(2)}, u32[]{:S(2)}) collective-permute-start(bf16[128,1024]{1,0:T(8,128)(2,1)S(1)} %get-tuple-element.31.image_t_ref), channel_id=1, source_target_pairs={{0,16},{4,20},{8,24},{12,28},{16,0},{20,4},{24,8},{28,12},{1,17},{... | collective-permute-start | bytes 786440 | tf_op jit(solution)/shard_map/ppermute | solution.py:20
  21.2 8.4 %collective-permute-start.8 = (bf16[128,1024]{1,0:T(8,128)(2,1)S(1)}, bf16[128,1024]{1,0:T(8,128)(2,1)S(1)}, u32[]{:S(2)}, u32[]{:S(2)}) collective-permute-start(bf16[128,1024]{1,0:T(8,128)(2,1)S(1)} %collective-permute-done.7.far_t), channel_id=1, source_target_pairs={{0,4},{4,0},{8,12},{12,8},{16,20},{20,16},{24,28},{28,24},{1,5},{5... | collective-permute-start | bytes 786440 | tf_op jit(solution)/shard_map/ppermute | solution.py:20
  24.2 1.5 %collective-permute-start.6 = (f32[192,128]{1,0:T(8,128)S(1)}, f32[192,128]{1,0:T(8,128)S(1)}, u32[]{:S(2)}, u32[]{:S(2)}) collective-permute-start(f32[192,128]{1,0:T(8,128)S(1)} %shard_map.49.own_ref.factor_ref), channel_id=1, source_target_pairs={{0,4},{4,0},{8,12},{12,8},{16,20},{20,16},{24,28},{28,24},{1,5},{5... | collective-permute-start | bytes 294920 | tf_op jit(solution)/shard_map/ppermute | solution.py:20
  25.0 5.3 %collective-permute-start.13 = (bf16[1024,128]{1,0:T(8,128)(2,1)S(1)}, bf16[1024,128]{1,0:T(8,128)(2,1)S(1)}, u32[]{:S(2)}, u32[]{:S(2)}) collective-permute-start(bf16[1024,128]{1,0:T(8,128)(2,1)S(1)} %shard_map.53.modes_own.refs_3_), channel_id=1, source_target_pairs={{0,4},{4,0},{8,12},{12,8},{16,20},{20,16},{24,28},{28,24},{1,5},{5... | collective-permute-start | bytes 786440 | tf_op jit(solution)/shard_map/ppermute | solution.py:20
  30.6 9.2 %collective-permute-start.14 = (bf16[1024,128]{1,0:T(8,128)(2,1)S(1)}, bf16[1024,128]{1,0:T(8,128)(2,1)S(1)}, u32[]{:S(2)}, u32[]{:S(2)}) collective-permute-start(bf16[1024,128]{1,0:T(8,128)(2,1)S(1)} %get-tuple-element.41), channel_id=1, source_target_pairs={{0,8},{4,12},{8,0},{12,4},{16,24},{20,28},{24,16},{28,20},{1,9},{5... | collective-permute-start | bytes 786440 | tf_op jit(solution)/shard_map/ppermute | solution.py:20
  31.1 8.7 %collective-permute-start.9 = (bf16[256,128]{1,0:T(8,128)(2,1)S(1)}, bf16[256,128]{1,0:T(8,128)(2,1)S(1)}, u32[]{:S(2)}, u32[]{:S(2)}) collective-permute-start(bf16[256,128]{1,0:T(8,128)(2,1)S(1)} %get-tuple-element.35.refs_0_), channel_id=1, source_target_pairs={{0,1},{1,0},{2,3},{3,2},{4,6},{5,7},{6,4},{7,5},{8,9},{9,8},{10,11... | collective-permute-start | bytes 196616 | tf_op jit(solution)/shard_map/ppermute | solution.py:31
  32.3 8.1 %collective-permute-start.10 = (bf16[256,128]{1,0:T(8,128)(2,1)S(1)}, bf16[256,128]{1,0:T(8,128)(2,1)S(1)}, u32[]{:S(2)}, u32[]{:S(2)}) collective-permute-start(bf16[256,128]{1,0:T(8,128)(2,1)S(1)} %get-tuple-element.36), channel_id=1, source_target_pairs={{0,3},{1,2},{2,1},{3,0},{4,12},{5,13},{6,14},{7,15},{8,11},{9,10},... | collective-permute-start | bytes 196616 | tf_op jit(solution)/shard_map/ppermute | solution.py:31
  33.8 11.5 %collective-permute-start.17 = (bf16[128,1024]{1,0:T(8,128)(2,1)S(1)}, bf16[128,1024]{1,0:T(8,128)(2,1)S(1)}, u32[]{:S(2)}, u32[]{:S(2)}) collective-permute-start(bf16[128,1024]{1,0:T(8,128)(2,1)S(1)} %collective-permute-done.16.far_t), channel_id=1, source_target_pairs={{0,4},{4,0},{8,12},{12,8},{16,20},{20,16},{24,28},{28,24},{1,5},{5... | collective-permute-start | bytes 786440 | tf_op jit(solution)/shard_map/ppermute | solution.py:20
  39.9 5.5 %collective-permute-start.15 = (bf16[1024,128]{1,0:T(8,128)(2,1)S(1)}, bf16[1024,128]{1,0:T(8,128)(2,1)S(1)}, u32[]{:S(2)}, u32[]{:S(2)}) collective-permute-start(bf16[1024,128]{1,0:T(8,128)(2,1)S(1)} %collective-permute-done.14.came_ref), channel_id=1, source_target_pairs={{0,4},{4,0},{8,12},{12,8},{16,20},{20,16},{24,28},{28,24},{1,5},{5... | collective-permute-start | bytes 786440 | tf_op jit(solution)/shard_map/ppermute | solution.py:20
  39.9 1.6 %collective-permute-start.11 = (bf16[256,128]{1,0:T(8,128)(2,1)S(1)}, bf16[256,128]{1,0:T(8,128)(2,1)S(1)}, u32[]{:S(2)}, u32[]{:S(2)}) collective-permute-start(bf16[256,128]{1,0:T(8,128)(2,1)S(1)} %collective-permute-done.9.refs_1_), channel_id=1, source_target_pairs={{0,4},{4,0},{8,12},{12,8},{16,20},{20,16},{24,28},{28,24},{1,5},{5... | collective-permute-start | bytes 196616 | tf_op jit(solution)/shard_map/ppermute | solution.py:20
  40.4 1.3 %collective-permute-start.12 = (bf16[256,128]{1,0:T(8,128)(2,1)S(1)}, bf16[256,128]{1,0:T(8,128)(2,1)S(1)}, u32[]{:S(2)}, u32[]{:S(2)}) collective-permute-start(bf16[256,128]{1,0:T(8,128)(2,1)S(1)} %collective-permute-done.10.refs_2_), channel_id=1, source_target_pairs={{0,4},{4,0},{8,12},{12,8},{16,20},{20,16},{24,28},{28,24},{1,5},{5... | collective-permute-start | bytes 196616 | tf_op jit(solution)/shard_map/ppermute | solution.py:20
  46.2 4.5 %collective-permute-start.18 = (bf16[256,128]{1,0:T(8,128)(2,1)S(1)}, bf16[256,128]{1,0:T(8,128)(2,1)S(1)}, u32[]{:S(2)}, u32[]{:S(2)}) collective-permute-start(bf16[256,128]{1,0:T(8,128)(2,1)S(1)} %get-tuple-element.42.refs_0_), channel_id=1, source_target_pairs={{0,1},{1,0},{2,3},{3,2},{4,6},{5,7},{6,4},{7,5},{8,9},{9,8},{10,11... | collective-permute-start | bytes 196616 | tf_op jit(solution)/shard_map/ppermute | solution.py:31
  47.7 10.2 %collective-permute-start.23 = (bf16[512,128]{1,0:T(8,128)(2,1)S(1)}, bf16[512,128]{1,0:T(8,128)(2,1)S(1)}, u32[]{:S(2)}, u32[]{:S(2)}) collective-permute-start(bf16[512,128]{1,0:T(8,128)(2,1)S(1)} %get-tuple-element.47), channel_id=1, source_target_pairs={{0,16},{4,20},{8,24},{12,28},{16,0},{20,4},{24,8},{28,12},{1,17},{... | collective-permute-start | bytes 393224 | tf_op jit(solution)/shard_map/ppermute | solution.py:20
  49.3 5.2 %collective-permute-start.19 = (bf16[256,128]{1,0:T(8,128)(2,1)S(1)}, bf16[256,128]{1,0:T(8,128)(2,1)S(1)}, u32[]{:S(2)}, u32[]{:S(2)}) collective-permute-start(bf16[256,128]{1,0:T(8,128)(2,1)S(1)} %get-tuple-element.43), channel_id=1, source_target_pairs={{0,3},{1,2},{2,1},{3,0},{4,20},{5,21},{6,22},{7,23},{8,11},{9,10},... | collective-permute-start | bytes 196616 | tf_op jit(solution)/shard_map/ppermute | solution.py:31
  50.8 7.1 %collective-permute-start.20 = (bf16[256,128]{1,0:T(8,128)(2,1)S(1)}, bf16[256,128]{1,0:T(8,128)(2,1)S(1)}, u32[]{:S(2)}, u32[]{:S(2)}) collective-permute-start(bf16[256,128]{1,0:T(8,128)(2,1)S(1)} %collective-permute-done.18.refs_1_), channel_id=1, source_target_pairs={{0,4},{4,0},{8,12},{12,8},{16,20},{20,16},{24,28},{28,24},{1,5},{5... | collective-permute-start | bytes 196616 | tf_op jit(solution)/shard_map/ppermute | solution.py:20
  54.5 4.3 %collective-permute-start.21 = (bf16[256,128]{1,0:T(8,128)(2,1)S(1)}, bf16[256,128]{1,0:T(8,128)(2,1)S(1)}, u32[]{:S(2)}, u32[]{:S(2)}) collective-permute-start(bf16[256,128]{1,0:T(8,128)(2,1)S(1)} %collective-permute-done.19.refs_2_), channel_id=1, source_target_pairs={{0,4},{4,0},{8,12},{12,8},{16,20},{20,16},{24,28},{28,24},{1,5},{5... | collective-permute-start | bytes 196616 | tf_op jit(solution)/shard_map/ppermute | solution.py:20
  57.9 8.9 %collective-permute-start.24 = (bf16[512,128]{1,0:T(8,128)(2,1)S(1)}, bf16[512,128]{1,0:T(8,128)(2,1)S(1)}, u32[]{:S(2)}, u32[]{:S(2)}) collective-permute-start(bf16[512,128]{1,0:T(8,128)(2,1)S(1)} %collective-permute-done.23.came_ref), channel_id=1, source_target_pairs={{0,4},{4,0},{8,12},{12,8},{16,20},{20,16},{24,28},{28,24},{1,5},{5... | collective-permute-start | bytes 393224 | tf_op jit(solution)/shard_map/ppermute | solution.py:20
  59.0 4.0 %collective-permute-start.22 = (bf16[128,128]{1,0:T(8,128)(2,1)S(1)}, bf16[128,128]{1,0:T(8,128)(2,1)S(1)}, u32[]{:S(2)}, u32[]{:S(2)}) collective-permute-start(bf16[128,128]{1,0:T(8,128)(2,1)S(1)} %shard_map.56.refs_0_), channel_id=1, source_target_pairs={{0,8},{4,12},{8,0},{12,4},{16,24},{20,28},{24,16},{28,20},{1,9},{5... | collective-permute-start | bytes 98312 | tf_op jit(solution)/shard_map/ppermute | solution.py:20

commit v10 on v9

--- a/solution.py
+++ b/solution.py
@@ -170,7 +170,8 @@
 
 def interior_kernel(
     index_hbm, energy_hbm, blocks_hbm, sketch_hbm,
-    image_ref, sketch_out, edges_ref, blocks_ref, index_ref, energy_ref, sketch_ref, sems,
+    image_ref, image_t_ref, gram_ref, sketch_out, edges_ref, blocks_ref,
+    index_ref, energy_ref, sketch_ref, sems,
 ):
     count = blocks_ref.shape[0]
     inner, slots = energy_ref.shape[:2]
@@ -200,6 +201,10 @@
             energy_ref, place, slots, lambda slot: blocks_ref[index_ref[b, slot] - first]
         )
         image_ref[place] = value.astype(BF16)
+    image = image_ref[...].reshape(image_t_ref.shape[1], image_t_ref.shape[0])
+    image_t = image.T
+    image_t_ref[...] = image_t
+    gram_ref[...] = dot_nn(image_t, image)
     copies[3].wait()
     for level in range(sketch_ref.shape[0]):
         upper = window // 2**level % 2
@@ -211,7 +216,7 @@
 
 
 def edge_kernel(
-    index_ref, edges_ref, near_ref, blocks_ref, wide_ref, inner_ref,
+    index_ref, edges_ref, near_ref, blocks_ref, wide_ref, inner_ref, inner_t_ref, inner_gram_ref,
     image_ref, image_t_ref, gram_ref, padded_ref,
 ):
     slots = edges_ref.shape[2]
@@ -222,19 +227,26 @@
     padded_ref[1, : 2 * HB] = blocks_ref[blocks - 2 * HB :]
     padded_ref[1, 2 * HB :] = after
     image_ref[HB : blocks - HB] = inner_ref[...]
+    width = gram_ref.shape[0]
+    reach = HB * image_ref.shape[1]
+    image_t_ref[:, reach : image_t_ref.shape[1] - reach] = inner_t_ref[...]
+    gram = inner_gram_ref[...]
     for side in range(2):
         first = lax.axis_index("space") * blocks - HB + side * (blocks - HB)
+        start = side * (blocks - HB)
         for place in range(HB):
-            b = side * (blocks - HB) + place
+            b = start + place
             value = 3.0 * blocks_ref[b].astype(F32) + coupled(
                 edges_ref.at[side], place, slots,
                 lambda slot: padded_ref[side, index_ref[b, slot] - first],
             )
             image_ref[b] = value.astype(BF16)
-    image = image_ref[...].reshape(image_t_ref.shape[1], image_t_ref.shape[0])
-    image_t = image.T
-    image_t_ref[...] = image_t
-    gram_ref[...] = dot_nn(image_t, image)
+        image = image_ref[start : start + HB].reshape(reach, width)
+        image_t = image.T
+        offset = start * image_ref.shape[1]
+        image_t_ref[:, offset : offset + reach] = image_t
+        gram = gram + dot_nn(image_t, image)
+    gram_ref[...] = gram
 
 
 def interior_of(neighbours, energy, blocks, sketch):
@@ -246,6 +258,8 @@
         interior_kernel,
         out_shape=[
             jax.ShapeDtypeStruct((inner, rows, width), BF16),
+            jax.ShapeDtypeStruct((width, inner * rows), BF16),
+            jax.ShapeDtypeStruct((width, width), F32),
             jax.ShapeDtypeStruct((levels, 2, width, width), F32),
             jax.ShapeDtypeStruct((2, HB, slots, rows, rows), BF16),
             jax.ShapeDtypeStruct(blocks.shape, BF16),
@@ -261,7 +275,7 @@
     )(*[pltpu.with_memory_space_constraint(item, pltpu.HBM) for item in (neighbours, energy, blocks, sketch)])
 
 
-def edge_of(neighbours, edges, came_near, blocks, came_wide, inner):
+def edge_of(neighbours, edges, came_near, blocks, came_wide, *inner):
     count, rows, width = blocks.shape
     image, image_t, gram = pl.pallas_call(
         edge_kernel,
@@ -271,10 +285,10 @@
             jax.ShapeDtypeStruct((width, width), F32),
         ],
         in_specs=[pl.BlockSpec(memory_space=pltpu.SMEM)]
-        + [pl.BlockSpec(memory_space=pltpu.VMEM)] * 5,
+        + [pl.BlockSpec(memory_space=pltpu.VMEM)] * 7,
         scratch_shapes=[pltpu.VMEM((2, 3 * HB, rows, width), BF16)],
         compiler_params=PARAMS,
-    )(neighbours, edges, came_near, blocks, came_wide, inner)
+    )(neighbours, edges, came_near, blocks, came_wide, *inner)
     return image.reshape(count * rows, width), image_t, gram
 
 
@@ -333,13 +347,6 @@
     else:
         part = outgoing_ref.shape[0]
         outgoing_ref[...] = choose("tm", modes[:part], modes[part:])[0]
-
-
-def read_modes(came_ref, shared_ref, rows):
-    first, second = choose("tm", came_ref[...], shared_ref[...])
-    if first.shape[0] == rows:
-        return first
-    return jnp.concatenate([first, second], axis=0)
 
 
 def first_merge_kernel(own_ref, other_ref, sketch_ref, halves_ref, slices_ref):
@@ -446,26 +453,17 @@
     write_bulk((modes_ref, outgoing_ref), modes, image_ref[0] if image_ref else None)
 
 
-def output_kernel(halves_ref, modes_own, came_ref, shared_ref, _, out_ref, modes_ref, sems):
-    rows = modes_own.shape[0]
-    modes_other = read_modes(came_ref, shared_ref, rows)
-    part = rows // 2
-    copies = []
-    for half in range(2):
-        span = slice(half * part, (half + 1) * part)
-        modes_ref[span] = combined(
-            modes_own[span], modes_other[span], halves_ref[0], halves_ref[1]
-        )
-        copies.append(
-            pltpu.make_async_copy(
-                modes_ref.at[pl.ds(half * part, part)],
-                out_ref.at[out_ref.shape[0] - 1, pl.ds(half * part, part)],
-                sems.at[half],
-            )
-        )
-        copies[-1].start()
-    for copy in copies:
-        copy.wait()
+def output_kernel(side, halves_ref, modes_own, modes_other, _, out_ref, modes_ref, sem):
+    part = modes_other.shape[0]
+    start = pl.multiple_of((lax.axis_index("tm") + side) % 2 * part, part)
+    modes_ref[...] = combined(
+        modes_own[pl.ds(start, part)], modes_other[...], halves_ref[0], halves_ref[1]
+    )
+    copy = pltpu.make_async_copy(
+        modes_ref, out_ref.at[out_ref.shape[0] - 1, pl.ds(start, part)], sem
+    )
+    copy.start()
+    copy.wait()
 
 
 def last_level(parts, sketch_t, kept, halves_shape):
@@ -483,18 +481,18 @@
     )(*parts, sketch_t, *kept)
 
 
-def last_modes(halves, modes, came, shared, out):
+def last_modes(side, halves, modes, came, out):
     vmem = pl.BlockSpec(memory_space=pltpu.VMEM)
     hbm = pl.BlockSpec(memory_space=pltpu.HBM)
     return pl.pallas_call(
-        output_kernel,
+        functools.partial(output_kernel, side),
         out_shape=jax.ShapeDtypeStruct(out.shape, BF16),
-        in_specs=[vmem] * 4 + [hbm],
+        in_specs=[vmem] * 3 + [hbm],
         out_specs=hbm,
-        scratch_shapes=[pltpu.VMEM(modes.shape, BF16), pltpu.SemaphoreType.DMA((2,))],
-        input_output_aliases={4: 0},
+        scratch_shapes=[pltpu.VMEM(came.shape, BF16), pltpu.SemaphoreType.DMA],
+        input_output_aliases={3: 0},
         compiler_params=PARAMS,
-    )(halves, modes, came, shared, out)
+    )(halves, modes, came, out)
 
 
 def cross_kernel(total_rows, *refs):
@@ -523,8 +521,8 @@
     slices_shape = jax.ShapeDtypeStruct((2 * width, width), F32)
     halves_shape = jax.ShapeDtypeStruct((2, width, width), BF16)
 
-    inner, sketch_t, edges, blocks = interior_of(neighbours, energy, blocks, sketch)
-    image, image_t, gram = edge_of(neighbours, edges, came_near, blocks, came_wide, inner)
+    *inner, sketch_t, edges, blocks = interior_of(neighbours, energy, blocks, sketch)
+    image, image_t, gram = edge_of(neighbours, edges, came_near, blocks, came_wide, *inner)
     other_image = swap(image, "tm", 1)
     pair = run_kernel(
         pair_kernel,
@@ -583,7 +581,8 @@
                 *parts, sketch_t[level], slices,
             )
         if last:
-            out = last_modes(halves, modes, came, shared, out)
+            out = last_modes(0, halves, modes, came, out)
+            out = last_modes(1, halves, modes, shared, out)
             break
         far = far_images[level]
         far_shared = swap(far, "tm", 1)

time: 68.2 us -> 69.1 us (1.013)
  Pallas kernels: 21.5 us -> 22.7 us
    pallas_call x1 -> x2, Pallas kernels: 1.02 us -> 1.79 us  [last_modes(): pl.pallas_call(functools.partial(output_kernel, side), out_shape=jax.Shap...]
  transfers between devices with their start and end apart: 25 -> 25, of which waited for: 9 -> 9; matrix products, arithmetic and copies ran while one was open for 0% -> 0% of each run, Pallas kernels for 27% -> 28%
where the time goes in v10:
time: 69.1 us; the launch traced here: 68.9 us
  starting transfers between devices  24.4 us (35%)
  Pallas kernels  22.7 us (33%)
  waiting for transfers between devices  20.6 us (30%)
  other arithmetic  0.9 us (1%)
    ppermute x19, waiting for transfers between devices, swap(): return lax.ppermute(value, axis, pairs)  15.3 us
    ppermute x19, starting transfers between devices, swap(): return lax.ppermute(value, axis, pairs)  14.7 us
    pallas_call x10, Pallas kernels, run_kernel(): pl.pallas_call(body, out_shape=outs, cost_estimate=cost, compiler_params=...  13.5 us
    ppermute x4, starting transfers between devices, mixed_swap(): return lax.ppermute(value, ('tm', 'space'), pairs)  5.15 us
    pallas_call x1, Pallas kernels, last_level(): pl.pallas_call(functools.partial(last_merge_kernel, len(parts)), out_shap...  3.82 us
    ppermute x4, waiting for transfers between devices, mixed_swap(): return lax.ppermute(value, ('tm', 'space'), pairs)  3.71 us
    ppermute x1, starting transfers between devices, modes_of(): came_near = lax.ppermute(jnp.where(odd, head, tail), 'space', near)  3.03 us
    pallas_call x1, Pallas kernels, interior_of(): pl.pallas_call(interior_kernel, out_shape=[jax.ShapeDtypeStruct((inner, r...  2.11 us
  transfers between devices with their start and end apart: 25, of which 9 were waited for; matrix products, arithmetic and copies ran while one was open for 0% of the time, Pallas kernels for 28%

profile of v10, /device:TPU:0, one launch (start us, length us, event | category | flops | bytes accessed | tf_op | source)
XLA Modules:
  0.0 68.9 jit_solution(2779397247787664432)
XLA Ops:
  0.0 0.9 %broadcast_select_fusion = (bf16[256,128]{1,0:T(8,128)(2,1)S(1)}, bf16[256,128]{1,0:T(8,128)(2,1)S(1)}) fusion(pred[]{:T(512)S(6)} %eq.3, bf16[1024,128]{1,0:T(8,128)(2,1)} %param.4), kind=kLoop, calls=%fused_computation.3 | loop fusion | flops 65536 | bytes 262145 | tf_op jit(solution)/shard_map/jit(_where)/select_n | solution.py:515
  0.9 3.0 %collective-permute-start = (bf16[2,128,128]{2,1,0:T(8,128)(2,1)S(1)}, bf16[2,128,128]{2,1,0:T(8,128)(2,1)S(1)}, u32[]{:S(2)}, u32[]{:S(2)}) collective-permute-start(bf16[2,128,128]{2,1,0:T(8,128)(2,1)S(1)} %bitcast.19), channel_id=1, source_target_pairs={{0,1},{1,0},{2,3},{3,2},{4,5},{5,4},{6,7},{7,6},{8,9},{9,8},{10,11... | collective-permute-start | bytes 196616 | tf_op jit(solution)/shard_map/ppermute | solution.py:514
  3.9 1.5 %collective-permute-start.1 = (bf16[2,128,128]{2,1,0:T(8,128)(2,1)S(1)}, bf16[2,128,128]{2,1,0:T(8,128)(2,1)S(1)}, u32[]{:S(2)}, u32[]{:S(2)}) collective-permute-start(bf16[2,128,128]{2,1,0:T(8,128)(2,1)S(1)} %bitcast.18), channel_id=1, source_target_pairs={{0,3},{1,2},{2,1},{3,0},{4,7},{5,6},{6,5},{7,4},{8,11},{9,10},{10,... | collective-permute-start | bytes 196616 | tf_op jit(solution)/shard_map/ppermute | solution.py:515
  5.4 2.1 %shard_map.46 = (bf16[4,128,128]{2,1,0:T(8,128)(2,1)S(1)}, bf16[128,512]{1,0:T(8,128)(2,1)S(1)}, f32[128,128]{1,0:T(8,128)S(1)}, f32[3,2,128,128]{3,2,1,0:T(8,12...) custom-call(s32[8,7]{1,0:T(8,128)} %index_ref.1, bf16[8,7,128,128]{3,2,1,0:T(8,128)(2,1)} %energy_hbm.1, ...), custom_call_target="tpu_custom_call" | custom-call | tf_op jit(solution)/shard_map/pallas_call | solution.py:257
  7.6 1.5 %collective-permute-done.1.wide_ref = bf16[2,128,128]{2,1,0:T(8,128)(2,1)S(1)} collective-permute-done((bf16[2,128,128]{2,1,0:T(8,128)(2,1)S(1)}, bf16[2,128,128]{2,1,0:T(8,128)(2,1)S(1)}, u32[]{:S(2)}, u32[]{:S(2)}) %collective-permute-start.1) | collective-permute-done | bytes 65568 | tf_op jit(solution)/shard_map/ppermute | solution.py:515
  9.1 1.5 %shard_map.47 = (bf16[8,128,128]{2,1,0:T(8,128)(2,1)S(1)}, bf16[128,1024]{1,0:T(8,128)(2,1)S(1)}, f32[128,128]{1,0:T(8,128)S(1)}) custom-call(s32[8,7]{1,0:T(8,128)S(1)} %copy-done, bf16[2,2,7,128,128]{4,3,2,1,0:T(8,128)(2,1)S(1)} %get-tuple-element.29.edges_ref, bf16[2,128,128]{2,1,0:T(8,128)(2,1)S(1)} %collective-permute-done.near_ref, ...), custom_call_target="tpu_custom_call" | custom-call | tf_op jit(solution)/shard_map/pallas_call | solution.py:280
  10.7 1.6 %collective-permute-start.7 = (bf16[128,1024]{1,0:T(8,128)(2,1)S(1)}, bf16[128,1024]{1,0:T(8,128)(2,1)S(1)}, u32[]{:S(2)}, u32[]{:S(2)}) collective-permute-start(bf16[128,1024]{1,0:T(8,128)(2,1)S(1)} %get-tuple-element.35.image_t_ref), channel_id=1, source_target_pairs={{0,8},{4,12},{8,0},{12,4},{16,24},{20,28},{24,16},{28,20},{1,9},{5... | collective-permute-start | bytes 786440 | tf_op jit(solution)/shard_map/ppermute | solution.py:20
  12.6 1.1 %collective-permute-start.3 = (f32[192,128]{1,0:T(8,128)S(1)}, f32[192,128]{1,0:T(8,128)S(1)}, u32[]{:S(2)}, u32[]{:S(2)}) collective-permute-start(f32[192,128]{1,0:T(8,128)S(1)} %shard_map.48.refs_0_), channel_id=1, source_target_pairs={{0,1},{1,0},{2,3},{3,2},{4,5},{5,4},{6,7},{7,6},{8,9},{9,8},{10,11... | collective-permute-start | bytes 294920 | tf_op jit(solution)/shard_map/ppermute | solution.py:20
  13.7 1.0 %collective-permute-start.4 = (f32[192,128]{1,0:T(8,128)S(1)}, f32[192,128]{1,0:T(8,128)S(1)}, u32[]{:S(2)}, u32[]{:S(2)}) collective-permute-start(f32[192,128]{1,0:T(8,128)S(1)} %shard_map.48.refs_0_), channel_id=1, source_target_pairs={{0,2},{1,3},{2,0},{3,1},{4,6},{5,7},{6,4},{7,5},{8,10},{9,11},{10,... | collective-permute-start | bytes 294920 | tf_op jit(solution)/shard_map/ppermute | solution.py:20
  14.7 1.4 %collective-permute-start.5 = (f32[192,128]{1,0:T(8,128)S(1)}, f32[192,128]{1,0:T(8,128)S(1)}, u32[]{:S(2)}, u32[]{:S(2)}) collective-permute-start(f32[192,128]{1,0:T(8,128)S(1)} %shard_map.48.refs_0_), channel_id=1, source_target_pairs={{0,3},{1,2},{2,1},{3,0},{4,7},{5,6},{6,5},{7,4},{8,11},{9,10},{10,... | collective-permute-start | bytes 294920 | tf_op jit(solution)/shard_map/ppermute | solution.py:20
  16.2 2.7 %collective-permute-start.16 = (bf16[128,1024]{1,0:T(8,128)(2,1)S(1)}, bf16[128,1024]{1,0:T(8,128)(2,1)S(1)}, u32[]{:S(2)}, u32[]{:S(2)}) collective-permute-start(bf16[128,1024]{1,0:T(8,128)(2,1)S(1)} %get-tuple-element.35.image_t_ref), channel_id=1, source_target_pairs={{0,16},{4,20},{8,24},{12,28},{16,0},{20,4},{24,8},{28,12},{1,17},{... | collective-permute-start | bytes 786440 | tf_op jit(solution)/shard_map/ppermute | solution.py:20
  18.8 2.6 %collective-permute-done.7.far_t = bf16[128,1024]{1,0:T(8,128)(2,1)S(1)} collective-permute-done((bf16[128,1024]{1,0:T(8,128)(2,1)S(1)}, bf16[128,1024]{1,0:T(8,128)(2,1)S(1)}, u32[]{:S(2)}, u32[]{:S(2)}) %collective-permute-start.7) | collective-permute-done | bytes 262176 | tf_op jit(solution)/shard_map/ppermute | solution.py:20
  21.4 3.0 %shard_map.49.own_ref.factor_ref = f32[192,128]{1,0:T(8,128)S(1)} custom-call(f32[192,128]{1,0:T(8,128)S(1)} %shard_map.48.refs_0_, f32[192,128]{1,0:T(8,128)S(1)} %collective-permute-done.3.refs_1_, f32[192,128]{1,0:T(8,128)S(1)} %collective-permute-done.4.refs_2_, f32[192,128]{1,0:T(8,128)S(1)} %collective-permute-done.5.refs_3_), custom_call_target="tpu_custom_call" | custom-call | flops 2000000000 | bytes 1000000 | tf_op jit(solution)/shard_map/pallas_call | solution.py:160
  25.3 0.6 collective-permute-done.6.other_ref
  25.9 3.8 %shard_map.50 = (bf16[2,128,128]{2,1,0:T(8,128)(2,1)S(1)}, f32[256,128]{1,0:T(8,128)S(1)}) custom-call(f32[192,128]{1,0:T(8,128)S(1)} %shard_map.49.own_ref.factor_ref, f32[192,128]{1,0:T(8,128)S(1)} %collective-permute-done.6.other_ref, f32[2,128,128]{2,1,0:T(8,128)S(1)} %get-tuple-element.55.sketch_ref), custom_call_target="tpu_custom_call" | custom-call | flops 2000000000 | bytes 1000000 | tf_op jit(solution)/shard_map/pallas_call | solution.py:160
  29.8 0.7 %shard_map.51 = (bf16[256,128]{1,0:T(8,128)(2,1)S(1)}, bf16[256,128]{1,0:T(8,128)(2,1)S(1)}, bf16[1024,128]{1,0:T(8,128)(2,1)S(1)}) custom-call(f32[256,128]{1,0:T(8,128)S(1)} %get-tuple-element.38.slices_ref.refs_6_, bf16[1024,128]{1,0:T(8,128)(2,1)S(1)} %bitcast.16, bf16[1024,128]{1,0:T(8,128)(2,1)S(1)} %collective-permute-done.2.other_ref.image_other, ...), custom_call_target="tpu_custom_call" | custom-call | flops 2000000000 | bytes 1000000 | tf_op jit(solution)/shard_map/pallas_call | solution.py:160
  31.3 1.2 %collective-permute-start.9 = (bf16[256,128]{1,0:T(8,128)(2,1)S(1)}, bf16[256,128]{1,0:T(8,128)(2,1)S(1)}, u32[]{:S(2)}, u32[]{:S(2)}) collective-permute-start(bf16[256,128]{1,0:T(8,128)(2,1)S(1)} %get-tuple-element.39.refs_0_), channel_id=1, source_target_pairs={{0,1},{1,0},{2,3},{3,2},{4,6},{5,7},{6,4},{7,5},{8,9},{9,8},{10,11... | collective-permute-start | bytes 196616 | tf_op jit(solution)/shard_map/ppermute | solution.py:31
  32.5 1.4 %collective-permute-start.10 = (bf16[256,128]{1,0:T(8,128)(2,1)S(1)}, bf16[256,128]{1,0:T(8,128)(2,1)S(1)}, u32[]{:S(2)}, u32[]{:S(2)}) collective-permute-start(bf16[256,128]{1,0:T(8,128)(2,1)S(1)} %get-tuple-element.40), channel_id=1, source_target_pairs={{0,3},{1,2},{2,1},{3,0},{4,12},{5,13},{6,14},{7,15},{8,11},{9,10},... | collective-permute-start | bytes 196616 | tf_op jit(solution)/shard_map/ppermute | solution.py:31
  33.9 6.1 %collective-permute-done.14.came_ref = bf16[1024,128]{1,0:T(8,128)(2,1)S(1)} collective-permute-done((bf16[1024,128]{1,0:T(8,128)(2,1)S(1)}, bf16[1024,128]{1,0:T(8,128)(2,1)S(1)}, u32[]{:S(2)}, u32[]{:S(2)}) %collective-permute-start.14) | collective-permute-done | bytes 262176 | tf_op jit(solution)/shard_map/ppermute | solution.py:20
  40.7 1.0 %collective-permute-done.11.refs_3_ = bf16[256,128]{1,0:T(8,128)(2,1)S(1)} collective-permute-done((bf16[256,128]{1,0:T(8,128)(2,1)S(1)}, bf16[256,128]{1,0:T(8,128)(2,1)S(1)}, u32[]{:S(2)}, u32[]{:S(2)}) %collective-permute-start.11) | collective-permute-done | bytes 65568 | tf_op jit(solution)/shard_map/ppermute | solution.py:20
  41.8 3.7 %shard_map.52 = (bf16[2,128,128]{2,1,0:T(8,128)(2,1)S(1)}, f32[256,128]{1,0:T(8,128)S(1)}) custom-call(bf16[256,128]{1,0:T(8,128)(2,1)S(1)} %get-tuple-element.39.refs_0_, bf16[256,128]{1,0:T(8,128)(2,1)S(1)} %collective-permute-done.9.refs_1_, bf16[256,128]{1,0:T(8,128)(2,1)S(1)} %collective-permute-done.10.refs_2_, ...), custom_call_target="tpu_custom_call" | custom-call | flops 2000000000 | bytes 1000000 | tf_op jit(solution)/shard_map/pallas_call | solution.py:160
  45.5 0.9 %shard_map.55 = (bf16[256,128]{1,0:T(8,128)(2,1)S(1)}, bf16[256,128]{1,0:T(8,128)(2,1)S(1)}) custom-call(bf16[2,128,128]{2,1,0:T(8,128)(2,1)S(1)} %get-tuple-element.41.halves_ref, f32[256,128]{1,0:T(8,128)S(1)} %get-tuple-element.42.slices_ref, bf16[1024,128]{1,0:T(8,128)(2,1)S(1)} %get-tuple-element.43.refs_0_.image_own, ...), custom_call_target="tpu_custom_call" | custom-call | flops 2000000000 | bytes 1000000 | tf_op jit(solution)/shard_map/pallas_call | solution.py:160
  46.4 1.1 %collective-permute-start.18 = (bf16[256,128]{1,0:T(8,128)(2,1)S(1)}, bf16[256,128]{1,0:T(8,128)(2,1)S(1)}, u32[]{:S(2)}, u32[]{:S(2)}) collective-permute-start(bf16[256,128]{1,0:T(8,128)(2,1)S(1)} %get-tuple-element.46.refs_0_), channel_id=1, source_target_pairs={{0,1},{1,0},{2,3},{3,2},{4,6},{5,7},{6,4},{7,5},{8,9},{9,8},{10,11... | collective-permute-start | bytes 196616 | tf_op jit(solution)/shard_map/ppermute | solution.py:31
  47.8 1.6 %collective-permute-start.23 = (bf16[512,128]{1,0:T(8,128)(2,1)S(1)}, bf16[512,128]{1,0:T(8,128)(2,1)S(1)}, u32[]{:S(2)}, u32[]{:S(2)}) collective-permute-start(bf16[512,128]{1,0:T(8,128)(2,1)S(1)} %get-tuple-element.51), channel_id=1, source_target_pairs={{0,16},{4,20},{8,24},{12,28},{16,0},{20,4},{24,8},{28,12},{1,17},{... | collective-permute-start | bytes 393224 | tf_op jit(solution)/shard_map/ppermute | solution.py:20
  49.5 1.5 %collective-permute-start.19 = (bf16[256,128]{1,0:T(8,128)(2,1)S(1)}, bf16[256,128]{1,0:T(8,128)(2,1)S(1)}, u32[]{:S(2)}, u32[]{:S(2)}) collective-permute-start(bf16[256,128]{1,0:T(8,128)(2,1)S(1)} %get-tuple-element.47), channel_id=1, source_target_pairs={{0,3},{1,2},{2,1},{3,0},{4,20},{5,21},{6,22},{7,23},{8,11},{9,10},... | collective-permute-start | bytes 196616 | tf_op jit(solution)/shard_map/ppermute | solution.py:31
  50.9 3.7 %collective-permute-done.19.refs_2_ = bf16[256,128]{1,0:T(8,128)(2,1)S(1)} collective-permute-done((bf16[256,128]{1,0:T(8,128)(2,1)S(1)}, bf16[256,128]{1,0:T(8,128)(2,1)S(1)}, u32[]{:S(2)}, u32[]{:S(2)}) %collective-permute-start.19) | collective-permute-done | bytes 65568 | tf_op jit(solution)/shard_map/ppermute | solution.py:31
  54.6 3.4 %collective-permute-start.21 = (bf16[256,128]{1,0:T(8,128)(2,1)S(1)}, bf16[256,128]{1,0:T(8,128)(2,1)S(1)}, u32[]{:S(2)}, u32[]{:S(2)}) collective-permute-start(bf16[256,128]{1,0:T(8,128)(2,1)S(1)} %collective-permute-done.19.refs_2_), channel_id=1, source_target_pairs={{0,4},{4,0},{8,12},{12,8},{16,20},{20,16},{24,28},{28,24},{1,5},{5... | collective-permute-start | bytes 196616 | tf_op jit(solution)/shard_map/ppermute | solution.py:20
  58.0 0.9 %collective-permute-done.21.refs_4_ = bf16[256,128]{1,0:T(8,128)(2,1)S(1)} collective-permute-done((bf16[256,128]{1,0:T(8,128)(2,1)S(1)}, bf16[256,128]{1,0:T(8,128)(2,1)S(1)}, u32[]{:S(2)}, u32[]{:S(2)}) %collective-permute-start.21) | collective-permute-done | bytes 65568 | tf_op jit(solution)/shard_map/ppermute | solution.py:20
  59.2 3.9 %collective-permute-done.22.refs_1_ = bf16[128,128]{1,0:T(8,128)(2,1)S(1)} collective-permute-done((bf16[128,128]{1,0:T(8,128)(2,1)S(1)}, bf16[128,128]{1,0:T(8,128)(2,1)S(1)}, u32[]{:S(2)}, u32[]{:S(2)}) %collective-permute-start.22) | collective-permute-done | bytes 32800 | tf_op jit(solution)/shard_map/ppermute | solution.py:20
  63.1 3.8 %shard_map.58 = (bf16[2,128,128]{2,1,0:T(8,128)(2,1)S(1)}, bf16[4,1024,128]{2,1,0:T(8,128)(2,1)}) custom-call(bf16[128,128]{1,0:T(8,128)(2,1)S(1)} %shard_map.56.refs_0_, bf16[128,128]{1,0:T(8,128)(2,1)S(1)} %collective-permute-done.22.refs_1_, f32[2,128,128]{2,1,0:T(8,128)S(1)} %get-tuple-element.53.refs_2_, ...), custom_call_target="tpu_custom_call" | custom-call | tf_op jit(solution)/shard_map/pallas_call | solution.py:474
  67.0 0.9 %shard_map.59._ = bf16[4,1024,128]{2,1,0:T(8,128)(2,1)} custom-call(bf16[2,128,128]{2,1,0:T(8,128)(2,1)S(1)} %get-tuple-element.50.halves_ref, bf16[1024,128]{1,0:T(8,128)(2,1)S(1)} %get-tuple-element.49.refs_5_.modes_own, bf16[512,128]{1,0:T(8,128)(2,1)S(1)} %collective-permute-done.23.modes_other, ...), custom_call_target="tpu_custom_call", output_to_operand_aliasing={{}: (3, {})} | custom-call | tf_op jit(solution)/shard_map/pallas_call | solution.py:487
  67.9 0.9 %shard_map.60 = bf16[4,1024,128]{2,1,0:T(8,128)(2,1)} custom-call(bf16[2,128,128]{2,1,0:T(8,128)(2,1)S(1)} %get-tuple-element.50.halves_ref, bf16[1024,128]{1,0:T(8,128)(2,1)S(1)} %get-tuple-element.49.refs_5_.modes_own, bf16[512,128]{1,0:T(8,128)(2,1)S(1)} %collective-permute-done.24.modes_other, ...), custom_call_target="tpu_custom_call", output_to_operand_aliasing={{}: (3, {})} | custom-call | tf_op jit(solution)/shard_map/pallas_call | solution.py:487
  (37 shorter events, 3.5 us)
Async XLA Ops:
  0.0 9.1 %copy-start = (s32[8,7]{1,0:T(8,128)S(1)}, s32[8,7]{1,0:T(8,128)}, u32[]{:S(2)}) copy-start(s32[8,7]{1,0:T(8,128)} %index_ref.1) | copy-start | bytes 676
  0.9 6.6 %collective-permute-start = (bf16[2,128,128]{2,1,0:T(8,128)(2,1)S(1)}, bf16[2,128,128]{2,1,0:T(8,128)(2,1)S(1)}, u32[]{:S(2)}, u32[]{:S(2)}) collective-permute-start(bf16[2,128,128]{2,1,0:T(8,128)(2,1)S(1)} %bitcast.19), channel_id=1, source_target_pairs={{0,1},{1,0},{2,3},{3,2},{4,5},{5,4},{6,7},{7,6},{8,9},{9,8},{10,11... | collective-permute-start | bytes 196616 | tf_op jit(solution)/shard_map/ppermute | solution.py:514
  3.9 5.2 %collective-permute-start.1 = (bf16[2,128,128]{2,1,0:T(8,128)(2,1)S(1)}, bf16[2,128,128]{2,1,0:T(8,128)(2,1)S(1)}, u32[]{:S(2)}, u32[]{:S(2)}) collective-permute-start(bf16[2,128,128]{2,1,0:T(8,128)(2,1)S(1)} %bitcast.18), channel_id=1, source_target_pairs={{0,3},{1,2},{2,1},{3,0},{4,7},{5,6},{6,5},{7,4},{8,11},{9,10},{10,... | collective-permute-start | bytes 196616 | tf_op jit(solution)/shard_map/ppermute | solution.py:515
  10.6 1.7 %collective-permute-start.2 = (bf16[1024,128]{1,0:T(8,128)(2,1)S(1)}, bf16[1024,128]{1,0:T(8,128)(2,1)S(1)}, u32[]{:S(2)}, u32[]{:S(2)}) collective-permute-start(bf16[1024,128]{1,0:T(8,128)(2,1)S(1)} %bitcast.15), channel_id=1, source_target_pairs={{0,4},{4,0},{8,12},{12,8},{16,20},{20,16},{24,28},{28,24},{1,5},{5... | collective-permute-start | bytes 786440 | tf_op jit(solution)/shard_map/ppermute | solution.py:20
  10.7 10.7 %collective-permute-start.7 = (bf16[128,1024]{1,0:T(8,128)(2,1)S(1)}, bf16[128,1024]{1,0:T(8,128)(2,1)S(1)}, u32[]{:S(2)}, u32[]{:S(2)}) collective-permute-start(bf16[128,1024]{1,0:T(8,128)(2,1)S(1)} %get-tuple-element.35.image_t_ref), channel_id=1, source_target_pairs={{0,8},{4,12},{8,0},{12,4},{16,24},{20,28},{24,16},{28,20},{1,9},{5... | collective-permute-start | bytes 786440 | tf_op jit(solution)/shard_map/ppermute | solution.py:20
  12.6 8.8 %collective-permute-start.3 = (f32[192,128]{1,0:T(8,128)S(1)}, f32[192,128]{1,0:T(8,128)S(1)}, u32[]{:S(2)}, u32[]{:S(2)}) collective-permute-start(f32[192,128]{1,0:T(8,128)S(1)} %shard_map.48.refs_0_), channel_id=1, source_target_pairs={{0,1},{1,0},{2,3},{3,2},{4,5},{5,4},{6,7},{7,6},{8,9},{9,8},{10,11... | collective-permute-start | bytes 294920 | tf_op jit(solution)/shard_map/ppermute | solution.py:20
  13.7 7.7 %collective-permute-start.4 = (f32[192,128]{1,0:T(8,128)S(1)}, f32[192,128]{1,0:T(8,128)S(1)}, u32[]{:S(2)}, u32[]{:S(2)}) collective-permute-start(f32[192,128]{1,0:T(8,128)S(1)} %shard_map.48.refs_0_), channel_id=1, source_target_pairs={{0,2},{1,3},{2,0},{3,1},{4,6},{5,7},{6,4},{7,5},{8,10},{9,11},{10,... | collective-permute-start | bytes 294920 | tf_op jit(solution)/shard_map/ppermute | solution.py:20
  14.7 6.7 %collective-permute-start.5 = (f32[192,128]{1,0:T(8,128)S(1)}, f32[192,128]{1,0:T(8,128)S(1)}, u32[]{:S(2)}, u32[]{:S(2)}) collective-permute-start(f32[192,128]{1,0:T(8,128)S(1)} %shard_map.48.refs_0_), channel_id=1, source_target_pairs={{0,3},{1,2},{2,1},{3,0},{4,7},{5,6},{6,5},{7,4},{8,11},{9,10},{10,... | collective-permute-start | bytes 294920 | tf_op jit(solution)/shard_map/ppermute | solution.py:20
  16.2 17.8 %collective-permute-start.16 = (bf16[128,1024]{1,0:T(8,128)(2,1)S(1)}, bf16[128,1024]{1,0:T(8,128)(2,1)S(1)}, u32[]{:S(2)}, u32[]{:S(2)}) collective-permute-start(bf16[128,1024]{1,0:T(8,128)(2,1)S(1)} %get-tuple-element.35.image_t_ref), channel_id=1, source_target_pairs={{0,16},{4,20},{8,24},{12,28},{16,0},{20,4},{24,8},{28,12},{1,17},{... | collective-permute-start | bytes 786440 | tf_op jit(solution)/shard_map/ppermute | solution.py:20
  21.4 8.4 %collective-permute-start.8 = (bf16[128,1024]{1,0:T(8,128)(2,1)S(1)}, bf16[128,1024]{1,0:T(8,128)(2,1)S(1)}, u32[]{:S(2)}, u32[]{:S(2)}) collective-permute-start(bf16[128,1024]{1,0:T(8,128)(2,1)S(1)} %collective-permute-done.7.far_t), channel_id=1, source_target_pairs={{0,4},{4,0},{8,12},{12,8},{16,20},{20,16},{24,28},{28,24},{1,5},{5... | collective-permute-start | bytes 786440 | tf_op jit(solution)/shard_map/ppermute | solution.py:20
  24.4 1.5 %collective-permute-start.6 = (f32[192,128]{1,0:T(8,128)S(1)}, f32[192,128]{1,0:T(8,128)S(1)}, u32[]{:S(2)}, u32[]{:S(2)}) collective-permute-start(f32[192,128]{1,0:T(8,128)S(1)} %shard_map.49.own_ref.factor_ref), channel_id=1, source_target_pairs={{0,4},{4,0},{8,12},{12,8},{16,20},{20,16},{24,28},{28,24},{1,5},{5... | collective-permute-start | bytes 294920 | tf_op jit(solution)/shard_map/ppermute | solution.py:20
  25.2 5.3 %collective-permute-start.13 = (bf16[1024,128]{1,0:T(8,128)(2,1)S(1)}, bf16[1024,128]{1,0:T(8,128)(2,1)S(1)}, u32[]{:S(2)}, u32[]{:S(2)}) collective-permute-start(bf16[1024,128]{1,0:T(8,128)(2,1)S(1)} %shard_map.53.modes_own.refs_3_), channel_id=1, source_target_pairs={{0,4},{4,0},{8,12},{12,8},{16,20},{20,16},{24,28},{28,24},{1,5},{5... | collective-permute-start | bytes 786440 | tf_op jit(solution)/shard_map/ppermute | solution.py:20
  30.8 9.2 %collective-permute-start.14 = (bf16[1024,128]{1,0:T(8,128)(2,1)S(1)}, bf16[1024,128]{1,0:T(8,128)(2,1)S(1)}, u32[]{:S(2)}, u32[]{:S(2)}) collective-permute-start(bf16[1024,128]{1,0:T(8,128)(2,1)S(1)} %get-tuple-element.45), channel_id=1, source_target_pairs={{0,8},{4,12},{8,0},{12,4},{16,24},{20,28},{24,16},{28,20},{1,9},{5... | collective-permute-start | bytes 786440 | tf_op jit(solution)/shard_map/ppermute | solution.py:20
  31.3 8.7 %collective-permute-start.9 = (bf16[256,128]{1,0:T(8,128)(2,1)S(1)}, bf16[256,128]{1,0:T(8,128)(2,1)S(1)}, u32[]{:S(2)}, u32[]{:S(2)}) collective-permute-start(bf16[256,128]{1,0:T(8,128)(2,1)S(1)} %get-tuple-element.39.refs_0_), channel_id=1, source_target_pairs={{0,1},{1,0},{2,3},{3,2},{4,6},{5,7},{6,4},{7,5},{8,9},{9,8},{10,11... | collective-permute-start | bytes 196616 | tf_op jit(solution)/shard_map/ppermute | solution.py:31
  32.5 8.1 %collective-permute-start.10 = (bf16[256,128]{1,0:T(8,128)(2,1)S(1)}, bf16[256,128]{1,0:T(8,128)(2,1)S(1)}, u32[]{:S(2)}, u32[]{:S(2)}) collective-permute-start(bf16[256,128]{1,0:T(8,128)(2,1)S(1)} %get-tuple-element.40), channel_id=1, source_target_pairs={{0,3},{1,2},{2,1},{3,0},{4,12},{5,13},{6,14},{7,15},{8,11},{9,10},... | collective-permute-start | bytes 196616 | tf_op jit(solution)/shard_map/ppermute | solution.py:31
  33.9 11.6 %collective-permute-start.17 = (bf16[128,1024]{1,0:T(8,128)(2,1)S(1)}, bf16[128,1024]{1,0:T(8,128)(2,1)S(1)}, u32[]{:S(2)}, u32[]{:S(2)}) collective-permute-start(bf16[128,1024]{1,0:T(8,128)(2,1)S(1)} %collective-permute-done.16.far_t), channel_id=1, source_target_pairs={{0,4},{4,0},{8,12},{12,8},{16,20},{20,16},{24,28},{28,24},{1,5},{5... | collective-permute-start | bytes 786440 | tf_op jit(solution)/shard_map/ppermute | solution.py:20
  40.1 5.5 %collective-permute-start.15 = (bf16[1024,128]{1,0:T(8,128)(2,1)S(1)}, bf16[1024,128]{1,0:T(8,128)(2,1)S(1)}, u32[]{:S(2)}, u32[]{:S(2)}) collective-permute-start(bf16[1024,128]{1,0:T(8,128)(2,1)S(1)} %collective-permute-done.14.came_ref), channel_id=1, source_target_pairs={{0,4},{4,0},{8,12},{12,8},{16,20},{20,16},{24,28},{28,24},{1,5},{5... | collective-permute-start | bytes 786440 | tf_op jit(solution)/shard_map/ppermute | solution.py:20
  40.1 1.6 %collective-permute-start.11 = (bf16[256,128]{1,0:T(8,128)(2,1)S(1)}, bf16[256,128]{1,0:T(8,128)(2,1)S(1)}, u32[]{:S(2)}, u32[]{:S(2)}) collective-permute-start(bf16[256,128]{1,0:T(8,128)(2,1)S(1)} %collective-permute-done.9.refs_1_), channel_id=1, source_target_pairs={{0,4},{4,0},{8,12},{12,8},{16,20},{20,16},{24,28},{28,24},{1,5},{5... | collective-permute-start | bytes 196616 | tf_op jit(solution)/shard_map/ppermute | solution.py:20
  40.6 1.3 %collective-permute-start.12 = (bf16[256,128]{1,0:T(8,128)(2,1)S(1)}, bf16[256,128]{1,0:T(8,128)(2,1)S(1)}, u32[]{:S(2)}, u32[]{:S(2)}) collective-permute-start(bf16[256,128]{1,0:T(8,128)(2,1)S(1)} %collective-permute-done.10.refs_2_), channel_id=1, source_target_pairs={{0,4},{4,0},{8,12},{12,8},{16,20},{20,16},{24,28},{28,24},{1,5},{5... | collective-permute-start | bytes 196616 | tf_op jit(solution)/shard_map/ppermute | solution.py:20
  46.4 4.5 %collective-permute-start.18 = (bf16[256,128]{1,0:T(8,128)(2,1)S(1)}, bf16[256,128]{1,0:T(8,128)(2,1)S(1)}, u32[]{:S(2)}, u32[]{:S(2)}) collective-permute-start(bf16[256,128]{1,0:T(8,128)(2,1)S(1)} %get-tuple-element.46.refs_0_), channel_id=1, source_target_pairs={{0,1},{1,0},{2,3},{3,2},{4,6},{5,7},{6,4},{7,5},{8,9},{9,8},{10,11... | collective-permute-start | bytes 196616 | tf_op jit(solution)/shard_map/ppermute | solution.py:31
  47.8 10.2 %collective-permute-start.23 = (bf16[512,128]{1,0:T(8,128)(2,1)S(1)}, bf16[512,128]{1,0:T(8,128)(2,1)S(1)}, u32[]{:S(2)}, u32[]{:S(2)}) collective-permute-start(bf16[512,128]{1,0:T(8,128)(2,1)S(1)} %get-tuple-element.51), channel_id=1, source_target_pairs={{0,16},{4,20},{8,24},{12,28},{16,0},{20,4},{24,8},{28,12},{1,17},{... | collective-permute-start | bytes 393224 | tf_op jit(solution)/shard_map/ppermute | solution.py:20
  49.5 5.2 %collective-permute-start.19 = (bf16[256,128]{1,0:T(8,128)(2,1)S(1)}, bf16[256,128]{1,0:T(8,128)(2,1)S(1)}, u32[]{:S(2)}, u32[]{:S(2)}) collective-permute-start(bf16[256,128]{1,0:T(8,128)(2,1)S(1)} %get-tuple-element.47), channel_id=1, source_target_pairs={{0,3},{1,2},{2,1},{3,0},{4,20},{5,21},{6,22},{7,23},{8,11},{9,10},... | collective-permute-start | bytes 196616 | tf_op jit(solution)/shard_map/ppermute | solution.py:31
  50.9 7.1 %collective-permute-start.20 = (bf16[256,128]{1,0:T(8,128)(2,1)S(1)}, bf16[256,128]{1,0:T(8,128)(2,1)S(1)}, u32[]{:S(2)}, u32[]{:S(2)}) collective-permute-start(bf16[256,128]{1,0:T(8,128)(2,1)S(1)} %collective-permute-done.18.refs_1_), channel_id=1, source_target_pairs={{0,4},{4,0},{8,12},{12,8},{16,20},{20,16},{24,28},{28,24},{1,5},{5... | collective-permute-start | bytes 196616 | tf_op jit(solution)/shard_map/ppermute | solution.py:20
  54.6 4.3 %collective-permute-start.21 = (bf16[256,128]{1,0:T(8,128)(2,1)S(1)}, bf16[256,128]{1,0:T(8,128)(2,1)S(1)}, u32[]{:S(2)}, u32[]{:S(2)}) collective-permute-start(bf16[256,128]{1,0:T(8,128)(2,1)S(1)} %collective-permute-done.19.refs_2_), channel_id=1, source_target_pairs={{0,4},{4,0},{8,12},{12,8},{16,20},{20,16},{24,28},{28,24},{1,5},{5... | collective-permute-start | bytes 196616 | tf_op jit(solution)/shard_map/ppermute | solution.py:20
  58.0 9.8 %collective-permute-start.24 = (bf16[512,128]{1,0:T(8,128)(2,1)S(1)}, bf16[512,128]{1,0:T(8,128)(2,1)S(1)}, u32[]{:S(2)}, u32[]{:S(2)}) collective-permute-start(bf16[512,128]{1,0:T(8,128)(2,1)S(1)} %collective-permute-done.23.modes_other), channel_id=1, source_target_pairs={{0,4},{4,0},{8,12},{12,8},{16,20},{20,16},{24,28},{28,24},{1,5},{5... | collective-permute-start | bytes 393224 | tf_op jit(solution)/shard_map/ppermute | solution.py:20
  59.1 4.0 %collective-permute-start.22 = (bf16[128,128]{1,0:T(8,128)(2,1)S(1)}, bf16[128,128]{1,0:T(8,128)(2,1)S(1)}, u32[]{:S(2)}, u32[]{:S(2)}) collective-permute-start(bf16[128,128]{1,0:T(8,128)(2,1)S(1)} %shard_map.56.refs_0_), channel_id=1, source_target_pairs={{0,8},{4,12},{8,0},{12,4},{16,24},{20,28},{24,16},{28,20},{1,9},{5... | collective-permute-start | bytes 98312 | tf_op jit(solution)/shard_map/ppermute | solution.py:20

commit v11 on v9

--- a/solution.py
+++ b/solution.py
@@ -332,14 +332,19 @@
         outgoing_ref[...] = choose("tm", modes, image_ref[...])[0]
     else:
         part = outgoing_ref.shape[0]
-        outgoing_ref[...] = choose("tm", modes[:part], modes[part:])[0]
-
-
-def read_modes(came_ref, shared_ref, rows):
-    first, second = choose("tm", came_ref[...], shared_ref[...])
-    if first.shape[0] == rows:
-        return first
-    return jnp.concatenate([first, second], axis=0)
+        half = jnp.where(upper_chip(), modes[2 * part :], modes[: 2 * part])
+        outgoing_ref[...] = choose("tm", half[:part], half[part:])[0]
+
+
+def upper_chip():
+    return (lax.axis_index("tm") & 2) == 2
+
+
+def read_modes(came_ref, shared_ref, far_ref, far_shared_ref):
+    near = jnp.concatenate(choose("tm", came_ref[...], shared_ref[...]), axis=0)
+    far = jnp.concatenate(choose("tm", far_ref[...], far_shared_ref[...]), axis=0)
+    upper = upper_chip()
+    return jnp.concatenate([jnp.where(upper, far, near), jnp.where(upper, near, far)], axis=0)
 
 
 def first_merge_kernel(own_ref, other_ref, sketch_ref, halves_ref, slices_ref):
@@ -446,9 +451,10 @@
     write_bulk((modes_ref, outgoing_ref), modes, image_ref[0] if image_ref else None)
 
 
-def output_kernel(halves_ref, modes_own, came_ref, shared_ref, _, out_ref, modes_ref, sems):
+def output_kernel(halves_ref, modes_own, *refs):
+    *quarters, _, out_ref, modes_ref, sems = refs
     rows = modes_own.shape[0]
-    modes_other = read_modes(came_ref, shared_ref, rows)
+    modes_other = read_modes(*quarters)
     part = rows // 2
     copies = []
     for half in range(2):
@@ -483,18 +489,18 @@
     )(*parts, sketch_t, *kept)
 
 
-def last_modes(halves, modes, came, shared, out):
+def last_modes(halves, modes, quarters, out):
     vmem = pl.BlockSpec(memory_space=pltpu.VMEM)
     hbm = pl.BlockSpec(memory_space=pltpu.HBM)
     return pl.pallas_call(
         output_kernel,
         out_shape=jax.ShapeDtypeStruct(out.shape, BF16),
-        in_specs=[vmem] * 4 + [hbm],
+        in_specs=[vmem] * 6 + [hbm],
         out_specs=hbm,
         scratch_shapes=[pltpu.VMEM(modes.shape, BF16), pltpu.SemaphoreType.DMA((2,))],
-        input_output_aliases={4: 0},
+        input_output_aliases={6: 0},
         compiler_params=PARAMS,
-    )(halves, modes, came, shared, out)
+    )(halves, modes, *quarters, out)
 
 
 def cross_kernel(total_rows, *refs):
@@ -516,7 +522,7 @@
     came_near = lax.ppermute(jnp.where(odd, head, tail), "space", near)
     came_wide = lax.ppermute(jnp.where(odd, tail, head), "space", wide)
     modes_shape = jax.ShapeDtypeStruct((rows_dev, width), BF16)
-    half_shape = jax.ShapeDtypeStruct((rows_dev // 2, width), BF16)
+    quarter_shape = jax.ShapeDtypeStruct((rows_dev // 4, width), BF16)
     factor_shape = jax.ShapeDtypeStruct((width + width // 2, width), F32)
     half_square = jax.ShapeDtypeStruct((width, width), BF16)
     pair_square = jax.ShapeDtypeStruct((2 * width, width), BF16)
@@ -545,7 +551,7 @@
         last = level + 1 == levels
         deep = level + 2 < levels
         probe_outs = [pair_square] * 2 + ([modes_shape] if deep else [])
-        modes_outs = [modes_shape, modes_shape if deep else half_shape]
+        modes_outs = [modes_shape, modes_shape if deep else quarter_shape]
         if level > 0:
             quarter = space // 4
             if quarter > 1:
@@ -583,7 +589,8 @@
                 *parts, sketch_t[level], slices,
             )
         if last:
-            out = last_modes(halves, modes, came, shared, out)
+            far_quarters = [swap(came, "tm", 2), swap(came, "tm", 3)]
+            out = last_modes(halves, modes, [came, shared, *far_quarters], out)
             break
         far = far_images[level]
         far_shared = swap(far, "tm", 1)

time: 68.2 us -> 67.1 us (0.984)
  starting transfers between devices: 24.5 us -> 23.3 us
    ppermute x19 -> x21, waiting for transfers between devices: 15.3 us -> 17.5 us  [swap(): return lax.ppermute(value, axis, pairs)]
    ppermute x4, waiting for transfers between devices: 3.72 us -> 1.74 us  [mixed_swap(): return lax.ppermute(value, ('tm', 'space'), pairs)]
    ppermute x19 -> x21, starting transfers between devices: 14.8 us -> 13 us  [swap(): return lax.ppermute(value, axis, pairs)]
  transfers between devices with their start and end apart: 25 -> 27, of which waited for: 9 -> 9; matrix products, arithmetic and copies ran while one was open for 0% -> 0% of each run, Pallas kernels for 27% -> 27%
where the time goes in v11:
time: 67.1 us; the launch traced here: 66.9 us
  starting transfers between devices  23.3 us (35%)
  Pallas kernels  21.4 us (32%)
  waiting for transfers between devices  21 us (31%)
  other arithmetic  0.9 us (1%)
    ppermute x21, waiting for transfers between devices, swap(): return lax.ppermute(value, axis, pairs)  17.5 us
    pallas_call x10, Pallas kernels, run_kernel(): pl.pallas_call(body, out_shape=outs, cost_estimate=cost, compiler_params=...  13.4 us
    ppermute x21, starting transfers between devices, swap(): return lax.ppermute(value, axis, pairs)  13 us
    ppermute x4, starting transfers between devices, mixed_swap(): return lax.ppermute(value, ('tm', 'space'), pairs)  5.68 us
    pallas_call x1, Pallas kernels, last_level(): pl.pallas_call(functools.partial(last_merge_kernel, len(parts)), out_shap...  3.82 us
    ppermute x1, starting transfers between devices, modes_of(): came_near = lax.ppermute(jnp.where(odd, head, tail), 'space', near)  3.03 us
    pallas_call x1, Pallas kernels, interior_of(): pl.pallas_call(interior_kernel, out_shape=[jax.ShapeDtypeStruct((inner, r...  1.89 us
    ppermute x1, waiting for transfers between devices, modes_of(): came_wide = lax.ppermute(jnp.where(odd, tail, head), 'space', wide)  1.77 us
  transfers between devices with their start and end apart: 27, of which 9 were waited for; matrix products, arithmetic and copies ran while one was open for 0% of the time, Pallas kernels for 27%

profile of v11, /device:TPU:0, one launch (start us, length us, event | category | flops | bytes accessed | tf_op | source)
XLA Modules:
  0.0 66.9 jit_solution(11832719628815764668)
XLA Ops:
  0.0 0.9 %broadcast_select_fusion = (bf16[256,128]{1,0:T(8,128)(2,1)S(1)}, bf16[256,128]{1,0:T(8,128)(2,1)S(1)}) fusion(pred[]{:T(512)S(6)} %eq.3, bf16[1024,128]{1,0:T(8,128)(2,1)} %param.4), kind=kLoop, calls=%fused_computation.3 | loop fusion | flops 65536 | bytes 262145 | tf_op jit(solution)/shard_map/jit(_where)/select_n | solution.py:523
  0.9 3.0 %collective-permute-start = (bf16[2,128,128]{2,1,0:T(8,128)(2,1)S(1)}, bf16[2,128,128]{2,1,0:T(8,128)(2,1)S(1)}, u32[]{:S(2)}, u32[]{:S(2)}) collective-permute-start(bf16[2,128,128]{2,1,0:T(8,128)(2,1)S(1)} %bitcast.19), channel_id=1, source_target_pairs={{0,1},{1,0},{2,3},{3,2},{4,5},{5,4},{6,7},{7,6},{8,9},{9,8},{10,11... | collective-permute-start | bytes 196616 | tf_op jit(solution)/shard_map/ppermute | solution.py:522
  3.9 1.5 %collective-permute-start.1 = (bf16[2,128,128]{2,1,0:T(8,128)(2,1)S(1)}, bf16[2,128,128]{2,1,0:T(8,128)(2,1)S(1)}, u32[]{:S(2)}, u32[]{:S(2)}) collective-permute-start(bf16[2,128,128]{2,1,0:T(8,128)(2,1)S(1)} %bitcast.18), channel_id=1, source_target_pairs={{0,3},{1,2},{2,1},{3,0},{4,7},{5,6},{6,5},{7,4},{8,11},{9,10},{10,... | collective-permute-start | bytes 196616 | tf_op jit(solution)/shard_map/ppermute | solution.py:523
  5.4 1.9 %shard_map.46 = (bf16[4,128,128]{2,1,0:T(8,128)(2,1)S(1)}, f32[3,2,128,128]{3,2,1,0:T(8,128)S(1)}, bf16[2,2,7,128,128]{4,3,2,1,0:T(8,128)(2,1)S(1)}, bf16[8,128,128]{2,1,0:T(8,128)(2,1)S(1)}) custom-call(s32[8,7]{1,0:T(8,128)} %index_ref.1, bf16[8,7,128,128]{3,2,1,0:T(8,128)(2,1)} %energy_hbm.1, bf16[8,128,128]{2,1,0:T(8,128)(2,1)} %bitcast.17, ...), custom_call_target="tpu_custom_call" | custom-call | tf_op jit(solution)/shard_map/pallas_call | solution.py:245
  7.3 1.8 %collective-permute-done.1.wide_ref = bf16[2,128,128]{2,1,0:T(8,128)(2,1)S(1)} collective-permute-done((bf16[2,128,128]{2,1,0:T(8,128)(2,1)S(1)}, bf16[2,128,128]{2,1,0:T(8,128)(2,1)S(1)}, u32[]{:S(2)}, u32[]{:S(2)}) %collective-permute-start.1) | collective-permute-done | bytes 65568 | tf_op jit(solution)/shard_map/ppermute | solution.py:523
  9.1 1.3 %shard_map.47 = (bf16[8,128,128]{2,1,0:T(8,128)(2,1)S(1)}, bf16[128,1024]{1,0:T(8,128)(2,1)S(1)}, f32[128,128]{1,0:T(8,128)S(1)}) custom-call(s32[8,7]{1,0:T(8,128)S(1)} %copy-done, bf16[2,2,7,128,128]{4,3,2,1,0:T(8,128)(2,1)S(1)} %get-tuple-element.27.edges_ref, bf16[2,128,128]{2,1,0:T(8,128)(2,1)S(1)} %collective-permute-done.near_ref, ...), custom_call_target="tpu_custom_call" | custom-call | tf_op jit(solution)/shard_map/pallas_call | solution.py:266
  10.5 1.6 %collective-permute-start.7 = (bf16[128,1024]{1,0:T(8,128)(2,1)S(1)}, bf16[128,1024]{1,0:T(8,128)(2,1)S(1)}, u32[]{:S(2)}, u32[]{:S(2)}) collective-permute-start(bf16[128,1024]{1,0:T(8,128)(2,1)S(1)} %get-tuple-element.31.image_t_ref), channel_id=1, source_target_pairs={{0,8},{4,12},{8,0},{12,4},{16,24},{20,28},{24,16},{28,20},{1,9},{5... | collective-permute-start | bytes 786440 | tf_op jit(solution)/shard_map/ppermute | solution.py:20
  12.4 1.1 %collective-permute-start.3 = (f32[192,128]{1,0:T(8,128)S(1)}, f32[192,128]{1,0:T(8,128)S(1)}, u32[]{:S(2)}, u32[]{:S(2)}) collective-permute-start(f32[192,128]{1,0:T(8,128)S(1)} %shard_map.48.refs_0_), channel_id=1, source_target_pairs={{0,1},{1,0},{2,3},{3,2},{4,5},{5,4},{6,7},{7,6},{8,9},{9,8},{10,11... | collective-permute-start | bytes 294920 | tf_op jit(solution)/shard_map/ppermute | solution.py:20
  13.5 1.0 %collective-permute-start.4 = (f32[192,128]{1,0:T(8,128)S(1)}, f32[192,128]{1,0:T(8,128)S(1)}, u32[]{:S(2)}, u32[]{:S(2)}) collective-permute-start(f32[192,128]{1,0:T(8,128)S(1)} %shard_map.48.refs_0_), channel_id=1, source_target_pairs={{0,2},{1,3},{2,0},{3,1},{4,6},{5,7},{6,4},{7,5},{8,10},{9,11},{10,... | collective-permute-start | bytes 294920 | tf_op jit(solution)/shard_map/ppermute | solution.py:20
  14.5 1.4 %collective-permute-start.5 = (f32[192,128]{1,0:T(8,128)S(1)}, f32[192,128]{1,0:T(8,128)S(1)}, u32[]{:S(2)}, u32[]{:S(2)}) collective-permute-start(f32[192,128]{1,0:T(8,128)S(1)} %shard_map.48.refs_0_), channel_id=1, source_target_pairs={{0,3},{1,2},{2,1},{3,0},{4,7},{5,6},{6,5},{7,4},{8,11},{9,10},{10,... | collective-permute-start | bytes 294920 | tf_op jit(solution)/shard_map/ppermute | solution.py:20
  16.0 2.7 %collective-permute-start.16 = (bf16[128,1024]{1,0:T(8,128)(2,1)S(1)}, bf16[128,1024]{1,0:T(8,128)(2,1)S(1)}, u32[]{:S(2)}, u32[]{:S(2)}) collective-permute-start(bf16[128,1024]{1,0:T(8,128)(2,1)S(1)} %get-tuple-element.31.image_t_ref), channel_id=1, source_target_pairs={{0,16},{4,20},{8,24},{12,28},{16,0},{20,4},{24,8},{28,12},{1,17},{... | collective-permute-start | bytes 786440 | tf_op jit(solution)/shard_map/ppermute | solution.py:20
  18.6 2.6 %collective-permute-done.7.far_t = bf16[128,1024]{1,0:T(8,128)(2,1)S(1)} collective-permute-done((bf16[128,1024]{1,0:T(8,128)(2,1)S(1)}, bf16[128,1024]{1,0:T(8,128)(2,1)S(1)}, u32[]{:S(2)}, u32[]{:S(2)}) %collective-permute-start.7) | collective-permute-done | bytes 262176 | tf_op jit(solution)/shard_map/ppermute | solution.py:20
  21.2 3.0 %shard_map.49.own_ref.factor_ref = f32[192,128]{1,0:T(8,128)S(1)} custom-call(f32[192,128]{1,0:T(8,128)S(1)} %shard_map.48.refs_0_, f32[192,128]{1,0:T(8,128)S(1)} %collective-permute-done.3.refs_1_, f32[192,128]{1,0:T(8,128)S(1)} %collective-permute-done.4.refs_2_, f32[192,128]{1,0:T(8,128)S(1)} %collective-permute-done.5.refs_3_), custom_call_target="tpu_custom_call" | custom-call | flops 2000000000 | bytes 1000000 | tf_op jit(solution)/shard_map/pallas_call | solution.py:160
  24.2 0.6 collective-permute-start.6
  25.1 0.6 collective-permute-done.6.other_ref
  25.7 3.8 %shard_map.50 = (bf16[2,128,128]{2,1,0:T(8,128)(2,1)S(1)}, f32[256,128]{1,0:T(8,128)S(1)}) custom-call(f32[192,128]{1,0:T(8,128)S(1)} %shard_map.49.own_ref.factor_ref, f32[192,128]{1,0:T(8,128)S(1)} %collective-permute-done.6.other_ref, f32[2,128,128]{2,1,0:T(8,128)S(1)} %get-tuple-element.51.sketch_ref), custom_call_target="tpu_custom_call" | custom-call | flops 2000000000 | bytes 1000000 | tf_op jit(solution)/shard_map/pallas_call | solution.py:160
  29.6 0.7 %shard_map.51 = (bf16[256,128]{1,0:T(8,128)(2,1)S(1)}, bf16[256,128]{1,0:T(8,128)(2,1)S(1)}, bf16[1024,128]{1,0:T(8,128)(2,1)S(1)}) custom-call(f32[256,128]{1,0:T(8,128)S(1)} %get-tuple-element.34.slices_ref.refs_6_, bf16[1024,128]{1,0:T(8,128)(2,1)S(1)} %bitcast.16, bf16[1024,128]{1,0:T(8,128)(2,1)S(1)} %collective-permute-done.2.other_ref.image_other, ...), custom_call_target="tpu_custom_call" | custom-call | flops 2000000000 | bytes 1000000 | tf_op jit(solution)/shard_map/pallas_call | solution.py:160
  31.1 1.2 %collective-permute-start.9 = (bf16[256,128]{1,0:T(8,128)(2,1)S(1)}, bf16[256,128]{1,0:T(8,128)(2,1)S(1)}, u32[]{:S(2)}, u32[]{:S(2)}) collective-permute-start(bf16[256,128]{1,0:T(8,128)(2,1)S(1)} %get-tuple-element.35.refs_0_), channel_id=1, source_target_pairs={{0,1},{1,0},{2,3},{3,2},{4,6},{5,7},{6,4},{7,5},{8,9},{9,8},{10,11... | collective-permute-start | bytes 196616 | tf_op jit(solution)/shard_map/ppermute | solution.py:31
  32.3 1.5 %collective-permute-start.10 = (bf16[256,128]{1,0:T(8,128)(2,1)S(1)}, bf16[256,128]{1,0:T(8,128)(2,1)S(1)}, u32[]{:S(2)}, u32[]{:S(2)}) collective-permute-start(bf16[256,128]{1,0:T(8,128)(2,1)S(1)} %get-tuple-element.36), channel_id=1, source_target_pairs={{0,3},{1,2},{2,1},{3,0},{4,12},{5,13},{6,14},{7,15},{8,11},{9,10},... | collective-permute-start | bytes 196616 | tf_op jit(solution)/shard_map/ppermute | solution.py:31
  33.8 6.1 %collective-permute-done.14.came_ref = bf16[1024,128]{1,0:T(8,128)(2,1)S(1)} collective-permute-done((bf16[1024,128]{1,0:T(8,128)(2,1)S(1)}, bf16[1024,128]{1,0:T(8,128)(2,1)S(1)}, u32[]{:S(2)}, u32[]{:S(2)}) %collective-permute-start.14) | collective-permute-done | bytes 262176 | tf_op jit(solution)/shard_map/ppermute | solution.py:20
  40.5 1.0 %collective-permute-done.11.refs_3_ = bf16[256,128]{1,0:T(8,128)(2,1)S(1)} collective-permute-done((bf16[256,128]{1,0:T(8,128)(2,1)S(1)}, bf16[256,128]{1,0:T(8,128)(2,1)S(1)}, u32[]{:S(2)}, u32[]{:S(2)}) %collective-permute-start.11) | collective-permute-done | bytes 65568 | tf_op jit(solution)/shard_map/ppermute | solution.py:20
  41.6 3.7 %shard_map.52 = (bf16[2,128,128]{2,1,0:T(8,128)(2,1)S(1)}, f32[256,128]{1,0:T(8,128)S(1)}) custom-call(bf16[256,128]{1,0:T(8,128)(2,1)S(1)} %get-tuple-element.35.refs_0_, bf16[256,128]{1,0:T(8,128)(2,1)S(1)} %collective-permute-done.9.refs_1_, bf16[256,128]{1,0:T(8,128)(2,1)S(1)} %collective-permute-done.10.refs_2_, ...), custom_call_target="tpu_custom_call" | custom-call | flops 2000000000 | bytes 1000000 | tf_op jit(solution)/shard_map/pallas_call | solution.py:160
  45.3 0.9 %shard_map.55 = (bf16[256,128]{1,0:T(8,128)(2,1)S(1)}, bf16[256,128]{1,0:T(8,128)(2,1)S(1)}) custom-call(bf16[2,128,128]{2,1,0:T(8,128)(2,1)S(1)} %get-tuple-element.37.halves_ref, f32[256,128]{1,0:T(8,128)S(1)} %get-tuple-element.38.slices_ref, bf16[1024,128]{1,0:T(8,128)(2,1)S(1)} %get-tuple-element.39.refs_0_.image_own, ...), custom_call_target="tpu_custom_call" | custom-call | flops 2000000000 | bytes 1000000 | tf_op jit(solution)/shard_map/pallas_call | solution.py:160
  46.2 1.1 %collective-permute-start.18 = (bf16[256,128]{1,0:T(8,128)(2,1)S(1)}, bf16[256,128]{1,0:T(8,128)(2,1)S(1)}, u32[]{:S(2)}, u32[]{:S(2)}) collective-permute-start(bf16[256,128]{1,0:T(8,128)(2,1)S(1)} %get-tuple-element.42.refs_0_), channel_id=1, source_target_pairs={{0,1},{1,0},{2,3},{3,2},{4,6},{5,7},{6,4},{7,5},{8,9},{9,8},{10,11... | collective-permute-start | bytes 196616 | tf_op jit(solution)/shard_map/ppermute | solution.py:31
  47.3 2.0 %collective-permute-start.19 = (bf16[256,128]{1,0:T(8,128)(2,1)S(1)}, bf16[256,128]{1,0:T(8,128)(2,1)S(1)}, u32[]{:S(2)}, u32[]{:S(2)}) collective-permute-start(bf16[256,128]{1,0:T(8,128)(2,1)S(1)} %get-tuple-element.43), channel_id=1, source_target_pairs={{0,3},{1,2},{2,1},{3,0},{4,20},{5,21},{6,22},{7,23},{8,11},{9,10},... | collective-permute-start | bytes 196616 | tf_op jit(solution)/shard_map/ppermute | solution.py:31
  49.6 1.2 %collective-permute-start.23 = (bf16[256,128]{1,0:T(8,128)(2,1)S(1)}, bf16[256,128]{1,0:T(8,128)(2,1)S(1)}, u32[]{:S(2)}, u32[]{:S(2)}) collective-permute-start(bf16[256,128]{1,0:T(8,128)(2,1)S(1)} %get-tuple-element.47), channel_id=1, source_target_pairs={{0,16},{4,20},{8,24},{12,28},{16,0},{20,4},{24,8},{28,12},{1,17},{... | collective-permute-start | bytes 196616 | tf_op jit(solution)/shard_map/ppermute | solution.py:20
  50.8 1.7 %collective-permute-done.19.refs_2_ = bf16[256,128]{1,0:T(8,128)(2,1)S(1)} collective-permute-done((bf16[256,128]{1,0:T(8,128)(2,1)S(1)}, bf16[256,128]{1,0:T(8,128)(2,1)S(1)}, u32[]{:S(2)}, u32[]{:S(2)}) %collective-permute-start.19) | collective-permute-done | bytes 65568 | tf_op jit(solution)/shard_map/ppermute | solution.py:31
  52.5 2.8 %collective-permute-done.23.refs_0_ = bf16[256,128]{1,0:T(8,128)(2,1)S(1)} collective-permute-done((bf16[256,128]{1,0:T(8,128)(2,1)S(1)}, bf16[256,128]{1,0:T(8,128)(2,1)S(1)}, u32[]{:S(2)}, u32[]{:S(2)}) %collective-permute-start.23) | collective-permute-done | bytes 65568 | tf_op jit(solution)/shard_map/ppermute | solution.py:20
  55.3 1.9 %collective-permute-start.26 = (bf16[256,128]{1,0:T(8,128)(2,1)S(1)}, bf16[256,128]{1,0:T(8,128)(2,1)S(1)}, u32[]{:S(2)}, u32[]{:S(2)}) collective-permute-start(bf16[256,128]{1,0:T(8,128)(2,1)S(1)} %collective-permute-done.23.refs_0_), channel_id=1, source_target_pairs={{0,12},{4,8},{8,4},{12,0},{16,28},{20,24},{24,20},{28,16},{1,13},{... | collective-permute-start | bytes 196616 | tf_op jit(solution)/shard_map/ppermute | solution.py:20
  57.7 4.2 %collective-permute-done.22.refs_1_ = bf16[128,128]{1,0:T(8,128)(2,1)S(1)} collective-permute-done((bf16[128,128]{1,0:T(8,128)(2,1)S(1)}, bf16[128,128]{1,0:T(8,128)(2,1)S(1)}, u32[]{:S(2)}, u32[]{:S(2)}) %collective-permute-start.22) | collective-permute-done | bytes 32800 | tf_op jit(solution)/shard_map/ppermute | solution.py:20
  61.9 3.8 %shard_map.58 = (bf16[2,128,128]{2,1,0:T(8,128)(2,1)S(1)}, bf16[4,1024,128]{2,1,0:T(8,128)(2,1)}) custom-call(bf16[128,128]{1,0:T(8,128)(2,1)S(1)} %shard_map.56.refs_0_, bf16[128,128]{1,0:T(8,128)(2,1)S(1)} %collective-permute-done.22.refs_1_, f32[2,128,128]{2,1,0:T(8,128)S(1)} %get-tuple-element.49.refs_2_, ...), custom_call_target="tpu_custom_call" | custom-call | tf_op jit(solution)/shard_map/pallas_call | solution.py:482
  65.8 1.0 %shard_map.59 = bf16[4,1024,128]{2,1,0:T(8,128)(2,1)} custom-call(bf16[2,128,128]{2,1,0:T(8,128)(2,1)S(1)} %get-tuple-element.46.halves_ref, bf16[1024,128]{1,0:T(8,128)(2,1)S(1)} %get-tuple-element.45.refs_5_.modes_own, bf16[256,128]{1,0:T(8,128)(2,1)S(1)} %collective-permute-done.23.refs_0_, ...), custom_call_target="tpu_custom_call", output_to_operand_aliasing={{}: (6, {})} | custom-call | tf_op jit(solution)/shard_map/pallas_call | solution.py:495
  (40 shorter events, 3.2 us)
Async XLA Ops:
  0.0 9.1 %copy-start = (s32[8,7]{1,0:T(8,128)S(1)}, s32[8,7]{1,0:T(8,128)}, u32[]{:S(2)}) copy-start(s32[8,7]{1,0:T(8,128)} %index_ref.1) | copy-start | bytes 676
  0.9 6.4 %collective-permute-start = (bf16[2,128,128]{2,1,0:T(8,128)(2,1)S(1)}, bf16[2,128,128]{2,1,0:T(8,128)(2,1)S(1)}, u32[]{:S(2)}, u32[]{:S(2)}) collective-permute-start(bf16[2,128,128]{2,1,0:T(8,128)(2,1)S(1)} %bitcast.19), channel_id=1, source_target_pairs={{0,1},{1,0},{2,3},{3,2},{4,5},{5,4},{6,7},{7,6},{8,9},{9,8},{10,11... | collective-permute-start | bytes 196616 | tf_op jit(solution)/shard_map/ppermute | solution.py:522
  3.9 5.2 %collective-permute-start.1 = (bf16[2,128,128]{2,1,0:T(8,128)(2,1)S(1)}, bf16[2,128,128]{2,1,0:T(8,128)(2,1)S(1)}, u32[]{:S(2)}, u32[]{:S(2)}) collective-permute-start(bf16[2,128,128]{2,1,0:T(8,128)(2,1)S(1)} %bitcast.18), channel_id=1, source_target_pairs={{0,3},{1,2},{2,1},{3,0},{4,7},{5,6},{6,5},{7,4},{8,11},{9,10},{10,... | collective-permute-start | bytes 196616 | tf_op jit(solution)/shard_map/ppermute | solution.py:523
  10.4 1.7 %collective-permute-start.2 = (bf16[1024,128]{1,0:T(8,128)(2,1)S(1)}, bf16[1024,128]{1,0:T(8,128)(2,1)S(1)}, u32[]{:S(2)}, u32[]{:S(2)}) collective-permute-start(bf16[1024,128]{1,0:T(8,128)(2,1)S(1)} %bitcast.15), channel_id=1, source_target_pairs={{0,4},{4,0},{8,12},{12,8},{16,20},{20,16},{24,28},{28,24},{1,5},{5... | collective-permute-start | bytes 786440 | tf_op jit(solution)/shard_map/ppermute | solution.py:20
  10.5 10.7 %collective-permute-start.7 = (bf16[128,1024]{1,0:T(8,128)(2,1)S(1)}, bf16[128,1024]{1,0:T(8,128)(2,1)S(1)}, u32[]{:S(2)}, u32[]{:S(2)}) collective-permute-start(bf16[128,1024]{1,0:T(8,128)(2,1)S(1)} %get-tuple-element.31.image_t_ref), channel_id=1, source_target_pairs={{0,8},{4,12},{8,0},{12,4},{16,24},{20,28},{24,16},{28,20},{1,9},{5... | collective-permute-start | bytes 786440 | tf_op jit(solution)/shard_map/ppermute | solution.py:20
  12.4 8.8 %collective-permute-start.3 = (f32[192,128]{1,0:T(8,128)S(1)}, f32[192,128]{1,0:T(8,128)S(1)}, u32[]{:S(2)}, u32[]{:S(2)}) collective-permute-start(f32[192,128]{1,0:T(8,128)S(1)} %shard_map.48.refs_0_), channel_id=1, source_target_pairs={{0,1},{1,0},{2,3},{3,2},{4,5},{5,4},{6,7},{7,6},{8,9},{9,8},{10,11... | collective-permute-start | bytes 294920 | tf_op jit(solution)/shard_map/ppermute | solution.py:20
  13.5 7.7 %collective-permute-start.4 = (f32[192,128]{1,0:T(8,128)S(1)}, f32[192,128]{1,0:T(8,128)S(1)}, u32[]{:S(2)}, u32[]{:S(2)}) collective-permute-start(f32[192,128]{1,0:T(8,128)S(1)} %shard_map.48.refs_0_), channel_id=1, source_target_pairs={{0,2},{1,3},{2,0},{3,1},{4,6},{5,7},{6,4},{7,5},{8,10},{9,11},{10,... | collective-permute-start | bytes 294920 | tf_op jit(solution)/shard_map/ppermute | solution.py:20
  14.5 6.7 %collective-permute-start.5 = (f32[192,128]{1,0:T(8,128)S(1)}, f32[192,128]{1,0:T(8,128)S(1)}, u32[]{:S(2)}, u32[]{:S(2)}) collective-permute-start(f32[192,128]{1,0:T(8,128)S(1)} %shard_map.48.refs_0_), channel_id=1, source_target_pairs={{0,3},{1,2},{2,1},{3,0},{4,7},{5,6},{6,5},{7,4},{8,11},{9,10},{10,... | collective-permute-start | bytes 294920 | tf_op jit(solution)/shard_map/ppermute | solution.py:20
  16.0 17.8 %collective-permute-start.16 = (bf16[128,1024]{1,0:T(8,128)(2,1)S(1)}, bf16[128,1024]{1,0:T(8,128)(2,1)S(1)}, u32[]{:S(2)}, u32[]{:S(2)}) collective-permute-start(bf16[128,1024]{1,0:T(8,128)(2,1)S(1)} %get-tuple-element.31.image_t_ref), channel_id=1, source_target_pairs={{0,16},{4,20},{8,24},{12,28},{16,0},{20,4},{24,8},{28,12},{1,17},{... | collective-permute-start | bytes 786440 | tf_op jit(solution)/shard_map/ppermute | solution.py:20
  21.2 8.4 %collective-permute-start.8 = (bf16[128,1024]{1,0:T(8,128)(2,1)S(1)}, bf16[128,1024]{1,0:T(8,128)(2,1)S(1)}, u32[]{:S(2)}, u32[]{:S(2)}) collective-permute-start(bf16[128,1024]{1,0:T(8,128)(2,1)S(1)} %collective-permute-done.7.far_t), channel_id=1, source_target_pairs={{0,4},{4,0},{8,12},{12,8},{16,20},{20,16},{24,28},{28,24},{1,5},{5... | collective-permute-start | bytes 786440 | tf_op jit(solution)/shard_map/ppermute | solution.py:20
  24.2 1.5 %collective-permute-start.6 = (f32[192,128]{1,0:T(8,128)S(1)}, f32[192,128]{1,0:T(8,128)S(1)}, u32[]{:S(2)}, u32[]{:S(2)}) collective-permute-start(f32[192,128]{1,0:T(8,128)S(1)} %shard_map.49.own_ref.factor_ref), channel_id=1, source_target_pairs={{0,4},{4,0},{8,12},{12,8},{16,20},{20,16},{24,28},{28,24},{1,5},{5... | collective-permute-start | bytes 294920 | tf_op jit(solution)/shard_map/ppermute | solution.py:20
  25.0 5.3 %collective-permute-start.13 = (bf16[1024,128]{1,0:T(8,128)(2,1)S(1)}, bf16[1024,128]{1,0:T(8,128)(2,1)S(1)}, u32[]{:S(2)}, u32[]{:S(2)}) collective-permute-start(bf16[1024,128]{1,0:T(8,128)(2,1)S(1)} %shard_map.53.modes_own.refs_3_), channel_id=1, source_target_pairs={{0,4},{4,0},{8,12},{12,8},{16,20},{20,16},{24,28},{28,24},{1,5},{5... | collective-permute-start | bytes 786440 | tf_op jit(solution)/shard_map/ppermute | solution.py:20
  30.6 9.2 %collective-permute-start.14 = (bf16[1024,128]{1,0:T(8,128)(2,1)S(1)}, bf16[1024,128]{1,0:T(8,128)(2,1)S(1)}, u32[]{:S(2)}, u32[]{:S(2)}) collective-permute-start(bf16[1024,128]{1,0:T(8,128)(2,1)S(1)} %get-tuple-element.41), channel_id=1, source_target_pairs={{0,8},{4,12},{8,0},{12,4},{16,24},{20,28},{24,16},{28,20},{1,9},{5... | collective-permute-start | bytes 786440 | tf_op jit(solution)/shard_map/ppermute | solution.py:20
  31.1 8.7 %collective-permute-start.9 = (bf16[256,128]{1,0:T(8,128)(2,1)S(1)}, bf16[256,128]{1,0:T(8,128)(2,1)S(1)}, u32[]{:S(2)}, u32[]{:S(2)}) collective-permute-start(bf16[256,128]{1,0:T(8,128)(2,1)S(1)} %get-tuple-element.35.refs_0_), channel_id=1, source_target_pairs={{0,1},{1,0},{2,3},{3,2},{4,6},{5,7},{6,4},{7,5},{8,9},{9,8},{10,11... | collective-permute-start | bytes 196616 | tf_op jit(solution)/shard_map/ppermute | solution.py:31
  32.3 8.1 %collective-permute-start.10 = (bf16[256,128]{1,0:T(8,128)(2,1)S(1)}, bf16[256,128]{1,0:T(8,128)(2,1)S(1)}, u32[]{:S(2)}, u32[]{:S(2)}) collective-permute-start(bf16[256,128]{1,0:T(8,128)(2,1)S(1)} %get-tuple-element.36), channel_id=1, source_target_pairs={{0,3},{1,2},{2,1},{3,0},{4,12},{5,13},{6,14},{7,15},{8,11},{9,10},... | collective-permute-start | bytes 196616 | tf_op jit(solution)/shard_map/ppermute | solution.py:31
  33.8 11.5 %collective-permute-start.17 = (bf16[128,1024]{1,0:T(8,128)(2,1)S(1)}, bf16[128,1024]{1,0:T(8,128)(2,1)S(1)}, u32[]{:S(2)}, u32[]{:S(2)}) collective-permute-start(bf16[128,1024]{1,0:T(8,128)(2,1)S(1)} %collective-permute-done.16.far_t), channel_id=1, source_target_pairs={{0,4},{4,0},{8,12},{12,8},{16,20},{20,16},{24,28},{28,24},{1,5},{5... | collective-permute-start | bytes 786440 | tf_op jit(solution)/shard_map/ppermute | solution.py:20
  39.9 5.5 %collective-permute-start.15 = (bf16[1024,128]{1,0:T(8,128)(2,1)S(1)}, bf16[1024,128]{1,0:T(8,128)(2,1)S(1)}, u32[]{:S(2)}, u32[]{:S(2)}) collective-permute-start(bf16[1024,128]{1,0:T(8,128)(2,1)S(1)} %collective-permute-done.14.came_ref), channel_id=1, source_target_pairs={{0,4},{4,0},{8,12},{12,8},{16,20},{20,16},{24,28},{28,24},{1,5},{5... | collective-permute-start | bytes 786440 | tf_op jit(solution)/shard_map/ppermute | solution.py:20
  39.9 1.6 %collective-permute-start.11 = (bf16[256,128]{1,0:T(8,128)(2,1)S(1)}, bf16[256,128]{1,0:T(8,128)(2,1)S(1)}, u32[]{:S(2)}, u32[]{:S(2)}) collective-permute-start(bf16[256,128]{1,0:T(8,128)(2,1)S(1)} %collective-permute-done.9.refs_1_), channel_id=1, source_target_pairs={{0,4},{4,0},{8,12},{12,8},{16,20},{20,16},{24,28},{28,24},{1,5},{5... | collective-permute-start | bytes 196616 | tf_op jit(solution)/shard_map/ppermute | solution.py:20
  40.4 1.3 %collective-permute-start.12 = (bf16[256,128]{1,0:T(8,128)(2,1)S(1)}, bf16[256,128]{1,0:T(8,128)(2,1)S(1)}, u32[]{:S(2)}, u32[]{:S(2)}) collective-permute-start(bf16[256,128]{1,0:T(8,128)(2,1)S(1)} %collective-permute-done.10.refs_2_), channel_id=1, source_target_pairs={{0,4},{4,0},{8,12},{12,8},{16,20},{20,16},{24,28},{28,24},{1,5},{5... | collective-permute-start | bytes 196616 | tf_op jit(solution)/shard_map/ppermute | solution.py:20
  46.2 4.5 %collective-permute-start.18 = (bf16[256,128]{1,0:T(8,128)(2,1)S(1)}, bf16[256,128]{1,0:T(8,128)(2,1)S(1)}, u32[]{:S(2)}, u32[]{:S(2)}) collective-permute-start(bf16[256,128]{1,0:T(8,128)(2,1)S(1)} %get-tuple-element.42.refs_0_), channel_id=1, source_target_pairs={{0,1},{1,0},{2,3},{3,2},{4,6},{5,7},{6,4},{7,5},{8,9},{9,8},{10,11... | collective-permute-start | bytes 196616 | tf_op jit(solution)/shard_map/ppermute | solution.py:31
  47.3 5.2 %collective-permute-start.19 = (bf16[256,128]{1,0:T(8,128)(2,1)S(1)}, bf16[256,128]{1,0:T(8,128)(2,1)S(1)}, u32[]{:S(2)}, u32[]{:S(2)}) collective-permute-start(bf16[256,128]{1,0:T(8,128)(2,1)S(1)} %get-tuple-element.43), channel_id=1, source_target_pairs={{0,3},{1,2},{2,1},{3,0},{4,20},{5,21},{6,22},{7,23},{8,11},{9,10},... | collective-permute-start | bytes 196616 | tf_op jit(solution)/shard_map/ppermute | solution.py:31
  49.6 5.7 %collective-permute-start.23 = (bf16[256,128]{1,0:T(8,128)(2,1)S(1)}, bf16[256,128]{1,0:T(8,128)(2,1)S(1)}, u32[]{:S(2)}, u32[]{:S(2)}) collective-permute-start(bf16[256,128]{1,0:T(8,128)(2,1)S(1)} %get-tuple-element.47), channel_id=1, source_target_pairs={{0,16},{4,20},{8,24},{12,28},{16,0},{20,4},{24,8},{28,12},{1,17},{... | collective-permute-start | bytes 196616 | tf_op jit(solution)/shard_map/ppermute | solution.py:20
  50.8 6.4 %collective-permute-start.20 = (bf16[256,128]{1,0:T(8,128)(2,1)S(1)}, bf16[256,128]{1,0:T(8,128)(2,1)S(1)}, u32[]{:S(2)}, u32[]{:S(2)}) collective-permute-start(bf16[256,128]{1,0:T(8,128)(2,1)S(1)} %collective-permute-done.18.refs_1_), channel_id=1, source_target_pairs={{0,4},{4,0},{8,12},{12,8},{16,20},{20,16},{24,28},{28,24},{1,5},{5... | collective-permute-start | bytes 196616 | tf_op jit(solution)/shard_map/ppermute | solution.py:20
  52.5 4.7 %collective-permute-start.21 = (bf16[256,128]{1,0:T(8,128)(2,1)S(1)}, bf16[256,128]{1,0:T(8,128)(2,1)S(1)}, u32[]{:S(2)}, u32[]{:S(2)}) collective-permute-start(bf16[256,128]{1,0:T(8,128)(2,1)S(1)} %collective-permute-done.19.refs_2_), channel_id=1, source_target_pairs={{0,4},{4,0},{8,12},{12,8},{16,20},{20,16},{24,28},{28,24},{1,5},{5... | collective-permute-start | bytes 196616 | tf_op jit(solution)/shard_map/ppermute | solution.py:20
  55.3 10.4 %collective-permute-start.24 = (bf16[256,128]{1,0:T(8,128)(2,1)S(1)}, bf16[256,128]{1,0:T(8,128)(2,1)S(1)}, u32[]{:S(2)}, u32[]{:S(2)}) collective-permute-start(bf16[256,128]{1,0:T(8,128)(2,1)S(1)} %collective-permute-done.23.refs_0_), channel_id=1, source_target_pairs={{0,4},{4,0},{8,12},{12,8},{16,20},{20,16},{24,28},{28,24},{1,5},{5... | collective-permute-start | bytes 196616 | tf_op jit(solution)/shard_map/ppermute | solution.py:20
  55.3 10.5 %collective-permute-start.25 = (bf16[256,128]{1,0:T(8,128)(2,1)S(1)}, bf16[256,128]{1,0:T(8,128)(2,1)S(1)}, u32[]{:S(2)}, u32[]{:S(2)}) collective-permute-start(bf16[256,128]{1,0:T(8,128)(2,1)S(1)} %collective-permute-done.23.refs_0_), channel_id=1, source_target_pairs={{0,8},{4,12},{8,0},{12,4},{16,24},{20,28},{24,16},{28,20},{1,9},{5... | collective-permute-start | bytes 196616 | tf_op jit(solution)/shard_map/ppermute | solution.py:20
  55.3 10.5 %collective-permute-start.26 = (bf16[256,128]{1,0:T(8,128)(2,1)S(1)}, bf16[256,128]{1,0:T(8,128)(2,1)S(1)}, u32[]{:S(2)}, u32[]{:S(2)}) collective-permute-start(bf16[256,128]{1,0:T(8,128)(2,1)S(1)} %collective-permute-done.23.refs_0_), channel_id=1, source_target_pairs={{0,12},{4,8},{8,4},{12,0},{16,28},{20,24},{24,20},{28,16},{1,13},{... | collective-permute-start | bytes 196616 | tf_op jit(solution)/shard_map/ppermute | solution.py:20
  57.4 4.5 %collective-permute-start.22 = (bf16[128,128]{1,0:T(8,128)(2,1)S(1)}, bf16[128,128]{1,0:T(8,128)(2,1)S(1)}, u32[]{:S(2)}, u32[]{:S(2)}) collective-permute-start(bf16[128,128]{1,0:T(8,128)(2,1)S(1)} %shard_map.56.refs_0_), channel_id=1, source_target_pairs={{0,8},{4,12},{8,0},{12,4},{16,24},{20,28},{24,16},{28,20},{1,9},{5... | collective-permute-start | bytes 98312 | tf_op jit(solution)/shard_map/ppermute | solution.py:20
